TPU v7x, 32 devices: a whole 2x2x4 slice. The times are simulated.
32 devices in a mesh: dp: 8 (over z, x), seq: 4 (over y, core).
Axes of the slice: x: 2, y: 2, z: 4, core: 2. Of those that a mesh axis runs over, the one named last changes fastest.
Arguments:
- tokens: bfloat16 [16384, 1024], P(('dp', 'seq')), may hold values from -6 to 6
- out_grad: bfloat16 [16384, 1024], P(('dp', 'seq')), may hold values from -6 to 6
- qkv_weight: bfloat16 [1024, 3072], P('dp'), may hold values from -0.25 to 0.25
- qv_bias: bfloat16 [2, 1024], P(None, 'dp'), may hold values from -3 to 3
- proj_weight: bfloat16 [1024, 1024], P('dp'), may hold values from -0.1875 to 0.1875
- fc1_weight: bfloat16 [1024, 4096], P('dp'), may hold values from -0.1875 to 0.1875
- fc1_bias: bfloat16 [4096], P('dp'), may hold values from -3 to 3
- fc2_weight: bfloat16 [4096, 1024], P('dp'), may hold values from -0.09375 to 0.09375
- out_bias: bfloat16 [2, 1024], P(None, 'dp'), may hold values from -3 to 3
- norm_gains: bfloat16 [4, 1024], P(None, 'dp'), may hold values from 0.5 to 1.5
- norm_shifts: bfloat16 [4, 1024], P(None, 'dp'), may hold values from -2 to 2
Outputs:
- layer_out: bfloat16 [16384, 1024], P(('dp', 'seq'))
- tokens_grad: bfloat16 [16384, 1024], P(('dp', 'seq'))
- qkv_weight_grad: float32 [1024, 3072], P('dp')
- qv_bias_grad: float32 [2, 1024], P(None, 'dp')
- proj_weight_grad: float32 [1024, 1024], P('dp')
- fc1_weight_grad: float32 [1024, 4096], P('dp')
- fc1_bias_grad: float32 [4096], P('dp')
- fc2_weight_grad: float32 [4096, 1024], P('dp')
- out_bias_grad: float32 [2, 1024], P(None, 'dp')
- norm_gains_grad: float32 [4, 1024], P(None, 'dp')
- norm_shifts_grad: float32 [4, 1024], P(None, 'dp')
All inputs are finite; a program needn't handle non-finite values.
Results may differ from a plain program's by a relative error of at most 0.015.
The roundings to bfloat16 on the way count: a program that leaves them out, or rounds other values in their place, can miss the bound.
Values may be sent and summed in bfloat16 or wider, within the bound.
No kernel may reach another device: no remote copies, remote signals or barrier semaphores. Data moves between devices by JAX's collectives and lax.ppermute only.
A program may use at most 192 MiB of HBM per device.

v0:
```python
from functools import partial
import math

import jax
import jax.numpy as jnp
from jax import lax
from jax.sharding import PartitionSpec as P

HEAD_DIM = 64


RELAX_ALPHA = 32.0
NORM_EPS = 1e-05


def layer_norm(values, gain_vec, shift_vec):
    centred = values - jnp.mean(values, axis=-1, keepdims=True)
    variance = jnp.mean(centred * centred, axis=-1, keepdims=True)
    return centred * lax.rsqrt(variance + NORM_EPS) * gain_vec + shift_vec


def contract_rows(left, right):
    return lax.dot_general(
        left, right, (((0,), (0,)), ((), ())), preferred_element_type=jnp.float32
    )


def contract_cols(left, right):
    return lax.dot_general(
        left, right, (((1,), (1,)), ((), ())), preferred_element_type=jnp.float32
    )


def norm_backward(values, gain_vec, shift_vec, upstream):
    unused_out, pullback = jax.vjp(layer_norm, values, gain_vec, shift_vec)
    return pullback(upstream)


def column_sums(values):
    return jnp.sum(values.astype(jnp.float32), axis=0)


def causal_logits(scores, block_start):
    row_index = block_start + lax.iota(jnp.int32, scores.shape[0])
    col_index = lax.iota(jnp.int32, scores.shape[1])
    return jnp.where(row_index[:, None] >= col_index[None, :], RELAX_ALPHA * scores, -1e30)


def block_layout(seq_len):
    block_rows = min(512, seq_len)
    return (block_rows, seq_len // block_rows)


def head_column(array, head_index):
    return lax.dynamic_index_in_dim(array, head_index, axis=1, keepdims=False)


def head_block(array, head_index, block_start, block_rows):
    piece = lax.dynamic_slice(
        array, (block_start, head_index, jnp.int32(0)), (block_rows, 1, array.shape[2])
    )
    return piece.reshape(block_rows, array.shape[2])


def scale_table():
    query_scale = 1.0 / (RELAX_ALPHA * math.sqrt(HEAD_DIM))
    return jnp.array([query_scale, 1.0, 1.0], jnp.float32)[:, None]


def gather_attention(qkv_weight, qv_bias, proj_weight, out_bias, norm_gains, norm_shifts):
    return (
        lax.all_gather(qkv_weight, "dp", axis=0, tiled=True),
        lax.all_gather(qv_bias, "dp", axis=1, tiled=True),
        lax.all_gather(proj_weight, "dp", axis=0, tiled=True),
        lax.all_gather(out_bias, "dp", axis=1, tiled=True),
        lax.all_gather(norm_gains, "dp", axis=1, tiled=True),
        lax.all_gather(norm_shifts, "dp", axis=1, tiled=True),
    )


def gather_mlp(fc1_weight, fc1_bias, fc2_weight):
    return (
        lax.all_gather(fc1_weight, "dp", axis=0, tiled=True),
        lax.all_gather(fc1_bias, "dp", axis=0, tiled=True),
        lax.all_gather(fc2_weight, "dp", axis=0, tiled=True),
    )


def run_forward(tokens, attn_full, mlp_full):
    qkv_w, qv_b, proj_w, out_b, gains_low, shifts_low = attn_full
    fc1_w, fc1_b, fc2_w = mlp_full
    gain_rows = gains_low.astype(jnp.float32)
    shift_rows = shifts_low.astype(jnp.float32)
    model_width = qkv_w.shape[0]
    tok_rows = tokens.shape[0]
    tok_vals = tokens.astype(jnp.float32)
    normed = layer_norm(tok_vals, gain_rows[0], shift_rows[0]).astype(jnp.bfloat16)
    mixed_cols = jnp.dot(normed, qkv_w, preferred_element_type=jnp.float32).reshape(
        tok_rows, 3, model_width
    )
    bias_rows = qv_b.astype(jnp.float32)
    bias_three = jnp.stack((bias_rows[0], jnp.zeros_like(bias_rows[0]), bias_rows[1]))
    stacked = ((mixed_cols + bias_three) * scale_table()).astype(jnp.bfloat16)
    by_heads = lax.all_to_all(stacked, "seq", split_axis=2, concat_axis=0, tiled=True)
    seq_len = by_heads.shape[0]
    local_heads = by_heads.shape[2] // HEAD_DIM
    head_split = by_heads.reshape(seq_len, 3, local_heads, HEAD_DIM)
    queries = head_split[:, 0]
    key_rows = head_split[:, 1]
    values = head_split[:, 2]
    block_rows, blocks = block_layout(seq_len)

    def one_block(step_index):
        head_index = step_index // blocks
        block_start = step_index % blocks * block_rows
        q_block = head_block(queries, head_index, block_start, block_rows)
        k_head = head_column(key_rows, head_index)
        v_head = head_column(values, head_index)
        scores = contract_cols(q_block, k_head)
        logits = causal_logits(scores, block_start)
        row_top = jnp.max(logits, axis=-1, keepdims=True)
        powers = jnp.exp(logits - row_top)
        row_total = jnp.sum(powers, axis=-1, keepdims=True)
        probs_low = (powers / row_total).astype(jnp.bfloat16)
        out_block = jnp.dot(probs_low, v_head, preferred_element_type=jnp.float32)
        return (out_block.astype(jnp.bfloat16), (row_top + jnp.log(row_total))[:, 0])

    out_blocks, lse_blocks = lax.map(one_block, lax.iota(jnp.int32, local_heads * blocks))
    attended_heads = (
        out_blocks.reshape(local_heads, seq_len, HEAD_DIM)
        .transpose(1, 0, 2)
        .reshape(seq_len, local_heads * HEAD_DIM)
    )
    attended = lax.all_to_all(attended_heads, "seq", split_axis=0, concat_axis=1, tiled=True)
    branch = jnp.dot(attended, proj_w, preferred_element_type=jnp.float32) + out_b[0].astype(
        jnp.float32
    )
    residual = tok_vals + layer_norm(branch, gain_rows[1], shift_rows[1])
    normed_two = layer_norm(residual, gain_rows[2], shift_rows[2]).astype(jnp.bfloat16)
    hidden = jnp.dot(normed_two, fc1_w, preferred_element_type=jnp.float32) + fc1_b.astype(
        jnp.float32
    )
    active = jax.nn.gelu(hidden, approximate=True).astype(jnp.bfloat16)
    second = jnp.dot(active, fc2_w, preferred_element_type=jnp.float32) + out_b[1].astype(
        jnp.float32
    )
    layer_out = residual + layer_norm(second, gain_rows[3], shift_rows[3])
    kept_state = (
        tok_vals,
        normed,
        queries,
        key_rows,
        values,
        lse_blocks,
        attended,
        branch,
        residual,
        normed_two,
        hidden,
        active,
        second,
    )
    return (layer_out, kept_state)


def per_device(
    tokens,
    out_grad,
    qkv_weight,
    qv_bias,
    proj_weight,
    fc1_weight,
    fc1_bias,
    fc2_weight,
    out_bias,
    norm_gains,
    norm_shifts,
):
    attn_full = gather_attention(
        qkv_weight, qv_bias, proj_weight, out_bias, norm_gains, norm_shifts
    )
    mlp_full = gather_mlp(fc1_weight, fc1_bias, fc2_weight)
    layer_out, kept_state = run_forward(tokens, attn_full, mlp_full)
    attn_full = gather_attention(
        qkv_weight, qv_bias, proj_weight, out_bias, norm_gains, norm_shifts
    )
    mlp_full = gather_mlp(fc1_weight, fc1_bias, fc2_weight)
    repeat_out, kept_state = run_forward(tokens, attn_full, mlp_full)
    qkv_w, qv_b, proj_w, out_b, gains_low, shifts_low = attn_full
    fc1_w, fc1_b, fc2_w = mlp_full
    gain_rows = gains_low.astype(jnp.float32)
    shift_rows = shifts_low.astype(jnp.float32)
    (
        tok_vals,
        normed,
        queries,
        key_rows,
        values,
        lse_blocks,
        attended,
        branch,
        residual,
        normed_two,
        hidden,
        active,
        second,
    ) = kept_state
    tok_rows = tok_vals.shape[0]
    model_width = qkv_w.shape[0]
    upstream = out_grad.astype(jnp.float32)
    d_second, grad_gain_three, grad_shift_three = norm_backward(
        second, gain_rows[3], shift_rows[3], upstream
    )
    d_second = d_second.astype(jnp.bfloat16)
    grad_fc2 = contract_rows(active, d_second)
    grad_bias_two = column_sums(d_second)
    d_active = contract_cols(d_second, fc2_w)
    unused_gelu, gelu_back = jax.vjp(partial(jax.nn.gelu, approximate=True), hidden)
    d_hidden = gelu_back(d_active)[0].astype(jnp.bfloat16)
    grad_fc1 = contract_rows(normed_two, d_hidden)
    grad_fc1_bias = column_sums(d_hidden)
    d_normed_two = contract_cols(d_hidden, fc1_w)
    d_resid_part, grad_gain_two, grad_shift_two = norm_backward(
        residual, gain_rows[2], shift_rows[2], d_normed_two
    )
    d_residual = upstream + d_resid_part
    d_branch, grad_gain_one, grad_shift_one = norm_backward(
        branch, gain_rows[1], shift_rows[1], d_residual
    )
    d_branch = d_branch.astype(jnp.bfloat16)
    grad_proj = contract_rows(attended, d_branch)
    grad_bias_one = column_sums(d_branch)
    d_attended = contract_cols(d_branch, proj_w).astype(jnp.bfloat16)
    seq_len = queries.shape[0]
    local_heads = queries.shape[1]
    block_rows, blocks = block_layout(seq_len)
    d_heads = lax.all_to_all(d_attended, "seq", split_axis=1, concat_axis=0, tiled=True).reshape(
        seq_len, local_heads, HEAD_DIM
    )
    zero_grad = jnp.zeros(queries.shape, jnp.float32)

    def back_step(grad_pair, step_index):
        key_grad, value_grad = grad_pair
        head_index = step_index // blocks
        block_start = step_index % blocks * block_rows
        q_block = head_block(queries, head_index, block_start, block_rows)
        d_block = head_block(d_heads, head_index, block_start, block_rows)
        k_head = head_column(key_rows, head_index)
        v_head = head_column(values, head_index)
        scores = contract_cols(q_block, k_head)
        probs = jnp.exp(causal_logits(scores, block_start) - lse_blocks[step_index][:, None])
        d_probs = contract_cols(d_block, v_head)
        row_delta = jnp.sum(probs * d_probs, axis=-1, keepdims=True)
        d_scores = (RELAX_ALPHA * probs * (d_probs - row_delta)).astype(jnp.bfloat16)
        query_grad = jnp.dot(d_scores, k_head, preferred_element_type=jnp.float32)
        key_add = contract_rows(d_scores, q_block)
        value_add = contract_rows(probs.astype(jnp.bfloat16), d_block)
        key_grad = lax.dynamic_update_index_in_dim(
            key_grad, head_column(key_grad, head_index) + key_add, head_index, 1
        )
        value_grad = lax.dynamic_update_index_in_dim(
            value_grad, head_column(value_grad, head_index) + value_add, head_index, 1
        )
        return ((key_grad, value_grad), query_grad.astype(jnp.bfloat16))

    (key_grad, value_grad), query_blocks = lax.scan(
        back_step, (zero_grad, zero_grad), lax.iota(jnp.int32, local_heads * blocks)
    )
    query_grad = query_blocks.reshape(local_heads, seq_len, HEAD_DIM).transpose(1, 0, 2)
    back_stack = jnp.stack(
        (query_grad, key_grad.astype(jnp.bfloat16), value_grad.astype(jnp.bfloat16)), axis=1
    ).reshape(seq_len, 3, local_heads * HEAD_DIM)
    back_tokens = lax.all_to_all(back_stack, "seq", split_axis=0, concat_axis=2, tiled=True)
    d_mixed = (
        (back_tokens.astype(jnp.float32) * scale_table())
        .astype(jnp.bfloat16)
        .reshape(tok_rows, 3 * model_width)
    )
    grad_qkv = contract_rows(normed, d_mixed)
    mixed_sums = column_sums(d_mixed).reshape(3, model_width)
    grad_qv_bias = jnp.stack((mixed_sums[0], mixed_sums[2]))
    d_normed = contract_cols(d_mixed, qkv_w)
    d_tok_part, grad_gain_zero, grad_shift_zero = norm_backward(
        tok_vals, gain_rows[0], shift_rows[0], d_normed
    )
    tokens_grad = (d_residual + d_tok_part).astype(jnp.bfloat16)
    grad_out_bias = jnp.stack((grad_bias_one, grad_bias_two))
    grad_gains = jnp.stack((grad_gain_zero, grad_gain_one, grad_gain_two, grad_gain_three))
    grad_shifts = jnp.stack((grad_shift_zero, grad_shift_one, grad_shift_two, grad_shift_three))
    owned = (
        lax.psum_scatter(grad_qkv, "dp", scatter_dimension=0, tiled=True),
        lax.psum_scatter(grad_qv_bias, "dp", scatter_dimension=1, tiled=True),
        lax.psum_scatter(grad_proj, "dp", scatter_dimension=0, tiled=True),
        lax.psum_scatter(grad_fc1, "dp", scatter_dimension=0, tiled=True),
        lax.psum_scatter(grad_fc1_bias, "dp", scatter_dimension=0, tiled=True),
        lax.psum_scatter(grad_fc2, "dp", scatter_dimension=0, tiled=True),
        lax.psum_scatter(grad_out_bias, "dp", scatter_dimension=1, tiled=True),
        lax.psum_scatter(grad_gains, "dp", scatter_dimension=1, tiled=True),
        lax.psum_scatter(grad_shifts, "dp", scatter_dimension=1, tiled=True),
    )
    totals = (
        lax.psum(owned[0].astype(jnp.bfloat16), "seq").astype(jnp.float32),
        lax.psum(owned[1].astype(jnp.bfloat16), "seq").astype(jnp.float32),
        lax.psum(owned[2].astype(jnp.bfloat16), "seq").astype(jnp.float32),
        lax.psum(owned[3].astype(jnp.bfloat16), "seq").astype(jnp.float32),
        lax.psum(owned[4].astype(jnp.bfloat16), "seq").astype(jnp.float32),
        lax.psum(owned[5].astype(jnp.bfloat16), "seq").astype(jnp.float32),
        lax.psum(owned[6].astype(jnp.bfloat16), "seq").astype(jnp.float32),
        lax.psum(owned[7].astype(jnp.bfloat16), "seq").astype(jnp.float32),
        lax.psum(owned[8].astype(jnp.bfloat16), "seq").astype(jnp.float32),
    )
    return (
        layer_out.astype(jnp.bfloat16),
        tokens_grad,
        totals[0],
        totals[1],
        totals[2],
        totals[3],
        totals[4],
        totals[5],
        totals[6],
        totals[7],
        totals[8],
    )


def solution(mesh):
    placed = (
        P(("dp", "seq"), None),
        P(("dp", "seq"), None),
        P("dp", None),
        P(None, "dp"),
        P("dp", None),
        P("dp", None),
        P("dp"),
        P("dp", None),
        P(None, "dp"),
        P(None, "dp"),
        P(None, "dp"),
    )
    return jax.shard_map(
        per_device,
        mesh=mesh,
        in_specs=placed,
        out_specs=(
            P(("dp", "seq"), None),
            P(("dp", "seq"), None),
            P("dp", None),
            P(None, "dp"),
            P("dp", None),
            P("dp", None),
            P("dp"),
            P("dp", None),
            P(None, "dp"),
            P(None, "dp"),
            P(None, "dp"),
        ),
        check_vma=False,
    )
```

profile of v0, /device:TPU:0, one launch (start us, length us, event | category | flops | bytes accessed | tf_op | source)
XLA Modules:
  0.0 2192.6 jit_solution(13262523268789830104)
XLA Ops:
  9.5 22.3 %all_gather.39 = bf16[2,1024]{1,0:T(2,128)(2,1)S(1)} all-gather(bf16[2,128]{1,0:T(2,128)(2,1)S(1)} %copy-done.48), channel_id=1, replica_groups=mesh['dp'=8,'seq'=4] {'dp'}, dimensions={1}, use_global_device_ids=true | all-gather | bytes 4608 | tf_op jit(solution)/shard_map/all_gather | solution.py:73
  31.8 16.7 all_gather.36
  48.5 18.3 all_gather.37
  69.3 42.9 %all-gather.6.cloned.1.call-done = bf16[1024,3072]{1,0:T(8,128)(2,1)} async-done(((bf16[128,3072]{1,0:T(8,128)(2,1)}), bf16[1024,3072]{1,0:T(8,128)(2,1)}) %all-gather.6.cloned.1.call-update) | async-done | bytes 6291472 | tf_op jit(solution)/shard_map/all_gather | solution.py:72
  112.2 5.9 fusion.95
  118.9 4.7 copy.51
  123.5 4.9 all-to-all-start
  129.0 47.6 %all-to-all-done = bf16[512,3,1024]{0,1,2:T(4,128)(2,1)} async-done(((bf16[512,3,1024]{0,1,2:T(4,128)(2,1)}), bf16[512,3,1024]{0,1,2:T(4,128)(2,1)}, u32[]{:S(2)}, u32[]{:S(2)}) %all-to-all-start) | async-done | bytes 3145760 | tf_op jit(solution)/shard_map/all_to_all | solution.py:104
  179.6 4.1 copy.53
  183.7 6.1 reshape.336
  194.1 119.6 %while.42 = (s32[]{:T(128)}, bf16[16,512,64]{1,2,0:T(8,128)(2,1)}, s32[16]{0:T(128)S(1)}, bf16[2048,4,64]{0,2,1:T(8,128)(2,1)}, bf16[2048,4,64]{0,2,1:T(8,128)(2...) while((s32[]{:T(128)}, bf16[16,512,64]{1,2,0:T(8,128)(2,1)}, ...), condition=%wide.region_5.6_spmd, body=%wide.region_2.5_spmd.sunk | while | flops 277904928 | bytes 13255076 | solution.py:128
  326.7 4.4 all-to-all-start.1
  332.2 174.0 %while.43 = (s32[]{:T(128)}, bf16[16,512,64]{1,2,0:T(8,128)(2,1)}, f32[16,512]{1,0:T(8,128)S(1)}, s32[16]{0:T(128)S(1)}, bf16[2048,4,64]{0,2,1:T(8,128)(2,1)}, /...) while((s32[]{:T(128)}, bf16[16,512,64]{1,2,0:T(8,128)(2,1)}, ...), condition=%wide.region_15.16_spmd, body=%wide.region_12.15_spmd.sunk | while | flops 277905440 | bytes 30042572 | solution.py:128
  339.3 4.4 fusion.172
  519.7 26.0 %all-gather = bf16[8,1,512]{2,1,0:T(2,128)(2,1)S(1)} all-gather(bf16[1,1,512]{2,1,0:T(2,128)(2,1)S(1)} %reshape.355), channel_id=1, replica_groups=mesh['dp'=8,'seq'=4] {'dp'}, dimensions={0}, use_global_device_ids=true | all-gather | bytes 9216 | tf_op jit(solution)/shard_map/all_gather | solution.py:84
  545.7 16.2 all_gather.41
  561.9 4.5 fusion.114
  567.4 4.1 add_reduce_fusion.1
  576.3 11.9 fusion.99
  588.2 12.5 add_reduce_fusion
  600.8 18.4 multiply_reduce_fusion.5
  619.3 4.1 fusion.84
  627.8 16.5 convert_reduce_fusion
  644.3 7.0 multiply_reduce_fusion.1
  666.2 10.6 all-to-all-done.3
  682.1 300.9 %while.44 = (s32[]{:T(128)}, f32[2048,4,64]{0,2,1:T(8,128)S(1)}, f32[2048,4,64]{0,2,1:T(8,128)}, bf16[16,512,64]{1,2,0:T(8,128)(2,1)}, s32[16]{0:T(128)S(1)}, /*...) while((s32[]{:T(128)}, f32[2048,4,64]{0,2,1:T(8,128)S(1)}, ...), condition=%wide.region_30.31_spmd, body=%wide.region_28.30_spmd.sunk | while | flops 682917888 | bytes 53564424 | solution.py:266
  690.3 4.1 multiply_reduce_fusion.12
  709.2 4.0 multiply_reduce_fusion.12
  747.0 4.0 multiply_reduce_fusion.12
  765.8 4.0 multiply_reduce_fusion.12
  990.2 4.8 copy.64
  995.0 5.0 all-to-all-start.4
  1000.2 48.1 %all-to-all-done.4 = bf16[2048,3,256]{2,1,0:T(4,128)(2,1)} async-done(((bf16[2048,3,256]{2,1,0:T(4,128)(2,1)}), bf16[2048,3,256]{2,1,0:T(4,128)(2,1)}, u32[]{:S(2)}, u32[]{:S(2)}) %all-to-all-start.4) | async-done | bytes 3145760 | tf_op jit(solution)/shard_map/all_to_all | solution.py:273
  1054.2 6.6 copy.66
  1066.1 6.9 fusion.93
  1074.6 10.4 fusion.98
  1086.3 15.5 fusion.100
  1103.6 6.9 fusion.102
  1120.5 157.8 %reduce-scatter.17.cloned.1.call-done = f32[128,3072]{1,0:T(8,128)} async-done(((f32[1024,3072]{1,0:T(8,128)}), f32[128,3072]{1,0:T(8,128)}) %reduce-scatter.17.cloned.1.call-update) | async-done | bytes 1572880 | tf_op jit(solution)/shard_map/reduce_scatter | solution.py:291
  1280.7 282.9 %reduce-scatter.21.cloned.1.call-done = f32[128,4096]{1,0:T(8,128)} async-done(((f32[1024,4096]{1,0:T(8,128)}), f32[128,4096]{1,0:T(8,128)}) %reduce-scatter.21.cloned.1.call-update) | async-done | bytes 2097168 | tf_op jit(solution)/shard_map/reduce_scatter | solution.py:294
  1566.3 282.8 %reduce-scatter.23.cloned.1.call-done = f32[512,1024]{1,0:T(8,128)} async-done(((f32[4096,1024]{1,0:T(8,128)}), f32[512,1024]{1,0:T(8,128)}) %reduce-scatter.23.cloned.1.call-update) | async-done | bytes 2097168 | tf_op jit(solution)/shard_map/reduce_scatter | solution.py:296
  1853.8 35.2 %all-reduce = bf16[4096]{0:T(1024)(128)(2,1)S(1)} all-reduce(f32[4096]{0:T(1024)S(1)} %get-tuple-element.399), channel_id=6, replica_groups=mesh['dp'=8,'seq'=4] {'dp'}, use_global_device_ids=true, to_apply=%region_43.44.clone | all-reduce | flops 4096 | bytes 24576
  1889.1 25.4 %reduce-scatter.27.cloned.1.call-done = f32[128,2]{1,0:T(8,128)} async-done(((f32[1024,2]{1,0:T(8,128)}), f32[128,2]{1,0:T(8,128)}) %reduce-scatter.27.cloned.1.call-update) | async-done | bytes 1040
  1918.7 60.5 %reduce-scatter.25.cloned.1.call-done = f32[128,2]{1,0:T(8,128)} async-done(((f32[1024,2]{1,0:T(8,128)}), f32[128,2]{1,0:T(8,128)}) %reduce-scatter.25.cloned.1.call-update) | async-done | bytes 1040
  1980.1 63.7 %reduce-scatter.31.cloned.1.call-done = f32[128,4]{1,0:T(8,128)} async-done(((f32[1024,4]{1,0:T(8,128)}), f32[128,4]{1,0:T(8,128)}) %reduce-scatter.31.cloned.1.call-update) | async-done | bytes 2064
  2044.7 63.2 %reduce-scatter.29.cloned.1.call-done = f32[128,4]{1,0:T(8,128)} async-done(((f32[1024,4]{1,0:T(8,128)}), f32[128,4]{1,0:T(8,128)}) %reduce-scatter.29.cloned.1.call-update) | async-done | bytes 2064
  2108.8 5.7 all-reduce.1
  2117.3 62.0 %all-reduce.5.cloned.1.call-done = (bf16[128,3072]{1,0:T(8,128)(2,1)}, bf16[128,1024]{1,0:T(8,128)(2,1)}, bf16[128,4096]{1,0:T(8,128)(2,1)}, bf16[512,1024]{1,0:T(8,128)(2,1)}) async-done(((bf16[128,3072]{1,0:T(8,128)(2,1)}, bf16[128,1024]{1,0:T(8,128)(2,1)}, bf16[128,4096]{1,0:T(8,128)(2,1)}, bf16[512,1024]{1,0:T(8,128)(2,1)}), (bf16[128,3072]{1,0:T(8,128)(2,1)}, bf16[128,1024]{1,0:T(8,128)(2,1)}, ...) | async-done | bytes 3145744 | tf_op jit(solution)/shard_map/psum | solution.py:302
  (660 shorter events, 555.1 us)
Async XLA Ops:
  7.2 24.6 %copy-start.45 = (bf16[4,128]{1,0:T(4,128)(2,1)S(1)}, bf16[4,128]{1,0:T(4,128)(2,1)}, u32[]{:S(2)}) copy-start(bf16[4,128]{1,0:T(4,128)(2,1)} %param.29) | copy-start | bytes 3076
  7.2 41.3 %copy-start.46 = (bf16[4,128]{1,0:T(4,128)(2,1)S(1)}, bf16[4,128]{1,0:T(4,128)(2,1)}, u32[]{:S(2)}) copy-start(bf16[4,128]{1,0:T(4,128)(2,1)} %param.30) | copy-start | bytes 3076
  7.2 59.6 %copy-start.2 = (bf16[512,1024]{1,0:T(8,128)(2,1)S(1)}, bf16[512,1024]{1,0:T(8,128)(2,1)}, u32[]{:S(2)}) copy-start(bf16[512,1024]{1,0:T(8,128)(2,1)} %param.20) | copy-start | bytes 3145732
  7.2 104.9 %all-gather.6.cloned.1.call-start = ((), (), s32[]{:S(2)}) async-start(), calls=%async_computation.13 | async-start | bytes 7077888 | tf_op jit(solution)/shard_map/all_gather | solution.py:72
  8.0 553.9 %all-gather.8.cloned.1.call-start = ((), (), s32[]{:S(2)}) async-start(), calls=%async_computation.14 | async-start | bytes 2359296 | tf_op jit(solution)/shard_map/all_gather | solution.py:74
  8.7 567.6 %all-gather.10.cloned.1.call-start = ((), (), s32[]{:S(2)}) async-start(), calls=%async_computation.15 | async-start | bytes 9437184 | tf_op jit(solution)/shard_map/all_gather | solution.py:83
  67.0 51.1 %copy-start.31 = (f32[512]{0:T(512)}, f32[512]{0:T(512)S(1)}, u32[]{:S(2)}) copy-start(f32[512]{0:T(512)S(1)} %broadcast_multiply_fusion.6) | copy-start | bytes 6148
  67.5 50.7 %copy-start.33 = (f32[512]{0:T(512)}, f32[512]{0:T(512)S(1)}, u32[]{:S(2)}) copy-start(f32[512]{0:T(512)S(1)} %fusion.89) | copy-start | bytes 6148
  68.7 49.4 %copy-start.29 = (f32[1,1024]{1,0:T(1,128)}, f32[1,1024]{1,0:T(1,128)S(1)}, u32[]{:S(2)}) copy-start(f32[1,1024]{1,0:T(1,128)S(1)} %get-tuple-element.431) | copy-start | bytes 12292
  69.3 48.8 %copy-start.43 = (f32[1,1024]{1,0:T(1,128)}, f32[1,1024]{1,0:T(1,128)S(1)}, u32[]{:S(2)}) copy-start(f32[1,1024]{1,0:T(1,128)S(1)} %get-tuple-element.435) | copy-start | bytes 12292
  112.2 6.0 copy-start.41
  123.5 53.1 %all-to-all-start = ((bf16[512,3,1024]{0,1,2:T(4,128)(2,1)}), bf16[512,3,1024]{0,1,2:T(4,128)(2,1)}, u32[]{:S(2)}, u32[]{:S(2)}) async-start(bf16[512,3,1024]{0,1,2:T(4,128)(2,1)} %copy.51), calls=%async_computation | async-start | bytes 8388608 | tf_op jit(solution)/shard_map/all_to_all | solution.py:104
  128.4 459.8 %all-gather.12.cloned.1.call-start = ((), (), s32[]{:S(2)}) async-start(), calls=%async_computation.16 | async-start | bytes 9437184 | tf_op jit(solution)/shard_map/all_gather | solution.py:85
  326.7 189.4 %all-to-all-start.1 = ((bf16[4,512,256]{1,2,0:T(8,128)(2,1)}), bf16[4,512,256]{1,2,0:T(8,128)(2,1)}, u32[]{:S(2)}, u32[]{:S(2)}) async-start(bf16[4,512,256]{1,2,0:T(8,128)(2,1)} %copy.56), calls=%async_computation.1 | async-start | bytes 2097152 | tf_op jit(solution)/shard_map/all_to_all | solution.py:134
  506.3 6.1 copy-start.13
  506.3 6.1 copy-start.18
  514.9 4.7 copy-start.47
  514.9 30.8 %copy-start.49 = (bf16[2,128]{1,0:T(2,128)(2,1)S(1)}, bf16[2,128]{1,0:T(2,128)(2,1)}, u32[]{:S(2)}) copy-start(bf16[2,128]{1,0:T(2,128)(2,1)} %param.28) | copy-start | bytes 1540
  516.1 50.3 %all-to-all-start.2 = ((bf16[4,512,256]{1,2,0:T(8,128)(2,1)}), bf16[4,512,256]{1,2,0:T(8,128)(2,1)S(1)}, u32[]{:S(2)}, u32[]{:S(2)}) async-start(bf16[4,512,256]{1,2,0:T(8,128)(2,1)} %copy.59), calls=%async_computation.2 | async-start | bytes 2097152 | tf_op jit(solution)/shard_map/all_to_all | solution.py:134
  600.8 18.4 copy-start.15
  600.8 18.5 copy-start.28
  619.2 4.2 copy-start.12
  627.0 17.4 slice-start
  627.8 16.5 copy-start.22
  627.8 16.5 copy-start.8
  627.8 16.5 slice-start.1
  657.5 5.3 copy-start.25
  658.8 18.0 all-to-all-start.3
  662.4 456.4 %reduce-scatter.19.cloned.1.call-start = ((), (), s32[]{:S(2)}) async-start(), calls=%async_computation.18 | async-start | bytes 4718592 | tf_op jit(solution)/shard_map/reduce_scatter | solution.py:293
  995.0 5.1 copy-start.42
  995.0 53.2 %all-to-all-start.4 = ((bf16[2048,3,256]{2,1,0:T(4,128)(2,1)}), bf16[2048,3,256]{2,1,0:T(4,128)(2,1)}, u32[]{:S(2)}, u32[]{:S(2)}) async-start(bf16[2048,3,256]{2,1,0:T(4,128)(2,1)} %copy.64), calls=%async_computation.4 | async-start | bytes 8388608 | tf_op jit(solution)/shard_map/all_to_all | solution.py:273
  1000.0 278.3 %reduce-scatter.17.cloned.1.call-start = ((), (), s32[]{:S(2)}) async-start(), calls=%async_computation.17 | async-start | bytes 14155776 | tf_op jit(solution)/shard_map/reduce_scatter | solution.py:291
  1060.8 5.3 copy-start.3
  1060.8 5.3 copy-start.30
  1060.8 5.3 copy-start.32
  1060.8 5.3 copy-start.34
  1060.8 5.3 copy-start.44
  1073.0 490.6 %reduce-scatter.21.cloned.1.call-start = ((), (), s32[]{:S(2)}) async-start(), calls=%async_computation.19 | async-start | bytes 18874368 | tf_op jit(solution)/shard_map/reduce_scatter | solution.py:294
  1085.1 764.1 %reduce-scatter.23.cloned.1.call-start = ((), (), s32[]{:S(2)}) async-start(), calls=%async_computation.20 | async-start | bytes 18874368 | tf_op jit(solution)/shard_map/reduce_scatter | solution.py:296
  1101.8 812.7 %reduce-scatter.27.cloned.1.call-start = ((), (), s32[]{:S(2)}) async-start(), calls=%async_computation.22 | async-start | bytes 589824
  1103.5 7.0 copy-start.36
  1103.5 875.7 %reduce-scatter.25.cloned.1.call-start = ((), (), s32[]{:S(2)}) async-start(), calls=%async_computation.21 | async-start | bytes 589824
  1110.5 6.1 copy-start.16
  1110.5 4.9 copy-start.40
  1115.4 928.4 %reduce-scatter.31.cloned.1.call-start = ((), (), s32[]{:S(2)}) async-start(), calls=%async_computation.24 | async-start | bytes 589824
  1116.6 991.3 %reduce-scatter.29.cloned.1.call-start = ((), (), s32[]{:S(2)}) async-start(), calls=%async_computation.23 | async-start | bytes 589824
  1118.7 1060.7 %all-reduce.5.cloned.1.call-start = ((), (), s32[]{:S(2)}) async-start(), calls=%async_computation.25 | async-start | bytes 6291456 | tf_op jit(solution)/shard_map/psum | solution.py:302
  1851.9 63.5 %copy-start.6 = (f32[512,1024]{1,0:T(8,128)S(1)}, f32[512,1024]{1,0:T(8,128)}, u32[]{:S(2)}) copy-start(f32[512,1024]{1,0:T(8,128)} %copy-done.5) | copy-start | bytes 6291460
  (53 other events, 136.9 us)
Sparse Core Ops, SparseCore 0:
  10.2 101.8 all-gather.5
  114.3 47.4 all-gather.7
  163.9 123.3 all-gather.9
  289.3 123.5 all-gather.11
  666.5 87.0 reduce-scatter.18
  1073.2 205.0 reduce-scatter.16
  1282.5 281.0 reduce-scatter.20
  1567.4 281.6 reduce-scatter.22
  1853.4 61.0 reduce-scatter.26
  1918.3 60.8 reduce-scatter.24
  1982.9 60.8 reduce-scatter.30
  2047.0 60.8 reduce-scatter.28
  2111.2 68.0 all-reduce.4
where the time goes:
time: 2210 us; the launch traced here: 2190 us
  waiting for transfers between devices  1150 us (52%)
  matrix products  473 us (21%)
  local copies, waits for them, and re-layouts  160 us (7%)
  loops' own time  148 us (7%)
  blocking collectives  140 us (6%)
  other arithmetic  82.7 us (4%)
  starting transfers between devices  22.9 us (1%)
    reduce_scatter x1, waiting for transfers between devices, per_device(): lax.psum_scatter(grad_fc1, 'dp', scatter_dimension=0, tiled=True)  283 us
    reduce_scatter x1, waiting for transfers between devices, per_device(): lax.psum_scatter(grad_fc2, 'dp', scatter_dimension=0, tiled=True)  283 us
    unnamed x17, waiting for transfers between devices  215 us
    dot_general x68, matrix products, contract_cols(): lax.dot_general(left, right, (((1,), (1,)), ((), ())), preferred_element_...  214 us
    reduce_scatter x1, waiting for transfers between devices, per_device(): lax.psum_scatter(grad_qkv, 'dp', scatter_dimension=0, tiled=True)  158 us
    dot_general x36, matrix products, contract_rows(): lax.dot_general(left, right, (((0,), (0,)), ((), ())), preferred_element_...  92.6 us
    dot_general x32, matrix products, one_block(): out_block = jnp.dot(probs_low, v_head, preferred_element_type=jnp.float32)  87.1 us
    another operation x2, loops' own time, run_forward(): lax.map(one_block, lax.iota(jnp.int32, local_heads * blocks))  84.9 us
  transfers between devices with their start and end apart: 18, of which 12 were waited for; matrix products, arithmetic and copies ran while one was open for 28% of the time, Pallas kernels for 0%

commit v1 on v0

v1 whole, which is shorter than its diff:
```python
import functools
import math

import jax
import jax.numpy as jnp
from jax.sharding import Mesh
from jax.sharding import PartitionSpec as P
from jax import lax
from jax.experimental import pallas as pl
from jax.experimental.pallas import tpu as pltpu
HD=64
RELAX=32.0
C2=RELAX*math.log2(math.e)
NEG=-1e30

def _nt(a,b):
    return lax.dot_general(a,b,(((1,),(1,)),((),())),preferred_element_type=jnp.float32)
def _nn(a,b):
    return lax.dot_general(a,b,(((1,),(0,)),((),())),preferred_element_type=jnp.float32)

def _tr(x):
    return jnp.transpose(x.astype(jnp.float32)).astype(jnp.bfloat16)

def fwd_kernel(q_ref,k_ref,v_ref,o_ref,ot_ref,lse_ref,vt_ref,*,nh,blk):
    seq=q_ref.shape[0]; w=nh*HD
    nb=seq//blk
    for b in range(nb):
        vt_ref[:,b*blk:(b+1)*blk]=_tr(v_ref[b*blk:(b+1)*blk,:])
    lane=lax.broadcasted_iota(jnp.int32,(1,w),1)//HD
    tri=lax.broadcasted_iota(jnp.int32,(blk,blk),0)<=lax.broadcasted_iota(jnp.int32,(blk,blk),1)
    def qstep(qb,_):
        q0=pl.multiple_of(qb*blk,blk)
        q=q_ref[pl.ds(q0,blk),:]
        qm=[jnp.where(lane==h,q,jnp.zeros_like(q)) for h in range(nh)]
        def kv(kb,carry,diag):
            k0=pl.multiple_of(kb*blk,blk)
            k=k_ref[pl.ds(k0,blk),:]
            out=[]
            for h in range(nh):
                m,l,acc=carry[3*h:3*h+3]
                s=_nt(k,qm[h])*C2
                if diag: s=jnp.where(tri,s,NEG)
                mn=jnp.maximum(m,jnp.max(s,axis=0,keepdims=True))
                a=jnp.exp2(m-mn)
                p=jnp.exp2(s-mn)
                l=l*a+jnp.sum(p,axis=0,keepdims=True)
                acc=acc*a+_nn(vt_ref[h*HD:(h+1)*HD,pl.ds(k0,blk)],p.astype(jnp.bfloat16))
                out+= [mn,l,acc]
            return tuple(out)
        init=[]
        for h in range(nh):
            init+=[jnp.full((1,blk),NEG,jnp.float32),jnp.zeros((1,blk),jnp.float32),jnp.zeros((HD,blk),jnp.float32)]
        c=kv(qb,tuple(init),True)
        c=lax.fori_loop(0,qb,lambda kb,cc: kv(kb,cc,False),c)
        for h in range(nh):
            m,l,acc=c[3*h:3*h+3]
            ot_ref[h*HD:(h+1)*HD,pl.ds(q0,blk)]=acc/l
            lse_ref[h:h+1,pl.ds(q0,blk)]=m+jnp.log2(l)
        o_ref[pl.ds(q0,blk),:]=jnp.transpose(ot_ref[:,pl.ds(q0,blk)]).astype(jnp.bfloat16)
        return 0
    lax.fori_loop(0,nb,qstep,0)

def attn_fwd(qkv, nh, blk=512):
    seq=qkv.shape[0]; w=nh*HD
    blk=min(blk,seq)
    vm=pl.BlockSpec(memory_space=pltpu.VMEM)
    return pl.pallas_call(functools.partial(fwd_kernel,nh=nh,blk=blk),
      grid=(1,),
      in_specs=[pl.BlockSpec((seq,w),lambda i,j=j:(0,j)) for j in range(3)],
      out_specs=[pl.BlockSpec((seq,w),lambda i:(0,0)),pl.BlockSpec((w,seq),lambda i:(0,0)),pl.BlockSpec((8,seq),lambda i:(0,0))],
      out_shape=[jax.ShapeDtypeStruct((seq,w),jnp.bfloat16),jax.ShapeDtypeStruct((w,seq),jnp.float32),jax.ShapeDtypeStruct((8,seq),jnp.float32)],
      scratch_shapes=[pltpu.VMEM((w,seq),jnp.bfloat16)],
      compiler_params=pltpu.CompilerParams(vmem_limit_bytes=48<<20),
      name="attn_fwd")(qkv,qkv,qkv)

def bwd_kernel(q_ref,k_ref,v_ref,do_ref,ot_ref,lse_ref,d_ref,kt_ref,dl_ref,dqt_ref,*,nh,blk):
    seq=q_ref.shape[0]; w=nh*HD
    nb=seq//blk
    for b in range(nb):
        sl=slice(b*blk,(b+1)*blk)
        kt_ref[:,sl]=_tr(k_ref[sl,:])
        dot_=jnp.transpose(do_ref[sl,:].astype(jnp.float32))
        pr=dot_*ot_ref[:,sl]
        for h in range(nh):
            dl_ref[h:h+1,sl]=jnp.sum(pr[h*HD:(h+1)*HD],axis=0,keepdims=True)
    dqt_ref[...]=jnp.zeros_like(dqt_ref)
    lane=lax.broadcasted_iota(jnp.int32,(1,w),1)//HD
    tri=lax.broadcasted_iota(jnp.int32,(blk,blk),0)<=lax.broadcasted_iota(jnp.int32,(blk,blk),1)
    def kstep(kb,_):
        k0=pl.multiple_of(kb*blk,blk)
        k=k_ref[pl.ds(k0,blk),:]
        v=v_ref[pl.ds(k0,blk),:]
        def qs(qb,carry,diag):
            dk,dv=carry
            q0=pl.multiple_of(qb*blk,blk)
            q=q_ref[pl.ds(q0,blk),:]
            do=do_ref[pl.ds(q0,blk),:]
            for h in range(nh):
                qm=jnp.where(lane==h,q,jnp.zeros_like(q))
                dom=jnp.where(lane==h,do,jnp.zeros_like(do))
                s=_nt(k,qm)
                dp=_nt(v,dom)
                p=jnp.exp2(s*C2-lse_ref[h:h+1,pl.ds(q0,blk)])
                if diag: p=jnp.where(tri,p,0.0)
                ds=(p*(dp-dl_ref[h:h+1,pl.ds(q0,blk)])).astype(jnp.bfloat16)
                dv=dv+_nn(p.astype(jnp.bfloat16),dom)
                dk=dk+_nn(ds,qm)
                dqt_ref[h*HD:(h+1)*HD,pl.ds(q0,blk)]+=_nn(kt_ref[h*HD:(h+1)*HD,pl.ds(k0,blk)],ds)
            return dk,dv
        z=jnp.zeros((blk,w),jnp.float32)
        c=qs(kb,(z,z),True)
        dk,dv=lax.fori_loop(kb+1,nb,lambda qb,cc: qs(qb,cc,False),c)
        d_ref[pl.ds(k0,blk),w:2*w]=(dk*RELAX).astype(jnp.bfloat16)
        d_ref[pl.ds(k0,blk),2*w:3*w]=dv.astype(jnp.bfloat16)
        return 0
    lax.fori_loop(0,nb,kstep,0)
    for b in range(nb):
        sl=slice(b*blk,(b+1)*blk)
        d_ref[sl,0:w]=(jnp.transpose(dqt_ref[:,sl])*(1.0/math.sqrt(HD))).astype(jnp.bfloat16)

def attn_bwd(qkv, do, ot, lse, nh, blk=512):
    seq=qkv.shape[0]; w=nh*HD
    blk=min(blk,seq)
    f=lambda s:pl.BlockSpec(s,lambda i:(0,0))
    return pl.pallas_call(functools.partial(bwd_kernel,nh=nh,blk=blk),
      grid=(1,),
      in_specs=[pl.BlockSpec((seq,w),lambda i,j=j:(0,j)) for j in range(3)]+[f((seq,w)),f((w,seq)),f((8,seq))],
      out_specs=f((seq,3*w)),
      out_shape=jax.ShapeDtypeStruct((seq,3*w),jnp.bfloat16),
      scratch_shapes=[pltpu.VMEM((w,seq),jnp.bfloat16),pltpu.VMEM((8,seq),jnp.float32),pltpu.VMEM((w,seq),jnp.float32)],
      compiler_params=pltpu.CompilerParams(vmem_limit_bytes=56<<20),
      name="attn_bwd")(qkv,qkv,qkv,do,ot,lse)


NORM_EPS = 1e-05
F32 = jnp.float32
BF16 = jnp.bfloat16
SWAP = [(0, 1), (1, 0)]
SEQ_AXES = ("y", "c")
DP_AXES = ("z", "x")


def layer_norm(values, gain_vec, shift_vec):
    centred = values - jnp.mean(values, axis=-1, keepdims=True)
    variance = jnp.mean(centred * centred, axis=-1, keepdims=True)
    return centred * lax.rsqrt(variance + NORM_EPS) * gain_vec + shift_vec


def contract_rows(left, right, out=F32):
    return lax.dot_general(
        left, right, (((0,), (0,)), ((), ())), preferred_element_type=F32
    ).astype(out)


def contract_cols(left, right):
    return lax.dot_general(left, right, (((1,), (1,)), ((), ())), preferred_element_type=F32)


def dot_halves(left, halves):
    return jnp.concatenate([jnp.dot(left, halves[i], preferred_element_type=F32) for i in range(2)], axis=1)


def back_halves(left, halves):
    half = halves.shape[2]
    return contract_cols(left[:, :half], halves[0]) + contract_cols(left[:, half:], halves[1])


def norm_backward(values, gain_vec, shift_vec, upstream):
    unused_out, pullback = jax.vjp(layer_norm, values, gain_vec, shift_vec)
    return pullback(upstream)


def column_sums(values):
    return jnp.sum(values.astype(F32), axis=0)


def add_low(a, b):
    return (a.astype(F32) + b.astype(F32)).astype(BF16)


def ring(n):
    return [(i, (i + 1) % n) for i in range(n)]


def gather_pieces(shard, by_core):
    rows, cols = shard.shape
    nz = lax.axis_size("z")
    cur = shard
    if by_core:
        cur = lax.dynamic_slice(shard, (0, lax.axis_index("c") * (cols // 2)), (rows, cols // 2))
    pieces = []
    for step in range(nz):
        if step > 0:
            cur = lax.ppermute(cur, "z", ring(nz))
        pair = [cur, lax.ppermute(cur, "x", SWAP)]
        pieces += pair
    if by_core:
        pieces += [lax.ppermute(piece, "c", SWAP) for piece in pieces]
    return pieces


def owner_of(index, nz, z, x):
    step, side = index // 2 % nz, index % 2
    return lax.rem(z + nz - step, nz) * 2 + (x if side == 0 else 1 - x)


def place_kernel(where_ref, *refs, nz):
    pieces, out, sems = refs[:-2], refs[-2], refs[-1]
    rows, half = pieces[0].shape
    z, x, c = where_ref[0], where_ref[1], where_ref[2]
    copies = []
    for i, piece in enumerate(pieces):
        row = pl.multiple_of(owner_of(i, nz, z, x) * rows, rows)
        side = c if i < 2 * nz else 1 - c
        copies.append(
            pltpu.make_async_copy(piece, out.at[side, pl.ds(row, rows), :], sems.at[i])
        )
    for copy in copies:
        copy.start()
    for copy in copies:
        copy.wait()


def here():
    return jnp.stack([lax.axis_index(a) for a in ("z", "x", "c")]).astype(jnp.int32)


def gather_weight(shard):
    rows, cols = shard.shape
    nz = lax.axis_size("z")
    pieces = gather_pieces(shard, True)
    return pl.pallas_call(
        functools.partial(place_kernel, nz=nz),
        grid_spec=pltpu.PrefetchScalarGridSpec(
            num_scalar_prefetch=1,
            grid=(1,),
            in_specs=[pl.BlockSpec(memory_space=pl.ANY)] * len(pieces),
            out_specs=pl.BlockSpec(memory_space=pltpu.VMEM),
            scratch_shapes=[pltpu.SemaphoreType.DMA((len(pieces),))],
        ),
        compiler_params=pltpu.CompilerParams(vmem_limit_bytes=40 << 20),
        out_shape=jax.ShapeDtypeStruct((2, 2 * nz * rows, cols // 2), BF16),
        name="place",
    )(here(), *pieces)


def gather_small(small, n_vec):
    nz = lax.axis_size("z")
    n, own = small.shape
    pieces = gather_pieces(small, False)
    z, x, unused_c = here()
    order = jnp.stack([owner_of(i, nz, z, x) for i in range(2 * nz)])
    stacked = jnp.stack(pieces).astype(F32)
    pick = (order[None, :] == jnp.arange(2 * nz)[:, None]).astype(F32)
    placed = jnp.einsum("oi,ird->ord", pick, stacked, precision=lax.Precision.HIGHEST)
    return placed


def reduce_grad(grad):
    all_rows, cols = grad.shape
    nz = lax.axis_size("z")
    z, x, c = (lax.axis_index(a) for a in ("z", "x", "c"))
    half = cols // 2
    rows = all_rows // (2 * nz)
    send = lax.dynamic_slice(grad, (0, (1 - c) * half), (all_rows, half))
    keep = lax.dynamic_slice(grad, (0, c * half), (all_rows, half))
    mine = add_low(keep, lax.ppermute(send, "c", SWAP)).reshape(nz, 2, rows, half)
    send = lax.dynamic_slice(mine, (0, 1 - x, 0, 0), (nz, 1, rows, half))[:, 0]
    keep = lax.dynamic_slice(mine, (0, x, 0, 0), (nz, 1, rows, half))[:, 0]
    got = lax.ppermute(send, "x", SWAP)

    def part(i):
        at = (i % nz, 0, 0)
        return add_low(
            lax.dynamic_slice(keep, at, (1, rows, half))[0],
            lax.dynamic_slice(got, at, (1, rows, half))[0],
        )

    cur = part(z - 1)
    for step in range(nz - 1):
        cur = add_low(lax.ppermute(cur, "z", ring(nz)), part(z - 2 - step))
    own = cur.astype(F32) + lax.ppermute(cur, "y", SWAP).astype(F32)
    low = own.astype(BF16)
    other = lax.ppermute(low, "c", SWAP)
    first = jnp.where(c == 0, low, other)
    second = jnp.where(c == 0, other, low)
    return jnp.concatenate((first, second), axis=1).astype(F32)


def reduce_small(grads):
    nz = lax.axis_size("z")
    z, x = lax.axis_index("z"), lax.axis_index("x")
    cur = grads.astype(BF16)
    for axis in ("c", "y"):
        cur = add_low(cur, lax.ppermute(cur, axis, SWAP))
    cur = cur.reshape((nz, 2) + cur.shape[1:])
    keep = lax.dynamic_index_in_dim(cur, x, 1, False)
    keep = add_low(keep, lax.ppermute(lax.dynamic_index_in_dim(cur, 1 - x, 1, False), "x", SWAP))
    cur = lax.dynamic_index_in_dim(keep, (z + nz - 1) % nz, 0, False)
    for step in range(nz - 1):
        own = lax.dynamic_index_in_dim(keep, (z + 2 * nz - 2 - step) % nz, 0, False)
        cur = add_low(lax.ppermute(cur, "z", ring(nz)), own)
    return cur.astype(F32)


def per_device(
    tokens,
    out_grad,
    qkv_weight,
    qv_bias,
    proj_weight,
    fc1_weight,
    fc1_bias,
    fc2_weight,
    out_bias,
    norm_gains,
    norm_shifts,
):
    n_dp = lax.axis_size("z") * lax.axis_size("x")
    n_seq = lax.axis_size("y") * lax.axis_size("c")
    width = tokens.shape[1]
    rows = tokens.shape[0]
    own = qv_bias.shape[1]
    grp = width // n_seq
    heads = grp // HD
    qkv_shard = (
        qkv_weight.reshape(-1, 3, n_seq, grp).transpose(0, 2, 1, 3).reshape(-1, 3 * width)
    )
    small = jnp.concatenate(
        (qv_bias, out_bias, norm_gains, norm_shifts, fc1_bias.reshape(-1, own)), axis=0
    )
    small = gather_small(small, 12)
    vecs = small[:, :12].transpose(1, 0, 2).reshape(12, width)
    qv_b, out_b, gain_rows, shift_rows = vecs[:2], vecs[2:4], vecs[4:8], vecs[8:12]
    fc1_b = small[:, 12:].reshape(-1)
    qkv_w = gather_weight(qkv_shard)
    proj_w = gather_weight(proj_weight)
    fc1_w = gather_weight(fc1_weight)
    fc2_w = gather_weight(fc2_weight)

    tok_vals = tokens.astype(F32)
    normed = layer_norm(tok_vals, gain_rows[0], shift_rows[0]).astype(BF16)
    bias_row = jnp.stack((qv_b[0], jnp.zeros_like(qv_b[0]), qv_b[1])).reshape(3, n_seq, grp)
    bias_row = bias_row.transpose(1, 0, 2).reshape(-1)
    scale = 1.0 / (RELAX * math.sqrt(HD))
    scale_row = jnp.tile(
        jnp.concatenate((jnp.full((grp,), scale, F32), jnp.ones((2 * grp,), F32))), n_seq
    )
    mixed = dot_halves(normed, qkv_w)
    stacked = ((mixed + bias_row) * scale_row).astype(BF16)
    by_heads = lax.all_to_all(stacked, SEQ_AXES, split_axis=1, concat_axis=0, tiled=True)
    out_heads, out_cols, lse = attn_fwd(by_heads, heads, 1024)
    attended = lax.all_to_all(out_heads, SEQ_AXES, split_axis=0, concat_axis=1, tiled=True)
    branch = dot_halves(attended, proj_w) + out_b[0]
    residual = tok_vals + layer_norm(branch, gain_rows[1], shift_rows[1])
    normed_two = layer_norm(residual, gain_rows[2], shift_rows[2]).astype(BF16)
    hidden = dot_halves(normed_two, fc1_w) + fc1_b
    active, gelu_back = jax.vjp(functools.partial(jax.nn.gelu, approximate=True), hidden)
    active = active.astype(BF16)
    second = dot_halves(active, fc2_w) + out_b[1]
    layer_out = residual + layer_norm(second, gain_rows[3], shift_rows[3])

    upstream = out_grad.astype(F32)
    d_second, grad_gain_three, grad_shift_three = norm_backward(
        second, gain_rows[3], shift_rows[3], upstream
    )
    d_second = d_second.astype(BF16)
    total_fc2 = reduce_grad(contract_rows(active, d_second, BF16))
    grad_bias_two = column_sums(d_second)
    d_active = back_halves(d_second, fc2_w)
    d_hidden = gelu_back(d_active)[0].astype(BF16)
    total_fc1 = reduce_grad(contract_rows(normed_two, d_hidden, BF16))
    grad_fc1_bias = column_sums(d_hidden)
    d_normed_two = back_halves(d_hidden, fc1_w)
    d_resid_part, grad_gain_two, grad_shift_two = norm_backward(
        residual, gain_rows[2], shift_rows[2], d_normed_two
    )
    d_residual = upstream + d_resid_part
    d_branch, grad_gain_one, grad_shift_one = norm_backward(
        branch, gain_rows[1], shift_rows[1], d_residual
    )
    d_branch = d_branch.astype(BF16)
    total_proj = reduce_grad(contract_rows(attended, d_branch, BF16))
    grad_bias_one = column_sums(d_branch)
    d_attended = back_halves(d_branch, proj_w).astype(BF16)
    d_heads = lax.all_to_all(d_attended, SEQ_AXES, split_axis=1, concat_axis=0, tiled=True)
    d_by_heads = attn_bwd(by_heads, d_heads, out_cols, lse, heads, 512)
    d_mixed = lax.all_to_all(d_by_heads, SEQ_AXES, split_axis=0, concat_axis=1, tiled=True)
    grad_qkv = contract_rows(normed, d_mixed, BF16)
    mixed_sums = column_sums(d_mixed).reshape(n_seq, 3, grp).transpose(1, 0, 2).reshape(3, width)
    d_normed = back_halves(d_mixed, qkv_w)
    d_tok_part, grad_gain_zero, grad_shift_zero = norm_backward(
        tok_vals, gain_rows[0], shift_rows[0], d_normed
    )
    tokens_grad = (d_residual + d_tok_part).astype(BF16)
    vec_grads = jnp.stack(
        (
            mixed_sums[0],
            mixed_sums[2],
            grad_bias_one,
            grad_bias_two,
            grad_gain_zero,
            grad_gain_one,
            grad_gain_two,
            grad_gain_three,
            grad_shift_zero,
            grad_shift_one,
            grad_shift_two,
            grad_shift_three,
        )
    )
    small_grads = jnp.concatenate(
        (
            vec_grads.reshape(12, n_dp, own).transpose(1, 0, 2),
            grad_fc1_bias.reshape(n_dp, -1, own),
        ),
        axis=1,
    )
    n_small = small_grads.shape[1]
    total_qkv = reduce_grad(grad_qkv)
    total_small = reduce_small(small_grads)
    total_qkv = total_qkv.reshape(-1, n_seq, 3, grp).transpose(0, 2, 1, 3).reshape(-1, 3 * width)
    return (
        layer_out.astype(BF16),
        tokens_grad,
        total_qkv,
        total_small[0:2],
        total_proj,
        total_fc1,
        total_small[12:n_small].reshape(-1),
        total_fc2,
        total_small[2:4],
        total_small[4:8],
        total_small[8:12],
    )


def solution(mesh):
    n_dp, n_seq = mesh.devices.shape
    fine = Mesh(mesh.devices.reshape(n_dp // 2, 2, n_seq // 2, 2), DP_AXES + SEQ_AXES)
    tok = P(DP_AXES + SEQ_AXES, None)
    by_row = P(DP_AXES, None)
    by_col = P(None, DP_AXES)
    weights = (by_row, by_col, by_row, by_row, P(DP_AXES), by_row, by_col, by_col, by_col)
    return jax.shard_map(
        per_device,
        mesh=fine,
        in_specs=(tok, tok) + weights,
        out_specs=(tok, tok) + weights,
        check_vma=False,
    )
```

time: 2210 us -> 688 us (0.31)
  waiting for transfers between devices: 1150 us -> 252 us
  matrix products: 473 us -> 92.9 us
  loops' own time: 148 us -> 0 us
  blocking collectives: 140 us -> 0 us
  Pallas kernels: 0 us -> 75.3 us
  starting transfers between devices: 22.9 us -> 90 us
  local copies, waits for them, and re-layouts: 160 us -> 93.8 us
    reduce_scatter x4 -> x0, waiting for transfers between devices: 724 us -> none  [the longest x1 283 us: per_device(): lax.psum_scatter(grad_fc1, 'dp', scatter_dimension=0, tiled=True)]
    ppermute x0 -> x101, waiting for transfers between devices: none -> 252 us  [the longest x4 70.4 us: reduce_grad(): got = lax.ppermute(send, 'x', SWAP)]
    unnamed x17 -> x0, waiting for transfers between devices: 215 us -> none
    dot_general x68 -> x8, matrix products: 214 us -> 40.8 us  [contract_cols(): lax.dot_general(left, right, (((1,), (1,)), ((), ())), preferred_element_...]
    another operation x3 -> x0, loops' own time: 148 us -> none  [the longest x2 84.9 us: run_forward(): lax.map(one_block, lax.iota(jnp.int32, local_heads * blocks))]
    dot_general x54 -> x9, matrix products: 167 us -> 24.7 us  [the longest x8 24.6 us: dot_halves(): jnp.dot(left, halves[i], preferred_element_type=F32)]
    all_to_all x5 -> x4, waiting for transfers between devices: 106 us -> 0.01 us  [the longest x1 0.01 us: per_device(): lax.all_to_all(stacked, SEQ_AXES, split_axis=1, concat_axis=0, tiled=True)]
    all_gather x5 -> x0, blocking collectives: 99.4 us -> none  [the longest x1 26 us: gather_mlp(): lax.all_gather(fc1_bias, 'dp', axis=0, tiled=True)]
  transfers between devices with their start and end apart: 18 -> 105, of which waited for: 12 -> 40; matrix products, arithmetic and copies ran while one was open for 28% -> 21% of each run, Pallas kernels for 0% -> 11%
where the time goes in v1:
time: 688 us; the launch traced here: 676 us
  waiting for transfers between devices  252 us (37%)
  local copies, waits for them, and re-layouts  93.8 us (14%)
  matrix products  92.9 us (14%)
  starting transfers between devices  90 us (13%)
  Pallas kernels  75.3 us (11%)
  other arithmetic  69.4 us (10%)
    ppermute x4, waiting for transfers between devices, reduce_grad(): got = lax.ppermute(send, 'x', SWAP)  70.4 us
    ppermute x12, waiting for transfers between devices, reduce_grad(): cur = add_low(lax.ppermute(cur, 'z', ring(nz)), part(z - 2 - step))  63.7 us
    unnamed x272, local copies, waits for them, and re-layouts  54 us
    ppermute x20, waiting for transfers between devices, gather_pieces(): pair = [cur, lax.ppermute(cur, 'x', SWAP)]  43.2 us
    dot_general x8, matrix products, contract_cols(): lax.dot_general(left, right, (((1,), (1,)), ((), ())), preferred_element_...  40.8 us
    ppermute x15, waiting for transfers between devices, gather_pieces(): cur = lax.ppermute(cur, 'z', ring(nz))  40.6 us
    pallas_call x1, Pallas kernels, attn_bwd(): pl.pallas_call(functools.partial(bwd_kernel, nh=nh, blk=blk), grid=(1,),...  36.6 us
    convert_element_type x25, other arithmetic, add_low(): return (a.astype(F32) + b.astype(F32)).astype(BF16)  36.1 us
  transfers between devices with their start and end apart: 105, of which 40 were waited for; matrix products, arithmetic and copies ran while one was open for 21% of the time, Pallas kernels for 11%

profile of v1, /device:TPU:0, one launch (start us, length us, event | category | flops | bytes accessed | tf_op | source)
XLA Modules:
  0.0 676.3 jit_solution(2154378515431896420)
XLA Ops:
  14.0 6.7 collective-permute-done.8.refs_2_
  24.2 7.7 %collective-permute-done.3 = bf16[16,128]{1,0:T(8,128)(2,1)S(1)} collective-permute-done((bf16[16,128]{1,0:T(8,128)(2,1)S(1)}, bf16[16,128]{1,0:T(8,128)(2,1)S(1)}, u32[]{:S(2)}, u32[]{:S(2)}) %collective-permute-start.3) | collective-permute-done | bytes 4128 | tf_op jit(solution)/shard_map/ppermute | solution.py:194
  58.2 7.8 %collective-permute-done.11.refs_5_ = bf16[128,1536]{1,0:T(8,128)(2,1)} collective-permute-done((bf16[128,1536]{1,0:T(8,128)(2,1)S(1)}, bf16[128,1536]{1,0:T(8,128)(2,1)}, u32[]{:S(2)}, u32[]{:S(2)}) %collective-permute-start.11) | collective-permute-done | bytes 393248 | tf_op jit(solution)/shard_map/ppermute | solution.py:195
  66.0 7.5 %collective-permute-done.13.refs_7_ = bf16[128,1536]{1,0:T(8,128)(2,1)} collective-permute-done((bf16[128,1536]{1,0:T(8,128)(2,1)}, bf16[128,1536]{1,0:T(8,128)(2,1)}, u32[]{:S(2)}, u32[]{:S(2)}) %collective-permute-start.13) | collective-permute-done | bytes 393248 | tf_op jit(solution)/shard_map/ppermute | solution.py:195
  88.1 4.7 copy.331
  92.7 6.1 fusion.61
  98.8 4.7 copy.329
  103.5 4.5 fusion.63
  119.7 4.7 all-to-all-start
  127.7 8.1 %collective-permute-done.28.refs_7_ = bf16[128,512]{1,0:T(8,128)(2,1)S(1)} collective-permute-done((bf16[128,512]{1,0:T(8,128)(2,1)}, bf16[128,512]{1,0:T(8,128)(2,1)S(1)}, u32[]{:S(2)}, u32[]{:S(2)}) %collective-permute-start.28) | collective-permute-done | bytes 131104 | tf_op jit(solution)/shard_map/ppermute | solution.py:195
  145.0 6.2 collective-permute-done.39.refs_3_
  158.0 4.1 collective-permute-done.54.refs_3_
  163.1 5.1 collective-permute-done.55.refs_4_
  172.3 6.2 collective-permute-done.42.refs_6_
  182.6 6.4 collective-permute-done.57.refs_6_
  193.3 19.2 %attn_fwd.1 = (bf16[2048,256]{1,0:T(8,128)(2,1)S(1)}, f32[256,2048]{1,0:T(8,128)S(1)}, f32[8,2048]{1,0:T(8,128)S(1)}) custom-call(bf16[2048,768]{1,0:T(8,128)(2,1)} %bitcast.38.q_ref.k_ref.v_ref, bf16[2048,768]{1,0:T(8,128)(2,1)} %bitcast.38.q_ref.k_ref.v_ref, bf16[2048,768]{1,0:T(8,128)(2,1)} %bitcast.38.q_ref.k_ref.v_ref), custom_call_target="tpu_custom_call" | custom-call | tf_op jit(solution)/shard_map/attn_fwd/pallas_call | solution.py:67
  215.9 4.6 all-to-all-start.1
  239.1 5.8 place.6
  245.1 6.7 place.7
  279.1 5.8 fusion.14
  284.9 14.0 %fusion.113 = (bf16[4096]{0:T(1024)(128)(2,1)S(1)}, bf16[512,4096]{1,0:T(8,128)(2,1)}) fusion(f32[4096]{0:T(1024)S(1)} %bitcast.348, f32[512,2048]{1,0:T(8,128)} %copy-done.72, f32[512,2048]{1,0:T(8,128)} %copy-done.73, f32[512,4096]{1,0:T(8,128)} %fusion.14, bf16[2,4096,512]{2,1,0:T(8,128)(2,1)} %place.7, bf16[512,1024]{0,1:T(8,128)(2,1)S(1)} %get-tuple-element.133), kind=kOutput, calls=%fused_computation.266 | convolution fusion | flops 2197811200 | bytes 25714688 | tf_op jit(solution)/shard_map/dot_general | solution.py:156
  298.9 5.3 fusion.11
  304.3 4.8 fusion.104
  332.3 6.6 collective-permute-done.81
  340.4 9.5 %convolution_convert_fusion.1 = bf16[1024,4096]{1,0:T(8,128)(2,1)} fusion(bf16[512,4096]{1,0:T(8,128)(2,1)} %get-tuple-element.178, f32[512,1024]{0,1:T(8,128)S(1)} %copy-done.68, f32[1024]{0:T(1024)S(1)} %get-tuple-element.157, f32[1024]{0:T(1024)S(1)} %get-tuple-element.158, f32[512]{0:T(512)S(1)} %fusion.97, f32[512]{0:T(512)S(1)} %broadcast_multiply_fusion.1), kind=kOutput, calls=%fused_computation.14 | convolution fusion | flops 4301783040 | bytes 14692352 | tf_op jit(solution)/shard_map/dot_general | solution.py:150
  350.9 36.6 %attn_bwd.1 = bf16[2048,768]{1,0:T(8,128)(2,1)} custom-call(bf16[2048,768]{1,0:T(8,128)(2,1)} %bitcast.38.q_ref.k_ref.v_ref, bf16[2048,768]{1,0:T(8,128)(2,1)} %bitcast.38.q_ref.k_ref.v_ref, bf16[2048,768]{1,0:T(8,128)(2,1)} %bitcast.38.q_ref.k_ref.v_ref, bf16[2048,256]{1,0:T(8,128)(2,1)} %bitcast.335, f32[256,2048]{1,0:T(8,128)} %copy-done.3, ...), custom_call_target="tpu_custom_call" | custom-call | tf_op jit(solution)/shard_map/attn_bwd/pallas_call | solution.py:125
  387.5 4.7 copy.308
  392.2 4.8 all-to-all-start.3
  400.7 9.1 %convolution_convert_fusion = bf16[4096,1024]{1,0:T(8,128)(2,1)} fusion(bf16[512,4096]{1,0:T(8,128)(2,1)} %copy-done.84, bf16[512,1024]{0,1:T(8,128)(2,1)S(1)} %copy-done.90), kind=kOutput, calls=%fused_computation.13 | convolution fusion | flops 4299161600 | bytes 13631488 | tf_op jit(solution)/shard_map/dot_general | solution.py:150
  421.0 4.6 constant_dynamic-slice_fusion
  425.6 11.1 %collective-permute-done.85 = bf16[128,512]{1,0:T(8,128)(2,1)S(1)} collective-permute-done((bf16[128,512]{1,0:T(8,128)(2,1)S(1)}, bf16[128,512]{1,0:T(8,128)(2,1)S(1)}, u32[]{:S(2)}, u32[]{:S(2)}) %collective-permute-start.85) | collective-permute-done | bytes 131104 | tf_op jit(solution)/shard_map/ppermute | solution.py:282
  436.8 4.3 fusion.16
  441.2 5.0 fusion.106
  453.2 5.9 convolution_convert_fusion.2
  463.1 4.6 add_convert_fusion.1
  472.4 4.0 add_convert_fusion
  484.9 4.7 collective-permute-done.78
  496.2 23.0 %collective-permute-done.88 = bf16[4,128,2048]{2,1,0:T(8,128)(2,1)} collective-permute-done((bf16[4,128,2048]{2,1,0:T(8,128)(2,1)}, bf16[4,128,2048]{2,1,0:T(8,128)(2,1)}, u32[]{:S(2)}, u32[]{:S(2)}) %collective-permute-start.88) | collective-permute-done | bytes 2097184 | tf_op jit(solution)/shard_map/ppermute | solution.py:270
  523.0 40.8 %collective-permute-done.95 = bf16[4,512,512]{2,1,0:T(8,128)(2,1)} collective-permute-done((bf16[4,512,512]{2,1,0:T(8,128)(2,1)S(1)}, bf16[4,512,512]{2,1,0:T(8,128)(2,1)}, u32[]{:S(2)}, u32[]{:S(2)}) %collective-permute-start.95) | collective-permute-done | bytes 2097184 | tf_op jit(solution)/shard_map/ppermute | solution.py:270
  567.7 3.7 add_convert_fusion.2
  576.6 4.1 collective-permute-done.96
  587.3 12.6 %collective-permute-done.97 = bf16[512,512]{1,0:T(8,128)(2,1)} collective-permute-done((bf16[512,512]{1,0:T(8,128)(2,1)}, bf16[512,512]{1,0:T(8,128)(2,1)}, u32[]{:S(2)}, u32[]{:S(2)}) %collective-permute-start.97) | collective-permute-done | bytes 524320 | tf_op jit(solution)/shard_map/ppermute | solution.py:281
  601.5 9.5 %collective-permute-done.90 = bf16[128,2048]{1,0:T(8,128)(2,1)S(1)} collective-permute-done((bf16[128,2048]{1,0:T(8,128)(2,1)}, bf16[128,2048]{1,0:T(8,128)(2,1)S(1)}, u32[]{:S(2)}, u32[]{:S(2)}) %collective-permute-start.90) | collective-permute-done | bytes 524320 | tf_op jit(solution)/shard_map/ppermute | solution.py:281
  613.7 8.5 %collective-permute-done.98 = bf16[512,512]{1,0:T(8,128)(2,1)S(1)} collective-permute-done((bf16[512,512]{1,0:T(8,128)(2,1)S(1)}, bf16[512,512]{1,0:T(8,128)(2,1)S(1)}, u32[]{:S(2)}, u32[]{:S(2)}) %collective-permute-start.98) | collective-permute-done | bytes 524320 | tf_op jit(solution)/shard_map/ppermute | solution.py:281
  625.2 8.3 %collective-permute-done.91 = bf16[128,2048]{1,0:T(8,128)(2,1)S(1)} collective-permute-done((bf16[128,2048]{1,0:T(8,128)(2,1)S(1)}, bf16[128,2048]{1,0:T(8,128)(2,1)S(1)}, u32[]{:S(2)}, u32[]{:S(2)}) %collective-permute-start.91) | collective-permute-done | bytes 524320 | tf_op jit(solution)/shard_map/ppermute | solution.py:281
  645.0 6.9 %collective-permute-done.70 = bf16[128,1536]{0,1:T(8,128)(2,1)S(1)} collective-permute-done((bf16[128,1536]{0,1:T(8,128)(2,1)S(1)}, bf16[128,1536]{0,1:T(8,128)(2,1)S(1)}, u32[]{:S(2)}, u32[]{:S(2)}) %collective-permute-start.70) | collective-permute-done | bytes 393248 | tf_op jit(solution)/shard_map/ppermute | solution.py:281
  654.8 8.2 %collective-permute-done.71 = bf16[128,1536]{0,1:T(8,128)(2,1)S(1)} collective-permute-done((bf16[128,1536]{0,1:T(8,128)(2,1)S(1)}, bf16[128,1536]{0,1:T(8,128)(2,1)S(1)}, u32[]{:S(2)}, u32[]{:S(2)}) %collective-permute-start.71) | collective-permute-done | bytes 393248 | tf_op jit(solution)/shard_map/ppermute | solution.py:281
  665.8 6.2 collective-permute-done.72
  (594 shorter events, 269.1 us)
Async XLA Ops:
  2.2 30.3 %collective-permute-start = (bf16[16,128]{1,0:T(8,128)(2,1)S(1)}, bf16[16,128]{1,0:T(8,128)(2,1)S(1)}, u32[]{:S(2)}, u32[]{:S(2)}) collective-permute-start(bf16[16,128]{1,0:T(8,128)(2,1)S(1)} %concatenate.40), channel_id=1, source_target_pairs={{0,4},{4,0},{1,5},{5,1},{2,6},{6,2},{3,7},{7,3},{8,12},{12,8},{9,1... | collective-permute-start | bytes 12296 | tf_op jit(solution)/shard_map/ppermute | solution.py:195
  20.7 18.7 %collective-permute-start.10 = (bf16[128,1536]{1,0:T(8,128)(2,1)S(1)}, bf16[128,1536]{1,0:T(8,128)(2,1)S(1)}, u32[]{:S(2)}, u32[]{:S(2)}) collective-permute-start(bf16[128,1536]{1,0:T(8,128)(2,1)S(1)} %collective-permute-done.8.refs_2_), channel_id=1, source_target_pairs={{0,8},{8,16},{16,24},{24,0},{1,9},{9,17},{17,25},{25,1},{2,10},{10... | collective-permute-start | bytes 1179656 | tf_op jit(solution)/shard_map/ppermute | solution.py:194
  32.5 20.9 %collective-permute-start.7 = (bf16[128,1536]{1,0:T(8,128)(2,1)S(1)}, bf16[128,1536]{1,0:T(8,128)(2,1)S(1)}, u32[]{:S(2)}, u32[]{:S(2)}) collective-permute-start(bf16[128,1536]{1,0:T(8,128)(2,1)S(1)} %copy.332.refs_0_), channel_id=1, source_target_pairs={{0,4},{4,0},{1,5},{5,1},{2,6},{6,2},{3,7},{7,3},{8,12},{12,8},{9,1... | collective-permute-start | bytes 1179656 | tf_op jit(solution)/shard_map/ppermute | solution.py:195
  34.0 19.9 %collective-permute-start.14 = (bf16[128,1536]{1,0:T(8,128)(2,1)S(1)}, bf16[128,1536]{1,0:T(8,128)(2,1)}, u32[]{:S(2)}, u32[]{:S(2)}) collective-permute-start(bf16[128,1536]{1,0:T(8,128)(2,1)S(1)} %copy.332.refs_0_), channel_id=1, source_target_pairs={{0,1},{1,0},{2,3},{3,2},{4,5},{5,4},{6,7},{7,6},{8,9},{9,8},{10,11... | collective-permute-start | bytes 1179656 | tf_op jit(solution)/shard_map/ppermute | solution.py:198
  54.4 19.1 %collective-permute-start.13 = (bf16[128,1536]{1,0:T(8,128)(2,1)}, bf16[128,1536]{1,0:T(8,128)(2,1)}, u32[]{:S(2)}, u32[]{:S(2)}) collective-permute-start(bf16[128,1536]{1,0:T(8,128)(2,1)} %collective-permute-done.12.refs_6_), channel_id=1, source_target_pairs={{0,4},{4,0},{1,5},{5,1},{2,6},{6,2},{3,7},{7,3},{8,12},{12,8},{9,1... | collective-permute-start | bytes 1179656 | tf_op jit(solution)/shard_map/ppermute | solution.py:195
  56.1 19.3 %collective-permute-start.18 = (bf16[128,1536]{1,0:T(8,128)(2,1)S(1)}, bf16[128,1536]{1,0:T(8,128)(2,1)}, u32[]{:S(2)}, u32[]{:S(2)}) collective-permute-start(bf16[128,1536]{1,0:T(8,128)(2,1)S(1)} %collective-permute-done.10.refs_4_), channel_id=1, source_target_pairs={{0,1},{1,0},{2,3},{3,2},{4,5},{5,4},{6,7},{7,6},{8,9},{9,8},{10,11... | collective-permute-start | bytes 1179656 | tf_op jit(solution)/shard_map/ppermute | solution.py:198
  56.9 17.9 %collective-permute-start.17 = (bf16[128,1536]{1,0:T(8,128)(2,1)}, bf16[128,1536]{1,0:T(8,128)(2,1)}, u32[]{:S(2)}, u32[]{:S(2)}) collective-permute-start(bf16[128,1536]{1,0:T(8,128)(2,1)} %collective-permute-done.9.refs_3_), channel_id=1, source_target_pairs={{0,1},{1,0},{2,3},{3,2},{4,5},{5,4},{6,7},{7,6},{8,9},{9,8},{10,11... | collective-permute-start | bytes 1179656 | tf_op jit(solution)/shard_map/ppermute | solution.py:198
  58.1 18.1 %collective-permute-start.20 = (bf16[128,1536]{1,0:T(8,128)(2,1)}, bf16[128,1536]{1,0:T(8,128)(2,1)}, u32[]{:S(2)}, u32[]{:S(2)}) collective-permute-start(bf16[128,1536]{1,0:T(8,128)(2,1)} %collective-permute-done.12.refs_6_), channel_id=1, source_target_pairs={{0,1},{1,0},{2,3},{3,2},{4,5},{5,4},{6,7},{7,6},{8,9},{9,8},{10,11... | collective-permute-start | bytes 1179656 | tf_op jit(solution)/shard_map/ppermute | solution.py:198
  74.8 28.6 %collective-permute-start.29 = (bf16[128,512]{1,0:T(8,128)(2,1)S(1)}, bf16[128,512]{1,0:T(8,128)(2,1)S(1)}, u32[]{:S(2)}, u32[]{:S(2)}) collective-permute-start(bf16[128,512]{1,0:T(8,128)(2,1)S(1)} %constant_dynamic-slice_fusion.15.refs_0_), channel_id=1, source_target_pairs={{0,1},{1,0},{2,3},{3,2},{4,5},{5,4},{6,7},{7,6},{8,9},{9,8},{10,11... | collective-permute-start | bytes 393224 | tf_op jit(solution)/shard_map/ppermute | solution.py:198
  75.4 32.7 %collective-permute-start.24 = (bf16[128,512]{1,0:T(8,128)(2,1)S(1)}, bf16[128,512]{1,0:T(8,128)(2,1)}, u32[]{:S(2)}, u32[]{:S(2)}) collective-permute-start(bf16[128,512]{1,0:T(8,128)(2,1)S(1)} %collective-permute-done.23.refs_2_), channel_id=1, source_target_pairs={{0,4},{4,0},{1,5},{5,1},{2,6},{6,2},{3,7},{7,3},{8,12},{12,8},{9,1... | collective-permute-start | bytes 393224 | tf_op jit(solution)/shard_map/ppermute | solution.py:195
  76.3 34.0 %collective-permute-start.31 = (bf16[128,512]{1,0:T(8,128)(2,1)S(1)}, bf16[128,512]{1,0:T(8,128)(2,1)S(1)}, u32[]{:S(2)}, u32[]{:S(2)}) collective-permute-start(bf16[128,512]{1,0:T(8,128)(2,1)S(1)} %collective-permute-done.23.refs_2_), channel_id=1, source_target_pairs={{0,1},{1,0},{2,3},{3,2},{4,5},{5,4},{6,7},{7,6},{8,9},{9,8},{10,11... | collective-permute-start | bytes 393224 | tf_op jit(solution)/shard_map/ppermute | solution.py:198
  76.3 32.8 %collective-permute-start.30 = (bf16[128,512]{1,0:T(8,128)(2,1)S(1)}, bf16[128,512]{1,0:T(8,128)(2,1)S(1)}, u32[]{:S(2)}, u32[]{:S(2)}) collective-permute-start(bf16[128,512]{1,0:T(8,128)(2,1)S(1)} %collective-permute-done.22.refs_1_), channel_id=1, source_target_pairs={{0,1},{1,0},{2,3},{3,2},{4,5},{5,4},{6,7},{7,6},{8,9},{9,8},{10,11... | collective-permute-start | bytes 393224 | tf_op jit(solution)/shard_map/ppermute | solution.py:198
  76.8 34.2 %collective-permute-start.26 = (bf16[128,512]{1,0:T(8,128)(2,1)}, bf16[128,512]{1,0:T(8,128)(2,1)}, u32[]{:S(2)}, u32[]{:S(2)}) collective-permute-start(bf16[128,512]{1,0:T(8,128)(2,1)} %collective-permute-done.25.refs_4_), channel_id=1, source_target_pairs={{0,4},{4,0},{1,5},{5,1},{2,6},{6,2},{3,7},{7,3},{8,12},{12,8},{9,1... | collective-permute-start | bytes 393224 | tf_op jit(solution)/shard_map/ppermute | solution.py:195
  114.6 24.4 %collective-permute-start.52 = (bf16[512,512]{1,0:T(8,128)(2,1)S(1)}, bf16[512,512]{1,0:T(8,128)(2,1)S(1)}, u32[]{:S(2)}, u32[]{:S(2)}) collective-permute-start(bf16[512,512]{1,0:T(8,128)(2,1)S(1)} %constant_dynamic-slice_fusion.13.refs_0_), channel_id=1, source_target_pairs={{0,4},{4,0},{1,5},{5,1},{2,6},{6,2},{3,7},{7,3},{8,12},{12,8},{9,1... | collective-permute-start | bytes 1572872 | tf_op jit(solution)/shard_map/ppermute | solution.py:195
  116.9 22.8 %collective-permute-start.53 = (bf16[512,512]{1,0:T(8,128)(2,1)S(1)}, bf16[512,512]{1,0:T(8,128)(2,1)}, u32[]{:S(2)}, u32[]{:S(2)}) collective-permute-start(bf16[512,512]{1,0:T(8,128)(2,1)S(1)} %constant_dynamic-slice_fusion.13.refs_0_), channel_id=1, source_target_pairs={{0,8},{8,16},{16,24},{24,0},{1,9},{9,17},{17,25},{25,1},{2,10},{10... | collective-permute-start | bytes 1572872 | tf_op jit(solution)/shard_map/ppermute | solution.py:194
  119.7 73.7 %all-to-all-start = ((bf16[512,4,768]{2,0,1:T(8,128)(2,1)}), bf16[512,4,768]{2,0,1:T(8,128)(2,1)}, u32[]{:S(2)}, u32[]{:S(2)}) async-start(bf16[512,4,768]{2,0,1:T(8,128)(2,1)} %fusion.8), calls=%async_computation | async-start | bytes 6291456 | tf_op jit(solution)/shard_map/all_to_all | solution.py:351
  143.9 18.3 %collective-permute-start.54 = (bf16[512,512]{1,0:T(8,128)(2,1)}, bf16[512,512]{1,0:T(8,128)(2,1)}, u32[]{:S(2)}, u32[]{:S(2)}) collective-permute-start(bf16[512,512]{1,0:T(8,128)(2,1)} %collective-permute-done.53.refs_2_), channel_id=1, source_target_pairs={{0,4},{4,0},{1,5},{5,1},{2,6},{6,2},{3,7},{7,3},{8,12},{12,8},{9,1... | collective-permute-start | bytes 1572872 | tf_op jit(solution)/shard_map/ppermute | solution.py:195
  157.2 21.3 %collective-permute-start.42 = (bf16[128,2048]{1,0:T(8,128)(2,1)S(1)}, bf16[128,2048]{1,0:T(8,128)(2,1)S(1)}, u32[]{:S(2)}, u32[]{:S(2)}) collective-permute-start(bf16[128,2048]{1,0:T(8,128)(2,1)S(1)} %collective-permute-done.40.refs_4_), channel_id=1, source_target_pairs={{0,8},{8,16},{16,24},{24,0},{1,9},{9,17},{17,25},{25,1},{2,10},{10... | collective-permute-start | bytes 1572872 | tf_op jit(solution)/shard_map/ppermute | solution.py:194
  162.2 17.9 %collective-permute-start.41 = (bf16[128,2048]{1,0:T(8,128)(2,1)S(1)}, bf16[128,2048]{1,0:T(8,128)(2,1)S(1)}, u32[]{:S(2)}, u32[]{:S(2)}) collective-permute-start(bf16[128,2048]{1,0:T(8,128)(2,1)S(1)} %collective-permute-done.40.refs_4_), channel_id=1, source_target_pairs={{0,4},{4,0},{1,5},{5,1},{2,6},{6,2},{3,7},{7,3},{8,12},{12,8},{9,1... | collective-permute-start | bytes 1572872 | tf_op jit(solution)/shard_map/ppermute | solution.py:195
  172.0 17.1 %collective-permute-start.57 = (bf16[512,512]{1,0:T(8,128)(2,1)}, bf16[512,512]{1,0:T(8,128)(2,1)}, u32[]{:S(2)}, u32[]{:S(2)}) collective-permute-start(bf16[512,512]{1,0:T(8,128)(2,1)} %collective-permute-done.55.refs_4_), channel_id=1, source_target_pairs={{0,8},{8,16},{16,24},{24,0},{1,9},{9,17},{17,25},{25,1},{2,10},{10... | collective-permute-start | bytes 1572872 | tf_op jit(solution)/shard_map/ppermute | solution.py:194
  180.0 40.4 %collective-permute-start.56 = (bf16[512,512]{1,0:T(8,128)(2,1)}, bf16[512,512]{1,0:T(8,128)(2,1)}, u32[]{:S(2)}, u32[]{:S(2)}) collective-permute-start(bf16[512,512]{1,0:T(8,128)(2,1)} %collective-permute-done.55.refs_4_), channel_id=1, source_target_pairs={{0,4},{4,0},{1,5},{5,1},{2,6},{6,2},{3,7},{7,3},{8,12},{12,8},{9,1... | collective-permute-start | bytes 1572872 | tf_op jit(solution)/shard_map/ppermute | solution.py:195
  181.3 39.6 %collective-permute-start.49 = (bf16[128,2048]{1,0:T(8,128)(2,1)S(1)}, bf16[128,2048]{1,0:T(8,128)(2,1)S(1)}, u32[]{:S(2)}, u32[]{:S(2)}) collective-permute-start(bf16[128,2048]{1,0:T(8,128)(2,1)S(1)} %collective-permute-done.41.refs_5_), channel_id=1, source_target_pairs={{0,1},{1,0},{2,3},{3,2},{4,5},{5,4},{6,7},{7,6},{8,9},{9,8},{10,11... | collective-permute-start | bytes 1572872 | tf_op jit(solution)/shard_map/ppermute | solution.py:198
  182.1 38.9 %collective-permute-start.50 = (bf16[128,2048]{1,0:T(8,128)(2,1)S(1)}, bf16[128,2048]{1,0:T(8,128)(2,1)}, u32[]{:S(2)}, u32[]{:S(2)}) collective-permute-start(bf16[128,2048]{1,0:T(8,128)(2,1)S(1)} %collective-permute-done.42.refs_6_), channel_id=1, source_target_pairs={{0,1},{1,0},{2,3},{3,2},{4,5},{5,4},{6,7},{7,6},{8,9},{9,8},{10,11... | collective-permute-start | bytes 1572872 | tf_op jit(solution)/shard_map/ppermute | solution.py:198
  189.1 32.4 %collective-permute-start.58 = (bf16[512,512]{1,0:T(8,128)(2,1)}, bf16[512,512]{1,0:T(8,128)(2,1)}, u32[]{:S(2)}, u32[]{:S(2)}) collective-permute-start(bf16[512,512]{1,0:T(8,128)(2,1)} %collective-permute-done.57.refs_6_), channel_id=1, source_target_pairs={{0,4},{4,0},{1,5},{5,1},{2,6},{6,2},{3,7},{7,3},{8,12},{12,8},{9,1... | collective-permute-start | bytes 1572872 | tf_op jit(solution)/shard_map/ppermute | solution.py:195
  193.3 28.2 %collective-permute-start.51 = (bf16[128,2048]{1,0:T(8,128)(2,1)S(1)}, bf16[128,2048]{1,0:T(8,128)(2,1)}, u32[]{:S(2)}, u32[]{:S(2)}) collective-permute-start(bf16[128,2048]{1,0:T(8,128)(2,1)S(1)} %collective-permute-done.43.refs_7_), channel_id=1, source_target_pairs={{0,1},{1,0},{2,3},{3,2},{4,5},{5,4},{6,7},{7,6},{8,9},{9,8},{10,11... | collective-permute-start | bytes 1572872 | tf_op jit(solution)/shard_map/ppermute | solution.py:198
  215.9 36.0 %all-to-all-start.1 = ((bf16[4,512,256]{1,2,0:T(8,128)(2,1)}), bf16[4,512,256]{1,2,0:T(8,128)(2,1)}, u32[]{:S(2)}, u32[]{:S(2)}) async-start(bf16[4,512,256]{1,2,0:T(8,128)(2,1)} %copy.302), calls=%async_computation.1 | async-start | bytes 2097152 | tf_op jit(solution)/shard_map/all_to_all | solution.py:353
  220.5 24.5 %collective-permute-start.63 = (bf16[512,512]{1,0:T(8,128)(2,1)}, bf16[512,512]{1,0:T(8,128)(2,1)}, u32[]{:S(2)}, u32[]{:S(2)}) collective-permute-start(bf16[512,512]{1,0:T(8,128)(2,1)} %collective-permute-done.55.refs_4_), channel_id=1, source_target_pairs={{0,1},{1,0},{2,3},{3,2},{4,5},{5,4},{6,7},{7,6},{8,9},{9,8},{10,11... | collective-permute-start | bytes 1572872 | tf_op jit(solution)/shard_map/ppermute | solution.py:198
  220.9 24.1 %collective-permute-start.62 = (bf16[512,512]{1,0:T(8,128)(2,1)}, bf16[512,512]{1,0:T(8,128)(2,1)}, u32[]{:S(2)}, u32[]{:S(2)}) collective-permute-start(bf16[512,512]{1,0:T(8,128)(2,1)} %collective-permute-done.54.refs_3_), channel_id=1, source_target_pairs={{0,1},{1,0},{2,3},{3,2},{4,5},{5,4},{6,7},{7,6},{8,9},{9,8},{10,11... | collective-permute-start | bytes 1572872 | tf_op jit(solution)/shard_map/ppermute | solution.py:198
  221.0 24.0 %collective-permute-start.65 = (bf16[512,512]{1,0:T(8,128)(2,1)}, bf16[512,512]{1,0:T(8,128)(2,1)}, u32[]{:S(2)}, u32[]{:S(2)}) collective-permute-start(bf16[512,512]{1,0:T(8,128)(2,1)} %collective-permute-done.57.refs_6_), channel_id=1, source_target_pairs={{0,1},{1,0},{2,3},{3,2},{4,5},{5,4},{6,7},{7,6},{8,9},{9,8},{10,11... | collective-permute-start | bytes 1572872 | tf_op jit(solution)/shard_map/ppermute | solution.py:198
  221.4 23.6 %collective-permute-start.64 = (bf16[512,512]{1,0:T(8,128)(2,1)}, bf16[512,512]{1,0:T(8,128)(2,1)}, u32[]{:S(2)}, u32[]{:S(2)}) collective-permute-start(bf16[512,512]{1,0:T(8,128)(2,1)} %collective-permute-done.56.refs_5_), channel_id=1, source_target_pairs={{0,1},{1,0},{2,3},{3,2},{4,5},{5,4},{6,7},{7,6},{8,9},{9,8},{10,11... | collective-permute-start | bytes 1572872 | tf_op jit(solution)/shard_map/ppermute | solution.py:198
  221.6 23.5 %collective-permute-start.66 = (bf16[512,512]{1,0:T(8,128)(2,1)}, bf16[512,512]{1,0:T(8,128)(2,1)}, u32[]{:S(2)}, u32[]{:S(2)}) collective-permute-start(bf16[512,512]{1,0:T(8,128)(2,1)} %collective-permute-done.58.refs_7_), channel_id=1, source_target_pairs={{0,1},{1,0},{2,3},{3,2},{4,5},{5,4},{6,7},{7,6},{8,9},{9,8},{10,11... | collective-permute-start | bytes 1572872 | tf_op jit(solution)/shard_map/ppermute | solution.py:198
  328.8 21.1 %all-to-all-start.2 = ((bf16[512,4,256]{2,0,1:T(8,128)(2,1)}), bf16[512,4,256]{2,0,1:T(8,128)(2,1)S(1)}, u32[]{:S(2)}, u32[]{:S(2)}) async-start(bf16[512,4,256]{2,0,1:T(8,128)(2,1)} %bitcast.301), calls=%async_computation.2 | async-start | bytes 2097152 | tf_op jit(solution)/shard_map/all_to_all | solution.py:386
  339.9 57.0 %collective-permute-start.82 = (bf16[128,512]{1,0:T(8,128)(2,1)S(1)}, bf16[128,512]{1,0:T(8,128)(2,1)S(1)}, u32[]{:S(2)}, u32[]{:S(2)}) collective-permute-start(bf16[128,512]{1,0:T(8,128)(2,1)S(1)} %fusion.81), channel_id=1, source_target_pairs={{0,8},{8,16},{16,24},{24,0},{1,9},{9,17},{17,25},{25,1},{2,10},{10... | collective-permute-start | bytes 393224 | tf_op jit(solution)/shard_map/ppermute | solution.py:281
  392.2 44.6 %all-to-all-start.3 = ((bf16[4,512,768]{1,2,0:T(8,128)(2,1)}), bf16[4,512,768]{1,2,0:T(8,128)(2,1)}, u32[]{:S(2)}, u32[]{:S(2)}) async-start(bf16[4,512,768]{1,2,0:T(8,128)(2,1)} %copy.308), calls=%async_computation.3 | async-start | bytes 6291456 | tf_op jit(solution)/shard_map/all_to_all | solution.py:388
  416.0 47.0 %collective-permute-start.87 = (bf16[1024,2048]{1,0:T(8,128)(2,1)}, bf16[1024,2048]{1,0:T(8,128)(2,1)}, u32[]{:S(2)}, u32[]{:S(2)}) collective-permute-start(bf16[1024,2048]{1,0:T(8,128)(2,1)} %constant_dynamic-slice_fusion.1), channel_id=1, source_target_pairs={{0,1},{1,0},{2,3},{3,2},{4,5},{5,4},{6,7},{7,6},{8,9},{9,8},{10,11... | collective-permute-start | bytes 12582920 | tf_op jit(solution)/shard_map/ppermute | solution.py:267
  419.3 17.4 %collective-permute-start.85 = (bf16[128,512]{1,0:T(8,128)(2,1)S(1)}, bf16[128,512]{1,0:T(8,128)(2,1)S(1)}, u32[]{:S(2)}, u32[]{:S(2)}) collective-permute-start(bf16[128,512]{1,0:T(8,128)(2,1)S(1)} %add_convert_fusion.23), channel_id=1, source_target_pairs={{0,2},{2,0},{1,3},{3,1},{4,6},{6,4},{5,7},{7,5},{8,10},{10,8},{9,1... | collective-permute-start | bytes 393224 | tf_op jit(solution)/shard_map/ppermute | solution.py:282
  425.6 46.8 %collective-permute-start.94 = (bf16[4096,512]{1,0:T(8,128)(2,1)}, bf16[4096,512]{1,0:T(8,128)(2,1)}, u32[]{:S(2)}, u32[]{:S(2)}) collective-permute-start(bf16[4096,512]{1,0:T(8,128)(2,1)} %constant_dynamic-slice_fusion), channel_id=1, source_target_pairs={{0,1},{1,0},{2,3},{3,2},{4,5},{5,4},{6,7},{7,6},{8,9},{9,8},{10,11... | collective-permute-start | bytes 12582920 | tf_op jit(solution)/shard_map/ppermute | solution.py:267
  462.9 104.8 %collective-permute-start.67 = (bf16[1024,1536]{1,0:T(8,128)(2,1)}, bf16[1024,1536]{1,0:T(8,128)(2,1)}, u32[]{:S(2)}, u32[]{:S(2)}) collective-permute-start(bf16[1024,1536]{1,0:T(8,128)(2,1)} %constant_dynamic-slice_fusion.12), channel_id=1, source_target_pairs={{0,1},{1,0},{2,3},{3,2},{4,5},{5,4},{6,7},{7,6},{8,9},{9,8},{10,11... | collective-permute-start | bytes 9437192 | tf_op jit(solution)/shard_map/ppermute | solution.py:267
  470.3 48.8 %collective-permute-start.88 = (bf16[4,128,2048]{2,1,0:T(8,128)(2,1)}, bf16[4,128,2048]{2,1,0:T(8,128)(2,1)}, u32[]{:S(2)}, u32[]{:S(2)}) collective-permute-start(bf16[4,128,2048]{2,1,0:T(8,128)(2,1)} %dynamic-slice_bitcast_fusion.1), channel_id=1, source_target_pairs={{0,4},{4,0},{1,5},{5,1},{2,6},{6,2},{3,7},{7,3},{8,12},{12,8},{9,1... | collective-permute-start | bytes 6291464 | tf_op jit(solution)/shard_map/ppermute | solution.py:270
  478.5 85.3 %collective-permute-start.95 = (bf16[4,512,512]{2,1,0:T(8,128)(2,1)S(1)}, bf16[4,512,512]{2,1,0:T(8,128)(2,1)}, u32[]{:S(2)}, u32[]{:S(2)}) collective-permute-start(bf16[4,512,512]{2,1,0:T(8,128)(2,1)S(1)} %dynamic-slice_bitcast_fusion), channel_id=1, source_target_pairs={{0,4},{4,0},{1,5},{5,1},{2,6},{6,2},{3,7},{7,3},{8,12},{12,8},{9,1... | collective-permute-start | bytes 6291464 | tf_op jit(solution)/shard_map/ppermute | solution.py:270
  520.5 63.1 %collective-permute-start.89 = (bf16[128,2048]{1,0:T(8,128)(2,1)S(1)}, bf16[128,2048]{1,0:T(8,128)(2,1)}, u32[]{:S(2)}, u32[]{:S(2)}) collective-permute-start(bf16[128,2048]{1,0:T(8,128)(2,1)S(1)} %fusion.60), channel_id=1, source_target_pairs={{0,8},{8,16},{16,24},{24,0},{1,9},{9,17},{17,25},{25,1},{2,10},{10... | collective-permute-start | bytes 1572872 | tf_op jit(solution)/shard_map/ppermute | solution.py:281
  574.8 37.7 %collective-permute-start.68 = (bf16[4,128,1536]{1,2,0:T(8,128)(2,1)}, bf16[4,128,1536]{1,2,0:T(8,128)(2,1)}, u32[]{:S(2)}, u32[]{:S(2)}) collective-permute-start(bf16[4,128,1536]{1,2,0:T(8,128)(2,1)} %bitcast.340), channel_id=1, source_target_pairs={{0,4},{4,0},{1,5},{5,1},{2,6},{6,2},{3,7},{7,3},{8,12},{12,8},{9,1... | collective-permute-start | bytes 4718600 | tf_op jit(solution)/shard_map/ppermute | solution.py:270
  586.0 25.0 %collective-permute-start.90 = (bf16[128,2048]{1,0:T(8,128)(2,1)}, bf16[128,2048]{1,0:T(8,128)(2,1)S(1)}, u32[]{:S(2)}, u32[]{:S(2)}) collective-permute-start(bf16[128,2048]{1,0:T(8,128)(2,1)} %add_convert_fusion.17), channel_id=1, source_target_pairs={{0,8},{8,16},{16,24},{24,0},{1,9},{9,17},{17,25},{25,1},{2,10},{10... | collective-permute-start | bytes 1572872 | tf_op jit(solution)/shard_map/ppermute | solution.py:281
  601.4 20.8 %collective-permute-start.98 = (bf16[512,512]{1,0:T(8,128)(2,1)S(1)}, bf16[512,512]{1,0:T(8,128)(2,1)S(1)}, u32[]{:S(2)}, u32[]{:S(2)}) collective-permute-start(bf16[512,512]{1,0:T(8,128)(2,1)S(1)} %add_convert_fusion.12), channel_id=1, source_target_pairs={{0,8},{8,16},{16,24},{24,0},{1,9},{9,17},{17,25},{25,1},{2,10},{10... | collective-permute-start | bytes 1572872 | tf_op jit(solution)/shard_map/ppermute | solution.py:281
  612.4 21.0 %collective-permute-start.91 = (bf16[128,2048]{1,0:T(8,128)(2,1)S(1)}, bf16[128,2048]{1,0:T(8,128)(2,1)S(1)}, u32[]{:S(2)}, u32[]{:S(2)}) collective-permute-start(bf16[128,2048]{1,0:T(8,128)(2,1)S(1)} %add_convert_fusion.16), channel_id=1, source_target_pairs={{0,8},{8,16},{16,24},{24,0},{1,9},{9,17},{17,25},{25,1},{2,10},{10... | collective-permute-start | bytes 1572872 | tf_op jit(solution)/shard_map/ppermute | solution.py:281
  613.6 26.2 %collective-permute-start.69 = (bf16[128,1536]{0,1:T(8,128)(2,1)S(1)}, bf16[128,1536]{0,1:T(8,128)(2,1)S(1)}, u32[]{:S(2)}, u32[]{:S(2)}) collective-permute-start(bf16[128,1536]{0,1:T(8,128)(2,1)S(1)} %fusion.71), channel_id=1, source_target_pairs={{0,8},{8,16},{16,24},{24,0},{1,9},{9,17},{17,25},{25,1},{2,10},{10... | collective-permute-start | bytes 1179656 | tf_op jit(solution)/shard_map/ppermute | solution.py:281
  623.6 17.4 %collective-permute-start.99 = (bf16[512,512]{1,0:T(8,128)(2,1)S(1)}, bf16[512,512]{1,0:T(8,128)(2,1)S(1)}, u32[]{:S(2)}, u32[]{:S(2)}) collective-permute-start(bf16[512,512]{1,0:T(8,128)(2,1)S(1)} %add_convert_fusion.11), channel_id=1, source_target_pairs={{0,2},{2,0},{1,3},{3,1},{4,6},{6,4},{5,7},{7,5},{8,10},{10,8},{9,1... | collective-permute-start | bytes 1572872 | tf_op jit(solution)/shard_map/ppermute | solution.py:282
  644.9 20.9 %collective-permute-start.93 = (bf16[128,2048]{1,0:T(8,128)(2,1)S(1)}, bf16[128,2048]{1,0:T(8,128)(2,1)S(1)}, u32[]{:S(2)}, u32[]{:S(2)}) collective-permute-start(bf16[128,2048]{1,0:T(8,128)(2,1)S(1)} %add_convert_fusion.14), channel_id=1, source_target_pairs={{0,1},{1,0},{2,3},{3,2},{4,5},{5,4},{6,7},{7,6},{8,9},{9,8},{10,11... | collective-permute-start | bytes 1572872 | tf_op jit(solution)/shard_map/ppermute | solution.py:284
  (183 other events, 1633.2 us)

commit v2 on v1

v2 whole, which is shorter than its diff:
```python
import functools
import math

import jax
import jax.numpy as jnp
from jax.sharding import Mesh
from jax.sharding import PartitionSpec as P
from jax import lax
from jax.experimental import pallas as pl
from jax.experimental.pallas import tpu as pltpu
HD=64
RELAX=32.0
C2=RELAX*math.log2(math.e)
NEG=-1e30

def _nt(a,b):
    return lax.dot_general(a,b,(((1,),(1,)),((),())),preferred_element_type=jnp.float32)
def _nn(a,b):
    return lax.dot_general(a,b,(((1,),(0,)),((),())),preferred_element_type=jnp.float32)

def _tr(x):
    return jnp.transpose(x.astype(jnp.float32)).astype(jnp.bfloat16)

def by_source(where, refs, dst, sems):
    rows = refs[0].shape[0]
    copies = []
    for i, ref in enumerate(refs):
        at = pl.multiple_of(jnp.bitwise_xor(where[3], i) * rows, rows)
        copies.append(pltpu.make_async_copy(ref, dst.at[pl.ds(at, rows), :], sems.at[i]))
    return copies

def by_target(where, src, refs, sems):
    rows = refs[0].shape[0]
    copies = []
    for i, ref in enumerate(refs):
        at = pl.multiple_of(jnp.bitwise_xor(where[3], i) * rows, rows)
        copies.append(pltpu.make_async_copy(src.at[pl.ds(at, rows), :], ref, sems.at[i]))
    return copies

def run_copies(copies):
    for copy in copies:
        copy.start()
    for copy in copies:
        copy.wait()

def fwd_kernel(where,*refs,nh,blk,n):
    ins,outs=refs[:n],refs[n:2*n]
    ot_ref,lse_ref,vt_ref,qkv_ref,o_ref,sems=refs[2*n:]
    seq=qkv_ref.shape[0]; w=nh*HD
    nb=seq//blk
    run_copies(by_source(where,ins,qkv_ref,sems))
    q_ref,k_ref,v_ref=(qkv_ref.at[:,i*w:(i+1)*w] for i in range(3))
    for b in range(nb):
        vt_ref[:,b*blk:(b+1)*blk]=_tr(v_ref[b*blk:(b+1)*blk,:])
    lane=lax.broadcasted_iota(jnp.int32,(1,w),1)//HD
    tri=lax.broadcasted_iota(jnp.int32,(blk,blk),0)<=lax.broadcasted_iota(jnp.int32,(blk,blk),1)
    def qstep(qb,_):
        q0=pl.multiple_of(qb*blk,blk)
        q=q_ref[pl.ds(q0,blk),:]
        qm=[jnp.where(lane==h,q,jnp.zeros_like(q)) for h in range(nh)]
        def kv(kb,carry,diag):
            k0=pl.multiple_of(kb*blk,blk)
            k=k_ref[pl.ds(k0,blk),:]
            out=[]
            for h in range(nh):
                m,l,acc=carry[3*h:3*h+3]
                s=_nt(k,qm[h])*C2
                if diag: s=jnp.where(tri,s,NEG)
                mn=jnp.maximum(m,jnp.max(s,axis=0,keepdims=True))
                a=jnp.exp2(m-mn)
                p=jnp.exp2(s-mn)
                l=l*a+jnp.sum(p,axis=0,keepdims=True)
                acc=acc*a+_nn(vt_ref[h*HD:(h+1)*HD,pl.ds(k0,blk)],p.astype(jnp.bfloat16))
                out+= [mn,l,acc]
            return tuple(out)
        init=[]
        for h in range(nh):
            init+=[jnp.full((1,blk),NEG,jnp.float32),jnp.zeros((1,blk),jnp.float32),jnp.zeros((HD,blk),jnp.float32)]
        c=kv(qb,tuple(init),True)
        c=lax.fori_loop(0,qb,lambda kb,cc: kv(kb,cc,False),c)
        for h in range(nh):
            m,l,acc=c[3*h:3*h+3]
            ot_ref[h*HD:(h+1)*HD,pl.ds(q0,blk)]=acc/l
            lse_ref[h:h+1,pl.ds(q0,blk)]=m+jnp.log2(l)
        o_ref[pl.ds(q0,blk),:]=jnp.transpose(ot_ref[:,pl.ds(q0,blk)]).astype(jnp.bfloat16)
        return 0
    lax.fori_loop(0,nb,qstep,0)
    run_copies(by_target(where,o_ref,outs,sems))

def attn_fwd(where, qkv, nh, blk=512):
    n=len(qkv); rows=qkv[0].shape[0]
    seq=n*rows; w=nh*HD
    blk=min(blk,seq)
    vm=pl.BlockSpec(memory_space=pltpu.VMEM)
    an=pl.BlockSpec(memory_space=pl.ANY)
    outs=pl.pallas_call(functools.partial(fwd_kernel,nh=nh,blk=blk,n=n),
      grid_spec=pltpu.PrefetchScalarGridSpec(num_scalar_prefetch=1,
        in_specs=[an]*n,out_specs=[an]*n+[vm]*2,
        scratch_shapes=[pltpu.VMEM((w,seq),jnp.bfloat16),pltpu.VMEM((seq,3*w),jnp.bfloat16),pltpu.VMEM((seq,w),jnp.bfloat16),pltpu.SemaphoreType.DMA((n,))]),
      out_shape=[jax.ShapeDtypeStruct((rows,w),jnp.bfloat16)]*n+[jax.ShapeDtypeStruct((w,seq),jnp.float32),jax.ShapeDtypeStruct((8,seq),jnp.float32)],
      compiler_params=pltpu.CompilerParams(vmem_limit_bytes=48<<20),
      cost_estimate=pl.CostEstimate(flops=int(nh*4.5*1.1e9), transcendentals=0, bytes_accessed=1<<20),
      name="attn_fwd")(where,*qkv)
    return outs[:n],outs[n],outs[n+1]

def bwd_kernel(where,*refs,nh,blk,n):
    ins,dos,outs=refs[:n],refs[n:2*n],refs[2*n+2:3*n+2]
    ot_ref,lse_ref=refs[2*n:2*n+2]
    kt_ref,dl_ref,dqt_ref,qkv_ref,do_ref,d_ref,sems,do_sems=refs[3*n+2:]
    seq=qkv_ref.shape[0]; w=nh*HD
    nb=seq//blk
    run_copies(by_source(where,ins,qkv_ref,sems)+by_source(where,dos,do_ref,do_sems))
    q_ref,k_ref,v_ref=(qkv_ref.at[:,i*w:(i+1)*w] for i in range(3))
    for b in range(nb):
        sl=slice(b*blk,(b+1)*blk)
        kt_ref[:,sl]=_tr(k_ref[sl,:])
        dot_=jnp.transpose(do_ref[sl,:].astype(jnp.float32))
        pr=dot_*ot_ref[:,sl]
        for h in range(nh):
            dl_ref[h:h+1,sl]=jnp.sum(pr[h*HD:(h+1)*HD],axis=0,keepdims=True)
    dqt_ref[...]=jnp.zeros_like(dqt_ref)
    lane=lax.broadcasted_iota(jnp.int32,(1,w),1)//HD
    tri=lax.broadcasted_iota(jnp.int32,(blk,blk),0)<=lax.broadcasted_iota(jnp.int32,(blk,blk),1)
    def kstep(kb,_):
        k0=pl.multiple_of(kb*blk,blk)
        k=k_ref[pl.ds(k0,blk),:]
        v=v_ref[pl.ds(k0,blk),:]
        def qs(qb,carry,diag):
            dk,dv=carry
            q0=pl.multiple_of(qb*blk,blk)
            q=q_ref[pl.ds(q0,blk),:]
            do=do_ref[pl.ds(q0,blk),:]
            for h in range(nh):
                qm=jnp.where(lane==h,q,jnp.zeros_like(q))
                dom=jnp.where(lane==h,do,jnp.zeros_like(do))
                s=_nt(k,qm)
                dp=_nt(v,dom)
                p=jnp.exp2(s*C2-lse_ref[h:h+1,pl.ds(q0,blk)])
                if diag: p=jnp.where(tri,p,0.0)
                ds=(p*(dp-dl_ref[h:h+1,pl.ds(q0,blk)])).astype(jnp.bfloat16)
                dv=dv+_nn(p.astype(jnp.bfloat16),dom)
                dk=dk+_nn(ds,qm)
                dqt_ref[h*HD:(h+1)*HD,pl.ds(q0,blk)]+=_nn(kt_ref[h*HD:(h+1)*HD,pl.ds(k0,blk)],ds)
            return dk,dv
        z=jnp.zeros((blk,w),jnp.float32)
        c=qs(kb,(z,z),True)
        dk,dv=lax.fori_loop(kb+1,nb,lambda qb,cc: qs(qb,cc,False),c)
        d_ref[pl.ds(k0,blk),w:2*w]=(dk*RELAX).astype(jnp.bfloat16)
        d_ref[pl.ds(k0,blk),2*w:3*w]=dv.astype(jnp.bfloat16)
        return 0
    lax.fori_loop(0,nb,kstep,0)
    for b in range(nb):
        sl=slice(b*blk,(b+1)*blk)
        d_ref[sl,0:w]=(jnp.transpose(dqt_ref[:,sl])*(1.0/math.sqrt(HD))).astype(jnp.bfloat16)
    run_copies(by_target(where,d_ref,outs,sems))

def attn_bwd(where, qkv, do, ot, lse, nh, blk=512):
    n=len(qkv); rows=qkv[0].shape[0]
    seq=n*rows; w=nh*HD
    blk=min(blk,seq)
    vm=pl.BlockSpec(memory_space=pltpu.VMEM)
    an=pl.BlockSpec(memory_space=pl.ANY)
    return pl.pallas_call(functools.partial(bwd_kernel,nh=nh,blk=blk,n=n),
      grid_spec=pltpu.PrefetchScalarGridSpec(num_scalar_prefetch=1,
        in_specs=[an]*(2*n)+[vm]*2,out_specs=[an]*n,
        scratch_shapes=[pltpu.VMEM((w,seq),jnp.bfloat16),pltpu.VMEM((8,seq),jnp.float32),pltpu.VMEM((w,seq),jnp.float32),
          pltpu.VMEM((seq,3*w),jnp.bfloat16),pltpu.VMEM((seq,w),jnp.bfloat16),pltpu.VMEM((seq,3*w),jnp.bfloat16),
          pltpu.SemaphoreType.DMA((n,)),pltpu.SemaphoreType.DMA((n,))]),
      out_shape=[jax.ShapeDtypeStruct((rows,3*w),jnp.bfloat16)]*n,
      compiler_params=pltpu.CompilerParams(vmem_limit_bytes=56<<20),
      cost_estimate=pl.CostEstimate(flops=int(nh*9.5*1.1e9), transcendentals=0, bytes_accessed=1<<20),
      name="attn_bwd")(where,*qkv,*do,ot,lse)


NORM_EPS = 1e-05
F32 = jnp.float32
BF16 = jnp.bfloat16
SWAP = [(0, 1), (1, 0)]
SEQ_AXES = ("y", "c")
DP_AXES = ("z", "x")
ANY = pl.BlockSpec(memory_space=pl.ANY)
VMEM = pl.BlockSpec(memory_space=pltpu.VMEM)
GELU_K = math.sqrt(2.0 / math.pi)
GELU_A = 0.044715
N_VEC = 12
N_SEQ = 4


def add_low(*terms):
    return sum(t.astype(F32) for t in terms).astype(BF16)


def ring(n):
    return [(i, (i + 1) % n) for i in range(n)]


def uses_rings():
    return lax.axis_size("z") * lax.axis_size("x") <= 8


def here():
    seq = lax.axis_index("y") * lax.axis_size("c") + lax.axis_index("c")
    return jnp.stack([lax.axis_index(a) for a in ("z", "x", "c")] + [seq]).astype(jnp.int32)


def call(kernel, name, where, args, specs, outs, scratch=(), grid=(), out_specs=None, cost=None):
    if out_specs is None:
        out_specs = [VMEM] * len(outs)
    return pl.pallas_call(
        kernel,
        grid_spec=pltpu.PrefetchScalarGridSpec(
            num_scalar_prefetch=1,
            grid=grid,
            in_specs=specs,
            out_specs=out_specs,
            scratch_shapes=list(scratch),
        ),
        out_shape=[jax.ShapeDtypeStruct(s, d) for s, d in outs],
        compiler_params=pltpu.CompilerParams(vmem_limit_bytes=60 << 20),
        cost_estimate=cost,
        name=name,
    )(where, *args)


def cost_of(microseconds):
    return pl.CostEstimate(flops=int(microseconds * 1.1e9), transcendentals=0, bytes_accessed=1 << 20)


def tie(value, *others):
    return lax.optimization_barrier((value,) + others)[0]


def together(*values):
    return list(lax.optimization_barrier(tuple(values)))


class Gather:
    def __init__(self, shards, core_halves=True):
        self.shards = shards
        self.core_halves = core_halves
        self.cur = shards
        if core_halves:
            self.cur = lax.dynamic_index_in_dim(shards, lax.axis_index("c"), 0, False)
        self.mine = []
        self.hops = 0

    def hop(self, *after):
        nz = lax.axis_size("z")
        if self.hops > 0:
            after = after + (self.mine[2 * self.hops - 2],)
        cur = tie(self.cur, *after) if after else self.cur
        if self.hops < nz - 1:
            self.cur = lax.ppermute(cur, "z", ring(nz))
        other = lax.ppermute(cur, "x", SWAP)
        self.mine.append(other)
        self.hops += 1
        if self.hops < nz:
            self.mine.append(self.cur)

    def arrive(self, value):
        value, self.cur, self.mine[-1], self.mine[2 * self.hops - 2] = together(
            value, self.cur, self.mine[-1], self.mine[2 * self.hops - 2]
        )
        return value

    def pieces(self):
        if not self.core_halves:
            return [self.shards] + self.mine
        return [self.shards] + self.mine + [lax.ppermute(piece, "c", SWAP) for piece in self.mine]


def in_halves(weight):
    rows, cols = weight.shape
    return weight.reshape(rows, 2, cols // 2).transpose(1, 0, 2)


def owner_of(index, nz, z, x):
    step, side = (index + 1) // 2, (index + 1) % 2
    return lax.rem(z + nz - step, nz) * 2 + (x if side == 0 else 1 - x)


class Loader:
    def __init__(self, where, pieces, dsts, sems, nz, first=0, col=0):
        self.copies = []
        self.sems, self.first = sems, first
        if not isinstance(dsts, (list, tuple)):
            dsts = [dsts]
        if len(pieces) == len(dsts) and len(pieces[0].shape) == 2:
            for piece, dst in zip(pieces, dsts):
                half = dst.shape[2]
                for side in range(2):
                    at = side * (piece.shape[1] // 2) + col
                    self.add(piece.at[:, at : at + half], dst.at[side])
            return
        z, x, c = where[0], where[1], where[2]
        rows = pieces[0].shape[1]
        others = (len(pieces) - 1) // 2
        self.marks = []
        for dst in dsts:
            half = dst.shape[2]
            groups = dst.shape[1] // (2 * nz * rows)
            for g in range(groups):
                cols = slice(col, col + half)
                col += half

                def to(side, owner):
                    row = pl.multiple_of((owner * groups + g) * rows, rows)
                    return dst.at[side, pl.ds(row, rows), :]

                for side in range(2):
                    self.add(pieces[0].at[side, :, cols], to(side, z * 2 + x))
                for i, piece in enumerate(pieces[1:]):
                    side = c if i < others else 1 - c
                    self.add(piece.at[:, cols], to(side, owner_of(i % others, nz, z, x)))
            self.marks.append(len(self.copies))

    def add(self, src, to):
        self.copies.append(
            pltpu.make_async_copy(src, to, self.sems.at[self.first + len(self.copies)])
        )

    def start(self):
        for copy in self.copies:
            copy.start()

    def wait(self, upto=None, since=0):
        for copy in self.copies[since:upto]:
            copy.wait()


def n_copies(pieces, groups=1):
    return (len(pieces) + 1) * groups


def norm_parts(v):
    c = v - jnp.mean(v, axis=-1, keepdims=True)
    inv = lax.rsqrt(jnp.mean(c * c, axis=-1, keepdims=True) + NORM_EPS)
    return c * inv, inv


def norm_back(n, inv, gain, e):
    ge = g_e = gain * e
    return (g_e - jnp.mean(ge, axis=-1, keepdims=True) - n * jnp.mean(ge * n, axis=-1, keepdims=True)) * inv


def rowsum(v):
    return jnp.sum(v, axis=0, keepdims=True)


def vectors_kernel(where, *refs, nz):
    pieces, vec, bias = refs[:-2], refs[-2], refs[-1]
    z, x = where[0], where[1]
    n_bias = pieces[0].shape[0] - N_VEC
    own = pieces[0].shape[1]
    order = [z * 2 + x] + [owner_of(i, nz, z, x) for i in range(2 * nz - 1)]
    tmp = refs[-2]
    for o in range(2 * nz):
        acc = jnp.zeros(pieces[0].shape, F32)
        for at, piece in zip(order, pieces):
            acc = jnp.where(at == o, piece[...].astype(F32), acc)
        vec[0:N_VEC, o * own : (o + 1) * own] = acc[:N_VEC]
        for j in range(n_bias):
            lo = (o * n_bias + j) * own
            bias[0:1, lo : lo + own] = acc[N_VEC + j : N_VEC + j + 1]


def small_vectors(pieces, width):
    nz = lax.axis_size("z")
    n, own = pieces[0].shape
    return call(
        functools.partial(vectors_kernel, nz=nz),
        "vectors",
        here(),
        pieces,
        [VMEM] * len(pieces),
        [((16, width), F32), ((1, (n - N_VEC) * 2 * nz * own), F32)],
        cost=cost_of(2),
    )


def plain_vectors(small, width):
    placed = lax.all_gather(small, DP_AXES, axis=0, tiled=False).astype(F32)
    vec = placed[:, :N_VEC].transpose(1, 0, 2).reshape(N_VEC, width)
    return jnp.pad(vec, ((0, 4), (0, 0))), placed[:, N_VEC:].reshape(1, -1)


def first_norm(tok, vec, normed):
    rows = min(64, tok.shape[0])

    def body(i, carry):
        at = pl.ds(pl.multiple_of(i * rows, rows), rows)
        n, inv = norm_parts(tok[at, :].astype(F32))
        normed[at, :] = (n * vec[4:5, :] + vec[8:9, :]).astype(BF16)
        return carry

    lax.fori_loop(0, tok.shape[0] // rows, body, 0)


def qkv_kernel(where, first, vec, *refs, nz, chunk, chunks, n_pieces):
    pieces, refs = refs[:n_pieces], list(refs[n_pieces:])
    n_seq = N_SEQ
    outs = [refs.pop(0) for _ in range(n_seq)]
    normed = refs.pop(0) if chunk == 0 else first
    w, stage, sems, out_sems = refs
    rows, cols = outs[0].shape
    per_side = n_seq // 2
    load = Loader(where, pieces, w, sems, nz, 0, chunk * per_side * cols)
    load.start()
    if chunk == 0:
        first_norm(first, vec, normed)
    load.wait()
    wide = cols // 3
    grp = wide * chunks
    scale = 1.0 / (RELAX * math.sqrt(HD))
    for side in range(2):
        mixed = _nn(normed[...], w[side])
        for j in range(per_side):
            s = side * per_side + j
            lo = s * grp + chunk * wide
            block = mixed[:, j * cols : (j + 1) * cols]
            at = slice(s * rows, (s + 1) * rows)
            stage[at, 0:wide] = ((block[:, 0:wide] + vec[0:1, lo : lo + wide]) * scale).astype(BF16)
            stage[at, wide : 2 * wide] = block[:, wide : 2 * wide].astype(BF16)
            stage[at, 2 * wide :] = (block[:, 2 * wide :] + vec[1:2, lo : lo + wide]).astype(BF16)
    run_copies(by_target(where, stage, outs, out_sems))


def gelu_parts(h):
    t = jnp.tanh(GELU_K * (h + GELU_A * (h * h * h)))
    return t


def mlp_kernel(where, *refs, nz, n_att, n_pieces):
    refs = list(refs)
    att_in = [[refs.pop(0) for _ in range(N_SEQ)] for _ in range(n_att)]
    tok, out_grad, vec, fc1_b = [refs.pop(0) for _ in range(4)]
    sets = [[refs.pop(0) for _ in range(n)] for n in n_pieces]
    layer_out, d_residual, d_second, active, d_hidden, normed_two, d_branch, attended, sums, fc1_sum = [
        refs.pop(0) for _ in range(10)
    ]
    d_att = [[refs.pop(0) for _ in range(N_SEQ)] for _ in range(n_att)]
    proj_w, fc1_w, fc2_w, hidden, branch, residual, wide = [refs.pop(0) for _ in range(7)]
    stages = [refs.pop(0) for _ in range(n_att)]
    out_sems = refs.pop(0)
    sems = refs
    dsts = (proj_w, fc1_w, fc2_w)
    if len(sets) == 2:
        ups = Loader(where, sets[0], dsts[:2], sems[0], nz)
        downs = Loader(where, sets[1], dsts[2:], sems[1], nz)
        ups.start()
        downs.start()
        mark = ups.marks[0]
        waits = [functools.partial(ups.wait, mark), functools.partial(ups.wait, None, mark), downs.wait]
    else:
        loads = [Loader(where, p, d, sem, nz) for p, d, sem in zip(sets, dsts, sems)]
        for load in loads:
            load.start()
        waits = [load.wait for load in loads]
    rows, width = tok.shape
    n_seq, part = N_SEQ, att_in[0][0].shape[1]
    for i in range(n_seq):
        s = jnp.bitwise_xor(where[3], i)
        for j in range(n_att):
            lo = pl.multiple_of((s * n_att + j) * part, part)
            attended[:, pl.ds(lo, part)] = att_in[j][i][...]
    waits[0]()
    half = width // 2
    for side in range(2):
        cols = slice(side * half, (side + 1) * half)
        branch[:, cols] = _nn(attended[...], proj_w[side]) + vec[2:3, cols]
    step = min(64, rows)

    def norms(i, carry):
        at = pl.ds(pl.multiple_of(i * step, step), step)
        n, inv = norm_parts(branch[at, :])
        r = tok[at, :].astype(F32) + (n * vec[5:6, :] + vec[9:10, :])
        residual[at, :] = r
        n, inv = norm_parts(r)
        normed_two[at, :] = (n * vec[6:7, :] + vec[10:11, :]).astype(BF16)
        return carry

    lax.fori_loop(0, rows // step, norms, 0)
    waits[1]()
    ff = hidden.shape[1]
    blk = 512
    per_side = ff // 2 // blk

    def up(i, carry):
        lo = pl.multiple_of(i * blk, blk)
        col = pl.multiple_of(lax.rem(i, per_side) * blk, blk)
        h = _nn(normed_two[...], fc1_w[i // per_side, :, pl.ds(col, blk)]) + fc1_b[:, pl.ds(lo, blk)]
        hidden[:, pl.ds(lo, blk)] = h
        active[:, pl.ds(lo, blk)] = (0.5 * h * (1.0 + gelu_parts(h))).astype(BF16)
        return carry

    lax.fori_loop(0, ff // blk, up, 0)
    waits[2]()
    for side in range(2):
        cols = slice(side * half, (side + 1) * half)
        wide[:, cols] = _nn(active[...], fc2_w[side]) + vec[3:4, cols]

    def top(i, carry):
        g_sum, s_sum, b_sum = carry
        at = pl.ds(pl.multiple_of(i * step, step), step)
        n, inv = norm_parts(wide[at, :])
        e = out_grad[at, :].astype(F32)
        layer_out[at, :] = (residual[at, :] + (n * vec[7:8, :] + vec[11:12, :])).astype(BF16)
        d = norm_back(n, inv, vec[7:8, :], e).astype(BF16)
        d_second[at, :] = d
        return g_sum + rowsum(e * n), s_sum + rowsum(e), b_sum + rowsum(d.astype(F32))

    zero = jnp.zeros((1, width), F32)
    g_sum, s_sum, b_sum = lax.fori_loop(0, rows // step, top, (zero, zero, zero))
    sums[3:4, :] = b_sum
    sums[7:8, :] = g_sum
    sums[11:12, :] = s_sum

    def down(i, carry):
        at = pl.ds(pl.multiple_of(i * blk, blk), blk)
        d = _nt(d_second[:, 0:half], fc2_w[0, at, :]) + _nt(d_second[:, half:], fc2_w[1, at, :])
        h = hidden[:, at]
        t = gelu_parts(h)
        slope = 0.5 * (1.0 + t) + (0.5 * h) * (1.0 - t * t) * (GELU_K * (1.0 + 3.0 * GELU_A * (h * h)))
        low = (d * slope).astype(BF16)
        d_hidden[:, at] = low
        fc1_sum[:, at] = rowsum(low.astype(F32))
        return carry

    lax.fori_loop(0, ff // blk, down, 0)
    quarter = width // 4
    for q in range(4):
        at = slice(q * quarter, (q + 1) * quarter)
        wide[:, at] = _nt(d_hidden[:, 0 : ff // 2], fc1_w[0, at, :]) + _nt(
            d_hidden[:, ff // 2 :], fc1_w[1, at, :]
        )

    def mid(i, carry):
        g2, s2, g1, s1, b_sum = carry
        at = pl.ds(pl.multiple_of(i * step, step), step)
        e = wide[at, :]
        n, inv = norm_parts(residual[at, :])
        d = out_grad[at, :].astype(F32) + norm_back(n, inv, vec[6:7, :], e)
        d_residual[at, :] = d
        g2, s2 = g2 + rowsum(e * n), s2 + rowsum(e)
        n, inv = norm_parts(branch[at, :])
        low = norm_back(n, inv, vec[5:6, :], d).astype(BF16)
        d_branch[at, :] = low
        return g2, s2, g1 + rowsum(d * n), s1 + rowsum(d), b_sum + rowsum(low.astype(F32))

    g2, s2, g1, s1, b_sum = lax.fori_loop(0, rows // step, mid, (zero,) * 5)
    for row, v in ((6, g2), (10, s2), (5, g1), (9, s1), (2, b_sum)):
        sums[row : row + 1, :] = v
    for row in (0, 1, 4, 8, 12, 13, 14, 15):
        sums[row : row + 1, :] = zero
    for s in range(n_seq):
        at = slice(s * n_att * part, (s + 1) * n_att * part)
        low = (_nt(d_branch[:, 0:half], proj_w[0, at, :]) + _nt(d_branch[:, half:], proj_w[1, at, :])).astype(BF16)
        for j in range(n_att):
            stages[j][s * rows : (s + 1) * rows, :] = low[:, j * part : (j + 1) * part]
    run_copies(
        [
            copy
            for j in range(n_att)
            for copy in by_target(where, stages[j], d_att[j], out_sems.at[j])
        ]
    )


def mlp(where, att, tokens, out_grad, vec, fc1_b, sets):
    nz = lax.axis_size("z")
    rows, width = tokens.shape
    ff = fc1_b.shape[1]
    n_pieces = [len(s) for s in sets]
    flat = [block for blocks in att for block in blocks]
    part = flat[0].shape[1]
    big = (rows, width)
    outs = [
        (big, BF16),
        (big, F32),
        (big, BF16),
        ((rows, ff), BF16),
        ((rows, ff), BF16),
        (big, BF16),
        (big, BF16),
        (big, BF16),
        ((16, width), F32),
        ((1, ff), F32),
    ] + [(a.shape, BF16) for a in flat]
    scratch = [
        pltpu.VMEM((2, width, width // 2), BF16),
        pltpu.VMEM((2, width, ff // 2), BF16),
        pltpu.VMEM((2, ff, width // 2), BF16),
        pltpu.VMEM((rows, ff), F32),
        pltpu.VMEM(big, F32),
        pltpu.VMEM(big, F32),
        pltpu.VMEM(big, F32),
    ] + [pltpu.VMEM((N_SEQ * rows, part), BF16)] * len(att)
    scratch += [pltpu.SemaphoreType.DMA((len(att), N_SEQ))]
    scratch += [pltpu.SemaphoreType.DMA((n_copies(s, max(2, ff // width)),)) for s in sets]
    args = flat + [tokens, out_grad, vec, fc1_b] + [p for s in sets for p in s]
    specs = [VMEM] * (len(flat) + 4) + [ANY] * sum(n_pieces)
    out_specs = [VMEM] * 10 + [ANY] * len(flat)
    return call(
        functools.partial(mlp_kernel, nz=nz, n_att=len(att), n_pieces=n_pieces),
        "mlp",
        where,
        args,
        specs,
        outs,
        scratch,
        out_specs=out_specs,
        cost=cost_of(45),
    )


def slot_owner(i, nz, where):
    z, x = where[0], where[1]
    return lax.rem(z + 2 * nz - 1 - i % nz, nz) * 2 + (1 - x if i < nz else x)


def contract_rows(left, right):
    return lax.dot_general(left, right, (((0,), (0,)), ((), ())), preferred_element_type=F32)


def halves_of(ref, c):
    half = ref.shape[1] // 2
    return [ref[:, pl.ds(pl.multiple_of(h * half, half), half)] for h in (1 - c, c)]


def columns_of(ref, owner, count):
    return ref[:, pl.ds(pl.multiple_of(owner * count, count), count)]


def up_grad_kernel(where, normed_two, d_hidden, attended, d_branch, *outs, nz):
    c = where[2]
    rows = outs[0].shape[1]
    half = d_branch.shape[1] // 2
    ff_half = d_hidden.shape[1] // 2
    blk = min(1024, ff_half)
    for side in range(2):
        owners = [slot_owner(side * nz + i, nz, where) for i in range(nz)]
        left = jnp.concatenate([columns_of(normed_two, o, rows) for o in owners], axis=1)
        for h in range(2):
            out = outs[2 * side + h]
            base = (1 - c if h == 0 else c) * ff_half
            for n in range(ff_half // blk):
                right = d_hidden[:, pl.ds(pl.multiple_of(base + n * blk, blk), blk)]
                low = contract_rows(left, right).astype(BF16)
                for i in range(nz):
                    out[i, :, half + n * blk : half + (n + 1) * blk] = low[i * rows : (i + 1) * rows]
        left = jnp.concatenate([columns_of(attended, o, rows) for o in owners], axis=1)
        for h, right in enumerate(halves_of(d_branch, c)):
            out = outs[2 * side + h]
            low = contract_rows(left, right).astype(BF16)
            for i in range(nz):
                out[i, :, 0:half] = low[i * rows : (i + 1) * rows]


def down_grad_kernel(where, active, d_second, *outs, nz):
    c = where[2]
    rows = outs[0].shape[1]
    wide = active.shape[1] // (2 * nz)
    half = d_second.shape[1] // 2
    rights = halves_of(d_second, c)
    for side in range(2):
        for i in range(nz):
            left = columns_of(active, slot_owner(side * nz + i, nz, where), wide)
            for h, right in enumerate(rights):
                low = contract_rows(left, right).astype(BF16)
                for g in range(wide // rows):
                    outs[2 * side + h][i, :, g * half : (g + 1) * half] = low[g * rows : (g + 1) * rows]


def grads(kernel, name, where, args, rows, half, specs=None, scratch=(), parts=2, after=()):
    nz = lax.axis_size("z")
    outs = call(
        functools.partial(kernel, nz=nz),
        name,
        where,
        args,
        specs or [VMEM] * len(args),
        [((nz, rows, half), BF16)] * 4,
        scratch,
        cost=cost_of(10),
    )
    outs = list(outs)
    if after:
        outs[0] = tie(outs[0], *after)
    return Reduce(outs[:2], outs[2:], parts)


def qkv_grad_kernel(where, normed, *refs, nz):
    blocks, outs, (stage, sems) = refs[:N_SEQ], refs[N_SEQ:-2], refs[-2:]
    c = where[2]
    rows = outs[0].shape[1]
    tok = normed.shape[0]
    per_side = N_SEQ // 2
    run_copies(by_source(where, blocks, stage, sems))
    for h in range(2):
        base = (1 - c if h == 0 else c) * per_side
        right = jnp.concatenate(
            [stage[pl.ds(pl.multiple_of((base + j) * tok, tok), tok), :] for j in range(per_side)], axis=1
        )
        for side in range(2):
            owners = [slot_owner(side * nz + i, nz, where) for i in range(nz)]
            left = jnp.concatenate([columns_of(normed, o, rows) for o in owners], axis=1)
            low = contract_rows(left, right).astype(BF16)
            for i in range(nz):
                outs[2 * side + h][i] = low[i * rows : (i + 1) * rows]


class Reduce:
    def __init__(self, first, second, parts=2):
        self.own = second[1]
        self.own_got = lax.ppermute(second[0], "c", SWAP)
        got = lax.ppermute(first[0], "c", SWAP)
        size = got.shape[0] // parts
        cuts = [slice(i * size, (i + 1) * size) for i in range(parts)]
        self.size = size
        self.out = [add_low(first[1][cut], got[cut]) for cut in cuts]
        self.from_x = []

    def cross(self, *after):
        block = self.out[len(self.from_x)]
        self.from_x.append(lax.ppermute(tie(block, *after) if after else block, "x", SWAP))
        return self.from_x[-1]

    def add(self, step):
        terms = (self.own[step], self.own_got[step], self.from_x[step // self.size][step % self.size])
        if step > 0:
            terms = (self.passed,) + terms
        self.cur = add_low(*terms)
        return self.cur

    def ring(self, *after):
        nz = lax.axis_size("z")
        self.passed = lax.ppermute(tie(self.cur, *after) if after else self.cur, "z", ring(nz))
        return self.passed

    def finish(self):
        c = lax.axis_index("c")
        low = add_low(self.cur, lax.ppermute(self.cur, "y", SWAP))
        other = lax.ppermute(low, "c", SWAP)
        return jnp.where(c == 0, low, other), jnp.where(c == 0, other, low)


def reduce_plain(lhs, rhs):
    grad = lax.dot_general(
        lhs, rhs, (((0,), (0,)), ((), ())), preferred_element_type=F32
    ).astype(BF16)
    part = lax.psum_scatter(grad, DP_AXES, scatter_dimension=0, tiled=True)
    return lax.psum(part, SEQ_AXES).astype(F32)


def last_kernel(where, *refs, nz, chunks, n_pieces, rings):
    refs = list(refs)
    blocks = [[refs.pop(0) for _ in range(N_SEQ)] for _ in range(chunks)]
    tok, d_residual, vec, sums, fc1_sum = [refs.pop(0) for _ in range(5)]
    pieces = [refs.pop(0) for _ in range(n_pieces)]
    tokens_grad, small = refs.pop(0), refs.pop(0)
    ws = [refs.pop(0) for _ in range(chunks)]
    stages = [refs.pop(0) for _ in range(chunks)]
    wide, total, in_sems = refs.pop(0), refs.pop(0), refs.pop(0)
    loads = [
        Loader(where, pieces, w, sem, nz, 0, j * w.shape[2]) for j, (w, sem) in enumerate(zip(ws, refs))
    ]
    for load in loads:
        load.start()
    rows, width = tok.shape
    n_seq, cols = N_SEQ, stages[0].shape[1]
    run_copies(
        [copy for j in range(chunks) for copy in by_source(where, blocks[j], stages[j], in_sems.at[j])]
    )
    d_mixed = [stage.reshape(n_seq, rows, cols) for stage in stages]
    part = cols // 3
    zero = jnp.zeros((1, width), F32)
    total[...] = sums[...]
    for j in range(chunks):
        for s in range(n_seq):
            lo = (s * chunks + j) * part
            total[0:1, lo : lo + part] = rowsum(d_mixed[j][s, :, 0:part].astype(F32))
            total[1:2, lo : lo + part] = rowsum(d_mixed[j][s, :, 2 * part :].astype(F32))
    for load in loads:
        load.wait()
    quarter = width // 4
    per_side = n_seq // 2
    for q in range(4):
        at = slice(q * quarter, (q + 1) * quarter)
        acc = None
        for j in range(chunks):
            for side in range(2):
                left = jnp.concatenate([d_mixed[j][side * per_side + i] for i in range(per_side)], axis=1)
                term = _nt(left, ws[j][side, at, :])
                acc = term if acc is None else acc + term
        wide[:, at] = acc
    step = min(64, rows)

    def norms(i, carry):
        g, s = carry
        at = pl.ds(pl.multiple_of(i * step, step), step)
        e = wide[at, :]
        n, inv = norm_parts(tok[at, :].astype(F32))
        tokens_grad[at, :] = (d_residual[at, :] + norm_back(n, inv, vec[4:5, :], e)).astype(BF16)
        return g + rowsum(e * n), s + rowsum(e)

    g, s = lax.fori_loop(0, rows // step, norms, (zero, zero))
    total[4:5, :] = g
    total[8:9, :] = s
    if not rings:
        small[...] = total[...]
        return
    z, x = where[0], where[1]
    own = width // (2 * nz)
    n_bias = fc1_sum.shape[1] // width
    for o in range(2 * nz):
        slot = lax.rem(z + 2 * nz - 1 - o // 2, nz) + jnp.where(x == o % 2, nz, 0)
        small[slot, 0:N_VEC, :] = total[0:N_VEC, o * own : (o + 1) * own]
        for j in range(n_bias):
            lo = (o * n_bias + j) * own
            small[slot, N_VEC + j : N_VEC + j + 1, :] = fc1_sum[:, lo : lo + own]


def last(where, d_mixed, tokens, d_residual, vec, sums, fc1_sum, pieces):
    nz = lax.axis_size("z")
    rings = uses_rings()
    rows, width = tokens.shape
    chunks = len(d_mixed)
    small = ((2 * nz, N_VEC + fc1_sum.shape[1] // width, width // (2 * nz)), F32) if rings else ((16, width), F32)
    return call(
        functools.partial(last_kernel, nz=nz, chunks=chunks, n_pieces=len(pieces), rings=rings),
        "last",
        where,
        [b for blocks in d_mixed for b in blocks] + [tokens, d_residual, vec, sums, fc1_sum] + list(pieces),
        [ANY] * (chunks * N_SEQ) + [VMEM] * 5 + [ANY] * len(pieces),
        [((rows, width), BF16), small],
        [pltpu.VMEM((2, width, 3 * width // chunks // 2), BF16)] * chunks
        + [pltpu.VMEM((N_SEQ * rows, 3 * width // chunks // N_SEQ), BF16)] * chunks
        + [pltpu.VMEM((rows, width), F32), pltpu.VMEM((16, width), F32), pltpu.SemaphoreType.DMA((chunks, N_SEQ))]
        + [pltpu.SemaphoreType.DMA((n_copies(pieces),))] * chunks,
        cost=cost_of(12),
    )


def reduce_small(small, fc1_sum, own):
    nz = lax.axis_size("z")
    if not uses_rings():
        n_dp = nz * lax.axis_size("x")
        low = jnp.concatenate(
            (small[:N_VEC].reshape(N_VEC, n_dp, own).transpose(1, 0, 2), fc1_sum.reshape(n_dp, -1, own)),
            axis=1,
        )
        part = lax.psum_scatter(low, DP_AXES, scatter_dimension=0, tiled=False)
        return lax.psum(part.astype(BF16), SEQ_AXES).astype(F32)
    cur = small.astype(BF16)
    for axis in ("c", "y"):
        cur = add_low(cur, lax.ppermute(cur, axis, SWAP))
    keep = add_low(cur[nz:], lax.ppermute(cur[:nz], "x", SWAP))
    cur = keep[0]
    for step in range(1, nz):
        cur = add_low(lax.ppermute(cur, "z", ring(nz)), keep[step])
    return cur.astype(F32)


def exchange(blocks):
    both = [(i, i ^ 3) for i in range(4)]
    return [
        blocks[0],
        lax.ppermute(blocks[1], "c", SWAP),
        lax.ppermute(blocks[2], "y", SWAP),
        lax.ppermute(blocks[3], SEQ_AXES, both),
    ]


def per_device(
    tokens,
    out_grad,
    qkv_weight,
    qv_bias,
    proj_weight,
    fc1_weight,
    fc1_bias,
    fc2_weight,
    out_bias,
    norm_gains,
    norm_shifts,
):
    n_seq = lax.axis_size("y") * lax.axis_size("c")
    rows, width = tokens.shape
    own = qv_bias.shape[1]
    chunks = CHUNKS
    grp = width // n_seq
    part = grp // chunks
    heads = part // HD
    seq_len = n_seq * rows
    nz = lax.axis_size("z")
    where = here()
    qkv_shards = qkv_weight.reshape(-1, 3, n_seq, chunks, part).transpose(3, 0, 2, 1, 4)
    qkv_shards = qkv_shards.reshape(chunks, -1, 3 * width // chunks)
    small = jnp.concatenate(
        (qv_bias, out_bias, norm_gains, norm_shifts, fc1_bias.reshape(-1, own)), axis=0
    )
    rings = uses_rings()
    if rings:
        groups = fc2_weight.shape[0] // proj_weight.shape[0]
        fc2_groups = fc2_weight.reshape(groups, -1, 2, width // 2).transpose(2, 1, 0, 3)
        vec_in = Gather(small, False)
        qkv_in = Gather(jnp.concatenate([in_halves(s) for s in qkv_shards], axis=2))
        up_in = Gather(jnp.concatenate((in_halves(proj_weight), in_halves(fc1_weight)), axis=2))
        down_in = Gather(fc2_groups.reshape(2, -1, groups * width // 2))
        for step in range(nz):
            if step == 1:
                qkv_in.cur, up_in.cur, down_in.cur = lax.optimization_barrier(
                    (qkv_in.cur, up_in.cur, down_in.cur)
                )
            vec_in.hop()
            qkv_in.hop(*vec_in.mine[-3:])
        vec, fc1_b = small_vectors(vec_in.pieces(), width)
        qkv_pieces = qkv_in.pieces()
        up_in.hop(qkv_in.cur)
    else:
        vec, fc1_b = plain_vectors(small, width)
        qkv_pieces = [lax.all_gather(jnp.concatenate(tuple(qkv_shards), axis=1), DP_AXES, axis=0, tiled=True)]
        half = 3 * width // chunks // 2
        order = [2 * j + side for side in range(2) for j in range(chunks)]
        qkv_pieces = [jnp.concatenate([qkv_pieces[0][:, o * half : (o + 1) * half] for o in order], axis=1)]
        rest_sets = [
            [lax.all_gather(w, DP_AXES, axis=0, tiled=True)]
            for w in (proj_weight, fc1_weight, fc2_weight)
        ]
    by_heads, att, kept = [], [], []
    first = tokens
    for j in range(chunks):
        outs = [((rows, 3 * part), BF16)] * n_seq
        if j == 0:
            outs.append(((rows, width), BF16))
        got = call(
            functools.partial(qkv_kernel, nz=nz, chunk=j, chunks=chunks, n_pieces=len(qkv_pieces)),
            "qkv",
            where,
            [first, vec] + qkv_pieces,
            [VMEM] * 2 + [ANY] * len(qkv_pieces),
            outs,
            [
                pltpu.VMEM((2, width, 3 * width // chunks // 2), BF16),
                pltpu.VMEM((seq_len, 3 * part), BF16),
                pltpu.SemaphoreType.DMA((n_copies(qkv_pieces),)),
                pltpu.SemaphoreType.DMA((n_seq,)),
            ],
            out_specs=[ANY] * n_seq + [VMEM] * (j == 0),
            cost=cost_of(7),
        )
        if j == 0:
            first = normed = got[n_seq]
            if rings:
                first = up_in.arrive(first)
                down_in.hop(up_in.cur)
                up_in.hop()
        by_heads.append(exchange(got[:n_seq]))
    for j in range(chunks):
        if rings and j == 0:
            by_heads[0][0] = down_in.arrive(by_heads[0][0])
            down_in.hop()
        if rings and j == 1:
            by_heads[1][0] = up_in.arrive(by_heads[1][0])
            by_heads[1][0] = down_in.arrive(by_heads[1][0])
            up_in.hop()
        out_heads, out_cols, lse = attn_fwd(where, by_heads[j], heads, 1024)
        kept.append((out_cols, lse))
        att.append(exchange(out_heads))
    if rings:
        while down_in.hops < nz:
            for flow in (down_in, up_in):
                if flow.hops < nz:
                    flow.hop()
        rest_sets = [up_in.pieces(), down_in.pieces()]
    outs = mlp(where, att, tokens, out_grad, vec, fc1_b, rest_sets)
    layer_out, d_residual, d_second, active, d_hidden, normed_two, d_branch, attended, sums, fc1_sum = outs[:10]
    d_heads = [exchange(outs[10 + j * n_seq : 10 + (j + 1) * n_seq]) for j in range(chunks)]
    ff = active.shape[1]
    r = proj_weight.shape[0]
    if rings:
        down_out = grads(
            down_grad_kernel, "down_grad", where, (active, d_second), r, groups * width // 2, parts=4
        )
        d_heads[0][0], *down_out.out = together(d_heads[0][0], *down_out.out)
        down_out.cross()
        down_out.cross()
    else:
        grad_fc2 = reduce_plain(active, d_second)
        grad_fc1 = reduce_plain(normed_two, d_hidden)
        grad_proj = reduce_plain(attended, d_branch)
    d_mixed, qkv_out, total_qkv = [], [], []
    for j in range(chunks):
        d_by_heads = list(attn_bwd(where, by_heads[j], d_heads[j], kept[j][0], kept[j][1], heads, 512))
        d_mixed.append(exchange(d_by_heads))
        if rings and j == 0:
            normed_two, d_by_heads[0], down_out.from_x[0], down_out.from_x[1] = together(
                normed_two, d_by_heads[0], down_out.from_x[0], down_out.from_x[1]
            )
            down_out.cross(down_out.from_x[0])
            down_out.add(0)
            down_out.ring()
            up_out = grads(
                up_grad_kernel,
                "up_grad",
                where,
                (normed_two, d_hidden, attended, d_branch),
                r,
                (width + ff) // 2,
                parts=4,
                after=(down_out.from_x[2], down_out.passed),
            )
            d_heads[1][0], *up_out.out = together(d_heads[1][0], *up_out.out)
            down_out.cross(down_out.passed)
            down_out.add(1)
            down_out.ring()
            up_out.cross(down_out.from_x[2])
        if rings and j == 1:
            d_mixed[0][0], down_out.from_x[3], down_out.passed, up_out.from_x[0], unused = together(
                d_mixed[0][0], down_out.from_x[3], down_out.passed, up_out.from_x[0], d_by_heads[0]
            )
            up_out.cross(down_out.from_x[3])
            down_out.add(2)
            down_out.cur = tie(down_out.cur, *d_mixed[1])
            down_out.ring()
            up_out.add(0)
            up_out.cur = tie(up_out.cur, *d_mixed[1])
            up_out.ring()
    for j in range(chunks):
        if rings and j == 1:
            d_mixed[1][0], up_out.from_x[1], down_out.passed, *qkv_out[0].out = together(
                d_mixed[1][0], up_out.from_x[1], down_out.passed, *qkv_out[0].out
            )
            down_out.add(3)
            up_out.cross(up_out.from_x[1])
            qkv_out[0].cross(up_out.from_x[1])
        if rings:
            qkv_out.append(
                grads(
                    qkv_grad_kernel,
                    "qkv_grad",
                    where,
                    [normed] + d_mixed[j],
                    r,
                    n_seq // 2 * 3 * part,
                    [VMEM] + [ANY] * n_seq,
                    [pltpu.VMEM((seq_len, 3 * part), BF16), pltpu.SemaphoreType.DMA((n_seq,))],
                )
            )
        else:
            me = where[3]
            blocks = jnp.stack(d_mixed[j])
            order = jnp.stack([jnp.bitwise_xor(me, i) for i in range(n_seq)])
            blocks = jnp.take(blocks, order, axis=0)
            total_qkv.append(reduce_plain(normed, blocks.transpose(1, 0, 2).reshape(rows, -1)))
    if rings:
        d_mixed[1][0], up_out.passed, up_out.from_x[2], *qkv_out[1].out = together(
            d_mixed[1][0], up_out.passed, up_out.from_x[2], *qkv_out[1].out
        )
        up_out.add(1)
        up_out.ring()
        up_out.cross(up_out.from_x[2])
        qkv_out[0].cross(up_out.from_x[2])
    tokens_grad, small_grads = last(
        where, d_mixed, tokens, d_residual, vec, sums, fc1_sum, qkv_pieces
    )
    if rings:
        small_grads, up_out.from_x[3], qkv_out[0].from_x[0] = together(
            small_grads, up_out.from_x[3], qkv_out[0].from_x[0]
        )
    total_small = reduce_small(small_grads, fc1_sum, own)
    if rings:
        qkv_out[1].cross(up_out.from_x[3])
        qkv_out[1].cross(up_out.from_x[3])
        for step in range(2, nz):
            up_out.add(step)
            if step < nz - 1:
                up_out.ring()
        for step in range(nz):
            for flow in qkv_out:
                flow.add(step)
                if step < nz - 1:
                    flow.ring()
        low = down_out.finish()
        grad_fc2 = jnp.stack(low).reshape(2, r, groups, width // 2).transpose(2, 1, 0, 3)
        grad_fc2 = grad_fc2.reshape(groups * r, width).astype(F32)
        low = up_out.finish()
        at = width // 2
        grad_proj = jnp.concatenate([part_[:, :at] for part_ in low], axis=1).astype(F32)
        grad_fc1 = jnp.concatenate([part_[:, at:] for part_ in low], axis=1).astype(F32)
        total_qkv = [jnp.concatenate(f.finish(), axis=1).astype(F32) for f in qkv_out]
    qkv_grad = jnp.stack([t.reshape(-1, n_seq, 3, part) for t in total_qkv])
    qkv_grad = qkv_grad.transpose(1, 3, 2, 0, 4).reshape(-1, 3 * width)
    return (
        layer_out,
        tokens_grad,
        qkv_grad,
        total_small[0:2],
        grad_proj,
        grad_fc1,
        total_small[N_VEC:].reshape(-1),
        grad_fc2,
        total_small[2:4],
        total_small[4:8],
        total_small[8:12],
    )


CHUNKS = 2


def solution(mesh):
    n_dp, n_seq = mesh.devices.shape
    fine = Mesh(mesh.devices.reshape(n_dp // 2, 2, n_seq // 2, 2), DP_AXES + SEQ_AXES)
    tok = P(DP_AXES + SEQ_AXES, None)
    by_row = P(DP_AXES, None)
    by_col = P(None, DP_AXES)
    weights = (by_row, by_col, by_row, by_row, P(DP_AXES), by_row, by_col, by_col, by_col)
    return jax.shard_map(
        per_device,
        mesh=fine,
        in_specs=(tok, tok) + weights,
        out_specs=(tok, tok) + weights,
        check_vma=False,
    )
```

time: 688 us -> 555 us (0.81)
  Pallas kernels: 75.3 us -> 183 us
  matrix products: 92.9 us -> 0 us
  local copies, waits for them, and re-layouts: 93.8 us -> 29.5 us
  waiting for transfers between devices: 252 us -> 210 us
  other arithmetic: 69.4 us -> 42.7 us
  starting transfers between devices: 90 us -> 79.5 us
    pallas_call x6 -> x13, Pallas kernels: 75.3 us -> 183 us  [the longest x9 120 us: call(): pl.pallas_call(kernel, grid_spec=pltpu.PrefetchScalarGridSpec(num_scalar_...]
    dot_general x21 -> x0, matrix products: 92.9 us -> none  [the longest x8 40.8 us: contract_cols(): lax.dot_general(left, right, (((1,), (1,)), ((), ())), preferred_element_...]
    ppermute x99 -> x117, waiting for transfers between devices: 251 us -> 210 us  [the longest x12 60.6 us: ring(): lax.ppermute(tie(self.cur, *after) if after else self.cur, 'z', ring(nz))]
    unnamed x272 -> x217, local copies, waits for them, and re-layouts: 54 us -> 16.8 us
    reduce_sum x17 -> x0, other arithmetic: 20.4 us -> none  [the longest x7 9.39 us: layer_norm(): return centred * lax.rsqrt(variance + NORM_EPS) * gain_vec + shift_vec]
    all_to_all x4 -> x0, starting transfers between devices: 17.5 us -> none  [the longest x1 4.79 us: per_device(): lax.all_to_all(d_by_heads, SEQ_AXES, split_axis=0, concat_axis=1, tiled=T...]
    dynamic_slice x11 -> x0, local copies, waits for them, and re-layouts: 12.8 us -> none  [the longest x4 9.86 us: reduce_grad(): send = lax.dynamic_slice(grad, (0, (1 - c) * half), (all_rows, half))]
    dot_general x3 -> x0, local copies, waits for them, and re-layouts: 12.8 us -> none  [dot_halves(): jnp.dot(left, halves[i], preferred_element_type=F32)]
  transfers between devices with their start and end apart: 105 -> 119, of which waited for: 40 -> 43; matrix products, arithmetic and copies ran while one was open for 21% -> 11% of each run, Pallas kernels for 11% -> 22%
where the time goes in v2:
time: 555 us; the launch traced here: 547 us
  waiting for transfers between devices  210 us (38%)
  Pallas kernels  183 us (33%)
  starting transfers between devices  79.5 us (14%)
  other arithmetic  42.7 us (8%)
  local copies, waits for them, and re-layouts  29.5 us (5%)
    pallas_call x9, Pallas kernels, call(): pl.pallas_call(kernel, grid_spec=pltpu.PrefetchScalarGridSpec(num_scalar_...  120 us
    ppermute x12, waiting for transfers between devices, ring(): lax.ppermute(tie(self.cur, *after) if after else self.cur, 'z', ring(nz))  60.6 us
    ppermute x16, waiting for transfers between devices, hop(): other = lax.ppermute(cur, 'x', SWAP)  46 us
    pallas_call x2, Pallas kernels, attn_bwd(): pl.pallas_call(functools.partial(bwd_kernel, nh=nh, blk=blk, n=n), grid_s...  41.4 us
    convert_element_type x29, other arithmetic, add_low(): return sum((t.astype(F32) for t in terms)).astype(BF16)  31.9 us
    ppermute x12, waiting for transfers between devices, hop(): self.cur = lax.ppermute(cur, 'z', ring(nz))  24.6 us
    pallas_call x2, Pallas kernels, attn_fwd(): pl.pallas_call(functools.partial(fwd_kernel, nh=nh, blk=blk, n=n), grid_s...  21.5 us
    ppermute x12, waiting for transfers between devices, cross(): lax.ppermute(tie(block, *after) if after else block, 'x', SWAP)  20.7 us
  transfers between devices with their start and end apart: 119, of which 43 were waited for; matrix products, arithmetic and copies ran while one was open for 11% of the time, Pallas kernels for 22%

profile of v2, /device:TPU:0, one launch (start us, length us, event | category | flops | bytes accessed | tf_op | source)
XLA Modules:
  0.0 546.8 jit_solution(13200960618248870071)
XLA Ops:
  2.1 3.1 collective-permute-start.1
  21.7 3.0 collective-permute-done.8.refs_2_.refs_15_
  28.2 8.1 %collective-permute-done.5.refs_6_ = bf16[16,128]{1,0:T(8,128)(2,1)S(1)} collective-permute-done((bf16[16,128]{1,0:T(8,128)(2,1)S(1)}, bf16[16,128]{1,0:T(8,128)(2,1)S(1)}, u32[]{:S(2)}, u32[]{:S(2)}) %collective-permute-start.5) | collective-permute-done | bytes 4128 | tf_op jit(solution)/shard_map/ppermute | solution.py:253
  39.0 6.1 %collective-permute-done.6.refs_7_ = bf16[16,128]{1,0:T(8,128)(2,1)S(1)} collective-permute-done((bf16[16,128]{1,0:T(8,128)(2,1)S(1)}, bf16[16,128]{1,0:T(8,128)(2,1)S(1)}, u32[]{:S(2)}, u32[]{:S(2)}) %collective-permute-start.6) | collective-permute-done | bytes 4128 | tf_op jit(solution)/shard_map/ppermute | solution.py:254
  48.9 5.9 %collective-permute-done.13.refs_7_.refs_20_ = bf16[128,1536]{1,0:T(8,128)(2,1)} collective-permute-done((bf16[128,1536]{1,0:T(8,128)(2,1)}, bf16[128,1536]{1,0:T(8,128)(2,1)}, u32[]{:S(2)}, u32[]{:S(2)}) %collective-permute-start.13) | collective-permute-done | bytes 393248 | tf_op jit(solution)/shard_map/ppermute | solution.py:254
  58.8 8.0 %qkv.2 = (bf16[512,384]{1,0:T(8,128)(2,1)}, bf16[512,384]{1,0:T(8,128)(2,1)}, bf16[512,384]{1,0:T(8,128)(2,1)}, bf16[512,384]{1,0:T(8,128)(2,1)}, bf16[512,1024]{1,0:T(8,128)(2,1)}) custom-call(s32[4]{0:T(128)} %pad_add_fusion.where, bf16[512,1024]{1,0:T(8,128)(2,1)} %refs_8_.3, f32[16,1024]{1,0:T(8,128)} %get-tuple-element.158.vec.refs_10_, ...), custom_call_target="tpu_custom_call" | custom-call | flops 7699999744 | bytes 1048576 | tf_op jit(solution)/shard_map/qkv/pallas_call | solution.py:209
  67.4 7.9 %collective-permute-done.22.refs_13_ = bf16[128,2560]{1,0:T(8,128)(2,1)S(1)} collective-permute-done((bf16[128,2560]{1,0:T(8,128)(2,1)S(1)}, bf16[128,2560]{1,0:T(8,128)(2,1)S(1)}, u32[]{:S(2)}, u32[]{:S(2)}) %collective-permute-start.22) | collective-permute-done | bytes 655392 | tf_op jit(solution)/shard_map/ppermute | solution.py:254
  81.1 6.9 %qkv.3 = (bf16[512,384]{1,0:T(8,128)(2,1)}, bf16[512,384]{1,0:T(8,128)(2,1)}, bf16[512,384]{1,0:T(8,128)(2,1)}, bf16[512,384]{1,0:T(8,128)(2,1)}) custom-call(s32[4]{0:T(128)} %pad_add_fusion.where, bf16[512,1024]{1,0:T(8,128)(2,1)} %get-tuple-element.179.first.normed, f32[16,1024]{1,0:T(8,128)} %get-tuple-element.158.vec.refs_10_, ...), custom_call_target="tpu_custom_call" | custom-call | flops 7699999744 | bytes 1048576 | tf_op jit(solution)/shard_map/qkv/pallas_call | solution.py:209
  89.7 2.6 collective-permute-done.24.refs_28_
  93.1 2.6 collective-permute-done.23.refs_29_
  97.2 3.8 collective-permute-done.27.refs_3_
  101.5 8.0 %collective-permute-done.36.refs_2_ = bf16[512,384]{1,0:T(8,128)(2,1)S(1)} collective-permute-done((bf16[512,384]{1,0:T(8,128)(2,1)}, bf16[512,384]{1,0:T(8,128)(2,1)S(1)}, u32[]{:S(2)}, u32[]{:S(2)}) %collective-permute-start.36) | collective-permute-done | bytes 393248 | tf_op jit(solution)/shard_map/ppermute | solution.py:869
  112.7 10.7 %attn_fwd.2 = (bf16[512,128]{1,0:T(8,128)(2,1)S(1)}, bf16[512,128]{1,0:T(8,128)(2,1)S(1)}, bf16[512,128]{1,0:T(8,128)(2,1)S(1)}, bf16[512,128]{1,0:T(8,128)(2,1)...) custom-call(s32[4]{0:T(128)S(1)} %copy-done, bf16[512,384]{1,0:T(8,128)(2,1)S(1)} %copy-done.8, ...), custom_call_target="tpu_custom_call" | custom-call | flops 9900000256 | bytes 1048576 | tf_op jit(solution)/shard_map/attn_fwd/pallas_call | solution.py:96
  133.4 10.7 %attn_fwd.3 = (bf16[512,128]{1,0:T(8,128)(2,1)S(1)}, bf16[512,128]{1,0:T(8,128)(2,1)S(1)}, bf16[512,128]{1,0:T(8,128)(2,1)S(1)}, bf16[512,128]{1,0:T(8,128)(2,1)...) custom-call(s32[4]{0:T(128)S(1)} %copy-done, bf16[512,384]{1,0:T(8,128)(2,1)S(1)} %copy-done.7, ...), custom_call_target="tpu_custom_call" | custom-call | flops 9900000256 | bytes 1048576 | tf_op jit(solution)/shard_map/attn_fwd/pallas_call | solution.py:96
  147.3 2.7 collective-permute-start.52
  154.6 3.5 collective-permute-done.40.refs_7_
  158.7 5.1 collective-permute-done.52.refs_33_
  163.8 2.2 collective-permute-done.51.refs_32_
  168.2 11.9 %collective-permute-done.43.refs_19_ = bf16[128,2560]{1,0:T(8,128)(2,1)S(1)} collective-permute-done((bf16[128,2560]{1,0:T(8,128)(2,1)S(1)}, bf16[128,2560]{1,0:T(8,128)(2,1)S(1)}, u32[]{:S(2)}, u32[]{:S(2)}) %collective-permute-start.43) | collective-permute-done | bytes 655392 | tf_op jit(solution)/shard_map/ppermute | solution.py:254
  180.7 9.3 %collective-permute-done.53.refs_34_ = bf16[128,2048]{1,0:T(8,128)(2,1)S(1)} collective-permute-done((bf16[128,2048]{1,0:T(8,128)(2,1)S(1)}, bf16[128,2048]{1,0:T(8,128)(2,1)S(1)}, u32[]{:S(2)}, u32[]{:S(2)}) %collective-permute-start.53) | collective-permute-done | bytes 524320 | tf_op jit(solution)/shard_map/ppermute | solution.py:254
  192.9 53.9 %mlp.1 = (bf16[512,1024]{1,0:T(8,128)(2,1)}, f32[512,1024]{1,0:T(8,128)}, bf16[512,1024]{1,0:T(8,128)(2,1)}, bf16[512,4096]{1,0:T(8,128)(2,1)}, bf16[512,4096]{1...) custom-call(s32[4]{0:T(128)} %pad_add_fusion.where, ...), custom_call_target="tpu_custom_call" | custom-call | flops 49500000256 | bytes 1048576 | tf_op jit(solution)/shard_map/mlp/pallas_call | solution.py:209
  246.9 9.6 %down_grad.1 = (bf16[4,128,2048]{2,1,0:T(8,128)(2,1)}, bf16[4,128,2048]{2,1,0:T(8,128)(2,1)}, bf16[4,128,2048]{2,1,0:T(8,128)(2,1)}, bf16[4,128,2048]{2,1,0:T(8,128)(2,1)}) custom-call(s32[4]{0:T(128)} %pad_add_fusion.where, bf16[512,4096]{1,0:T(8,128)(2,1)} %get-tuple-element.210.active, bf16[512,1024]{1,0:T(8,128)(2,1)} %get-tuple-element.211.d_second), custom_call_target="tpu_custom_call" | custom-call | flops 11000000512 | bytes 1048576 | tf_op jit(solution)/shard_map/down_grad/pallas_call | solution.py:209
  259.2 2.4 collective-permute-done.61
  261.6 3.1 add_convert_fusion.8
  267.4 20.7 %attn_bwd.2 = (bf16[512,384]{1,0:T(8,128)(2,1)}, bf16[512,384]{1,0:T(8,128)(2,1)}, bf16[512,384]{1,0:T(8,128)(2,1)}, bf16[512,384]{1,0:T(8,128)(2,1)}) custom-call(s32[4]{0:T(128)} %pad_add_fusion.where, bf16[512,384]{1,0:T(8,128)(2,1)} %get-tuple-element.171.refs_0_, bf16[512,384]{1,0:T(8,128)(2,1)} %copy-done.4, bf16[512,384]{1,0:T(8,128)(2,1)} %copy-done.5, ...), custom_call_target="tpu_custom_call" | custom-call | flops 20899999744 | bytes 1048576 | tf_op jit(solution)/shard_map/attn_bwd/pallas_call | solution.py:163
  293.7 2.4 collective-permute-start.68
  296.1 12.2 %up_grad.1 = (bf16[4,128,2560]{2,1,0:T(8,128)(2,1)}, bf16[4,128,2560]{2,1,0:T(8,128)(2,1)}, bf16[4,128,2560]{2,1,0:T(8,128)(2,1)}, bf16[4,128,2560]{2,1,0:T(8,128)(2,1)}) custom-call(s32[4]{0:T(128)} %pad_add_fusion.where, bf16[512,1024]{1,0:T(8,128)(2,1)} %get-tuple-element.231.normed_two, bf16[512,4096]{1,0:T(8,128)(2,1)} %get-tuple-element.232.d_hidden, ...), custom_call_target="tpu_custom_call" | custom-call | flops 11000000512 | bytes 1048576 | tf_op jit(solution)/shard_map/up_grad/pallas_call | solution.py:209
  319.1 9.1 %collective-permute-done.69 = bf16[1,128,2048]{2,1,0:T(8,128)(2,1)S(1)} collective-permute-done((bf16[1,128,2048]{2,1,0:T(8,128)(2,1)S(1)}, bf16[1,128,2048]{2,1,0:T(8,128)(2,1)S(1)}, u32[]{:S(2)}, u32[]{:S(2)}) %collective-permute-start.69) | collective-permute-done | bytes 524320 | tf_op jit(solution)/shard_map/ppermute | solution.py:725
  328.7 20.7 %attn_bwd.3 = (bf16[512,384]{1,0:T(8,128)(2,1)}, bf16[512,384]{1,0:T(8,128)(2,1)}, bf16[512,384]{1,0:T(8,128)(2,1)}, bf16[512,384]{1,0:T(8,128)(2,1)}) custom-call(s32[4]{0:T(128)} %pad_add_fusion.where, bf16[512,384]{1,0:T(8,128)(2,1)} %get-tuple-element.187.refs_0_, bf16[512,384]{1,0:T(8,128)(2,1)} %copy-done.1, bf16[512,384]{1,0:T(8,128)(2,1)} %copy-done.2, ...), custom_call_target="tpu_custom_call" | custom-call | flops 20899999744 | bytes 1048576 | tf_op jit(solution)/shard_map/attn_bwd/pallas_call | solution.py:163
  350.9 6.3 %qkv_grad.2 = (bf16[4,128,768]{2,1,0:T(8,128)(2,1)}, bf16[4,128,768]{2,1,0:T(8,128)(2,1)}, bf16[4,128,768]{2,1,0:T(8,128)(2,1)}, bf16[4,128,768]{2,1,0:T(8,128)(2,1)}) custom-call(s32[4]{0:T(128)} %pad_add_fusion.where, bf16[512,1024]{1,0:T(8,128)(2,1)} %get-tuple-element.179.first.normed, bf16[512,384]{1,0:T(8,128)(2,1)} %get-tuple-element.249.refs_0_, ...), custom_call_target="tpu_custom_call" | custom-call | flops 11000000512 | bytes 1048576 | tf_op jit(solution)/shard_map/qkv_grad/pallas_call | solution.py:209
  360.8 2.5 fusion.4
  363.2 6.4 %collective-permute-done.82.refs_2_.refs_6_ = bf16[512,384]{1,0:T(8,128)(2,1)S(1)} collective-permute-done((bf16[512,384]{1,0:T(8,128)(2,1)}, bf16[512,384]{1,0:T(8,128)(2,1)S(1)}, u32[]{:S(2)}, u32[]{:S(2)}) %collective-permute-start.82) | collective-permute-done | bytes 393248 | tf_op jit(solution)/shard_map/ppermute | solution.py:869
  369.6 7.4 %collective-permute-done.83.refs_3_.refs_7_ = bf16[512,384]{1,0:T(8,128)(2,1)} collective-permute-done((bf16[512,384]{1,0:T(8,128)(2,1)}, bf16[512,384]{1,0:T(8,128)(2,1)}, u32[]{:S(2)}, u32[]{:S(2)}) %collective-permute-start.83) | collective-permute-done | bytes 393248 | tf_op jit(solution)/shard_map/ppermute | solution.py:870
  378.6 14.6 %collective-permute-done.84 = bf16[128,2048]{1,0:T(8,128)(2,1)S(1)} collective-permute-done((bf16[128,2048]{1,0:T(8,128)(2,1)}, bf16[128,2048]{1,0:T(8,128)(2,1)S(1)}, u32[]{:S(2)}, u32[]{:S(2)}) %collective-permute-start.84) | collective-permute-done | bytes 524320 | tf_op jit(solution)/shard_map/ppermute | solution.py:737
  394.0 6.4 %qkv_grad.3 = (bf16[4,128,768]{2,1,0:T(8,128)(2,1)}, bf16[4,128,768]{2,1,0:T(8,128)(2,1)}, bf16[4,128,768]{2,1,0:T(8,128)(2,1)}, bf16[4,128,768]{2,1,0:T(8,128)(2,1)}) custom-call(s32[4]{0:T(128)} %pad_add_fusion.where, bf16[512,1024]{1,0:T(8,128)(2,1)} %get-tuple-element.179.first.normed, bf16[512,384]{1,0:T(8,128)(2,1)} %get-tuple-element.273.refs_0_.refs_4_, ...), custom_call_target="tpu_custom_call" | custom-call | flops 11000000512 | bytes 1048576 | tf_op jit(solution)/shard_map/qkv_grad/pallas_call | solution.py:209
  409.7 11.8 %collective-permute-done.87 = bf16[128,2560]{1,0:T(8,128)(2,1)S(1)} collective-permute-done((bf16[128,2560]{1,0:T(8,128)(2,1)S(1)}, bf16[128,2560]{1,0:T(8,128)(2,1)S(1)}, u32[]{:S(2)}, u32[]{:S(2)}) %collective-permute-start.87) | collective-permute-done | bytes 655392 | tf_op jit(solution)/shard_map/ppermute | solution.py:737
  421.6 7.0 %collective-permute-done.88 = bf16[1,128,2560]{2,1,0:T(8,128)(2,1)S(1)} collective-permute-done((bf16[1,128,2560]{2,1,0:T(8,128)(2,1)S(1)}, bf16[1,128,2560]{2,1,0:T(8,128)(2,1)S(1)}, u32[]{:S(2)}, u32[]{:S(2)}) %collective-permute-start.88) | collective-permute-done | bytes 655392 | tf_op jit(solution)/shard_map/ppermute | solution.py:725
  431.0 14.1 %last.1 = (bf16[512,1024]{1,0:T(8,128)(2,1)}, f32[8,16,128]{2,1,0:T(8,128)}) custom-call(s32[4]{0:T(128)} %pad_add_fusion.where, bf16[512,384]{1,0:T(8,128)(2,1)} %get-tuple-element.249.refs_0_, bf16[512,384]{1,0:T(8,128)(2,1)} %copy-done.78, bf16[512,384]{1,0:T(8,128)(2,1)} %copy-done.79, bf16[512,384]{1,0:T(8,128)(2,1)} %collective-permute-done.79.refs_3_, ...), custom_call_target="tpu_custom_call" | custom-call | flops 13200000000 | bytes 1048576 | tf_op jit(solution)/shard_map/last/pallas_call | solution.py:209
  451.6 2.4 fusion.2
  465.4 7.6 %collective-permute-done.110 = bf16[16,128]{1,0:T(8,128)(2,1)S(1)} collective-permute-done((bf16[16,128]{1,0:T(8,128)(2,1)S(1)}, bf16[16,128]{1,0:T(8,128)(2,1)S(1)}, u32[]{:S(2)}, u32[]{:S(2)}) %collective-permute-start.110) | collective-permute-done | bytes 4128 | tf_op jit(solution)/shard_map/ppermute | solution.py:860
  474.5 3.9 collective-permute-done.111
  480.7 3.7 collective-permute-done.112
  491.6 17.7 %collective-permute-done.94 = bf16[128,768]{1,0:T(8,128)(2,1)S(1)} collective-permute-done((bf16[128,768]{1,0:T(8,128)(2,1)S(1)}, bf16[128,768]{1,0:T(8,128)(2,1)S(1)}, u32[]{:S(2)}, u32[]{:S(2)}) %collective-permute-start.94) | collective-permute-done | bytes 196640 | tf_op jit(solution)/shard_map/ppermute | solution.py:737
  510.4 3.0 collective-permute-done.101
  514.5 3.3 collective-permute-done.96
  520.2 3.9 collective-permute-done.102
  527.3 5.5 %collective-permute-done.104 = bf16[128,768]{1,0:T(8,128)(2,1)S(1)} collective-permute-done((bf16[128,768]{1,0:T(8,128)(2,1)S(1)}, bf16[128,768]{1,0:T(8,128)(2,1)S(1)}, u32[]{:S(2)}, u32[]{:S(2)}) %collective-permute-start.104) | collective-permute-done | bytes 196640 | tf_op jit(solution)/shard_map/ppermute | solution.py:737
  534.5 5.4 collective-permute-done.105
  (491 shorter events, 155.0 us)
Async XLA Ops:
  58.1 17.2 %collective-permute-start.22 = (bf16[128,2560]{1,0:T(8,128)(2,1)S(1)}, bf16[128,2560]{1,0:T(8,128)(2,1)S(1)}, u32[]{:S(2)}, u32[]{:S(2)}) collective-permute-start(bf16[128,2560]{1,0:T(8,128)(2,1)S(1)} %copy-done.30), channel_id=1, source_target_pairs={{0,4},{4,0},{1,5},{5,1},{2,6},{6,2},{3,7},{7,3},{8,12},{12,8},{9,1... | collective-permute-start | bytes 1966088 | tf_op jit(solution)/shard_map/ppermute | solution.py:254
  58.7 18.8 %collective-permute-start.21 = (bf16[128,2560]{1,0:T(8,128)(2,1)S(1)}, bf16[128,2560]{1,0:T(8,128)(2,1)}, u32[]{:S(2)}, u32[]{:S(2)}) collective-permute-start(bf16[128,2560]{1,0:T(8,128)(2,1)S(1)} %copy-done.30), channel_id=1, source_target_pairs={{0,8},{8,16},{16,24},{24,0},{1,9},{9,17},{17,25},{25,1},{2,10},{10... | collective-permute-start | bytes 1966088 | tf_op jit(solution)/shard_map/ppermute | solution.py:253
  79.0 16.8 %collective-permute-start.23 = (bf16[128,2048]{1,0:T(8,128)(2,1)S(1)}, bf16[128,2048]{1,0:T(8,128)(2,1)}, u32[]{:S(2)}, u32[]{:S(2)}) collective-permute-start(bf16[128,2048]{1,0:T(8,128)(2,1)S(1)} %copy-done.44), channel_id=1, source_target_pairs={{0,8},{8,16},{16,24},{24,0},{1,9},{9,17},{17,25},{25,1},{2,10},{10... | collective-permute-start | bytes 1572872 | tf_op jit(solution)/shard_map/ppermute | solution.py:253
  79.0 30.6 %collective-permute-start.32 = (bf16[128,2560]{1,0:T(8,128)(2,1)}, bf16[128,2560]{1,0:T(8,128)(2,1)}, u32[]{:S(2)}, u32[]{:S(2)}) collective-permute-start(bf16[128,2560]{1,0:T(8,128)(2,1)} %collective-permute-done.21.refs_14_), channel_id=1, source_target_pairs={{0,4},{4,0},{1,5},{5,1},{2,6},{6,2},{3,7},{7,3},{8,12},{12,8},{9,1... | collective-permute-start | bytes 1966088 | tf_op jit(solution)/shard_map/ppermute | solution.py:254
  79.5 31.6 %collective-permute-start.31 = (bf16[128,2560]{1,0:T(8,128)(2,1)}, bf16[128,2560]{1,0:T(8,128)(2,1)}, u32[]{:S(2)}, u32[]{:S(2)}) collective-permute-start(bf16[128,2560]{1,0:T(8,128)(2,1)} %collective-permute-done.21.refs_14_), channel_id=1, source_target_pairs={{0,8},{8,16},{16,24},{24,0},{1,9},{9,17},{17,25},{25,1},{2,10},{10... | collective-permute-start | bytes 1966088 | tf_op jit(solution)/shard_map/ppermute | solution.py:253
  101.0 28.6 %collective-permute-start.44 = (bf16[128,2560]{1,0:T(8,128)(2,1)S(1)}, bf16[128,2560]{1,0:T(8,128)(2,1)S(1)}, u32[]{:S(2)}, u32[]{:S(2)}) collective-permute-start(bf16[128,2560]{1,0:T(8,128)(2,1)S(1)} %collective-permute-done.22.refs_13_), channel_id=1, source_target_pairs={{0,1},{1,0},{2,3},{3,2},{4,5},{5,4},{6,7},{7,6},{8,9},{9,8},{10,11... | collective-permute-start | bytes 1966088 | tf_op jit(solution)/shard_map/ppermute | solution.py:269
  101.4 27.7 %collective-permute-start.45 = (bf16[128,2560]{1,0:T(8,128)(2,1)}, bf16[128,2560]{1,0:T(8,128)(2,1)S(1)}, u32[]{:S(2)}, u32[]{:S(2)}) collective-permute-start(bf16[128,2560]{1,0:T(8,128)(2,1)} %collective-permute-done.21.refs_14_), channel_id=1, source_target_pairs={{0,1},{1,0},{2,3},{3,2},{4,5},{5,4},{6,7},{7,6},{8,9},{9,8},{10,11... | collective-permute-start | bytes 1966088 | tf_op jit(solution)/shard_map/ppermute | solution.py:269
  109.5 19.5 %collective-permute-start.37 = (bf16[512,384]{1,0:T(8,128)(2,1)}, bf16[512,384]{1,0:T(8,128)(2,1)S(1)}, u32[]{:S(2)}, u32[]{:S(2)}) collective-permute-start(bf16[512,384]{1,0:T(8,128)(2,1)} %get-tuple-element.190), channel_id=1, source_target_pairs={{0,3},{1,2},{2,1},{3,0},{4,7},{5,6},{6,5},{7,4},{8,11},{9,10},{10,... | collective-permute-start | bytes 1179656 | tf_op jit(solution)/shard_map/ppermute | solution.py:870
  109.6 15.5 %collective-permute-start.34 = (bf16[128,2048]{1,0:T(8,128)(2,1)}, bf16[128,2048]{1,0:T(8,128)(2,1)S(1)}, u32[]{:S(2)}, u32[]{:S(2)}) collective-permute-start(bf16[128,2048]{1,0:T(8,128)(2,1)} %collective-permute-done.23.refs_29_), channel_id=1, source_target_pairs={{0,4},{4,0},{1,5},{5,1},{2,6},{6,2},{3,7},{7,3},{8,12},{12,8},{9,1... | collective-permute-start | bytes 1572872 | tf_op jit(solution)/shard_map/ppermute | solution.py:254
  111.1 15.9 %collective-permute-start.33 = (bf16[128,2048]{1,0:T(8,128)(2,1)}, bf16[128,2048]{1,0:T(8,128)(2,1)S(1)}, u32[]{:S(2)}, u32[]{:S(2)}) collective-permute-start(bf16[128,2048]{1,0:T(8,128)(2,1)} %collective-permute-done.23.refs_29_), channel_id=1, source_target_pairs={{0,8},{8,16},{16,24},{24,0},{1,9},{9,17},{17,25},{25,1},{2,10},{10... | collective-permute-start | bytes 1572872 | tf_op jit(solution)/shard_map/ppermute | solution.py:253
  129.0 18.1 %collective-permute-start.54 = (bf16[128,2048]{1,0:T(8,128)(2,1)S(1)}, bf16[128,2048]{1,0:T(8,128)(2,1)S(1)}, u32[]{:S(2)}, u32[]{:S(2)}) collective-permute-start(bf16[128,2048]{1,0:T(8,128)(2,1)S(1)} %copy-done.62), channel_id=1, source_target_pairs={{0,1},{1,0},{2,3},{3,2},{4,5},{5,4},{6,7},{7,6},{8,9},{9,8},{10,11... | collective-permute-start | bytes 1572872 | tf_op jit(solution)/shard_map/ppermute | solution.py:269
  129.1 16.2 %collective-permute-start.55 = (bf16[128,2048]{1,0:T(8,128)(2,1)}, bf16[128,2048]{1,0:T(8,128)(2,1)S(1)}, u32[]{:S(2)}, u32[]{:S(2)}) collective-permute-start(bf16[128,2048]{1,0:T(8,128)(2,1)} %collective-permute-done.23.refs_29_), channel_id=1, source_target_pairs={{0,1},{1,0},{2,3},{3,2},{4,5},{5,4},{6,7},{7,6},{8,9},{9,8},{10,11... | collective-permute-start | bytes 1572872 | tf_op jit(solution)/shard_map/ppermute | solution.py:269
  130.9 21.8 %collective-permute-start.42 = (bf16[128,2560]{1,0:T(8,128)(2,1)}, bf16[128,2560]{1,0:T(8,128)(2,1)S(1)}, u32[]{:S(2)}, u32[]{:S(2)}) collective-permute-start(bf16[128,2560]{1,0:T(8,128)(2,1)} %collective-permute-done.31.refs_16_), channel_id=1, source_target_pairs={{0,8},{8,16},{16,24},{24,0},{1,9},{9,17},{17,25},{25,1},{2,10},{10... | collective-permute-start | bytes 1966088 | tf_op jit(solution)/shard_map/ppermute | solution.py:253
  132.9 19.9 %collective-permute-start.41 = (bf16[128,2560]{1,0:T(8,128)(2,1)}, bf16[128,2560]{1,0:T(8,128)(2,1)S(1)}, u32[]{:S(2)}, u32[]{:S(2)}) collective-permute-start(bf16[128,2560]{1,0:T(8,128)(2,1)} %collective-permute-done.31.refs_16_), channel_id=1, source_target_pairs={{0,4},{4,0},{1,5},{5,1},{2,6},{6,2},{3,7},{7,3},{8,12},{12,8},{9,1... | collective-permute-start | bytes 1966088 | tf_op jit(solution)/shard_map/ppermute | solution.py:254
  147.1 18.9 %collective-permute-start.47 = (bf16[128,2560]{1,0:T(8,128)(2,1)}, bf16[128,2560]{1,0:T(8,128)(2,1)S(1)}, u32[]{:S(2)}, u32[]{:S(2)}) collective-permute-start(bf16[128,2560]{1,0:T(8,128)(2,1)} %collective-permute-done.31.refs_16_), channel_id=1, source_target_pairs={{0,1},{1,0},{2,3},{3,2},{4,5},{5,4},{6,7},{7,6},{8,9},{9,8},{10,11... | collective-permute-start | bytes 1966088 | tf_op jit(solution)/shard_map/ppermute | solution.py:269
  147.3 16.5 %collective-permute-start.52 = (bf16[128,2048]{1,0:T(8,128)(2,1)S(1)}, bf16[128,2048]{1,0:T(8,128)(2,1)S(1)}, u32[]{:S(2)}, u32[]{:S(2)}) collective-permute-start(bf16[128,2048]{1,0:T(8,128)(2,1)S(1)} %collective-permute-done.33.refs_31_), channel_id=1, source_target_pairs={{0,8},{8,16},{16,24},{24,0},{1,9},{9,17},{17,25},{25,1},{2,10},{10... | collective-permute-start | bytes 1572872 | tf_op jit(solution)/shard_map/ppermute | solution.py:253
  158.1 22.0 %collective-permute-start.43 = (bf16[128,2560]{1,0:T(8,128)(2,1)S(1)}, bf16[128,2560]{1,0:T(8,128)(2,1)S(1)}, u32[]{:S(2)}, u32[]{:S(2)}) collective-permute-start(bf16[128,2560]{1,0:T(8,128)(2,1)S(1)} %collective-permute-done.42.refs_18_), channel_id=1, source_target_pairs={{0,4},{4,0},{1,5},{5,1},{2,6},{6,2},{3,7},{7,3},{8,12},{12,8},{9,1... | collective-permute-start | bytes 1966088 | tf_op jit(solution)/shard_map/ppermute | solution.py:254
  166.6 23.3 %collective-permute-start.53 = (bf16[128,2048]{1,0:T(8,128)(2,1)S(1)}, bf16[128,2048]{1,0:T(8,128)(2,1)S(1)}, u32[]{:S(2)}, u32[]{:S(2)}) collective-permute-start(bf16[128,2048]{1,0:T(8,128)(2,1)S(1)} %collective-permute-done.52.refs_33_), channel_id=1, source_target_pairs={{0,4},{4,0},{1,5},{5,1},{2,6},{6,2},{3,7},{7,3},{8,12},{12,8},{9,1... | collective-permute-start | bytes 1572872 | tf_op jit(solution)/shard_map/ppermute | solution.py:254
  168.2 23.0 %collective-permute-start.48 = (bf16[128,2560]{1,0:T(8,128)(2,1)S(1)}, bf16[128,2560]{1,0:T(8,128)(2,1)S(1)}, u32[]{:S(2)}, u32[]{:S(2)}) collective-permute-start(bf16[128,2560]{1,0:T(8,128)(2,1)S(1)} %collective-permute-done.41.refs_17_), channel_id=1, source_target_pairs={{0,1},{1,0},{2,3},{3,2},{4,5},{5,4},{6,7},{7,6},{8,9},{9,8},{10,11... | collective-permute-start | bytes 1966088 | tf_op jit(solution)/shard_map/ppermute | solution.py:269
  258.8 32.8 %collective-permute-start.65 = (bf16[4,128,2048]{2,1,0:T(8,128)(2,1)}, bf16[4,128,2048]{2,1,0:T(8,128)(2,1)}, u32[]{:S(2)}, u32[]{:S(2)}) collective-permute-start(bf16[4,128,2048]{2,1,0:T(8,128)(2,1)} %get-tuple-element.223), channel_id=1, source_target_pairs={{0,1},{1,0},{2,3},{3,2},{4,5},{5,4},{6,7},{7,6},{8,9},{9,8},{10,11... | collective-permute-start | bytes 6291464 | tf_op jit(solution)/shard_map/ppermute | solution.py:715
  264.7 23.5 %collective-permute-start.66 = (bf16[1,128,2048]{2,1,0:T(8,128)(2,1)S(1)}, bf16[1,128,2048]{2,1,0:T(8,128)(2,1)S(1)}, u32[]{:S(2)}, u32[]{:S(2)}) collective-permute-start(bf16[1,128,2048]{2,1,0:T(8,128)(2,1)S(1)} %get-tuple-element.225), channel_id=1, source_target_pairs={{0,4},{4,0},{1,5},{5,1},{2,6},{6,2},{3,7},{7,3},{8,12},{12,8},{9,1... | collective-permute-start | bytes 1572872 | tf_op jit(solution)/shard_map/ppermute | solution.py:725
  266.2 23.9 %collective-permute-start.67 = (bf16[1,128,2048]{2,1,0:T(8,128)(2,1)S(1)}, bf16[1,128,2048]{2,1,0:T(8,128)(2,1)S(1)}, u32[]{:S(2)}, u32[]{:S(2)}) collective-permute-start(bf16[1,128,2048]{2,1,0:T(8,128)(2,1)S(1)} %get-tuple-element.226), channel_id=1, source_target_pairs={{0,4},{4,0},{1,5},{5,1},{2,6},{6,2},{3,7},{7,3},{8,12},{12,8},{9,1... | collective-permute-start | bytes 1572872 | tf_op jit(solution)/shard_map/ppermute | solution.py:725
  290.1 18.2 %collective-permute-start.71 = (bf16[1,128,2048]{2,1,0:T(8,128)(2,1)}, bf16[1,128,2048]{2,1,0:T(8,128)(2,1)S(1)}, u32[]{:S(2)}, u32[]{:S(2)}) collective-permute-start(bf16[1,128,2048]{2,1,0:T(8,128)(2,1)} %get-tuple-element.238), channel_id=1, source_target_pairs={{0,4},{4,0},{1,5},{5,1},{2,6},{6,2},{3,7},{7,3},{8,12},{12,8},{9,1... | collective-permute-start | bytes 1572872 | tf_op jit(solution)/shard_map/ppermute | solution.py:725
  293.7 15.4 %collective-permute-start.68 = (bf16[128,2048]{1,0:T(8,128)(2,1)}, bf16[128,2048]{1,0:T(8,128)(2,1)}, u32[]{:S(2)}, u32[]{:S(2)}) collective-permute-start(bf16[128,2048]{1,0:T(8,128)(2,1)} %fusion.9), channel_id=1, source_target_pairs={{0,8},{8,16},{16,24},{24,0},{1,9},{9,17},{17,25},{25,1},{2,10},{10... | collective-permute-start | bytes 1572872 | tf_op jit(solution)/shard_map/ppermute | solution.py:737
  311.4 38.7 %collective-permute-start.77 = (bf16[512,384]{1,0:T(8,128)(2,1)}, bf16[512,384]{1,0:T(8,128)(2,1)S(1)}, u32[]{:S(2)}, u32[]{:S(2)}) collective-permute-start(bf16[512,384]{1,0:T(8,128)(2,1)} %get-tuple-element.250), channel_id=1, source_target_pairs={{0,1},{1,0},{2,3},{3,2},{4,5},{5,4},{6,7},{7,6},{8,9},{9,8},{10,11... | collective-permute-start | bytes 1179656 | tf_op jit(solution)/shard_map/ppermute | solution.py:868
  316.5 33.5 %collective-permute-start.78 = (bf16[512,384]{1,0:T(8,128)(2,1)S(1)}, bf16[512,384]{1,0:T(8,128)(2,1)S(1)}, u32[]{:S(2)}, u32[]{:S(2)}) collective-permute-start(bf16[512,384]{1,0:T(8,128)(2,1)S(1)} %copy-done.81), channel_id=1, source_target_pairs={{0,2},{2,0},{1,3},{3,1},{4,6},{6,4},{5,7},{7,5},{8,10},{10,8},{9,1... | collective-permute-start | bytes 1179656 | tf_op jit(solution)/shard_map/ppermute | solution.py:869
  318.3 31.7 %collective-permute-start.79 = (bf16[512,384]{1,0:T(8,128)(2,1)S(1)}, bf16[512,384]{1,0:T(8,128)(2,1)}, u32[]{:S(2)}, u32[]{:S(2)}) collective-permute-start(bf16[512,384]{1,0:T(8,128)(2,1)S(1)} %copy-done.80), channel_id=1, source_target_pairs={{0,3},{1,2},{2,1},{3,0},{4,7},{5,6},{6,5},{7,4},{8,11},{9,10},{10,... | collective-permute-start | bytes 1179656 | tf_op jit(solution)/shard_map/ppermute | solution.py:870
  318.4 31.0 %collective-permute-start.70 = (bf16[128,2048]{1,0:T(8,128)(2,1)S(1)}, bf16[128,2048]{1,0:T(8,128)(2,1)S(1)}, u32[]{:S(2)}, u32[]{:S(2)}) collective-permute-start(bf16[128,2048]{1,0:T(8,128)(2,1)S(1)} %fusion.5), channel_id=1, source_target_pairs={{0,8},{8,16},{16,24},{24,0},{1,9},{9,17},{17,25},{25,1},{2,10},{10... | collective-permute-start | bytes 1572872 | tf_op jit(solution)/shard_map/ppermute | solution.py:737
  328.2 21.4 %collective-permute-start.73 = (bf16[1,128,2560]{2,1,0:T(8,128)(2,1)S(1)}, bf16[1,128,2560]{2,1,0:T(8,128)(2,1)}, u32[]{:S(2)}, u32[]{:S(2)}) collective-permute-start(bf16[1,128,2560]{2,1,0:T(8,128)(2,1)S(1)} %get-tuple-element.241), channel_id=1, source_target_pairs={{0,4},{4,0},{1,5},{5,1},{2,6},{6,2},{3,7},{7,3},{8,12},{12,8},{9,1... | collective-permute-start | bytes 1966088 | tf_op jit(solution)/shard_map/ppermute | solution.py:725
  349.5 51.1 %collective-permute-start.86 = (bf16[4,128,2560]{2,1,0:T(8,128)(2,1)}, bf16[4,128,2560]{2,1,0:T(8,128)(2,1)}, u32[]{:S(2)}, u32[]{:S(2)}) collective-permute-start(bf16[4,128,2560]{2,1,0:T(8,128)(2,1)} %get-tuple-element.265), channel_id=1, source_target_pairs={{0,1},{1,0},{2,3},{3,2},{4,5},{5,4},{6,7},{7,6},{8,9},{9,8},{10,11... | collective-permute-start | bytes 7864328 | tf_op jit(solution)/shard_map/ppermute | solution.py:715
  357.2 20.3 %collective-permute-start.85 = (bf16[4,128,768]{2,1,0:T(8,128)(2,1)}, bf16[4,128,768]{2,1,0:T(8,128)(2,1)S(1)}, u32[]{:S(2)}, u32[]{:S(2)}) collective-permute-start(bf16[4,128,768]{2,1,0:T(8,128)(2,1)} %get-tuple-element.262), channel_id=1, source_target_pairs={{0,1},{1,0},{2,3},{3,2},{4,5},{5,4},{6,7},{7,6},{8,9},{9,8},{10,11... | collective-permute-start | bytes 2359304 | tf_op jit(solution)/shard_map/ppermute | solution.py:716
  359.2 17.8 %collective-permute-start.83 = (bf16[512,384]{1,0:T(8,128)(2,1)}, bf16[512,384]{1,0:T(8,128)(2,1)}, u32[]{:S(2)}, u32[]{:S(2)}) collective-permute-start(bf16[512,384]{1,0:T(8,128)(2,1)} %get-tuple-element.259), channel_id=1, source_target_pairs={{0,3},{1,2},{2,1},{3,0},{4,7},{5,6},{6,5},{7,4},{8,11},{9,10},{10,... | collective-permute-start | bytes 1179656 | tf_op jit(solution)/shard_map/ppermute | solution.py:870
  359.2 34.0 %collective-permute-start.80 = (bf16[1,128,2560]{2,1,0:T(8,128)(2,1)}, bf16[1,128,2560]{2,1,0:T(8,128)(2,1)}, u32[]{:S(2)}, u32[]{:S(2)}) collective-permute-start(bf16[1,128,2560]{2,1,0:T(8,128)(2,1)} %get-tuple-element.255), channel_id=1, source_target_pairs={{0,4},{4,0},{1,5},{5,1},{2,6},{6,2},{3,7},{7,3},{8,12},{12,8},{9,1... | collective-permute-start | bytes 1966088 | tf_op jit(solution)/shard_map/ppermute | solution.py:725
  377.0 16.2 %collective-permute-start.84 = (bf16[128,2048]{1,0:T(8,128)(2,1)}, bf16[128,2048]{1,0:T(8,128)(2,1)S(1)}, u32[]{:S(2)}, u32[]{:S(2)}) collective-permute-start(bf16[128,2048]{1,0:T(8,128)(2,1)} %fusion.4), channel_id=1, source_target_pairs={{0,8},{8,16},{16,24},{24,0},{1,9},{9,17},{17,25},{25,1},{2,10},{10... | collective-permute-start | bytes 1572872 | tf_op jit(solution)/shard_map/ppermute | solution.py:737
  402.2 19.3 %collective-permute-start.87 = (bf16[128,2560]{1,0:T(8,128)(2,1)S(1)}, bf16[128,2560]{1,0:T(8,128)(2,1)S(1)}, u32[]{:S(2)}, u32[]{:S(2)}) collective-permute-start(bf16[128,2560]{1,0:T(8,128)(2,1)S(1)} %fusion.8), channel_id=1, source_target_pairs={{0,8},{8,16},{16,24},{24,0},{1,9},{9,17},{17,25},{25,1},{2,10},{10... | collective-permute-start | bytes 1966088 | tf_op jit(solution)/shard_map/ppermute | solution.py:737
  402.8 70.2 %collective-permute-start.90 = (bf16[4,128,768]{2,1,0:T(8,128)(2,1)}, bf16[4,128,768]{2,1,0:T(8,128)(2,1)}, u32[]{:S(2)}, u32[]{:S(2)}) collective-permute-start(bf16[4,128,768]{2,1,0:T(8,128)(2,1)} %get-tuple-element.279), channel_id=1, source_target_pairs={{0,1},{1,0},{2,3},{3,2},{4,5},{5,4},{6,7},{7,6},{8,9},{9,8},{10,11... | collective-permute-start | bytes 2359304 | tf_op jit(solution)/shard_map/ppermute | solution.py:715
  403.2 41.9 %collective-permute-start.92 = (bf16[2,128,768]{2,1,0:T(8,128)(2,1)}, bf16[2,128,768]{2,1,0:T(8,128)(2,1)}, u32[]{:S(2)}, u32[]{:S(2)}) collective-permute-start(bf16[2,128,768]{2,1,0:T(8,128)(2,1)} %get-tuple-element.285), channel_id=1, source_target_pairs={{0,4},{4,0},{1,5},{5,1},{2,6},{6,2},{3,7},{7,3},{8,12},{12,8},{9,1... | collective-permute-start | bytes 1179656 | tf_op jit(solution)/shard_map/ppermute | solution.py:725
  404.8 23.8 %collective-permute-start.88 = (bf16[1,128,2560]{2,1,0:T(8,128)(2,1)S(1)}, bf16[1,128,2560]{2,1,0:T(8,128)(2,1)S(1)}, u32[]{:S(2)}, u32[]{:S(2)}) collective-permute-start(bf16[1,128,2560]{2,1,0:T(8,128)(2,1)S(1)} %copy-done.37), channel_id=1, source_target_pairs={{0,4},{4,0},{1,5},{5,1},{2,6},{6,2},{3,7},{7,3},{8,12},{12,8},{9,1... | collective-permute-start | bytes 1966088 | tf_op jit(solution)/shard_map/ppermute | solution.py:725
  406.8 39.7 %collective-permute-start.117 = (bf16[128,2048]{1,0:T(8,128)(2,1)S(1)}, bf16[128,2048]{1,0:T(8,128)(2,1)}, u32[]{:S(2)}, u32[]{:S(2)}) collective-permute-start(bf16[128,2048]{1,0:T(8,128)(2,1)S(1)} %fusion.3), channel_id=1, source_target_pairs={{0,2},{2,0},{1,3},{3,1},{4,6},{6,4},{5,7},{7,5},{8,10},{10,8},{9,1... | collective-permute-start | bytes 1572872 | tf_op jit(solution)/shard_map/ppermute | solution.py:742
  421.6 66.7 %collective-permute-start.99 = (bf16[4,128,768]{2,1,0:T(8,128)(2,1)}, bf16[4,128,768]{2,1,0:T(8,128)(2,1)}, u32[]{:S(2)}, u32[]{:S(2)}) collective-permute-start(bf16[4,128,768]{2,1,0:T(8,128)(2,1)} %get-tuple-element.290), channel_id=1, source_target_pairs={{0,1},{1,0},{2,3},{3,2},{4,5},{5,4},{6,7},{7,6},{8,9},{9,8},{10,11... | collective-permute-start | bytes 2359304 | tf_op jit(solution)/shard_map/ppermute | solution.py:715
  429.4 16.1 %collective-permute-start.91 = (bf16[1,128,2560]{2,1,0:T(8,128)(2,1)}, bf16[1,128,2560]{2,1,0:T(8,128)(2,1)S(1)}, u32[]{:S(2)}, u32[]{:S(2)}) collective-permute-start(bf16[1,128,2560]{2,1,0:T(8,128)(2,1)} %get-tuple-element.283), channel_id=1, source_target_pairs={{0,4},{4,0},{1,5},{5,1},{2,6},{6,2},{3,7},{7,3},{8,12},{12,8},{9,1... | collective-permute-start | bytes 1966088 | tf_op jit(solution)/shard_map/ppermute | solution.py:725
  448.2 43.3 %collective-permute-start.95 = (bf16[2,128,768]{2,1,0:T(8,128)(2,1)}, bf16[2,128,768]{2,1,0:T(8,128)(2,1)}, u32[]{:S(2)}, u32[]{:S(2)}) collective-permute-start(bf16[2,128,768]{2,1,0:T(8,128)(2,1)} %get-tuple-element.288), channel_id=1, source_target_pairs={{0,4},{4,0},{1,5},{5,1},{2,6},{6,2},{3,7},{7,3},{8,12},{12,8},{9,1... | collective-permute-start | bytes 1179656 | tf_op jit(solution)/shard_map/ppermute | solution.py:725
  454.1 24.9 %collective-permute-start.113 = (bf16[128,2560]{1,0:T(8,128)(2,1)}, bf16[128,2560]{1,0:T(8,128)(2,1)}, u32[]{:S(2)}, u32[]{:S(2)}) collective-permute-start(bf16[128,2560]{1,0:T(8,128)(2,1)} %fusion.2), channel_id=1, source_target_pairs={{0,8},{8,16},{16,24},{24,0},{1,9},{9,17},{17,25},{25,1},{2,10},{10... | collective-permute-start | bytes 1966088 | tf_op jit(solution)/shard_map/ppermute | solution.py:737
  484.4 35.8 %collective-permute-start.103 = (bf16[2,128,768]{2,1,0:T(8,128)(2,1)S(1)}, bf16[2,128,768]{2,1,0:T(8,128)(2,1)S(1)}, u32[]{:S(2)}, u32[]{:S(2)}) collective-permute-start(bf16[2,128,768]{2,1,0:T(8,128)(2,1)S(1)} %copy-done.45), channel_id=1, source_target_pairs={{0,4},{4,0},{1,5},{5,1},{2,6},{6,2},{3,7},{7,3},{8,12},{12,8},{9,1... | collective-permute-start | bytes 1179656 | tf_op jit(solution)/shard_map/ppermute | solution.py:725
  487.1 38.2 %collective-permute-start.114 = (bf16[128,2560]{1,0:T(8,128)(2,1)S(1)}, bf16[128,2560]{1,0:T(8,128)(2,1)S(1)}, u32[]{:S(2)}, u32[]{:S(2)}) collective-permute-start(bf16[128,2560]{1,0:T(8,128)(2,1)S(1)} %fusion.1), channel_id=1, source_target_pairs={{0,8},{8,16},{16,24},{24,0},{1,9},{9,17},{17,25},{25,1},{2,10},{10... | collective-permute-start | bytes 1966088 | tf_op jit(solution)/shard_map/ppermute | solution.py:737
  488.2 21.0 %collective-permute-start.94 = (bf16[128,768]{1,0:T(8,128)(2,1)S(1)}, bf16[128,768]{1,0:T(8,128)(2,1)S(1)}, u32[]{:S(2)}, u32[]{:S(2)}) collective-permute-start(bf16[128,768]{1,0:T(8,128)(2,1)S(1)} %fusion.17), channel_id=1, source_target_pairs={{0,8},{8,16},{16,24},{24,0},{1,9},{9,17},{17,25},{25,1},{2,10},{10... | collective-permute-start | bytes 589832 | tf_op jit(solution)/shard_map/ppermute | solution.py:737
  491.5 22.0 %collective-permute-start.101 = (bf16[128,768]{1,0:T(8,128)(2,1)S(1)}, bf16[128,768]{1,0:T(8,128)(2,1)S(1)}, u32[]{:S(2)}, u32[]{:S(2)}) collective-permute-start(bf16[128,768]{1,0:T(8,128)(2,1)S(1)} %fusion.19), channel_id=1, source_target_pairs={{0,8},{8,16},{16,24},{24,0},{1,9},{9,17},{17,25},{25,1},{2,10},{10... | collective-permute-start | bytes 589832 | tf_op jit(solution)/shard_map/ppermute | solution.py:737
  519.0 15.3 %collective-permute-start.97 = (bf16[128,768]{1,0:T(8,128)(2,1)S(1)}, bf16[128,768]{1,0:T(8,128)(2,1)S(1)}, u32[]{:S(2)}, u32[]{:S(2)}) collective-permute-start(bf16[128,768]{1,0:T(8,128)(2,1)S(1)} %fusion.15), channel_id=1, source_target_pairs={{0,2},{2,0},{1,3},{3,1},{4,6},{6,4},{5,7},{7,5},{8,10},{10,8},{9,1... | collective-permute-start | bytes 589832 | tf_op jit(solution)/shard_map/ppermute | solution.py:742
  (177 other events, 2287.3 us)

commit v3 on v2

v3 whole, which is shorter than its diff:
```python
import functools
import math

import jax
import jax.numpy as jnp
from jax.sharding import Mesh
from jax.sharding import PartitionSpec as P
from jax import lax
from jax.experimental import pallas as pl
from jax.experimental.pallas import tpu as pltpu
HD=64
RELAX=32.0
C2=RELAX*math.log2(math.e)
NEG=-1e30

def _nt(a,b):
    return lax.dot_general(a,b,(((1,),(1,)),((),())),preferred_element_type=jnp.float32)
def _nn(a,b):
    return lax.dot_general(a,b,(((1,),(0,)),((),())),preferred_element_type=jnp.float32)

def _tr(x):
    return jnp.transpose(x.astype(jnp.float32)).astype(jnp.bfloat16)

def by_source(where, refs, dst, sems):
    rows = refs[0].shape[0]
    copies = []
    for i, ref in enumerate(refs):
        at = pl.multiple_of(jnp.bitwise_xor(where[3], i) * rows, rows)
        copies.append(pltpu.make_async_copy(ref, dst.at[pl.ds(at, rows), :], sems.at[i]))
    return copies

def by_target(where, src, refs, sems):
    rows = refs[0].shape[0]
    copies = []
    for i, ref in enumerate(refs):
        at = pl.multiple_of(jnp.bitwise_xor(where[3], i) * rows, rows)
        copies.append(pltpu.make_async_copy(src.at[pl.ds(at, rows), :], ref, sems.at[i]))
    return copies

def run_copies(copies):
    for copy in copies:
        copy.start()
    for copy in copies:
        copy.wait()

def fwd_kernel(where,*refs,nh,blk,n):
    ins,outs=refs[:n],refs[n:2*n]
    ot_ref,lse_ref,vt_ref,qkv_ref,o_ref,sems=refs[2*n:]
    seq=qkv_ref.shape[0]; w=nh*HD
    nb=seq//blk
    run_copies(by_source(where,ins,qkv_ref,sems))
    q_ref,k_ref,v_ref=(qkv_ref.at[:,i*w:(i+1)*w] for i in range(3))
    for b in range(nb):
        vt_ref[:,b*blk:(b+1)*blk]=_tr(v_ref[b*blk:(b+1)*blk,:])
    lane=lax.broadcasted_iota(jnp.int32,(1,w),1)//HD
    tri=lax.broadcasted_iota(jnp.int32,(blk,blk),0)<=lax.broadcasted_iota(jnp.int32,(blk,blk),1)
    def qstep(qb,_):
        q0=pl.multiple_of(qb*blk,blk)
        q=q_ref[pl.ds(q0,blk),:]
        qm=[jnp.where(lane==h,q,jnp.zeros_like(q)) for h in range(nh)]
        def kv(kb,carry,diag):
            k0=pl.multiple_of(kb*blk,blk)
            k=k_ref[pl.ds(k0,blk),:]
            out=[]
            for h in range(nh):
                m,l,acc=carry[3*h:3*h+3]
                s=_nt(k,qm[h])*C2
                if diag: s=jnp.where(tri,s,NEG)
                mn=jnp.maximum(m,jnp.max(s,axis=0,keepdims=True))
                a=jnp.exp2(m-mn)
                p=jnp.exp2(s-mn)
                l=l*a+jnp.sum(p,axis=0,keepdims=True)
                acc=acc*a+_nn(vt_ref[h*HD:(h+1)*HD,pl.ds(k0,blk)],p.astype(jnp.bfloat16))
                out+= [mn,l,acc]
            return tuple(out)
        init=[]
        for h in range(nh):
            init+=[jnp.full((1,blk),NEG,jnp.float32),jnp.zeros((1,blk),jnp.float32),jnp.zeros((HD,blk),jnp.float32)]
        c=kv(qb,tuple(init),True)
        c=lax.fori_loop(0,qb,lambda kb,cc: kv(kb,cc,False),c)
        for h in range(nh):
            m,l,acc=c[3*h:3*h+3]
            ot_ref[h*HD:(h+1)*HD,pl.ds(q0,blk)]=acc/l
            lse_ref[h:h+1,pl.ds(q0,blk)]=m+jnp.log2(l)
        o_ref[pl.ds(q0,blk),:]=jnp.transpose(ot_ref[:,pl.ds(q0,blk)]).astype(jnp.bfloat16)
        return 0
    lax.fori_loop(0,nb,qstep,0)
    run_copies(by_target(where,o_ref,outs,sems))

def attn_fwd(where, qkv, nh, blk=512):
    n=len(qkv); rows=qkv[0].shape[0]
    seq=n*rows; w=nh*HD
    blk=min(blk,seq)
    vm=pl.BlockSpec(memory_space=pltpu.VMEM)
    an=pl.BlockSpec(memory_space=pl.ANY)
    outs=pl.pallas_call(functools.partial(fwd_kernel,nh=nh,blk=blk,n=n),
      grid_spec=pltpu.PrefetchScalarGridSpec(num_scalar_prefetch=1,
        in_specs=[an]*n,out_specs=[an]*n+[vm]*2,
        scratch_shapes=[pltpu.VMEM((w,seq),jnp.bfloat16),pltpu.VMEM((seq,3*w),jnp.bfloat16),pltpu.VMEM((seq,w),jnp.bfloat16),pltpu.SemaphoreType.DMA((n,))]),
      out_shape=[jax.ShapeDtypeStruct((rows,w),jnp.bfloat16)]*n+[jax.ShapeDtypeStruct((w,seq),jnp.float32),jax.ShapeDtypeStruct((8,seq),jnp.float32)],
      compiler_params=pltpu.CompilerParams(vmem_limit_bytes=48<<20),
      cost_estimate=pl.CostEstimate(flops=int(nh*4.5*1.1e9), transcendentals=0, bytes_accessed=1<<20),
      name="attn_fwd")(where,*qkv)
    return outs[:n],outs[n],outs[n+1]

def bwd_kernel(where,*refs,nh,blk,n):
    ins,dos,outs=refs[:n],refs[n:2*n],refs[2*n+2:3*n+2]
    ot_ref,lse_ref=refs[2*n:2*n+2]
    kt_ref,dl_ref,dqt_ref,qkv_ref,do_ref,d_ref,sems,do_sems=refs[3*n+2:]
    seq=qkv_ref.shape[0]; w=nh*HD
    nb=seq//blk
    run_copies(by_source(where,ins,qkv_ref,sems)+by_source(where,dos,do_ref,do_sems))
    q_ref,k_ref,v_ref=(qkv_ref.at[:,i*w:(i+1)*w] for i in range(3))
    for b in range(nb):
        sl=slice(b*blk,(b+1)*blk)
        kt_ref[:,sl]=_tr(k_ref[sl,:])
        dot_=jnp.transpose(do_ref[sl,:].astype(jnp.float32))
        pr=dot_*ot_ref[:,sl]
        for h in range(nh):
            dl_ref[h:h+1,sl]=jnp.sum(pr[h*HD:(h+1)*HD],axis=0,keepdims=True)
    dqt_ref[...]=jnp.zeros_like(dqt_ref)
    lane=lax.broadcasted_iota(jnp.int32,(1,w),1)//HD
    tri=lax.broadcasted_iota(jnp.int32,(blk,blk),0)<=lax.broadcasted_iota(jnp.int32,(blk,blk),1)
    def kstep(kb,_):
        k0=pl.multiple_of(kb*blk,blk)
        k=k_ref[pl.ds(k0,blk),:]
        v=v_ref[pl.ds(k0,blk),:]
        def qs(qb,carry,diag):
            dk,dv=carry
            q0=pl.multiple_of(qb*blk,blk)
            q=q_ref[pl.ds(q0,blk),:]
            do=do_ref[pl.ds(q0,blk),:]
            for h in range(nh):
                qm=jnp.where(lane==h,q,jnp.zeros_like(q))
                dom=jnp.where(lane==h,do,jnp.zeros_like(do))
                s=_nt(k,qm)
                dp=_nt(v,dom)
                p=jnp.exp2(s*C2-lse_ref[h:h+1,pl.ds(q0,blk)])
                if diag: p=jnp.where(tri,p,0.0)
                ds=(p*(dp-dl_ref[h:h+1,pl.ds(q0,blk)])).astype(jnp.bfloat16)
                dv=dv+_nn(p.astype(jnp.bfloat16),dom)
                dk=dk+_nn(ds,qm)
                dqt_ref[h*HD:(h+1)*HD,pl.ds(q0,blk)]+=_nn(kt_ref[h*HD:(h+1)*HD,pl.ds(k0,blk)],ds)
            return dk,dv
        z=jnp.zeros((blk,w),jnp.float32)
        c=qs(kb,(z,z),True)
        dk,dv=lax.fori_loop(kb+1,nb,lambda qb,cc: qs(qb,cc,False),c)
        d_ref[pl.ds(k0,blk),w:2*w]=(dk*RELAX).astype(jnp.bfloat16)
        d_ref[pl.ds(k0,blk),2*w:3*w]=dv.astype(jnp.bfloat16)
        return 0
    lax.fori_loop(0,nb,kstep,0)
    for b in range(nb):
        sl=slice(b*blk,(b+1)*blk)
        d_ref[sl,0:w]=(jnp.transpose(dqt_ref[:,sl])*(1.0/math.sqrt(HD))).astype(jnp.bfloat16)
    run_copies(by_target(where,d_ref,outs,sems))

def attn_bwd(where, qkv, do, ot, lse, nh, blk=512):
    n=len(qkv); rows=qkv[0].shape[0]
    seq=n*rows; w=nh*HD
    blk=min(blk,seq)
    vm=pl.BlockSpec(memory_space=pltpu.VMEM)
    an=pl.BlockSpec(memory_space=pl.ANY)
    return pl.pallas_call(functools.partial(bwd_kernel,nh=nh,blk=blk,n=n),
      grid_spec=pltpu.PrefetchScalarGridSpec(num_scalar_prefetch=1,
        in_specs=[an]*(2*n)+[vm]*2,out_specs=[an]*n,
        scratch_shapes=[pltpu.VMEM((w,seq),jnp.bfloat16),pltpu.VMEM((8,seq),jnp.float32),pltpu.VMEM((w,seq),jnp.float32),
          pltpu.VMEM((seq,3*w),jnp.bfloat16),pltpu.VMEM((seq,w),jnp.bfloat16),pltpu.VMEM((seq,3*w),jnp.bfloat16),
          pltpu.SemaphoreType.DMA((n,)),pltpu.SemaphoreType.DMA((n,))]),
      out_shape=[jax.ShapeDtypeStruct((rows,3*w),jnp.bfloat16)]*n,
      compiler_params=pltpu.CompilerParams(vmem_limit_bytes=56<<20),
      cost_estimate=pl.CostEstimate(flops=int(nh*9.5*1.1e9), transcendentals=0, bytes_accessed=1<<20),
      name="attn_bwd")(where,*qkv,*do,ot,lse)


NORM_EPS = 1e-05
F32 = jnp.float32
BF16 = jnp.bfloat16
SWAP = [(0, 1), (1, 0)]
SEQ_AXES = ("y", "c")
DP_AXES = ("z", "x")
ANY = pl.BlockSpec(memory_space=pl.ANY)
VMEM = pl.BlockSpec(memory_space=pltpu.VMEM)
GELU_K = math.sqrt(2.0 / math.pi)
GELU_A = 0.044715
N_VEC = 12
N_SEQ = 4


def add_low(*terms):
    return sum(t.astype(F32) for t in terms).astype(BF16)


def ring(n):
    return [(i, (i + 1) % n) for i in range(n)]


def uses_rings():
    return lax.axis_size("z") * lax.axis_size("x") <= 8


def here():
    seq = lax.axis_index("y") * lax.axis_size("c") + lax.axis_index("c")
    return jnp.stack([lax.axis_index(a) for a in ("z", "x", "c")] + [seq]).astype(jnp.int32)


def call(kernel, name, where, args, specs, outs, scratch=(), grid=(), out_specs=None, cost=None):
    if out_specs is None:
        out_specs = [VMEM] * len(outs)
    return list(pl.pallas_call(
        kernel,
        grid_spec=pltpu.PrefetchScalarGridSpec(
            num_scalar_prefetch=1,
            grid=grid,
            in_specs=specs,
            out_specs=out_specs,
            scratch_shapes=list(scratch),
        ),
        out_shape=[jax.ShapeDtypeStruct(s, d) for s, d in outs],
        compiler_params=pltpu.CompilerParams(vmem_limit_bytes=60 << 20),
        cost_estimate=cost,
        name=name,
    )(where, *args))


def cost_of(microseconds):
    return pl.CostEstimate(flops=int(microseconds * 1.1e9), transcendentals=0, bytes_accessed=1 << 20)


def tie(value, *others):
    return lax.optimization_barrier((value,) + others)[0]


def together(*values):
    return list(lax.optimization_barrier(tuple(values)))


class Box:
    def __init__(self, v):
        self.v = v


class Stages:
    def __init__(self):
        self.every = []

    def box(self, v):
        self.every.append(Box(v))
        return self.every[-1]

    def boxes(self, values):
        return [self.box(v) for v in values]

    def begin(self, *some):
        return [b.v for b in some]

    def sync(self):
        for box, v in zip(self.every, together(*[b.v for b in self.every])):
            box.v = v


class Gather:
    def __init__(self, stages, shards, core_halves=True):
        self.stages, self.shards, self.core_halves = stages, shards, core_halves
        cur = shards
        if core_halves:
            cur = lax.dynamic_index_in_dim(shards, lax.axis_index("c"), 0, False)
        self.box = stages.box
        self.blocks, self.others = [self.box(cur)], []
        self.swapped = {}

    def z(self):
        (block,) = self.stages.begin(self.blocks[-1])
        self.blocks.append(self.box(lax.ppermute(block, "z", ring(lax.axis_size("z")))))
        return self.blocks[-1]

    def x(self):
        (block,) = self.stages.begin(self.blocks[len(self.others)])
        self.others.append(self.box(lax.ppermute(block, "x", SWAP)))
        return self.others[-1]

    def c(self):
        new = [b for b in self.blocks[1:] + self.others if id(b) not in self.swapped]
        for box, v in zip(new, self.stages.begin(*new)):
            self.swapped[id(box)] = self.box(lax.ppermute(v, "c", SWAP))
        return [self.swapped[id(box)] for box in new]

    def pieces(self):
        mine = [self.others[0]]
        for block, other in zip(self.blocks[1:], self.others[1:]):
            mine += [block, other]
        if not self.core_halves:
            return [self.shards] + self.stages.begin(*mine)
        self.c()
        return [self.shards] + self.stages.begin(*mine, *[self.swapped[id(b)] for b in mine])


def in_halves(weight):
    rows, cols = weight.shape
    return weight.reshape(rows, 2, cols // 2).transpose(1, 0, 2)


def owner_of(index, nz, z, x):
    step, side = (index + 1) // 2, (index + 1) % 2
    return lax.rem(z + nz - step, nz) * 2 + (x if side == 0 else 1 - x)


class Loader:
    def __init__(self, where, pieces, dsts, sems, nz, col=0):
        self.copies = []
        self.sems = sems
        if len(pieces[0].shape) == 2:
            self.sides = (0, 1)
            for i, (piece, dst) in enumerate(zip(pieces, dsts)):
                half = dst.shape[2]
                for side in range(2):
                    at = side * (piece.shape[1] // 2) + col
                    self.add(i, side, piece.at[:, at : at + half], dst.at[side])
            return
        z, x, c = where[0], where[1], where[2]
        self.sides = (c, 1 - c)
        rows = pieces[0].shape[1]
        others = (len(pieces) - 1) // 2
        for i, dst in enumerate(dsts):
            half = dst.shape[2]
            groups = dst.shape[1] // (2 * nz * rows)
            for g in range(groups):
                cols = slice(col, col + half)
                col += half
                for k in range(2):
                    side = self.sides[k]
                    blocks = [(z * 2 + x, pieces[0].at[side, :, cols])]
                    for n in range(others):
                        blocks.append((owner_of(n, nz, z, x), pieces[1 + k * others + n].at[:, cols]))
                    for owner, block in blocks:
                        row = pl.multiple_of((owner * groups + g) * rows, rows)
                        self.add(i, k, block, dst.at[side, pl.ds(row, rows), :])

    def add(self, i, k, src, to):
        self.copies.append((i, k, pltpu.make_async_copy(src, to, self.sems.at[len(self.copies)])))

    def pick(self, dst, half):
        return [
            copy
            for i, k, copy in self.copies
            if (dst is None or i == dst) and (half is None or k == half)
        ]

    def start(self, dst=None, half=None):
        for copy in self.pick(dst, half):
            copy.start()

    def wait(self, dst=None, half=None):
        for copy in self.pick(dst, half):
            copy.wait()


class Writer:
    def __init__(self, sems):
        self.sems, self.copies = sems, []

    def put(self, src, to):
        copy = pltpu.make_async_copy(src, to, self.sems.at[len(self.copies)])
        copy.start()
        self.copies.append(copy)

    def wait(self):
        for copy in self.copies:
            copy.wait()


def n_copies(pieces, groups=1):
    return (len(pieces) + 1) * groups


def norm_parts(v):
    c = v - jnp.mean(v, axis=-1, keepdims=True)
    inv = lax.rsqrt(jnp.mean(c * c, axis=-1, keepdims=True) + NORM_EPS)
    return c * inv, inv


def norm_back(n, inv, gain, e):
    ge = g_e = gain * e
    return (g_e - jnp.mean(ge, axis=-1, keepdims=True) - n * jnp.mean(ge * n, axis=-1, keepdims=True)) * inv


def rowsum(v):
    return jnp.sum(v, axis=0, keepdims=True)


def vectors_kernel(where, *refs, nz, n_bias):
    pieces, vec, bias = refs[:-2], refs[-2], refs[-1]
    z, x = where[0], where[1]
    own = pieces[0].shape[0]
    order = [z * 2 + x] + [owner_of(i, nz, z, x) for i in range(2 * nz - 1)]
    got = [jnp.transpose(piece[...].astype(F32))[: N_VEC + n_bias] for piece in pieces]
    for o in range(2 * nz):
        acc = jnp.zeros(got[0].shape, F32)
        for at, piece in zip(order, got):
            acc = jnp.where(at == o, piece, acc)
        vec[0:N_VEC, o * own : (o + 1) * own] = acc[:N_VEC]
        for j in range(n_bias):
            lo = (o * n_bias + j) * own
            bias[0:1, lo : lo + own] = acc[N_VEC + j : N_VEC + j + 1]


def small_vectors(pieces, width, n_bias):
    nz = lax.axis_size("z")
    own = pieces[0].shape[-2]
    at = pieces[1].shape[1] // own - 1
    blocks = pieces[: 2 * nz]
    return call(
        functools.partial(vectors_kernel, nz=nz, n_bias=n_bias),
        "vectors",
        here(),
        blocks,
        [pl.BlockSpec((None, own, own), lambda i, w: (0, 0, at))]
        + [pl.BlockSpec((own, own), lambda i, w: (0, at))] * (len(blocks) - 1),
        [((16, width), F32), ((1, n_bias * 2 * nz * own), F32)],
        grid=(1,),
        out_specs=[
            pl.BlockSpec((16, width), lambda i, w: (0, 0)),
            pl.BlockSpec((1, n_bias * 2 * nz * own), lambda i, w: (0, 0)),
        ],
        cost=cost_of(2),
    )


def plain_vectors(small, width):
    placed = lax.all_gather(small, DP_AXES, axis=0, tiled=False).astype(F32)
    vec = placed[:, :N_VEC].transpose(1, 0, 2).reshape(N_VEC, width)
    return jnp.pad(vec, ((0, 4), (0, 0))), placed[:, N_VEC:].reshape(1, -1)


def first_norm(tok, vec, normed):
    rows = min(64, tok.shape[0])

    def body(i, carry):
        at = pl.ds(pl.multiple_of(i * rows, rows), rows)
        n, inv = norm_parts(tok[at, :].astype(F32))
        normed[at, :] = (n * vec[4:5, :] + vec[8:9, :]).astype(BF16)
        return carry

    lax.fori_loop(0, tok.shape[0] // rows, body, 0)


def qkv_kernel(where, first, vec, *refs, nz, chunk, chunks, n_pieces):
    pieces, refs = refs[:n_pieces], list(refs[n_pieces:])
    n_seq = N_SEQ
    outs = [refs.pop(0) for _ in range(n_seq)]
    normed = refs.pop(0) if chunk == 0 else first
    w, stage, sems, out_sems = refs
    rows, cols = outs[0].shape
    per_side = n_seq // 2
    load = Loader(where, pieces, [w], sems, nz, chunk * per_side * cols)
    load.start()
    if chunk == 0:
        first_norm(first, vec, normed)
    load.wait()
    wide = cols // 3
    grp = wide * chunks
    scale = 1.0 / (RELAX * math.sqrt(HD))
    for side in range(2):
        mixed = _nn(normed[...], w[side])
        for j in range(per_side):
            s = side * per_side + j
            lo = s * grp + chunk * wide
            block = mixed[:, j * cols : (j + 1) * cols]
            at = slice(s * rows, (s + 1) * rows)
            stage[at, 0:wide] = ((block[:, 0:wide] + vec[0:1, lo : lo + wide]) * scale).astype(BF16)
            stage[at, wide : 2 * wide] = block[:, wide : 2 * wide].astype(BF16)
            stage[at, 2 * wide :] = (block[:, 2 * wide :] + vec[1:2, lo : lo + wide]).astype(BF16)
    run_copies(by_target(where, stage, outs, out_sems))


def gelu_parts(h):
    return jnp.tanh(h * (GELU_K + (GELU_K * GELU_A) * (h * h)))


def up_kernel(where, *refs, nz, n_att, n_pieces):
    refs = list(refs)
    att_in = [[refs.pop(0) for _ in range(N_SEQ)] for _ in range(n_att)]
    tok, vec, fc1_b = [refs.pop(0) for _ in range(3)]
    pieces = [refs.pop(0) for _ in range(n_pieces)]
    out_att, out_branch, out_residual, out_normed, out_hidden, out_active = [refs.pop(0) for _ in range(6)]
    proj_w, fc1_w, attended, branch, residual, normed_two, hidden, active, in_sems, out_sems = refs
    load = Loader(where, pieces, (proj_w, fc1_w), in_sems, nz)
    load.start(0)
    load.start(1)
    out = Writer(out_sems)
    rows, width = tok.shape
    part = att_in[0][0].shape[1]
    for i in range(N_SEQ):
        s = jnp.bitwise_xor(where[3], i)
        for j in range(n_att):
            lo = pl.multiple_of((s * n_att + j) * part, part)
            attended[:, pl.ds(lo, part)] = att_in[j][i][...]
    out.put(attended, out_att)
    load.wait(0)
    half = width // 2
    for side in range(2):
        cols = slice(side * half, (side + 1) * half)
        branch[:, cols] = _nn(attended[...], proj_w[side]) + vec[2:3, cols]
    out.put(branch, out_branch)
    step = min(64, rows)

    def norms(i, carry):
        at = pl.ds(pl.multiple_of(i * step, step), step)
        n, inv = norm_parts(branch[at, :])
        r = tok[at, :].astype(F32) + (n * vec[5:6, :] + vec[9:10, :])
        residual[at, :] = r
        n, inv = norm_parts(r)
        normed_two[at, :] = (n * vec[6:7, :] + vec[10:11, :]).astype(BF16)
        return carry

    lax.fori_loop(0, rows // step, norms, 0)
    out.put(residual, out_residual)
    out.put(normed_two, out_normed)
    load.wait(1)
    ff = hidden.shape[1]
    blk = 512
    for i in range(ff // blk):
        at = slice(i * blk, (i + 1) * blk)
        side, col = divmod(i * blk, ff // 2)
        h = _nn(normed_two[...], fc1_w[side, :, col : col + blk]) + fc1_b[:, at]
        hidden[:, at] = h
        active[:, at] = (0.5 * h * (1.0 + gelu_parts(h))).astype(BF16)
        out.put(hidden.at[:, at], out_hidden.at[:, at])
        out.put(active.at[:, at], out_active.at[:, at])
    out.wait()


def mid_kernel(where, active_in, residual_in, hidden_in, out_grad, vec, *refs, nz, n_pieces):
    pieces, refs = refs[:n_pieces], list(refs[n_pieces:])
    layer_out, d_second, out_hidden, sums, fc1_sum = [refs.pop(0) for _ in range(5)]
    fc2_w, active, residual, wide, hidden, d_hidden, load_sems, in_sems, out_sems = refs
    rows, width = out_grad.shape
    ff = hidden.shape[1]
    blk = 512
    load = Loader(where, pieces, (fc2_w,), load_sems, nz)
    out = Writer(out_sems)
    blocks = [slice(i * blk, (i + 1) * blk) for i in range(ff // blk)]
    ins = [
        pltpu.make_async_copy(active_in, active, in_sems.at[0]),
        pltpu.make_async_copy(residual_in, residual, in_sems.at[1]),
    ] + [
        pltpu.make_async_copy(hidden_in.at[:, at], hidden.at[:, at], in_sems.at[2 + i])
        for i, at in enumerate(blocks)
    ]
    ins[0].start()
    load.start(0, 0)
    load.start(0, 1)
    for copy in ins[1:]:
        copy.start()
    half = width // 2
    ins[0].wait()
    for k in range(2):
        load.wait(0, k)
        side = load.sides[k]
        cols = pl.ds(pl.multiple_of(side * half, half), half)
        wide[:, cols] = _nn(active[...], fc2_w[side]) + vec[3:4, cols]
    ins[1].wait()
    step = min(64, rows)

    def top(i, carry):
        g_sum, s_sum, b_sum = carry
        at = pl.ds(pl.multiple_of(i * step, step), step)
        n, inv = norm_parts(wide[at, :])
        e = out_grad[at, :].astype(F32)
        layer_out[at, :] = (residual[at, :] + (n * vec[7:8, :] + vec[11:12, :])).astype(BF16)
        d = norm_back(n, inv, vec[7:8, :], e).astype(BF16)
        d_second[at, :] = d
        return g_sum + rowsum(e * n), s_sum + rowsum(e), b_sum + rowsum(d.astype(F32))

    zero = jnp.zeros((1, width), F32)
    g_sum, s_sum, b_sum = lax.fori_loop(0, rows // step, top, (zero, zero, zero))
    sums[...] = jnp.zeros_like(sums)
    sums[3:4, :] = b_sum
    sums[7:8, :] = g_sum
    sums[11:12, :] = s_sum
    for copy in ins[2:]:
        copy.wait()
    for i, at in enumerate(blocks):
        d = _nt(d_second[:, 0:half], fc2_w[0, at, :]) + _nt(d_second[:, half:], fc2_w[1, at, :])
        h = hidden[:, at]
        t = gelu_parts(h)
        square = h * h
        bend = h * (0.5 * GELU_K + (1.5 * GELU_K * GELU_A) * square)
        low = (d * ((0.5 + 0.5 * t) + (1.0 - t * t) * bend)).astype(BF16)
        d_hidden[:, at] = low
        fc1_sum[:, at] = rowsum(low.astype(F32))
        if i % 2 == 1:
            pair = slice((i - 1) * blk, (i + 1) * blk)
            out.put(d_hidden.at[:, pair], out_hidden.at[:, pair])
    out.wait()


def back_kernel(where, out_grad, vec, sums_in, d_hidden_in, residual_in, branch_in, *refs, nz, n_att, n_pieces):
    refs = list(refs)
    ups = [refs.pop(0) for _ in range(n_pieces)]
    out_residual, out_branch, sums = [refs.pop(0) for _ in range(3)]
    d_att = [[refs.pop(0) for _ in range(N_SEQ)] for _ in range(n_att)]
    proj_w, fc1_w, d_hidden, residual, branch, wide, d_residual, d_branch = [refs.pop(0) for _ in range(8)]
    stages = [refs.pop(0) for _ in range(n_att)]
    up_sems, in_sems, out_sems = refs
    rows, width = out_grad.shape
    ff = d_hidden.shape[1]
    load = Loader(where, ups, (proj_w, fc1_w), up_sems, nz)
    out = Writer(out_sems)
    ff_half = ff // 2
    ins = []
    for k in range(2):
        at = pl.ds(pl.multiple_of(load.sides[k] * ff_half, ff_half), ff_half)
        ins.append(pltpu.make_async_copy(d_hidden_in.at[:, at], d_hidden.at[:, at], in_sems.at[k]))
        ins[k].start()
        load.start(1, k)
    ins.append(pltpu.make_async_copy(residual_in, residual, in_sems.at[2]))
    ins.append(pltpu.make_async_copy(branch_in, branch, in_sems.at[3]))
    ins[2].start()
    ins[3].start()
    load.start(0)
    half = width // 2
    for k in range(2):
        ins[k].wait()
        load.wait(1, k)
        side = load.sides[k]
        at = pl.ds(pl.multiple_of(side * ff_half, ff_half), ff_half)
        for q in range(2):
            rows_at = slice(q * half, (q + 1) * half)
            part = _nt(d_hidden[:, at], fc1_w[side, rows_at, :])
            wide[:, rows_at] = part if k == 0 else wide[:, rows_at] + part
    ins[2].wait()
    ins[3].wait()
    step = min(64, rows)

    def mid(i, carry):
        g2, s2, g1, s1, b_sum = carry
        at = pl.ds(pl.multiple_of(i * step, step), step)
        e = wide[at, :]
        n, inv = norm_parts(residual[at, :])
        d = out_grad[at, :].astype(F32) + norm_back(n, inv, vec[6:7, :], e)
        d_residual[at, :] = d
        g2, s2 = g2 + rowsum(e * n), s2 + rowsum(e)
        n, inv = norm_parts(branch[at, :])
        low = norm_back(n, inv, vec[5:6, :], d).astype(BF16)
        d_branch[at, :] = low
        return g2, s2, g1 + rowsum(d * n), s1 + rowsum(d), b_sum + rowsum(low.astype(F32))

    zero = jnp.zeros((1, width), F32)
    g2, s2, g1, s1, b_sum = lax.fori_loop(0, rows // step, mid, (zero,) * 5)
    out.put(d_residual, out_residual)
    out.put(d_branch, out_branch)
    sums[...] = sums_in[...]
    for row, v in ((6, g2), (10, s2), (5, g1), (9, s1), (2, b_sum)):
        sums[row : row + 1, :] = v
    load.wait(0)
    part = stages[0].shape[1]
    for s in range(N_SEQ):
        at = slice(s * n_att * part, (s + 1) * n_att * part)
        low = (_nt(d_branch[:, 0:half], proj_w[0, at, :]) + _nt(d_branch[:, half:], proj_w[1, at, :])).astype(BF16)
        for j in range(n_att):
            stages[j][s * rows : (s + 1) * rows, :] = low[:, j * part : (j + 1) * part]
    for j in range(n_att):
        for i, ref in enumerate(d_att[j]):
            at = pl.multiple_of(jnp.bitwise_xor(where[3], i) * rows, rows)
            out.put(stages[j].at[pl.ds(at, rows), :], ref)
    out.wait()


def run_up(where, att, tokens, vec, fc1_b, ups):
    nz = lax.axis_size("z")
    rows, width = tokens.shape
    ff = fc1_b.shape[1]
    flat = [block for blocks in att for block in blocks]
    big = (rows, width)
    outs = [(big, BF16), (big, F32), (big, F32), (big, BF16), ((rows, ff), F32), ((rows, ff), BF16)]
    return call(
        functools.partial(up_kernel, nz=nz, n_att=len(att), n_pieces=len(ups)),
        "up",
        where,
        flat + [tokens, vec, fc1_b] + ups,
        [VMEM] * (len(flat) + 3) + [ANY] * len(ups),
        outs,
        [
            pltpu.VMEM((2, width, width // 2), BF16),
            pltpu.VMEM((2, width, ff // 2), BF16),
        ]
        + [pltpu.VMEM(shape, dtype) for shape, dtype in outs]
        + [pltpu.SemaphoreType.DMA((n_copies(ups, 2),)), pltpu.SemaphoreType.DMA((4 + 2 * (ff // 512),))],
        out_specs=[ANY] * len(outs),
        cost=cost_of(20),
    )


def run_mid(where, active, residual, hidden, out_grad, vec, downs):
    nz = lax.axis_size("z")
    rows, width = out_grad.shape
    ff = active.shape[1]
    big = (rows, width)
    return call(
        functools.partial(mid_kernel, nz=nz, n_pieces=len(downs)),
        "mid",
        where,
        [active, residual, hidden, out_grad, vec] + downs,
        [ANY] * 3 + [VMEM] * 2 + [ANY] * len(downs),
        [(big, BF16), (big, BF16), ((rows, ff), BF16), ((16, width), F32), ((1, ff), F32)],
        [
            pltpu.VMEM((2, ff, width // 2), BF16),
            pltpu.VMEM((rows, ff), BF16),
            pltpu.VMEM(big, F32),
            pltpu.VMEM(big, F32),
            pltpu.VMEM((rows, ff), F32),
            pltpu.VMEM((rows, ff), BF16),
            pltpu.SemaphoreType.DMA((n_copies(downs, ff // width),)),
            pltpu.SemaphoreType.DMA((2 + ff // 512,)),
            pltpu.SemaphoreType.DMA((ff // 512,)),
        ],
        out_specs=[VMEM] * 2 + [ANY] + [VMEM] * 2,
        cost=cost_of(28),
    )


def run_back(where, out_grad, vec, sums, d_hidden, residual, branch, ups, n_att):
    nz = lax.axis_size("z")
    rows, width = out_grad.shape
    ff = d_hidden.shape[1]
    big = (rows, width)
    part = width // N_SEQ // n_att
    outs = [(big, F32), (big, BF16), ((16, width), F32)]
    outs += [((rows, part), BF16)] * (n_att * N_SEQ)
    return call(
        functools.partial(back_kernel, nz=nz, n_att=n_att, n_pieces=len(ups)),
        "back",
        where,
        [out_grad, vec, sums, d_hidden, residual, branch] + ups,
        [VMEM] * 3 + [ANY] * (3 + len(ups)),
        outs,
        [
            pltpu.VMEM((2, width, width // 2), BF16),
            pltpu.VMEM((2, width, ff // 2), BF16),
            pltpu.VMEM((rows, ff), BF16),
            pltpu.VMEM(big, F32),
            pltpu.VMEM(big, F32),
            pltpu.VMEM(big, F32),
            pltpu.VMEM(big, F32),
            pltpu.VMEM(big, BF16),
        ]
        + [pltpu.VMEM((N_SEQ * rows, part), BF16)] * n_att
        + [
            pltpu.SemaphoreType.DMA((n_copies(ups, 2),)),
            pltpu.SemaphoreType.DMA((4,)),
            pltpu.SemaphoreType.DMA((2 + n_att * N_SEQ,)),
        ],
        out_specs=[ANY] * 2 + [VMEM] + [ANY] * (n_att * N_SEQ),
        cost=cost_of(20),
    )


def slot_owner(i, nz, where):
    z, x = where[0], where[1]
    return lax.rem(z + 2 * nz - 1 - i % nz, nz) * 2 + (1 - x if i < nz else x)


def contract_rows(left, right):
    return lax.dot_general(left, right, (((0,), (0,)), ((), ())), preferred_element_type=F32)


def halves_of(ref, c):
    half = ref.shape[1] // 2
    return [ref[:, pl.ds(pl.multiple_of(h * half, half), half)] for h in (1 - c, c)]


def columns_of(ref, owner, count):
    return ref[:, pl.ds(pl.multiple_of(owner * count, count), count)]


def row_grad_kernel(where, lhs, rhs, *outs, nz):
    c = where[2]
    rows = outs[0].shape[1]
    half = rhs.shape[1] // 2
    blk = min(1024, half)
    for side in range(2):
        owners = [slot_owner(side * nz + i, nz, where) for i in range(nz)]
        left = jnp.concatenate([columns_of(lhs, o, rows) for o in owners], axis=1)
        for h in range(2):
            out = outs[2 * side + h]
            base = (1 - c if h == 0 else c) * half
            for n in range(half // blk):
                right = rhs[:, pl.ds(pl.multiple_of(base + n * blk, blk), blk)]
                low = contract_rows(left, right).astype(BF16)
                for i in range(nz):
                    out[i, :, n * blk : (n + 1) * blk] = low[i * rows : (i + 1) * rows]


def wide_grad_kernel(where, *refs, nz, side):
    ins, outs = refs[:4], refs[4:6]
    normed_two, d_hidden, active, d_second = refs[6:10]
    stages, in_sems, out_sems = refs[10:12], refs[12], refs[13]
    c = where[2]
    rows = outs[0].shape[1]
    owners = [slot_owner(side * nz + i, nz, where) for i in range(nz)]
    half = d_hidden.shape[1] // 2
    blk = min(1024, half)
    loads = [pltpu.make_async_copy(ins[0], normed_two, in_sems.at[0])]
    for k, h in enumerate((1 - c, c)):
        at = pl.ds(pl.multiple_of(h * half, half), half)
        loads.append(pltpu.make_async_copy(ins[1].at[:, at], d_hidden.at[:, at], in_sems.at[1 + k]))
    loads.append(pltpu.make_async_copy(ins[3], d_second, in_sems.at[3]))
    wide = active.shape[1] // (2 * nz)
    for i in range(nz):
        at = pl.ds(pl.multiple_of(owners[i] * wide, wide), wide)
        loads.append(pltpu.make_async_copy(ins[2].at[:, at], active.at[:, at], in_sems.at[4 + i]))
    for load in loads:
        load.start()
    write = Writer(out_sems)
    loads[0].wait()
    left = jnp.concatenate([columns_of(normed_two, o, rows) for o in owners], axis=1)
    for h, out in enumerate(stages):
        loads[1 + h].wait()
        base = (1 - c if h == 0 else c) * half
        for n in range(half // blk):
            right = d_hidden[:, pl.ds(pl.multiple_of(base + n * blk, blk), blk)]
            low = contract_rows(left, right).astype(BF16)
            for i in range(nz):
                out[i, :, n * blk : (n + 1) * blk] = low[i * rows : (i + 1) * rows]
    loads[3].wait()
    rights = halves_of(d_second, c)
    cols = d_second.shape[1] // 2
    for i in range(nz):
        loads[4 + i].wait()
        left = columns_of(active, owners[i], wide)
        for stage, out, right in zip(stages, outs, rights):
            low = contract_rows(left, right).astype(BF16)
            for g in range(wide // rows):
                lo = half + g * cols
                stage[i, :, lo : lo + cols] = low[g * rows : (g + 1) * rows]
            write.put(stage.at[i], out.at[i])
    write.wait()


def run_wide_grad(where, normed_two, d_hidden, active, d_second, rows, side):
    nz = lax.axis_size("z")
    tok, width = normed_two.shape
    ff = active.shape[1]
    out = ((nz, rows, ff // 2 + ff // width * width // 2), BF16)
    return call(
        functools.partial(wide_grad_kernel, nz=nz, side=side),
        "wide_grad",
        where,
        (normed_two, d_hidden, active, d_second),
        [ANY] * 4,
        [out] * 2,
        [
            pltpu.VMEM((tok, width), BF16),
            pltpu.VMEM((tok, ff), BF16),
            pltpu.VMEM((tok, ff), BF16),
            pltpu.VMEM((tok, width), BF16),
            pltpu.VMEM(*out),
            pltpu.VMEM(*out),
            pltpu.SemaphoreType.DMA((4 + nz,)),
            pltpu.SemaphoreType.DMA((2 * nz,)),
        ],
        out_specs=[ANY] * 2,
        cost=cost_of(9),
    )


def grads(kernel, name, where, args, rows, half, specs=None, scratch=(), count=4, **more):
    nz = lax.axis_size("z")
    return call(
        functools.partial(kernel, nz=nz, **more),
        name,
        where,
        args,
        specs or [VMEM] * len(args),
        [((nz, rows, half), BF16)] * count,
        scratch,
        cost=cost_of(2.5 * count),
    )


def qkv_grad_kernel(where, normed, *refs, nz):
    blocks, outs, (stage, sems) = refs[:N_SEQ], refs[N_SEQ:-2], refs[-2:]
    c = where[2]
    rows = outs[0].shape[1]
    tok = normed.shape[0]
    per_side = N_SEQ // 2
    run_copies(by_source(where, blocks, stage, sems))
    for h in range(2):
        base = (1 - c if h == 0 else c) * per_side
        right = jnp.concatenate(
            [stage[pl.ds(pl.multiple_of((base + j) * tok, tok), tok), :] for j in range(per_side)], axis=1
        )
        for side in range(2):
            owners = [slot_owner(side * nz + i, nz, where) for i in range(nz)]
            left = jnp.concatenate([columns_of(normed, o, rows) for o in owners], axis=1)
            low = contract_rows(left, right).astype(BF16)
            for i in range(nz):
                outs[2 * side + h][i] = low[i * rows : (i + 1) * rows]


class Reduce:
    def __init__(self, stages, parts):
        self.stages, self.parts_x = stages, parts
        self.box = stages.box
        self.from_x, self.out = [], []
        self.steps = 0

    def set_first(self, outs):
        self.first = self.stages.boxes(outs)

    def set_second(self, outs):
        self.second = self.stages.boxes(outs)

    def c_first(self):
        self.got = self.box(lax.ppermute(self.first[0].v, "c", SWAP))

    def c_second(self):
        self.own_got = self.box(lax.ppermute(self.second[0].v, "c", SWAP))

    def c(self):
        self.c_first()
        self.c_second()

    def sum(self, count=1):
        got, kept = self.got.v, self.first[1].v
        self.size = got.shape[0] // self.parts_x
        for unused in range(count):
            at = len(self.out) * self.size
            self.out.append(self.box(add_low(kept[at : at + self.size], got[at : at + self.size])))

    def x(self):
        if len(self.out) == len(self.from_x):
            self.sum()
        self.from_x.append(self.box(lax.ppermute(self.out[len(self.from_x)].v, "x", SWAP)))

    def add(self):
        step = self.steps
        ready = [self.from_x[step // self.size]] + ([self.passed] if step > 0 else [])
        ready = self.stages.begin(*ready)
        terms = [self.second[1].v[step], self.own_got.v[step], ready[0][step % self.size]] + ready[1:]
        self.cur = self.box(add_low(*terms))
        self.steps += 1

    def z(self):
        self.add()
        self.passed = self.box(lax.ppermute(self.cur.v, "z", ring(lax.axis_size("z"))))
        return self.passed

    def direct(self):
        nz = lax.axis_size("z")
        (crossed,) = self.stages.begin(self.from_x[0])
        blocks = [add_low(self.second[1].v[i], self.own_got.v[i], crossed[i]) for i in range(nz)]
        self.kept = blocks[-1]
        self.parts = [
            self.box(lax.ppermute(blocks[i], "z", [(s, (s - 1 - i) % nz) for s in range(nz)]))
            for i in range(nz - 1)
        ]
        return self.parts

    def gather_parts(self):
        self.cur = self.box(add_low(self.kept, *self.stages.begin(*self.parts)))

    def y(self):
        if hasattr(self, "parts"):
            self.gather_parts()
        else:
            self.add()
        self.from_y = self.box(lax.ppermute(self.cur.v, "y", SWAP))
        return self.from_y

    def last_c(self):
        (got,) = self.stages.begin(self.from_y)
        self.low = add_low(self.cur.v, got)
        self.other = self.box(lax.ppermute(self.low, "c", SWAP))
        return self.other

    def finish(self):
        c = lax.axis_index("c")
        low, (other,) = self.low, self.stages.begin(self.other)
        return jnp.where(c == 0, low, other), jnp.where(c == 0, other, low)


class SmallReduce:
    def __init__(self, stages, grads):
        self.stages, self.box = stages, stages.box
        self.cur = self.box(grads.astype(BF16))

    def seq(self):
        (cur,) = self.stages.begin(self.cur)
        both = [(i, i ^ 3) for i in range(4)]
        self.parts = [
            self.box(lax.ppermute(cur, "c", SWAP)),
            self.box(lax.ppermute(cur, "y", SWAP)),
            self.box(lax.ppermute(cur, SEQ_AXES, both)),
        ]
        return self.parts

    def x(self):
        nz = lax.axis_size("z")
        cur = add_low(self.cur.v, *self.stages.begin(*self.parts))
        self.keep = cur[nz:]
        self.got = self.box(lax.ppermute(cur[:nz], "x", SWAP))
        return [self.got]

    def z(self):
        nz = lax.axis_size("z")
        (got,) = self.stages.begin(self.got)
        cur = add_low(self.keep, got)
        self.keep = cur[nz - 1]
        self.parts = [
            self.box(lax.ppermute(cur[i], "z", [(s, (s - 1 - i) % nz) for s in range(nz)]))
            for i in range(nz - 1)
        ]
        return self.parts

    def finish(self):
        return add_low(self.keep, *self.stages.begin(*self.parts)).astype(F32)


def reduce_plain(lhs, rhs):
    grad = lax.dot_general(
        lhs, rhs, (((0,), (0,)), ((), ())), preferred_element_type=F32
    ).astype(BF16)
    part = lax.psum_scatter(grad, DP_AXES, scatter_dimension=0, tiled=True)
    return lax.psum(part, SEQ_AXES).astype(F32)


def last_kernel(where, *refs, nz, chunks, n_pieces, rings):
    refs = list(refs)
    blocks = [[refs.pop(0) for _ in range(N_SEQ)] for _ in range(chunks)]
    tok, d_residual, vec, sums, fc1_sum = [refs.pop(0) for _ in range(5)]
    pieces = [refs.pop(0) for _ in range(n_pieces)]
    tokens_grad, small = refs.pop(0), refs.pop(0)
    ws = [refs.pop(0) for _ in range(chunks)]
    stages = [refs.pop(0) for _ in range(chunks)]
    wide, total, in_sems = refs.pop(0), refs.pop(0), refs.pop(0)
    loads = [
        Loader(where, pieces, [w], sem, nz, j * w.shape[2]) for j, (w, sem) in enumerate(zip(ws, refs))
    ]
    for load in loads:
        load.start()
    rows, width = tok.shape
    n_seq, cols = N_SEQ, stages[0].shape[1]
    run_copies(
        [copy for j in range(chunks) for copy in by_source(where, blocks[j], stages[j], in_sems.at[j])]
    )
    d_mixed = [stage.reshape(n_seq, rows, cols) for stage in stages]
    part = cols // 3
    zero = jnp.zeros((1, width), F32)
    total[...] = sums[...]
    for j in range(chunks):
        for s in range(n_seq):
            lo = (s * chunks + j) * part
            total[0:1, lo : lo + part] = rowsum(d_mixed[j][s, :, 0:part].astype(F32))
            total[1:2, lo : lo + part] = rowsum(d_mixed[j][s, :, 2 * part :].astype(F32))
    for load in loads:
        load.wait()
    quarter = width // 4
    per_side = n_seq // 2
    for q in range(4):
        at = slice(q * quarter, (q + 1) * quarter)
        acc = None
        for j in range(chunks):
            for side in range(2):
                left = jnp.concatenate([d_mixed[j][side * per_side + i] for i in range(per_side)], axis=1)
                term = _nt(left, ws[j][side, at, :])
                acc = term if acc is None else acc + term
        wide[:, at] = acc
    step = min(64, rows)

    def norms(i, carry):
        g, s = carry
        at = pl.ds(pl.multiple_of(i * step, step), step)
        e = wide[at, :]
        n, inv = norm_parts(tok[at, :].astype(F32))
        tokens_grad[at, :] = (d_residual[at, :] + norm_back(n, inv, vec[4:5, :], e)).astype(BF16)
        return g + rowsum(e * n), s + rowsum(e)

    g, s = lax.fori_loop(0, rows // step, norms, (zero, zero))
    total[4:5, :] = g
    total[8:9, :] = s
    if not rings:
        small[...] = total[...]
        return
    z, x = where[0], where[1]
    own = width // (2 * nz)
    n_bias = fc1_sum.shape[1] // width
    for o in range(2 * nz):
        slot = lax.rem(z + 2 * nz - 1 - o // 2, nz) + jnp.where(x == o % 2, nz, 0)
        small[slot, 0:N_VEC, :] = total[0:N_VEC, o * own : (o + 1) * own]
        for j in range(n_bias):
            lo = (o * n_bias + j) * own
            small[slot, N_VEC + j : N_VEC + j + 1, :] = fc1_sum[:, lo : lo + own]


def last(where, d_mixed, tokens, d_residual, vec, sums, fc1_sum, pieces):
    nz = lax.axis_size("z")
    rings = uses_rings()
    rows, width = tokens.shape
    chunks = len(d_mixed)
    small = ((2 * nz, N_VEC + fc1_sum.shape[1] // width, width // (2 * nz)), F32) if rings else ((16, width), F32)
    return call(
        functools.partial(last_kernel, nz=nz, chunks=chunks, n_pieces=len(pieces), rings=rings),
        "last",
        where,
        [b for blocks in d_mixed for b in blocks] + [tokens, d_residual, vec, sums, fc1_sum] + list(pieces),
        [ANY] * (chunks * N_SEQ) + [VMEM] * 5 + [ANY] * len(pieces),
        [((rows, width), BF16), small],
        [pltpu.VMEM((2, width, 3 * width // chunks // 2), BF16)] * chunks
        + [pltpu.VMEM((N_SEQ * rows, 3 * width // chunks // N_SEQ), BF16)] * chunks
        + [pltpu.VMEM((rows, width), F32), pltpu.VMEM((16, width), F32), pltpu.SemaphoreType.DMA((chunks, N_SEQ))]
        + [pltpu.SemaphoreType.DMA((n_copies(pieces),))] * chunks,
        cost=cost_of(12),
    )


def reduce_small(small, fc1_sum, own):
    n_dp = lax.axis_size("z") * lax.axis_size("x")
    low = jnp.concatenate(
        (small[:N_VEC].reshape(N_VEC, n_dp, own).transpose(1, 0, 2), fc1_sum.reshape(n_dp, -1, own)),
        axis=1,
    )
    part = lax.psum_scatter(low, DP_AXES, scatter_dimension=0, tiled=False)
    return lax.psum(part.astype(BF16), SEQ_AXES).astype(F32)


def exchange(blocks):
    both = [(i, i ^ 3) for i in range(4)]
    return [
        blocks[0],
        lax.ppermute(blocks[1], "c", SWAP),
        lax.ppermute(blocks[2], "y", SWAP),
        lax.ppermute(blocks[3], SEQ_AXES, both),
    ]


def per_device(
    tokens,
    out_grad,
    qkv_weight,
    qv_bias,
    proj_weight,
    fc1_weight,
    fc1_bias,
    fc2_weight,
    out_bias,
    norm_gains,
    norm_shifts,
):
    n_seq = lax.axis_size("y") * lax.axis_size("c")
    rows, width = tokens.shape
    own = qv_bias.shape[1]
    chunks = CHUNKS
    grp = width // n_seq
    part = grp // chunks
    heads = part // HD
    seq_len = n_seq * rows
    nz = lax.axis_size("z")
    where = here()
    qkv_shards = qkv_weight.reshape(-1, 3, n_seq, chunks, part).transpose(3, 0, 2, 1, 4)
    qkv_shards = qkv_shards.reshape(chunks, -1, 3 * width // chunks)
    small = jnp.concatenate(
        (qv_bias, out_bias, norm_gains, norm_shifts, fc1_bias.reshape(-1, own)), axis=0
    )
    rings = uses_rings()
    st = Stages()
    ff = fc1_weight.shape[1]
    r = proj_weight.shape[0]
    qkv_cat = jnp.concatenate([in_halves(w) for w in qkv_shards], axis=2)
    groups = fc2_weight.shape[0] // r
    if rings:
        fc2_groups = fc2_weight.reshape(groups, -1, 2, width // 2).transpose(2, 1, 0, 3)
        n_bias = small.shape[0] - N_VEC
        columns = jnp.pad(small.T, ((0, 0), (0, own - small.shape[0])))
        qkv_in = Gather(st, jnp.concatenate((qkv_cat, jnp.stack((columns, columns))), axis=2))
        up_in = Gather(st, jnp.concatenate((in_halves(proj_weight), in_halves(fc1_weight)), axis=2))
        down_in = Gather(st, fc2_groups.reshape(2, -1, groups * width // 2))
        for step in range(nz):
            if step > 0:
                st.sync()
                qkv_in.c()
            qkv_in.x()
            if step < nz - 1:
                qkv_in.z()
            else:
                up_in.z()
        st.sync()
        qkv_pieces = qkv_in.pieces()
        vec, fc1_b = small_vectors(qkv_pieces, width, n_bias)
    else:
        vec, fc1_b = plain_vectors(small, width)
        whole = lax.all_gather(qkv_cat, DP_AXES, axis=1, tiled=True)
        qkv_pieces = [jnp.concatenate((whole[0], whole[1]), axis=1)]
        ups, downs = [
            [lax.all_gather(w, DP_AXES, axis=0, tiled=True) for w in ws]
            for ws in ((proj_weight, fc1_weight), (fc2_weight,))
        ]

    def project(j, first, vec):
        outs = [((rows, 3 * part), BF16)] * n_seq
        if j == 0:
            outs.append(((rows, width), BF16))
        return call(
            functools.partial(qkv_kernel, nz=nz, chunk=j, chunks=chunks, n_pieces=len(qkv_pieces)),
            "qkv",
            where,
            [first, vec] + qkv_pieces,
            [VMEM] * 2 + [ANY] * len(qkv_pieces),
            outs,
            [
                pltpu.VMEM((2, width, 3 * width // chunks // 2), BF16),
                pltpu.VMEM((seq_len, 3 * part), BF16),
                pltpu.SemaphoreType.DMA((n_copies(qkv_pieces),)),
                pltpu.SemaphoreType.DMA((n_seq,)),
            ],
            out_specs=[ANY] * n_seq + [VMEM] * (j == 0),
            cost=cost_of(7),
        )

    def swap(blocks):
        return st.boxes(exchange(st.begin(*blocks)))

    def hops(*some):
        for hop in some if rings else []:
            hop()

    vec_box = st.box(vec)
    st.sync()
    vec = vec_box.v
    if not rings:
        up_in = down_in = Gather(st, qkv_cat)
    got = st.boxes(project(0, tokens, vec_box.v))
    sent_a, normed_box = got[:n_seq], got[n_seq]
    hops(up_in.x, up_in.z)
    st.sync()
    normed = normed_box.v
    heads_a = swap(sent_a)
    sent_b = st.boxes(project(1, normed, vec))
    hops(up_in.x, up_in.z)
    st.sync()
    heads_b = swap(sent_b)
    by_a = st.begin(*heads_a)
    out_a, cols_a, lse_a = attn_fwd(where, by_a, heads, 1024)
    out_a = st.boxes(out_a)
    hops(up_in.x, down_in.z)
    st.sync()
    att_a = swap(out_a)
    by_b = st.begin(*heads_b)
    out_b, cols_b, lse_b = attn_fwd(where, by_b, heads, 1024)
    out_b = st.boxes(out_b)
    hops(up_in.x, down_in.z)
    st.sync()
    att_b = swap(out_b)
    hops(down_in.x, down_in.x, down_in.z)
    st.sync()
    if rings:
        ups = up_in.pieces()
    hops(down_in.c, down_in.x, down_in.x)
    arrived = st.begin(*att_a, *att_b)
    kept = run_up(where, [arrived[:n_seq], arrived[n_seq:]], tokens, vec, fc1_b, ups)
    attended, branch, residual, normed_two, hidden, active = kept
    active_box = st.box(active)
    st.sync()
    if rings:
        downs = down_in.pieces()
    active = active_box.v
    layer_out, d_second, d_hidden, sums, fc1_sum = run_mid(
        where, active, residual, hidden, out_grad, vec, downs
    )

    hidden_box = st.box(d_hidden)

    def reduction(outs, parts):
        flow = Reduce(st, parts)
        flow.set_first(outs[:2])
        flow.set_second(outs[2:])
        return flow

    if rings:
        wide = Reduce(st, nz)

        def wide_grads(side):
            return run_wide_grad(where, normed_two, hidden_box.v, active, d_second, r, side)

        wide.set_first(wide_grads(0))
        st.sync()
        wide.c_first()
        wide.set_second(wide_grads(1))
        st.sync()
        wide.sum()
        st.sync()
        hops(wide.x, wide.c_second)
    else:
        grad_fc2 = reduce_plain(active, d_second)
        grad_fc1 = reduce_plain(normed_two, d_hidden)
    outs = run_back(where, out_grad, vec, sums, hidden_box.v, residual, branch, ups, chunks)
    d_residual, d_branch, sums = outs[:3]
    branch_box = st.box(d_branch)
    d_out = st.boxes(outs[3:])
    st.sync()
    d_heads_a = swap(d_out[:n_seq])
    d_branch = branch_box.v
    if rings:
        wide.sum(nz - 1)
        proj = reduction(
            grads(row_grad_kernel, "proj_grad", where, (attended, d_branch), r, width // 2), 1
        )
    else:
        grad_proj = reduce_plain(attended, d_branch)
    st.sync()
    hops(*([wide.x, wide.z] if rings else []))
    d_heads_b = swap(d_out[n_seq:])
    d_by_a = st.boxes(attn_bwd(where, by_a, st.begin(*d_heads_a), cols_a, lse_a, heads, 512))
    st.sync()
    d_mixed_a = swap(d_by_a)
    hops(*([wide.x, wide.z] if rings else []))
    d_by_b = st.boxes(attn_bwd(where, by_b, st.begin(*d_heads_b), cols_b, lse_b, heads, 512))
    st.sync()
    d_mixed_b = swap(d_by_b)
    hops(*([wide.x, wide.z] if rings else []))

    def qkv_grads(d_mixed):
        outs = grads(
            qkv_grad_kernel,
            "qkv_grad",
            where,
            [normed] + st.begin(*d_mixed),
            r,
            n_seq // 2 * 3 * part,
            [VMEM] + [ANY] * n_seq,
            [pltpu.VMEM((seq_len, 3 * part), BF16), pltpu.SemaphoreType.DMA((n_seq,))],
        )
        return reduction(outs, 1)

    if rings:
        qkv_a = qkv_grads(d_mixed_a)
        st.sync()
        hops(qkv_a.c)
        st.sync()
        hops(qkv_a.x, wide.y)
        qkv_b = qkv_grads(d_mixed_b)
        st.sync()
        hops(qkv_b.c, proj.c)
        st.sync()
        hops(qkv_b.x, qkv_a.direct, proj.x)
    both = st.begin(*d_mixed_a, *d_mixed_b)
    d_mixed_a, d_mixed_b = both[:n_seq], both[n_seq:]
    tokens_grad, small_grads = last(
        where, [d_mixed_a, d_mixed_b], tokens, d_residual, vec, sums, fc1_sum, qkv_pieces
    )
    if rings:
        vecs = SmallReduce(st, small_grads)
        st.sync()
        hops(qkv_b.direct, qkv_a.y, wide.last_c)
        st.sync()
        hops(vecs.seq, qkv_b.y, qkv_a.last_c, proj.direct)
        st.sync()
        hops(qkv_b.last_c, vecs.x, proj.y)
        st.sync()
        hops(vecs.z, proj.last_c)
        total_small = vecs.finish()
    else:
        total_small = reduce_small(small_grads, fc1_sum, own)
    if rings:
        low = wide.finish()
        at = ff // 2
        grad_fc1 = jnp.concatenate([half[:, :at] for half in low], axis=1).astype(F32)
        grad_fc2 = jnp.stack([half[:, at:] for half in low]).reshape(2, r, groups, width // 2)
        grad_fc2 = grad_fc2.transpose(2, 1, 0, 3).reshape(groups * r, width).astype(F32)
        grad_proj = jnp.concatenate(proj.finish(), axis=1).astype(F32)
        total_qkv = [jnp.concatenate(f.finish(), axis=1).astype(F32) for f in (qkv_a, qkv_b)]
    else:
        total_qkv = []
        order = jnp.stack([jnp.bitwise_xor(where[3], i) for i in range(n_seq)])
        for d_mixed in (d_mixed_a, d_mixed_b):
            blocks = jnp.take(jnp.stack(d_mixed), order, axis=0)
            total_qkv.append(reduce_plain(normed, blocks.transpose(1, 0, 2).reshape(rows, -1)))
    qkv_grad = jnp.stack([t.reshape(-1, n_seq, 3, part) for t in total_qkv])
    qkv_grad = qkv_grad.transpose(1, 3, 2, 0, 4).reshape(-1, 3 * width)
    return (
        layer_out,
        tokens_grad,
        qkv_grad,
        total_small[0:2],
        grad_proj,
        grad_fc1,
        total_small[N_VEC:].reshape(-1),
        grad_fc2,
        total_small[2:4],
        total_small[4:8],
        total_small[8:12],
    )


CHUNKS = 2


def solution(mesh):
    n_dp, n_seq = mesh.devices.shape
    fine = Mesh(mesh.devices.reshape(n_dp // 2, 2, n_seq // 2, 2), DP_AXES + SEQ_AXES)
    tok = P(DP_AXES + SEQ_AXES, None)
    by_row = P(DP_AXES, None)
    by_col = P(None, DP_AXES)
    weights = (by_row, by_col, by_row, by_row, P(DP_AXES), by_row, by_col, by_col, by_col)
    return jax.shard_map(
        per_device,
        mesh=fine,
        in_specs=(tok, tok) + weights,
        out_specs=(tok, tok) + weights,
        check_vma=False,
    )
```

time: 555 us -> 532 us (0.959)
  waiting for transfers between devices: 210 us -> 192 us
  Pallas kernels: 183 us -> 192 us
  other arithmetic: 42.7 us -> 35.9 us
    ppermute x95 -> x84, waiting for transfers between devices: 178 us -> 159 us  [the longest x12 57.4 us: x(): self.others.append(self.box(lax.ppermute(block, 'x', SWAP)))]
    pallas_call x9 -> x12, Pallas kernels: 120 us -> 129 us  [call(): pl.pallas_call(kernel, grid_spec=pltpu.PrefetchScalarGridSpec(num_scalar_...]
    ppermute x8, waiting for transfers between devices: 14.7 us -> 22.2 us  [exchange(): lax.ppermute(blocks[3], SEQ_AXES, both)]
    ppermute x8, waiting for transfers between devices: 17.3 us -> 10.9 us  [exchange(): lax.ppermute(blocks[2], 'y', SWAP)]
    unnamed x217 -> x181, local copies, waits for them, and re-layouts: 16.8 us -> 14.2 us
    convert_element_type x29 -> x21, other arithmetic: 31.9 us -> 29.7 us  [add_low(): return sum((t.astype(F32) for t in terms)).astype(BF16)]
    ppermute x95 -> x84, starting transfers between devices: 61.3 us -> 61.9 us  [the longest x12 13.4 us: x(): self.others.append(self.box(lax.ppermute(block, 'x', SWAP)))]
  transfers between devices with their start and end apart: 119 -> 108, of which waited for: 43 -> 50; matrix products, arithmetic and copies ran while one was open for 11% -> 5% of each run, Pallas kernels for 22% -> 30%
where the time goes in v3:
time: 532 us; the launch traced here: 524 us
  waiting for transfers between devices  192 us (36%)
  Pallas kernels  192 us (36%)
  starting transfers between devices  77.7 us (15%)
  other arithmetic  35.9 us (7%)
  local copies, waits for them, and re-layouts  24 us (5%)
    pallas_call x12, Pallas kernels, call(): pl.pallas_call(kernel, grid_spec=pltpu.PrefetchScalarGridSpec(num_scalar_...  129 us
    ppermute x12, waiting for transfers between devices, x(): self.others.append(self.box(lax.ppermute(block, 'x', SWAP)))  57.4 us
    pallas_call x2, Pallas kernels, attn_bwd(): pl.pallas_call(functools.partial(bwd_kernel, nh=nh, blk=blk, n=n), grid_s...  41.5 us
    convert_element_type x21, other arithmetic, add_low(): return sum((t.astype(F32) for t in terms)).astype(BF16)  29.7 us
    ppermute x7, waiting for transfers between devices, x(): lax.ppermute(self.out[len(self.from_x)].v, 'x', SWAP)  26.9 us
    ppermute x9, waiting for transfers between devices, direct(): lax.ppermute(blocks[i], 'z', [(s, (s - 1 - i) % nz) for s in range(nz)])  26 us
    ppermute x8, waiting for transfers between devices, exchange(): lax.ppermute(blocks[3], SEQ_AXES, both)  22.2 us
    pallas_call x2, Pallas kernels, attn_fwd(): pl.pallas_call(functools.partial(fwd_kernel, nh=nh, blk=blk, n=n), grid_s...  21.5 us
  transfers between devices with their start and end apart: 108, of which 50 were waited for; matrix products, arithmetic and copies ran while one was open for 5% of the time, Pallas kernels for 30%

profile of v3, /device:TPU:0, one launch (start us, length us, event | category | flops | bytes accessed | tf_op | source)
XLA Modules:
  0.0 524.3 jit_solution(4737261781498449157)
XLA Ops:
  4.0 2.9 collective-permute-start
  17.1 3.4 collective-permute-done.1.refs_2_.refs_15_
  22.4 10.5 %collective-permute-done.4.refs_3_.refs_16_ = bf16[128,1664]{1,0:T(8,128)(2,1)S(1)} collective-permute-done((bf16[128,1664]{1,0:T(8,128)(2,1)}, bf16[128,1664]{1,0:T(8,128)(2,1)S(1)}, u32[]{:S(2)}, u32[]{:S(2)}) %collective-permute-start.4) | collective-permute-done | bytes 426016 | tf_op jit(solution)/shard_map/ppermute | solution.py:278
  37.4 9.9 %collective-permute-done.8.refs_5_.refs_18_ = bf16[128,1664]{1,0:T(8,128)(2,1)S(1)} collective-permute-done((bf16[128,1664]{1,0:T(8,128)(2,1)S(1)}, bf16[128,1664]{1,0:T(8,128)(2,1)S(1)}, u32[]{:S(2)}, u32[]{:S(2)}) %collective-permute-start.8) | collective-permute-done | bytes 426016 | tf_op jit(solution)/shard_map/ppermute | solution.py:278
  47.3 3.0 collective-permute-done.9.refs_6_.refs_19_
  52.7 10.0 %collective-permute-done.12.refs_7_.refs_20_ = bf16[128,1664]{1,0:T(8,128)(2,1)} collective-permute-done((bf16[128,1664]{1,0:T(8,128)(2,1)S(1)}, bf16[128,1664]{1,0:T(8,128)(2,1)}, u32[]{:S(2)}, u32[]{:S(2)}) %collective-permute-start.12) | collective-permute-done | bytes 426016 | tf_op jit(solution)/shard_map/ppermute | solution.py:278
  62.8 4.9 collective-permute-done.13.refs_13_.refs_2_
  71.4 7.9 %qkv.2 = (bf16[512,384]{1,0:T(8,128)(2,1)}, bf16[512,384]{1,0:T(8,128)(2,1)}, bf16[512,384]{1,0:T(8,128)(2,1)}, bf16[512,384]{1,0:T(8,128)(2,1)}, bf16[512,1024]{1,0:T(8,128)(2,1)}) custom-call(s32[4]{0:T(128)} %pad_add_fusion.where, bf16[512,1024]{1,0:T(8,128)(2,1)} %refs_8_.3, f32[16,1024]{1,0:T(8,128)} %get-tuple-element.715.vec.refs_9_.refs_10_, ...), custom_call_target="tpu_custom_call" | custom-call | flops 7699999744 | bytes 1048576 | tf_op jit(solution)/shard_map/qkv/pallas_call | solution.py:209
  79.3 8.6 %collective-permute-done.15.refs_12_.refs_1_ = bf16[128,2560]{1,0:T(8,128)(2,1)S(1)} collective-permute-done((bf16[128,2560]{1,0:T(8,128)(2,1)S(1)}, bf16[128,2560]{1,0:T(8,128)(2,1)S(1)}, u32[]{:S(2)}, u32[]{:S(2)}) %collective-permute-start.15) | collective-permute-done | bytes 655392 | tf_op jit(solution)/shard_map/ppermute | solution.py:278
  93.5 6.9 %qkv.3 = (bf16[512,384]{1,0:T(8,128)(2,1)}, bf16[512,384]{1,0:T(8,128)(2,1)}, bf16[512,384]{1,0:T(8,128)(2,1)}, bf16[512,384]{1,0:T(8,128)(2,1)}) custom-call(s32[4]{0:T(128)} %pad_add_fusion.where, bf16[512,1024]{1,0:T(8,128)(2,1)} %get-tuple-element.744.first.normed, f32[16,1024]{1,0:T(8,128)} %get-tuple-element.715.vec.refs_9_.refs_10_, ...), custom_call_target="tpu_custom_call" | custom-call | flops 7699999744 | bytes 1048576 | tf_op jit(solution)/shard_map/qkv/pallas_call | solution.py:209
  100.5 3.3 collective-permute-done.18.refs_2_
  103.8 7.7 %collective-permute-done.19.refs_3_ = bf16[512,384]{1,0:T(8,128)(2,1)S(1)} collective-permute-done((bf16[512,384]{1,0:T(8,128)(2,1)}, bf16[512,384]{1,0:T(8,128)(2,1)S(1)}, u32[]{:S(2)}, u32[]{:S(2)}) %collective-permute-start.19) | collective-permute-done | bytes 393248 | tf_op jit(solution)/shard_map/ppermute | solution.py:1133
  114.5 10.7 %attn_fwd.2 = (bf16[512,128]{1,0:T(8,128)(2,1)S(1)}, bf16[512,128]{1,0:T(8,128)(2,1)S(1)}, bf16[512,128]{1,0:T(8,128)(2,1)S(1)}, bf16[512,128]{1,0:T(8,128)(2,1)...) custom-call(s32[4]{0:T(128)S(1)} %copy-done, bf16[512,384]{1,0:T(8,128)(2,1)S(1)} %copy-done.8, ...), custom_call_target="tpu_custom_call" | custom-call | flops 9900000256 | bytes 1048576 | tf_op jit(solution)/shard_map/attn_fwd/pallas_call | solution.py:96
  127.6 4.8 collective-permute-done.24.refs_3_
  136.3 10.7 %attn_fwd.3 = (bf16[512,128]{1,0:T(8,128)(2,1)S(1)}, bf16[512,128]{1,0:T(8,128)(2,1)S(1)}, bf16[512,128]{1,0:T(8,128)(2,1)S(1)}, bf16[512,128]{1,0:T(8,128)(2,1)...) custom-call(s32[4]{0:T(128)S(1)} %copy-done, bf16[512,384]{1,0:T(8,128)(2,1)S(1)} %copy-done.7, ...), custom_call_target="tpu_custom_call" | custom-call | flops 9900000256 | bytes 1048576 | tf_op jit(solution)/shard_map/attn_fwd/pallas_call | solution.py:96
  152.0 4.1 collective-permute-start.37
  158.7 3.7 collective-permute-done.33.refs_6_
  164.8 10.2 %collective-permute-done.36.refs_3_ = bf16[128,2048]{1,0:T(8,128)(2,1)} collective-permute-done((bf16[128,2048]{1,0:T(8,128)(2,1)S(1)}, bf16[128,2048]{1,0:T(8,128)(2,1)}, u32[]{:S(2)}, u32[]{:S(2)}) %collective-permute-start.36) | collective-permute-done | bytes 524320 | tf_op jit(solution)/shard_map/ppermute | solution.py:278
  176.2 3.5 collective-permute-done.45.refs_9_
  185.8 16.7 %up.1 = (bf16[512,1024]{1,0:T(8,128)(2,1)}, f32[512,1024]{1,0:T(8,128)}, f32[512,1024]{1,0:T(8,128)}, bf16[512,1024]{1,0:T(8,128)(2,1)}, f32[512,4096]{1,0:T(8,128)}, /*index=5*/bf16[512,4096]{1,0:T(8,128)(2,1)}) custom-call(s32[4]{0:T(128)} %pad_add_fusion.where, bf16[512,128]{1,0:T(8,128)(2,1)} %copy-done.11, bf16[512,128]{1,0:T(8,128)(2,1)} %copy-done.73, ...), custom_call_target="tpu_custom_call" | custom-call | flops 22000001024 | bytes 1048576 | tf_op jit(solution)/shard_map/up/pallas_call | solution.py:209
  202.5 5.2 %collective-permute-done.51.refs_7_ = bf16[128,2048]{1,0:T(8,128)(2,1)} collective-permute-done((bf16[128,2048]{1,0:T(8,128)(2,1)}, bf16[128,2048]{1,0:T(8,128)(2,1)}, u32[]{:S(2)}, u32[]{:S(2)}) %collective-permute-start.51) | collective-permute-done | bytes 524320 | tf_op jit(solution)/shard_map/ppermute | solution.py:278
  211.5 26.1 %mid.1 = (bf16[512,1024]{1,0:T(8,128)(2,1)}, bf16[512,1024]{1,0:T(8,128)(2,1)}, bf16[512,4096]{1,0:T(8,128)(2,1)}, f32[16,1024]{1,0:T(8,128)}, f32[1,4096]{1,0:T(1,128)}) custom-call(s32[4]{0:T(128)} %pad_add_fusion.where, bf16[512,4096]{1,0:T(8,128)(2,1)} %get-tuple-element.962.active_in.refs_2_, f32[512,1024]{1,0:T(8,128)} %get-tuple-element.963.residual_in, ...), custom_call_target="tpu_custom_call" | custom-call | flops 30799998976 | bytes 1048576 | tf_op jit(solution)/shard_map/mid/pallas_call | solution.py:209
  237.6 9.4 %wide_grad.2 = (bf16[4,128,4096]{2,1,0:T(8,128)(2,1)}, bf16[4,128,4096]{2,1,0:T(8,128)(2,1)}) custom-call(s32[4]{0:T(128)} %pad_add_fusion.where, bf16[512,1024]{1,0:T(8,128)(2,1)} %get-tuple-element.1044.refs_0_, bf16[512,4096]{1,0:T(8,128)(2,1)} %get-tuple-element.1058.refs_1_.d_hidden_in, bf16[512,4096]{1,0:T(8,128)(2,1)} %get-tuple-element.962.active_in.refs_2_, ...), custom_call_target="tpu_custom_call" | custom-call | flops 9900000256 | bytes 1048576 | tf_op jit(solution)/shard_map/wide_grad/pallas_call | solution.py:209
  247.2 9.8 %wide_grad.3 = (bf16[4,128,4096]{2,1,0:T(8,128)(2,1)}, bf16[4,128,4096]{2,1,0:T(8,128)(2,1)}) custom-call(s32[4]{0:T(128)} %pad_add_fusion.where, bf16[512,1024]{1,0:T(8,128)(2,1)} %get-tuple-element.1044.refs_0_, bf16[512,4096]{1,0:T(8,128)(2,1)} %get-tuple-element.1058.refs_1_.d_hidden_in, bf16[512,4096]{1,0:T(8,128)(2,1)} %get-tuple-element.962.active_in.refs_2_, ...), custom_call_target="tpu_custom_call" | custom-call | flops 9900000256 | bytes 1048576 | tf_op jit(solution)/shard_map/wide_grad/pallas_call | solution.py:209
  260.0 18.9 %back.1 = (f32[512,1024]{1,0:T(8,128)}, bf16[512,1024]{1,0:T(8,128)(2,1)}, f32[16,1024]{1,0:T(8,128)}, bf16[512,128]{1,0:T(8,128)(2,1)}, bf16[512,128]{1,0:T(8,1...) custom-call(s32[4]{0:T(128)} %pad_add_fusion.where, ...), custom_call_target="tpu_custom_call" | custom-call | flops 22000001024 | bytes 1048576 | tf_op jit(solution)/shard_map/back/pallas_call | solution.py:209
  278.9 5.5 %collective-permute-done.55 = bf16[1,128,4096]{2,1,0:T(8,128)(2,1)S(1)} collective-permute-done((bf16[1,128,4096]{2,1,0:T(8,128)(2,1)S(1)}, bf16[1,128,4096]{2,1,0:T(8,128)(2,1)S(1)}, u32[]{:S(2)}, u32[]{:S(2)}) %collective-permute-start.55) | collective-permute-done | bytes 1048608 | tf_op jit(solution)/shard_map/ppermute | solution.py:934
  286.3 4.4 proj_grad.1
  290.7 4.2 add_convert_fusion.2
  298.4 4.4 collective-permute-start.61
  305.2 20.6 %attn_bwd.2 = (bf16[512,384]{1,0:T(8,128)(2,1)}, bf16[512,384]{1,0:T(8,128)(2,1)}, bf16[512,384]{1,0:T(8,128)(2,1)}, bf16[512,384]{1,0:T(8,128)(2,1)}) custom-call(s32[4]{0:T(128)} %pad_add_fusion.where, bf16[512,384]{1,0:T(8,128)(2,1)} %get-tuple-element.777.refs_0_, bf16[512,384]{1,0:T(8,128)(2,1)} %copy-done.4, bf16[512,384]{1,0:T(8,128)(2,1)} %copy-done.5, ...), custom_call_target="tpu_custom_call" | custom-call | flops 20899999744 | bytes 1048576 | tf_op jit(solution)/shard_map/attn_bwd/pallas_call | solution.py:163
  328.1 3.5 fusion.2
  334.6 20.8 %attn_bwd.3 = (bf16[512,384]{1,0:T(8,128)(2,1)}, bf16[512,384]{1,0:T(8,128)(2,1)}, bf16[512,384]{1,0:T(8,128)(2,1)}, bf16[512,384]{1,0:T(8,128)(2,1)}) custom-call(s32[4]{0:T(128)} %pad_add_fusion.where, bf16[512,384]{1,0:T(8,128)(2,1)} %get-tuple-element.827.refs_0_, bf16[512,384]{1,0:T(8,128)(2,1)} %copy-done.1, bf16[512,384]{1,0:T(8,128)(2,1)} %copy-done.2, ...), custom_call_target="tpu_custom_call" | custom-call | flops 20899999744 | bytes 1048576 | tf_op jit(solution)/shard_map/attn_bwd/pallas_call | solution.py:163
  357.9 3.2 fusion.1
  363.6 6.3 %qkv_grad.2 = (bf16[4,128,768]{2,1,0:T(8,128)(2,1)}, bf16[4,128,768]{2,1,0:T(8,128)(2,1)}, bf16[4,128,768]{2,1,0:T(8,128)(2,1)}, bf16[4,128,768]{2,1,0:T(8,128)(2,1)}) custom-call(s32[4]{0:T(128)} %pad_add_fusion.where, bf16[512,1024]{1,0:T(8,128)(2,1)} %get-tuple-element.744.first.normed, bf16[512,384]{1,0:T(8,128)(2,1)} %get-tuple-element.1228.refs_0_, ...), custom_call_target="tpu_custom_call" | custom-call | flops 11000000512 | bytes 1048576 | tf_op jit(solution)/shard_map/qkv_grad/pallas_call | solution.py:209
  369.9 4.0 collective-permute-done.71.refs_2_.refs_6_
  373.9 7.8 %collective-permute-done.72.refs_3_.refs_7_ = bf16[512,384]{1,0:T(8,128)(2,1)} collective-permute-done((bf16[512,384]{1,0:T(8,128)(2,1)}, bf16[512,384]{1,0:T(8,128)(2,1)}, u32[]{:S(2)}, u32[]{:S(2)}) %collective-permute-start.72) | collective-permute-done | bytes 393248 | tf_op jit(solution)/shard_map/ppermute | solution.py:1133
  381.6 5.2 collective-permute-done.74
  396.4 6.3 %qkv_grad.3 = (bf16[4,128,768]{2,1,0:T(8,128)(2,1)}, bf16[4,128,768]{2,1,0:T(8,128)(2,1)}, bf16[4,128,768]{2,1,0:T(8,128)(2,1)}, bf16[4,128,768]{2,1,0:T(8,128)(2,1)}) custom-call(s32[4]{0:T(128)} %pad_add_fusion.where, bf16[512,1024]{1,0:T(8,128)(2,1)} %get-tuple-element.744.first.normed, bf16[512,384]{1,0:T(8,128)(2,1)} %get-tuple-element.1232.refs_0_.refs_4_, ...), custom_call_target="tpu_custom_call" | custom-call | flops 11000000512 | bytes 1048576 | tf_op jit(solution)/shard_map/qkv_grad/pallas_call | solution.py:209
  402.7 11.6 %collective-permute-done.77 = bf16[4,128,768]{2,1,0:T(8,128)(2,1)S(1)} collective-permute-done((bf16[4,128,768]{2,1,0:T(8,128)(2,1)S(1)}, bf16[4,128,768]{2,1,0:T(8,128)(2,1)S(1)}, u32[]{:S(2)}, u32[]{:S(2)}) %collective-permute-start.77) | collective-permute-done | bytes 786464 | tf_op jit(solution)/shard_map/ppermute | solution.py:934
  414.3 4.1 collective-permute-done.78
  419.4 3.3 collective-permute-done.81
  434.1 14.1 %last.1 = (bf16[512,1024]{1,0:T(8,128)(2,1)}, f32[8,16,128]{2,1,0:T(8,128)}) custom-call(s32[4]{0:T(128)} %pad_add_fusion.where, bf16[512,384]{1,0:T(8,128)(2,1)} %get-tuple-element.1228.refs_0_, bf16[512,384]{1,0:T(8,128)(2,1)} %copy-done.69, bf16[512,384]{1,0:T(8,128)(2,1)} %copy-done.70, bf16[512,384]{1,0:T(8,128)(2,1)} %collective-permute-done.67.refs_3_, ...), custom_call_target="tpu_custom_call" | custom-call | flops 13200000000 | bytes 1048576 | tf_op jit(solution)/shard_map/last/pallas_call | solution.py:209
  449.1 7.8 %collective-permute-done.83 = bf16[4,128,768]{2,1,0:T(8,128)(2,1)} collective-permute-done((bf16[4,128,768]{2,1,0:T(8,128)(2,1)S(1)}, bf16[4,128,768]{2,1,0:T(8,128)(2,1)}, u32[]{:S(2)}, u32[]{:S(2)}) %collective-permute-start.83) | collective-permute-done | bytes 786464 | tf_op jit(solution)/shard_map/ppermute | solution.py:934
  466.1 3.6 collective-permute-done.88
  469.7 11.6 %collective-permute-done.89 = bf16[128,768]{1,0:T(8,128)(2,1)S(1)} collective-permute-done((bf16[128,768]{1,0:T(8,128)(2,1)S(1)}, bf16[128,768]{1,0:T(8,128)(2,1)S(1)}, u32[]{:S(2)}, u32[]{:S(2)}) %collective-permute-start.89) | collective-permute-done | bytes 196640 | tf_op jit(solution)/shard_map/ppermute | solution.py:955
  487.4 3.1 collective-permute-start.98
  491.3 3.5 collective-permute-done.100
  496.0 6.2 %collective-permute-done.99 = bf16[128,512]{1,0:T(8,128)(2,1)S(1)} collective-permute-done((bf16[128,512]{1,0:T(8,128)(2,1)S(1)}, bf16[128,512]{1,0:T(8,128)(2,1)S(1)}, u32[]{:S(2)}, u32[]{:S(2)}) %collective-permute-start.99) | collective-permute-done | bytes 131104 | tf_op jit(solution)/shard_map/ppermute | solution.py:955
  (428 shorter events, 144.0 us)
Async XLA Ops:
  50.4 17.4 %collective-permute-start.13 = (bf16[128,2560]{1,0:T(8,128)(2,1)S(1)}, bf16[128,2560]{1,0:T(8,128)(2,1)S(1)}, u32[]{:S(2)}, u32[]{:S(2)}) collective-permute-start(bf16[128,2560]{1,0:T(8,128)(2,1)S(1)} %fusion.5), channel_id=1, source_target_pairs={{0,8},{8,16},{16,24},{24,0},{1,9},{9,17},{17,25},{25,1},{2,10},{10... | collective-permute-start | bytes 1966088 | tf_op jit(solution)/shard_map/ppermute | solution.py:273
  70.8 17.1 %collective-permute-start.15 = (bf16[128,2560]{1,0:T(8,128)(2,1)S(1)}, bf16[128,2560]{1,0:T(8,128)(2,1)S(1)}, u32[]{:S(2)}, u32[]{:S(2)}) collective-permute-start(bf16[128,2560]{1,0:T(8,128)(2,1)S(1)} %fusion.5), channel_id=1, source_target_pairs={{0,4},{4,0},{1,5},{5,1},{2,6},{6,2},{3,7},{7,3},{8,12},{12,8},{9,1... | collective-permute-start | bytes 1966088 | tf_op jit(solution)/shard_map/ppermute | solution.py:278
  71.4 18.7 %collective-permute-start.16 = (bf16[128,2560]{1,0:T(8,128)(2,1)S(1)}, bf16[128,2560]{1,0:T(8,128)(2,1)}, u32[]{:S(2)}, u32[]{:S(2)}) collective-permute-start(bf16[128,2560]{1,0:T(8,128)(2,1)S(1)} %collective-permute-done.13.refs_13_.refs_2_), channel_id=1, source_target_pairs={{0,8},{8,16},{16,24},{24,0},{1,9},{9,17},{17,25},{25,1},{2,10},{10... | collective-permute-start | bytes 1966088 | tf_op jit(solution)/shard_map/ppermute | solution.py:273
  90.1 21.3 %collective-permute-start.20 = (bf16[128,2560]{1,0:T(8,128)(2,1)S(1)}, bf16[128,2560]{1,0:T(8,128)(2,1)}, u32[]{:S(2)}, u32[]{:S(2)}) collective-permute-start(bf16[128,2560]{1,0:T(8,128)(2,1)S(1)} %collective-permute-done.13.refs_13_.refs_2_), channel_id=1, source_target_pairs={{0,4},{4,0},{1,5},{5,1},{2,6},{6,2},{3,7},{7,3},{8,12},{12,8},{9,1... | collective-permute-start | bytes 1966088 | tf_op jit(solution)/shard_map/ppermute | solution.py:278
  91.7 19.8 %collective-permute-start.21 = (bf16[128,2560]{1,0:T(8,128)(2,1)}, bf16[128,2560]{1,0:T(8,128)(2,1)}, u32[]{:S(2)}, u32[]{:S(2)}) collective-permute-start(bf16[128,2560]{1,0:T(8,128)(2,1)} %collective-permute-done.16.refs_15_.refs_4_), channel_id=1, source_target_pairs={{0,8},{8,16},{16,24},{24,0},{1,9},{9,17},{17,25},{25,1},{2,10},{10... | collective-permute-start | bytes 1966088 | tf_op jit(solution)/shard_map/ppermute | solution.py:273
  93.2 18.3 %collective-permute-start.19 = (bf16[512,384]{1,0:T(8,128)(2,1)}, bf16[512,384]{1,0:T(8,128)(2,1)S(1)}, u32[]{:S(2)}, u32[]{:S(2)}) collective-permute-start(bf16[512,384]{1,0:T(8,128)(2,1)} %get-tuple-element.743), channel_id=1, source_target_pairs={{0,3},{1,2},{2,1},{3,0},{4,7},{5,6},{6,5},{7,4},{8,11},{9,10},{10,... | collective-permute-start | bytes 1179656 | tf_op jit(solution)/shard_map/ppermute | solution.py:1133
  111.5 20.9 %collective-permute-start.25 = (bf16[128,2560]{1,0:T(8,128)(2,1)}, bf16[128,2560]{1,0:T(8,128)(2,1)S(1)}, u32[]{:S(2)}, u32[]{:S(2)}) collective-permute-start(bf16[128,2560]{1,0:T(8,128)(2,1)} %collective-permute-done.16.refs_15_.refs_4_), channel_id=1, source_target_pairs={{0,4},{4,0},{1,5},{5,1},{2,6},{6,2},{3,7},{7,3},{8,12},{12,8},{9,1... | collective-permute-start | bytes 1966088 | tf_op jit(solution)/shard_map/ppermute | solution.py:278
  112.1 20.3 %collective-permute-start.26 = (bf16[128,2048]{1,0:T(8,128)(2,1)S(1)}, bf16[128,2048]{1,0:T(8,128)(2,1)S(1)}, u32[]{:S(2)}, u32[]{:S(2)}) collective-permute-start(bf16[128,2048]{1,0:T(8,128)(2,1)S(1)} %copy-done.31), channel_id=1, source_target_pairs={{0,8},{8,16},{16,24},{24,0},{1,9},{9,17},{17,25},{25,1},{2,10},{10... | collective-permute-start | bytes 1572872 | tf_op jit(solution)/shard_map/ppermute | solution.py:273
  112.5 15.0 %collective-permute-start.22 = (bf16[512,384]{1,0:T(8,128)(2,1)}, bf16[512,384]{1,0:T(8,128)(2,1)S(1)}, u32[]{:S(2)}, u32[]{:S(2)}) collective-permute-start(bf16[512,384]{1,0:T(8,128)(2,1)} %get-tuple-element.782), channel_id=1, source_target_pairs={{0,1},{1,0},{2,3},{3,2},{4,5},{5,4},{6,7},{7,6},{8,9},{9,8},{10,11... | collective-permute-start | bytes 1179656 | tf_op jit(solution)/shard_map/ppermute | solution.py:1131
  112.6 14.9 %collective-permute-start.23 = (bf16[512,384]{1,0:T(8,128)(2,1)}, bf16[512,384]{1,0:T(8,128)(2,1)S(1)}, u32[]{:S(2)}, u32[]{:S(2)}) collective-permute-start(bf16[512,384]{1,0:T(8,128)(2,1)} %get-tuple-element.783), channel_id=1, source_target_pairs={{0,2},{2,0},{1,3},{3,1},{4,6},{6,4},{5,7},{7,5},{8,10},{10,8},{9,1... | collective-permute-start | bytes 1179656 | tf_op jit(solution)/shard_map/ppermute | solution.py:1132
  114.2 18.1 %collective-permute-start.24 = (bf16[512,384]{1,0:T(8,128)(2,1)}, bf16[512,384]{1,0:T(8,128)(2,1)S(1)}, u32[]{:S(2)}, u32[]{:S(2)}) collective-permute-start(bf16[512,384]{1,0:T(8,128)(2,1)} %get-tuple-element.784), channel_id=1, source_target_pairs={{0,3},{1,2},{2,1},{3,0},{4,7},{5,6},{6,5},{7,4},{8,11},{9,10},{10,... | collective-permute-start | bytes 1179656 | tf_op jit(solution)/shard_map/ppermute | solution.py:1133
  132.4 17.6 %collective-permute-start.30 = (bf16[128,2560]{1,0:T(8,128)(2,1)}, bf16[128,2560]{1,0:T(8,128)(2,1)S(1)}, u32[]{:S(2)}, u32[]{:S(2)}) collective-permute-start(bf16[128,2560]{1,0:T(8,128)(2,1)} %collective-permute-done.21.refs_17_.refs_6_), channel_id=1, source_target_pairs={{0,4},{4,0},{1,5},{5,1},{2,6},{6,2},{3,7},{7,3},{8,12},{12,8},{9,1... | collective-permute-start | bytes 1966088 | tf_op jit(solution)/shard_map/ppermute | solution.py:278
  133.9 16.0 %collective-permute-start.31 = (bf16[128,2048]{1,0:T(8,128)(2,1)S(1)}, bf16[128,2048]{1,0:T(8,128)(2,1)}, u32[]{:S(2)}, u32[]{:S(2)}) collective-permute-start(bf16[128,2048]{1,0:T(8,128)(2,1)S(1)} %collective-permute-done.26.refs_2_), channel_id=1, source_target_pairs={{0,8},{8,16},{16,24},{24,0},{1,9},{9,17},{17,25},{25,1},{2,10},{10... | collective-permute-start | bytes 1572872 | tf_op jit(solution)/shard_map/ppermute | solution.py:273
  134.5 14.9 %collective-permute-start.28 = (bf16[512,128]{1,0:T(8,128)(2,1)S(1)}, bf16[512,128]{1,0:T(8,128)(2,1)S(1)}, u32[]{:S(2)}, u32[]{:S(2)}) collective-permute-start(bf16[512,128]{1,0:T(8,128)(2,1)S(1)} %get-tuple-element.833), channel_id=1, source_target_pairs={{0,2},{2,0},{1,3},{3,1},{4,6},{6,4},{5,7},{7,5},{8,10},{10,8},{9,1... | collective-permute-start | bytes 393224 | tf_op jit(solution)/shard_map/ppermute | solution.py:1132
  151.1 23.9 %collective-permute-start.36 = (bf16[128,2048]{1,0:T(8,128)(2,1)S(1)}, bf16[128,2048]{1,0:T(8,128)(2,1)}, u32[]{:S(2)}, u32[]{:S(2)}) collective-permute-start(bf16[128,2048]{1,0:T(8,128)(2,1)S(1)} %collective-permute-done.26.refs_2_), channel_id=1, source_target_pairs={{0,4},{4,0},{1,5},{5,1},{2,6},{6,2},{3,7},{7,3},{8,12},{12,8},{9,1... | collective-permute-start | bytes 1572872 | tf_op jit(solution)/shard_map/ppermute | solution.py:278
  152.0 23.0 %collective-permute-start.37 = (bf16[128,2048]{1,0:T(8,128)(2,1)}, bf16[128,2048]{1,0:T(8,128)(2,1)}, u32[]{:S(2)}, u32[]{:S(2)}) collective-permute-start(bf16[128,2048]{1,0:T(8,128)(2,1)} %collective-permute-done.31.refs_4_), channel_id=1, source_target_pairs={{0,8},{8,16},{16,24},{24,0},{1,9},{9,17},{17,25},{25,1},{2,10},{10... | collective-permute-start | bytes 1572872 | tf_op jit(solution)/shard_map/ppermute | solution.py:273
  182.3 20.3 %collective-permute-start.50 = (bf16[128,2048]{1,0:T(8,128)(2,1)}, bf16[128,2048]{1,0:T(8,128)(2,1)}, u32[]{:S(2)}, u32[]{:S(2)}) collective-permute-start(bf16[128,2048]{1,0:T(8,128)(2,1)} %collective-permute-done.31.refs_4_), channel_id=1, source_target_pairs={{0,4},{4,0},{1,5},{5,1},{2,6},{6,2},{3,7},{7,3},{8,12},{12,8},{9,1... | collective-permute-start | bytes 1572872 | tf_op jit(solution)/shard_map/ppermute | solution.py:278
  183.0 19.4 %collective-permute-start.47 = (bf16[128,2048]{1,0:T(8,128)(2,1)}, bf16[128,2048]{1,0:T(8,128)(2,1)S(1)}, u32[]{:S(2)}, u32[]{:S(2)}) collective-permute-start(bf16[128,2048]{1,0:T(8,128)(2,1)} %collective-permute-done.37.refs_6_), channel_id=1, source_target_pairs={{0,1},{1,0},{2,3},{3,2},{4,5},{5,4},{6,7},{7,6},{8,9},{9,8},{10,11... | collective-permute-start | bytes 1572872 | tf_op jit(solution)/shard_map/ppermute | solution.py:284
  183.9 23.9 %collective-permute-start.51 = (bf16[128,2048]{1,0:T(8,128)(2,1)}, bf16[128,2048]{1,0:T(8,128)(2,1)}, u32[]{:S(2)}, u32[]{:S(2)}) collective-permute-start(bf16[128,2048]{1,0:T(8,128)(2,1)} %collective-permute-done.37.refs_6_), channel_id=1, source_target_pairs={{0,4},{4,0},{1,5},{5,1},{2,6},{6,2},{3,7},{7,3},{8,12},{12,8},{9,1... | collective-permute-start | bytes 1572872 | tf_op jit(solution)/shard_map/ppermute | solution.py:278
  184.7 17.8 %collective-permute-start.48 = (bf16[128,2048]{1,0:T(8,128)(2,1)S(1)}, bf16[128,2048]{1,0:T(8,128)(2,1)}, u32[]{:S(2)}, u32[]{:S(2)}) collective-permute-start(bf16[128,2048]{1,0:T(8,128)(2,1)S(1)} %collective-permute-done.35.refs_1_), channel_id=1, source_target_pairs={{0,1},{1,0},{2,3},{3,2},{4,5},{5,4},{6,7},{7,6},{8,9},{9,8},{10,11... | collective-permute-start | bytes 1572872 | tf_op jit(solution)/shard_map/ppermute | solution.py:284
  184.7 17.8 %collective-permute-start.49 = (bf16[128,2048]{1,0:T(8,128)(2,1)}, bf16[128,2048]{1,0:T(8,128)(2,1)}, u32[]{:S(2)}, u32[]{:S(2)}) collective-permute-start(bf16[128,2048]{1,0:T(8,128)(2,1)} %collective-permute-done.36.refs_3_), channel_id=1, source_target_pairs={{0,1},{1,0},{2,3},{3,2},{4,5},{5,4},{6,7},{7,6},{8,9},{9,8},{10,11... | collective-permute-start | bytes 1572872 | tf_op jit(solution)/shard_map/ppermute | solution.py:284
  258.8 25.6 %collective-permute-start.56 = (bf16[4,128,4096]{2,1,0:T(8,128)(2,1)}, bf16[4,128,4096]{2,1,0:T(8,128)(2,1)}, u32[]{:S(2)}, u32[]{:S(2)}) collective-permute-start(bf16[4,128,4096]{2,1,0:T(8,128)(2,1)} %get-tuple-element.1061), channel_id=1, source_target_pairs={{0,1},{1,0},{2,3},{3,2},{4,5},{5,4},{6,7},{7,6},{8,9},{9,8},{10,11... | collective-permute-start | bytes 12582920 | tf_op jit(solution)/shard_map/ppermute | solution.py:918
  259.2 25.2 %collective-permute-start.55 = (bf16[1,128,4096]{2,1,0:T(8,128)(2,1)S(1)}, bf16[1,128,4096]{2,1,0:T(8,128)(2,1)S(1)}, u32[]{:S(2)}, u32[]{:S(2)}) collective-permute-start(bf16[1,128,4096]{2,1,0:T(8,128)(2,1)S(1)} %add_convert_fusion.5), channel_id=1, source_target_pairs={{0,4},{4,0},{1,5},{5,1},{2,6},{6,2},{3,7},{7,3},{8,12},{12,8},{9,1... | collective-permute-start | bytes 3145736 | tf_op jit(solution)/shard_map/ppermute | solution.py:934
  298.4 27.7 %collective-permute-start.61 = (bf16[128,4096]{1,0:T(8,128)(2,1)}, bf16[128,4096]{1,0:T(8,128)(2,1)}, u32[]{:S(2)}, u32[]{:S(2)}) collective-permute-start(bf16[128,4096]{1,0:T(8,128)(2,1)} %fusion.3), channel_id=1, source_target_pairs={{0,8},{8,16},{16,24},{24,0},{1,9},{9,17},{17,25},{25,1},{2,10},{10... | collective-permute-start | bytes 3145736 | tf_op jit(solution)/shard_map/ppermute | solution.py:946
  302.9 25.2 %collective-permute-start.60 = (bf16[1,128,4096]{2,1,0:T(8,128)(2,1)S(1)}, bf16[1,128,4096]{2,1,0:T(8,128)(2,1)}, u32[]{:S(2)}, u32[]{:S(2)}) collective-permute-start(bf16[1,128,4096]{2,1,0:T(8,128)(2,1)S(1)} %get-tuple-element.1104), channel_id=1, source_target_pairs={{0,4},{4,0},{1,5},{5,1},{2,6},{6,2},{3,7},{7,3},{8,12},{12,8},{9,1... | collective-permute-start | bytes 3145736 | tf_op jit(solution)/shard_map/ppermute | solution.py:934
  303.4 22.5 %collective-permute-start.62 = (bf16[512,128]{1,0:T(8,128)(2,1)S(1)}, bf16[512,128]{1,0:T(8,128)(2,1)S(1)}, u32[]{:S(2)}, u32[]{:S(2)}) collective-permute-start(bf16[512,128]{1,0:T(8,128)(2,1)S(1)} %copy-done.81), channel_id=1, source_target_pairs={{0,1},{1,0},{2,3},{3,2},{4,5},{5,4},{6,7},{7,6},{8,9},{9,8},{10,11... | collective-permute-start | bytes 393224 | tf_op jit(solution)/shard_map/ppermute | solution.py:1131
  303.4 22.5 %collective-permute-start.63 = (bf16[512,128]{1,0:T(8,128)(2,1)S(1)}, bf16[512,128]{1,0:T(8,128)(2,1)S(1)}, u32[]{:S(2)}, u32[]{:S(2)}) collective-permute-start(bf16[512,128]{1,0:T(8,128)(2,1)S(1)} %copy-done.80), channel_id=1, source_target_pairs={{0,2},{2,0},{1,3},{3,1},{4,6},{6,4},{5,7},{7,5},{8,10},{10,8},{9,1... | collective-permute-start | bytes 393224 | tf_op jit(solution)/shard_map/ppermute | solution.py:1132
  304.9 21.0 %collective-permute-start.64 = (bf16[512,128]{1,0:T(8,128)(2,1)S(1)}, bf16[512,128]{1,0:T(8,128)(2,1)S(1)}, u32[]{:S(2)}, u32[]{:S(2)}) collective-permute-start(bf16[512,128]{1,0:T(8,128)(2,1)S(1)} %copy-done.79), channel_id=1, source_target_pairs={{0,3},{1,2},{2,1},{3,0},{4,7},{5,6},{6,5},{7,4},{8,11},{9,10},{10,... | collective-permute-start | bytes 393224 | tf_op jit(solution)/shard_map/ppermute | solution.py:1133
  331.6 26.3 %collective-permute-start.69 = (bf16[128,4096]{1,0:T(8,128)(2,1)}, bf16[128,4096]{1,0:T(8,128)(2,1)S(1)}, u32[]{:S(2)}, u32[]{:S(2)}) collective-permute-start(bf16[128,4096]{1,0:T(8,128)(2,1)} %fusion.2), channel_id=1, source_target_pairs={{0,8},{8,16},{16,24},{24,0},{1,9},{9,17},{17,25},{25,1},{2,10},{10... | collective-permute-start | bytes 3145736 | tf_op jit(solution)/shard_map/ppermute | solution.py:946
  332.1 25.8 %collective-permute-start.68 = (bf16[1,128,4096]{2,1,0:T(8,128)(2,1)S(1)}, bf16[1,128,4096]{2,1,0:T(8,128)(2,1)}, u32[]{:S(2)}, u32[]{:S(2)}) collective-permute-start(bf16[1,128,4096]{2,1,0:T(8,128)(2,1)S(1)} %get-tuple-element.1120), channel_id=1, source_target_pairs={{0,4},{4,0},{1,5},{5,1},{2,6},{6,2},{3,7},{7,3},{8,12},{12,8},{9,1... | collective-permute-start | bytes 3145736 | tf_op jit(solution)/shard_map/ppermute | solution.py:934
  332.7 22.7 %collective-permute-start.65 = (bf16[512,384]{1,0:T(8,128)(2,1)}, bf16[512,384]{1,0:T(8,128)(2,1)S(1)}, u32[]{:S(2)}, u32[]{:S(2)}) collective-permute-start(bf16[512,384]{1,0:T(8,128)(2,1)} %get-tuple-element.1132), channel_id=1, source_target_pairs={{0,1},{1,0},{2,3},{3,2},{4,5},{5,4},{6,7},{7,6},{8,9},{9,8},{10,11... | collective-permute-start | bytes 1179656 | tf_op jit(solution)/shard_map/ppermute | solution.py:1131
  332.7 22.7 %collective-permute-start.66 = (bf16[512,384]{1,0:T(8,128)(2,1)}, bf16[512,384]{1,0:T(8,128)(2,1)S(1)}, u32[]{:S(2)}, u32[]{:S(2)}) collective-permute-start(bf16[512,384]{1,0:T(8,128)(2,1)} %get-tuple-element.1133), channel_id=1, source_target_pairs={{0,2},{2,0},{1,3},{3,1},{4,6},{6,4},{5,7},{7,5},{8,10},{10,8},{9,1... | collective-permute-start | bytes 1179656 | tf_op jit(solution)/shard_map/ppermute | solution.py:1132
  334.3 21.2 %collective-permute-start.67 = (bf16[512,384]{1,0:T(8,128)(2,1)}, bf16[512,384]{1,0:T(8,128)(2,1)}, u32[]{:S(2)}, u32[]{:S(2)}) collective-permute-start(bf16[512,384]{1,0:T(8,128)(2,1)} %get-tuple-element.1134), channel_id=1, source_target_pairs={{0,3},{1,2},{2,1},{3,0},{4,7},{5,6},{6,5},{7,4},{8,11},{9,10},{10,... | collective-permute-start | bytes 1179656 | tf_op jit(solution)/shard_map/ppermute | solution.py:1133
  361.1 25.7 %collective-permute-start.74 = (bf16[128,4096]{1,0:T(8,128)(2,1)}, bf16[128,4096]{1,0:T(8,128)(2,1)S(1)}, u32[]{:S(2)}, u32[]{:S(2)}) collective-permute-start(bf16[128,4096]{1,0:T(8,128)(2,1)} %fusion.1), channel_id=1, source_target_pairs={{0,8},{8,16},{16,24},{24,0},{1,9},{9,17},{17,25},{25,1},{2,10},{10... | collective-permute-start | bytes 3145736 | tf_op jit(solution)/shard_map/ppermute | solution.py:946
  361.1 25.7 %collective-permute-start.73 = (bf16[1,128,4096]{2,1,0:T(8,128)(2,1)S(1)}, bf16[1,128,4096]{2,1,0:T(8,128)(2,1)S(1)}, u32[]{:S(2)}, u32[]{:S(2)}) collective-permute-start(bf16[1,128,4096]{2,1,0:T(8,128)(2,1)S(1)} %get-tuple-element.1144), channel_id=1, source_target_pairs={{0,4},{4,0},{1,5},{5,1},{2,6},{6,2},{3,7},{7,3},{8,12},{12,8},{9,1... | collective-permute-start | bytes 3145736 | tf_op jit(solution)/shard_map/ppermute | solution.py:934
  363.3 18.4 %collective-permute-start.72 = (bf16[512,384]{1,0:T(8,128)(2,1)}, bf16[512,384]{1,0:T(8,128)(2,1)}, u32[]{:S(2)}, u32[]{:S(2)}) collective-permute-start(bf16[512,384]{1,0:T(8,128)(2,1)} %get-tuple-element.1157), channel_id=1, source_target_pairs={{0,3},{1,2},{2,1},{3,0},{4,7},{5,6},{6,5},{7,4},{8,11},{9,10},{10,... | collective-permute-start | bytes 1179656 | tf_op jit(solution)/shard_map/ppermute | solution.py:1133
  393.2 25.3 %collective-permute-start.78 = (bf16[128,4096]{1,0:T(8,128)(2,1)S(1)}, bf16[128,4096]{1,0:T(8,128)(2,1)S(1)}, u32[]{:S(2)}, u32[]{:S(2)}) collective-permute-start(bf16[128,4096]{1,0:T(8,128)(2,1)S(1)} %fusion), channel_id=1, source_target_pairs={{0,2},{2,0},{1,3},{3,1},{4,6},{6,4},{5,7},{7,5},{8,10},{10,8},{9,1... | collective-permute-start | bytes 3145736 | tf_op jit(solution)/shard_map/ppermute | solution.py:968
  394.9 19.4 %collective-permute-start.77 = (bf16[4,128,768]{2,1,0:T(8,128)(2,1)S(1)}, bf16[4,128,768]{2,1,0:T(8,128)(2,1)S(1)}, u32[]{:S(2)}, u32[]{:S(2)}) collective-permute-start(bf16[4,128,768]{2,1,0:T(8,128)(2,1)S(1)} %add_convert_fusion.7), channel_id=1, source_target_pairs={{0,4},{4,0},{1,5},{5,1},{2,6},{6,2},{3,7},{7,3},{8,12},{12,8},{9,1... | collective-permute-start | bytes 2359304 | tf_op jit(solution)/shard_map/ppermute | solution.py:934
  425.7 23.3 %collective-permute-start.87 = (bf16[4,128,512]{2,1,0:T(8,128)(2,1)}, bf16[4,128,512]{2,1,0:T(8,128)(2,1)}, u32[]{:S(2)}, u32[]{:S(2)}) collective-permute-start(bf16[4,128,512]{2,1,0:T(8,128)(2,1)} %add_convert_fusion.8), channel_id=1, source_target_pairs={{0,4},{4,0},{1,5},{5,1},{2,6},{6,2},{3,7},{7,3},{8,12},{12,8},{9,1... | collective-permute-start | bytes 1572872 | tf_op jit(solution)/shard_map/ppermute | solution.py:934
  429.6 19.5 %collective-permute-start.84 = (bf16[128,768]{1,0:T(8,128)(2,1)}, bf16[128,768]{1,0:T(8,128)(2,1)}, u32[]{:S(2)}, u32[]{:S(2)}) collective-permute-start(bf16[128,768]{1,0:T(8,128)(2,1)} %get-tuple-element.1323), channel_id=1, source_target_pairs={{0,24},{8,0},{16,8},{24,16},{1,25},{9,1},{17,9},{25,17},{2,26},{10... | collective-permute-start | bytes 589832 | tf_op jit(solution)/shard_map/ppermute | solution.py:955
  431.1 17.9 %collective-permute-start.85 = (bf16[128,768]{1,0:T(8,128)(2,1)S(1)}, bf16[128,768]{1,0:T(8,128)(2,1)}, u32[]{:S(2)}, u32[]{:S(2)}) collective-permute-start(bf16[128,768]{1,0:T(8,128)(2,1)S(1)} %get-tuple-element.1322), channel_id=1, source_target_pairs={{0,16},{8,24},{16,0},{24,8},{1,17},{9,25},{17,1},{25,9},{2,18},{10... | collective-permute-start | bytes 589832 | tf_op jit(solution)/shard_map/ppermute | solution.py:955
  431.1 17.9 %collective-permute-start.86 = (bf16[128,768]{1,0:T(8,128)(2,1)S(1)}, bf16[128,768]{1,0:T(8,128)(2,1)}, u32[]{:S(2)}, u32[]{:S(2)}) collective-permute-start(bf16[128,768]{1,0:T(8,128)(2,1)S(1)} %get-tuple-element.1321), channel_id=1, source_target_pairs={{0,8},{8,16},{16,24},{24,0},{1,9},{9,17},{17,25},{25,1},{2,10},{10... | collective-permute-start | bytes 589832 | tf_op jit(solution)/shard_map/ppermute | solution.py:955
  433.6 23.3 %collective-permute-start.83 = (bf16[4,128,768]{2,1,0:T(8,128)(2,1)S(1)}, bf16[4,128,768]{2,1,0:T(8,128)(2,1)}, u32[]{:S(2)}, u32[]{:S(2)}) collective-permute-start(bf16[4,128,768]{2,1,0:T(8,128)(2,1)S(1)} %add_convert_fusion.6), channel_id=1, source_target_pairs={{0,4},{4,0},{1,5},{5,1},{2,6},{6,2},{3,7},{7,3},{8,12},{12,8},{9,1... | collective-permute-start | bytes 2359304 | tf_op jit(solution)/shard_map/ppermute | solution.py:934
  457.1 24.2 %collective-permute-start.92 = (bf16[128,4096]{1,0:T(8,128)(2,1)S(1)}, bf16[128,4096]{1,0:T(8,128)(2,1)S(1)}, u32[]{:S(2)}, u32[]{:S(2)}) collective-permute-start(bf16[128,4096]{1,0:T(8,128)(2,1)S(1)} %add_convert_fusion), channel_id=1, source_target_pairs={{0,1},{1,0},{2,3},{3,2},{4,5},{5,4},{6,7},{7,6},{8,9},{9,8},{10,11... | collective-permute-start | bytes 3145736 | tf_op jit(solution)/shard_map/ppermute | solution.py:974
  463.4 17.9 %collective-permute-start.89 = (bf16[128,768]{1,0:T(8,128)(2,1)S(1)}, bf16[128,768]{1,0:T(8,128)(2,1)S(1)}, u32[]{:S(2)}, u32[]{:S(2)}) collective-permute-start(bf16[128,768]{1,0:T(8,128)(2,1)S(1)} %get-tuple-element.1319), channel_id=1, source_target_pairs={{0,16},{8,24},{16,0},{24,8},{1,17},{9,25},{17,1},{25,9},{2,18},{10... | collective-permute-start | bytes 589832 | tf_op jit(solution)/shard_map/ppermute | solution.py:955
  463.4 17.8 %collective-permute-start.90 = (bf16[128,768]{1,0:T(8,128)(2,1)S(1)}, bf16[128,768]{1,0:T(8,128)(2,1)S(1)}, u32[]{:S(2)}, u32[]{:S(2)}) collective-permute-start(bf16[128,768]{1,0:T(8,128)(2,1)S(1)} %get-tuple-element.1318), channel_id=1, source_target_pairs={{0,8},{8,16},{16,24},{24,0},{1,9},{9,17},{17,25},{25,1},{2,10},{10... | collective-permute-start | bytes 589832 | tf_op jit(solution)/shard_map/ppermute | solution.py:955
  483.2 18.9 %collective-permute-start.97 = (bf16[128,768]{1,0:T(8,128)(2,1)S(1)}, bf16[128,768]{1,0:T(8,128)(2,1)S(1)}, u32[]{:S(2)}, u32[]{:S(2)}) collective-permute-start(bf16[128,768]{1,0:T(8,128)(2,1)S(1)} %add_convert_fusion.11), channel_id=1, source_target_pairs={{0,1},{1,0},{2,3},{3,2},{4,5},{5,4},{6,7},{7,6},{8,9},{9,8},{10,11... | collective-permute-start | bytes 589832 | tf_op jit(solution)/shard_map/ppermute | solution.py:974
  484.8 17.3 %collective-permute-start.96 = (bf16[128,768]{1,0:T(8,128)(2,1)S(1)}, bf16[128,768]{1,0:T(8,128)(2,1)S(1)}, u32[]{:S(2)}, u32[]{:S(2)}) collective-permute-start(bf16[128,768]{1,0:T(8,128)(2,1)S(1)} %fusion.8), channel_id=1, source_target_pairs={{0,2},{2,0},{1,3},{3,1},{4,6},{6,4},{5,7},{7,5},{8,10},{10,8},{9,1... | collective-permute-start | bytes 589832 | tf_op jit(solution)/shard_map/ppermute | solution.py:968
  (148 other events, 1713.1 us)

commit v4 on v3

--- a/solution.py
+++ b/solution.py
@@ -278,6 +278,13 @@
         self.others.append(self.box(lax.ppermute(block, "x", SWAP)))
         return self.others[-1]
 
+    def x_pair(self):
+        block = jnp.where(lax.axis_index("y") == 0, self.blocks[0].v, self.blocks[1].v)
+        self.others.append(self.box(lax.ppermute(block, "x", SWAP)))
+
+    def y_pair(self):
+        self.others.append(self.box(lax.ppermute(self.others[0].v, "y", SWAP)))
+
     def c(self):
         new = [b for b in self.blocks[1:] + self.others if id(b) not in self.swapped]
         for box, v in zip(new, self.stages.begin(*new)):
@@ -304,8 +311,14 @@
     return lax.rem(z + nz - step, nz) * 2 + (x if side == 0 else 1 - x)
 
 
+def paired_owner(index, nz, where):
+    y = where[3] // 2
+    step = y if index == 0 else 1 - y
+    return lax.rem(where[0] + nz - step, nz) * 2 + 1 - where[1]
+
+
 class Loader:
-    def __init__(self, where, pieces, dsts, sems, nz, col=0):
+    def __init__(self, where, pieces, dsts, sems, nz, col=0, paired=False):
         self.copies = []
         self.sems = sems
         if len(pieces[0].shape) == 2:
@@ -330,7 +343,10 @@
                     side = self.sides[k]
                     blocks = [(z * 2 + x, pieces[0].at[side, :, cols])]
                     for n in range(others):
-                        blocks.append((owner_of(n, nz, z, x), pieces[1 + k * others + n].at[:, cols]))
+                        owner = owner_of(n, nz, z, x)
+                        if paired and n in (0, 2):
+                            owner = paired_owner(n, nz, where)
+                        blocks.append((owner, pieces[1 + k * others + n].at[:, cols]))
                     for owner, block in blocks:
                         row = pl.multiple_of((owner * groups + g) * rows, rows)
                         self.add(i, k, block, dst.at[side, pl.ds(row, rows), :])
@@ -536,7 +552,7 @@
     rows, width = out_grad.shape
     ff = hidden.shape[1]
     blk = 512
-    load = Loader(where, pieces, (fc2_w,), load_sems, nz)
+    load = Loader(where, pieces, (fc2_w,), load_sems, nz, 0, True)
     out = Writer(out_sems)
     blocks = [slice(i * blk, (i + 1) * blk) for i in range(ff // blk)]
     ins = [
@@ -903,7 +919,7 @@
         self.stages, self.parts_x = stages, parts
         self.box = stages.box
         self.from_x, self.out = [], []
-        self.steps = 0
+        self.steps, self.ready, self.blocks_out = 0, False, []
 
     def set_first(self, outs):
         self.first = self.stages.boxes(outs)
@@ -942,14 +958,30 @@
         self.steps += 1
 
     def z(self):
-        self.add()
+        if not self.ready:
+            self.add()
+        self.ready = False
         self.passed = self.box(lax.ppermute(self.cur.v, "z", ring(lax.axis_size("z"))))
         return self.passed
 
+    def blocks(self):
+        crossed = self.from_x[0].v
+        return [
+            add_low(self.second[1].v[i], self.own_got.v[i], crossed[i])
+            for i in range(lax.axis_size("z"))
+        ]
+
+    def prepare(self, *others):
+        blocks = self.blocks()
+        if others:
+            blocks = [jnp.concatenate(b, axis=1) for b in zip(blocks, *[o.blocks() for o in others])]
+        self.blocks_out = self.stages.boxes(blocks)
+
     def direct(self):
         nz = lax.axis_size("z")
-        (crossed,) = self.stages.begin(self.from_x[0])
-        blocks = [add_low(self.second[1].v[i], self.own_got.v[i], crossed[i]) for i in range(nz)]
+        if not self.blocks_out:
+            self.prepare()
+        blocks = [b.v for b in self.blocks_out]
         self.kept = blocks[-1]
         self.parts = [
             self.box(lax.ppermute(blocks[i], "z", [(s, (s - 1 - i) % nz) for s in range(nz)]))
@@ -963,7 +995,7 @@
     def y(self):
         if hasattr(self, "parts"):
             self.gather_parts()
-        else:
+        elif not self.ready:
             self.add()
         self.from_y = self.box(lax.ppermute(self.cur.v, "y", SWAP))
         return self.from_y
@@ -1184,7 +1216,7 @@
                 qkv_in.z()
             else:
                 up_in.z()
-        st.sync()
+                up_in.x()
         qkv_pieces = qkv_in.pieces()
         vec, fc1_b = small_vectors(qkv_pieces, width, n_bias)
     else:
@@ -1224,14 +1256,10 @@
         for hop in some if rings else []:
             hop()
 
-    vec_box = st.box(vec)
-    st.sync()
-    vec = vec_box.v
     if not rings:
         up_in = down_in = Gather(st, qkv_cat)
-    got = st.boxes(project(0, tokens, vec_box.v))
+    got = st.boxes(project(0, tokens, vec))
     sent_a, normed_box = got[:n_seq], got[n_seq]
-    hops(up_in.x, up_in.z)
     st.sync()
     normed = normed_box.v
     heads_a = swap(sent_a)
@@ -1240,26 +1268,28 @@
     st.sync()
     heads_b = swap(sent_b)
     by_a = st.begin(*heads_a)
-    out_a, cols_a, lse_a = attn_fwd(where, by_a, heads, 1024)
+    out_a, cols_a, lse_a = attn_fwd(where, by_a, heads, 512)
     out_a = st.boxes(out_a)
-    hops(up_in.x, down_in.z)
+    hops(up_in.x, up_in.z)
     st.sync()
     att_a = swap(out_a)
     by_b = st.begin(*heads_b)
-    out_b, cols_b, lse_b = attn_fwd(where, by_b, heads, 1024)
+    out_b, cols_b, lse_b = attn_fwd(where, by_b, heads, 512)
     out_b = st.boxes(out_b)
     hops(up_in.x, down_in.z)
     st.sync()
     att_b = swap(out_b)
-    hops(down_in.x, down_in.x, down_in.z)
+    hops(*([down_in.x_pair, down_in.z] if rings else []))
     st.sync()
     if rings:
         ups = up_in.pieces()
-    hops(down_in.c, down_in.x, down_in.x)
+    hops(*([down_in.c, down_in.y_pair, down_in.x, down_in.z] if rings else []))
     arrived = st.begin(*att_a, *att_b)
     kept = run_up(where, [arrived[:n_seq], arrived[n_seq:]], tokens, vec, fc1_b, ups)
     attended, branch, residual, normed_two, hidden, active = kept
     active_box = st.box(active)
+    st.sync()
+    hops(down_in.x)
     st.sync()
     if rings:
         downs = down_in.pieces()
@@ -1269,6 +1299,10 @@
     )
 
     hidden_box = st.box(d_hidden)
+
+    def proj_grads():
+        outs = grads(row_grad_kernel, "proj_grad", where, (attended, d_branch), r, width // 2)
+        return reduction(outs, 1)
 
     def reduction(outs, parts):
         flow = Reduce(st, parts)
@@ -1302,9 +1336,8 @@
     d_branch = branch_box.v
     if rings:
         wide.sum(nz - 1)
-        proj = reduction(
-            grads(row_grad_kernel, "proj_grad", where, (attended, d_branch), r, width // 2), 1
-        )
+        wide.add()
+        wide.ready = True
     else:
         grad_proj = reduce_plain(attended, d_branch)
     st.sync()
@@ -1334,15 +1367,19 @@
 
     if rings:
         qkv_a = qkv_grads(d_mixed_a)
+        proj = proj_grads()
         st.sync()
-        hops(qkv_a.c)
+        hops(qkv_a.c, proj.c)
         st.sync()
-        hops(qkv_a.x, wide.y)
+        hops(qkv_a.x)
         qkv_b = qkv_grads(d_mixed_b)
         st.sync()
-        hops(qkv_b.c, proj.c)
+        hops(qkv_b.c)
+        qkv_a.prepare()
+        wide.add()
+        wide.ready = True
         st.sync()
-        hops(qkv_b.x, qkv_a.direct, proj.x)
+        hops(qkv_b.x, wide.y, qkv_a.direct)
     both = st.begin(*d_mixed_a, *d_mixed_b)
     d_mixed_a, d_mixed_b = both[:n_seq], both[n_seq:]
     tokens_grad, small_grads = last(
@@ -1351,22 +1388,24 @@
     if rings:
         vecs = SmallReduce(st, small_grads)
         st.sync()
-        hops(qkv_b.direct, qkv_a.y, wide.last_c)
+        hops(wide.last_c, qkv_b.direct, qkv_a.y, proj.x)
         st.sync()
         hops(vecs.seq, qkv_b.y, qkv_a.last_c, proj.direct)
+        low = wide.finish()
+        at = ff // 2
+        grad_fc1 = jnp.concatenate([half[:, :at] for half in low], axis=1).astype(F32)
+        grad_fc2 = jnp.stack([half[:, at:] for half in low]).reshape(2, r, groups, width // 2)
+        grad_fc2 = grad_fc2.transpose(2, 1, 0, 3).reshape(groups * r, width).astype(F32)
+        ffs = st.boxes((grad_fc1, grad_fc2))
         st.sync()
-        hops(qkv_b.last_c, vecs.x, proj.y)
+        grad_fc1, grad_fc2 = [b.v for b in ffs]
+        hops(vecs.x, qkv_b.last_c, proj.y)
         st.sync()
         hops(vecs.z, proj.last_c)
         total_small = vecs.finish()
     else:
         total_small = reduce_small(small_grads, fc1_sum, own)
     if rings:
-        low = wide.finish()
-        at = ff // 2
-        grad_fc1 = jnp.concatenate([half[:, :at] for half in low], axis=1).astype(F32)
-        grad_fc2 = jnp.stack([half[:, at:] for half in low]).reshape(2, r, groups, width // 2)
-        grad_fc2 = grad_fc2.transpose(2, 1, 0, 3).reshape(groups * r, width).astype(F32)
         grad_proj = jnp.concatenate(proj.finish(), axis=1).astype(F32)
         total_qkv = [jnp.concatenate(f.finish(), axis=1).astype(F32) for f in (qkv_a, qkv_b)]
     else:

time: 532 us -> 510 us (0.959)
  waiting for transfers between devices: 192 us -> 165 us
    ppermute x12 -> x10, waiting for transfers between devices: 57.4 us -> 45.4 us  [x(): self.others.append(self.box(lax.ppermute(block, 'x', SWAP)))]
    ppermute x7, waiting for transfers between devices: 26.9 us -> 18 us  [x(): lax.ppermute(self.out[len(self.from_x)].v, 'x', SWAP)]
    ppermute x9, waiting for transfers between devices: 26 us -> 19.9 us  [direct(): lax.ppermute(blocks[i], 'z', [(s, (s - 1 - i) % nz) for s in range(nz)])]
    pallas_call x2, Pallas kernels: 21.5 us -> 27.3 us  [attn_fwd(): pl.pallas_call(functools.partial(fwd_kernel, nh=nh, blk=blk, n=n), grid_s...]
    ppermute x12 -> x10, starting transfers between devices: 13.4 us -> 10.9 us  [x(): self.others.append(self.box(lax.ppermute(block, 'x', SWAP)))]
    unnamed x181 -> x193, local copies, waits for them, and re-layouts: 14.2 us -> 13 us
  transfers between devices with their start and end apart: 108 -> 108, of which waited for: 50 -> 42; matrix products, arithmetic and copies ran while one was open for 5% -> 7% of each run, Pallas kernels for 30% -> 32%
where the time goes in v4:
time: 510 us; the launch traced here: 500 us
  Pallas kernels  197 us (39%)
  waiting for transfers between devices  165 us (32%)
  starting transfers between devices  77.4 us (15%)
  other arithmetic  35.5 us (7%)
  local copies, waits for them, and re-layouts  22.8 us (4%)
    pallas_call x12, Pallas kernels, call(): pl.pallas_call(kernel, grid_spec=pltpu.PrefetchScalarGridSpec(num_scalar_...  128 us
    ppermute x10, waiting for transfers between devices, x(): self.others.append(self.box(lax.ppermute(block, 'x', SWAP)))  45.4 us
    pallas_call x2, Pallas kernels, attn_bwd(): pl.pallas_call(functools.partial(bwd_kernel, nh=nh, blk=blk, n=n), grid_s...  41.3 us
    convert_element_type x21, other arithmetic, add_low(): return sum((t.astype(F32) for t in terms)).astype(BF16)  28.6 us
    pallas_call x2, Pallas kernels, attn_fwd(): pl.pallas_call(functools.partial(fwd_kernel, nh=nh, blk=blk, n=n), grid_s...  27.3 us
    ppermute x9, waiting for transfers between devices, direct(): lax.ppermute(blocks[i], 'z', [(s, (s - 1 - i) % nz) for s in range(nz)])  19.9 us
    ppermute x9, waiting for transfers between devices, z(): lax.ppermute(block, 'z', ring(lax.axis_size('z')))  19.6 us
    ppermute x8, waiting for transfers between devices, exchange(): lax.ppermute(blocks[3], SEQ_AXES, both)  19.4 us
  transfers between devices with their start and end apart: 108, of which 42 were waited for; matrix products, arithmetic and copies ran while one was open for 7% of the time, Pallas kernels for 32%

profile of v4, /device:TPU:0, one launch (start us, length us, event | category | flops | bytes accessed | tf_op | source)
XLA Modules:
  0.0 500.5 jit_solution(511634866295775564)
XLA Ops:
  4.0 2.9 collective-permute-start
  17.1 3.4 collective-permute-done.1.refs_2_.refs_15_
  22.6 10.3 %collective-permute-done.4.refs_3_.refs_16_ = bf16[128,1664]{1,0:T(8,128)(2,1)S(1)} collective-permute-done((bf16[128,1664]{1,0:T(8,128)(2,1)}, bf16[128,1664]{1,0:T(8,128)(2,1)S(1)}, u32[]{:S(2)}, u32[]{:S(2)}) %collective-permute-start.4) | collective-permute-done | bytes 426016 | tf_op jit(solution)/shard_map/ppermute | solution.py:278
  37.4 10.0 %collective-permute-done.8.refs_5_.refs_18_ = bf16[128,1664]{1,0:T(8,128)(2,1)} collective-permute-done((bf16[128,1664]{1,0:T(8,128)(2,1)S(1)}, bf16[128,1664]{1,0:T(8,128)(2,1)}, u32[]{:S(2)}, u32[]{:S(2)}) %collective-permute-start.8) | collective-permute-done | bytes 426016 | tf_op jit(solution)/shard_map/ppermute | solution.py:278
  47.5 3.0 collective-permute-done.9.refs_6_.refs_19_
  51.5 9.9 %collective-permute-done.12.refs_7_.refs_20_ = bf16[128,1664]{1,0:T(8,128)(2,1)} collective-permute-done((bf16[128,1664]{1,0:T(8,128)(2,1)}, bf16[128,1664]{1,0:T(8,128)(2,1)}, u32[]{:S(2)}, u32[]{:S(2)}) %collective-permute-start.12) | collective-permute-done | bytes 426016 | tf_op jit(solution)/shard_map/ppermute | solution.py:278
  64.9 7.9 %qkv.2 = (bf16[512,384]{1,0:T(8,128)(2,1)}, bf16[512,384]{1,0:T(8,128)(2,1)}, bf16[512,384]{1,0:T(8,128)(2,1)}, bf16[512,384]{1,0:T(8,128)(2,1)}, bf16[512,1024]{1,0:T(8,128)(2,1)}) custom-call(s32[4]{0:T(128)} %pad_add_fusion.where, bf16[512,1024]{1,0:T(8,128)(2,1)} %refs_8_.3, f32[16,1024]{1,0:T(8,128)} %get-tuple-element.694.vec.refs_9_.refs_10_, ...), custom_call_target="tpu_custom_call" | custom-call | flops 7699999744 | bytes 1048576 | tf_op jit(solution)/shard_map/qkv/pallas_call | solution.py:209
  72.8 8.1 %collective-permute-done.13.refs_13_.refs_2_ = bf16[128,2560]{1,0:T(8,128)(2,1)S(1)} collective-permute-done((bf16[128,2560]{1,0:T(8,128)(2,1)S(1)}, bf16[128,2560]{1,0:T(8,128)(2,1)S(1)}, u32[]{:S(2)}, u32[]{:S(2)}) %collective-permute-start.13) | collective-permute-done | bytes 655392 | tf_op jit(solution)/shard_map/ppermute | solution.py:273
  83.5 7.0 %qkv.3 = (bf16[512,384]{1,0:T(8,128)(2,1)}, bf16[512,384]{1,0:T(8,128)(2,1)}, bf16[512,384]{1,0:T(8,128)(2,1)}, bf16[512,384]{1,0:T(8,128)(2,1)}) custom-call(s32[4]{0:T(128)} %pad_add_fusion.where, bf16[512,1024]{1,0:T(8,128)(2,1)} %get-tuple-element.723.first.normed, f32[16,1024]{1,0:T(8,128)} %get-tuple-element.694.vec.refs_9_.refs_10_, ...), custom_call_target="tpu_custom_call" | custom-call | flops 7699999744 | bytes 1048576 | tf_op jit(solution)/shard_map/qkv/pallas_call | solution.py:209
  90.4 3.3 collective-permute-done.17.refs_2_
  93.7 7.7 %collective-permute-done.18.refs_3_ = bf16[512,384]{1,0:T(8,128)(2,1)S(1)} collective-permute-done((bf16[512,384]{1,0:T(8,128)(2,1)}, bf16[512,384]{1,0:T(8,128)(2,1)S(1)}, u32[]{:S(2)}, u32[]{:S(2)}) %collective-permute-start.18) | collective-permute-done | bytes 393248 | tf_op jit(solution)/shard_map/ppermute | solution.py:1165
  104.8 13.6 %attn_fwd.2 = (bf16[512,128]{1,0:T(8,128)(2,1)S(1)}, bf16[512,128]{1,0:T(8,128)(2,1)S(1)}, bf16[512,128]{1,0:T(8,128)(2,1)S(1)}, bf16[512,128]{1,0:T(8,128)(2,1)...) custom-call(s32[4]{0:T(128)S(1)} %copy-done, bf16[512,384]{1,0:T(8,128)(2,1)S(1)} %copy-done.8, ...), custom_call_target="tpu_custom_call" | custom-call | flops 9900000256 | bytes 1048576 | tf_op jit(solution)/shard_map/attn_fwd/pallas_call | solution.py:96
  123.4 3.2 collective-permute-start.30
  128.5 13.6 %attn_fwd.3 = (bf16[512,128]{1,0:T(8,128)(2,1)S(1)}, bf16[512,128]{1,0:T(8,128)(2,1)S(1)}, bf16[512,128]{1,0:T(8,128)(2,1)S(1)}, bf16[512,128]{1,0:T(8,128)(2,1)...) custom-call(s32[4]{0:T(128)S(1)} %copy-done, bf16[512,384]{1,0:T(8,128)(2,1)S(1)} %copy-done.7, ...), custom_call_target="tpu_custom_call" | custom-call | flops 9900000256 | bytes 1048576 | tf_op jit(solution)/shard_map/attn_fwd/pallas_call | solution.py:96
  148.0 4.4 collective-permute-done.32.refs_6_
  156.7 3.0 collective-permute-done.35.refs_4_
  160.8 3.6 collective-permute-done.43.refs_9_
  169.8 16.8 %up.1 = (bf16[512,1024]{1,0:T(8,128)(2,1)}, f32[512,1024]{1,0:T(8,128)}, f32[512,1024]{1,0:T(8,128)}, bf16[512,1024]{1,0:T(8,128)(2,1)}, f32[512,4096]{1,0:T(8,128)}, /*index=5*/bf16[512,4096]{1,0:T(8,128)(2,1)}) custom-call(s32[4]{0:T(128)} %pad_add_fusion.where, bf16[512,128]{1,0:T(8,128)(2,1)} %copy-done.11, bf16[512,128]{1,0:T(8,128)(2,1)} %copy-done.79, ...), custom_call_target="tpu_custom_call" | custom-call | flops 22000001024 | bytes 1048576 | tf_op jit(solution)/shard_map/up/pallas_call | solution.py:209
  188.3 12.5 %collective-permute-done.49.refs_7_ = bf16[128,2048]{1,0:T(8,128)(2,1)S(1)} collective-permute-done((bf16[128,2048]{1,0:T(8,128)(2,1)S(1)}, bf16[128,2048]{1,0:T(8,128)(2,1)S(1)}, u32[]{:S(2)}, u32[]{:S(2)}) %collective-permute-start.49) | collective-permute-done | bytes 524320 | tf_op jit(solution)/shard_map/ppermute | solution.py:278
  205.8 25.8 %mid.1 = (bf16[512,1024]{1,0:T(8,128)(2,1)}, bf16[512,1024]{1,0:T(8,128)(2,1)}, bf16[512,4096]{1,0:T(8,128)(2,1)}, f32[16,1024]{1,0:T(8,128)}, f32[1,4096]{1,0:T(1,128)}) custom-call(s32[4]{0:T(128)} %pad_add_fusion.where, bf16[512,4096]{1,0:T(8,128)(2,1)} %get-tuple-element.1004.active_in.refs_2_, f32[512,1024]{1,0:T(8,128)} %get-tuple-element.1005.residual_in, ...), custom_call_target="tpu_custom_call" | custom-call | flops 30799998976 | bytes 1048576 | tf_op jit(solution)/shard_map/mid/pallas_call | solution.py:209
  231.6 9.4 %wide_grad.2 = (bf16[4,128,4096]{2,1,0:T(8,128)(2,1)}, bf16[4,128,4096]{2,1,0:T(8,128)(2,1)}) custom-call(s32[4]{0:T(128)} %pad_add_fusion.where, bf16[512,1024]{1,0:T(8,128)(2,1)} %get-tuple-element.1083.refs_0_, bf16[512,4096]{1,0:T(8,128)(2,1)} %get-tuple-element.1097.refs_1_.d_hidden_in, bf16[512,4096]{1,0:T(8,128)(2,1)} %get-tuple-element.1004.active_in.refs_2_, ...), custom_call_target="tpu_custom_call" | custom-call | flops 9900000256 | bytes 1048576 | tf_op jit(solution)/shard_map/wide_grad/pallas_call | solution.py:209
  241.2 9.6 %wide_grad.3 = (bf16[4,128,4096]{2,1,0:T(8,128)(2,1)}, bf16[4,128,4096]{2,1,0:T(8,128)(2,1)}) custom-call(s32[4]{0:T(128)} %pad_add_fusion.where, bf16[512,1024]{1,0:T(8,128)(2,1)} %get-tuple-element.1083.refs_0_, bf16[512,4096]{1,0:T(8,128)(2,1)} %get-tuple-element.1097.refs_1_.d_hidden_in, bf16[512,4096]{1,0:T(8,128)(2,1)} %get-tuple-element.1004.active_in.refs_2_, ...), custom_call_target="tpu_custom_call" | custom-call | flops 9900000256 | bytes 1048576 | tf_op jit(solution)/shard_map/wide_grad/pallas_call | solution.py:209
  254.6 18.7 %back.1 = (f32[512,1024]{1,0:T(8,128)}, bf16[512,1024]{1,0:T(8,128)(2,1)}, f32[16,1024]{1,0:T(8,128)}, bf16[512,128]{1,0:T(8,128)(2,1)}, bf16[512,128]{1,0:T(8,1...) custom-call(s32[4]{0:T(128)} %pad_add_fusion.where, ...), custom_call_target="tpu_custom_call" | custom-call | flops 22000001024 | bytes 1048576 | tf_op jit(solution)/shard_map/back/pallas_call | solution.py:209
  273.2 5.0 collective-permute-done.55
  280.2 4.2 add_convert_fusion.2
  284.4 2.7 fusion.3
  291.4 20.6 %attn_bwd.2 = (bf16[512,384]{1,0:T(8,128)(2,1)}, bf16[512,384]{1,0:T(8,128)(2,1)}, bf16[512,384]{1,0:T(8,128)(2,1)}, bf16[512,384]{1,0:T(8,128)(2,1)}) custom-call(s32[4]{0:T(128)} %pad_add_fusion.where, bf16[512,384]{1,0:T(8,128)(2,1)} %get-tuple-element.752.refs_0_, bf16[512,384]{1,0:T(8,128)(2,1)} %copy-done.4, bf16[512,384]{1,0:T(8,128)(2,1)} %copy-done.5, ...), custom_call_target="tpu_custom_call" | custom-call | flops 20899999744 | bytes 1048576 | tf_op jit(solution)/shard_map/attn_bwd/pallas_call | solution.py:163
  312.8 3.6 collective-permute-done.61
  316.4 3.5 fusion.2
  322.8 20.6 %attn_bwd.3 = (bf16[512,384]{1,0:T(8,128)(2,1)}, bf16[512,384]{1,0:T(8,128)(2,1)}, bf16[512,384]{1,0:T(8,128)(2,1)}, bf16[512,384]{1,0:T(8,128)(2,1)}) custom-call(s32[4]{0:T(128)} %pad_add_fusion.where, bf16[512,384]{1,0:T(8,128)(2,1)} %get-tuple-element.800.refs_0_, bf16[512,384]{1,0:T(8,128)(2,1)} %copy-done.1, bf16[512,384]{1,0:T(8,128)(2,1)} %copy-done.2, ...), custom_call_target="tpu_custom_call" | custom-call | flops 20899999744 | bytes 1048576 | tf_op jit(solution)/shard_map/attn_bwd/pallas_call | solution.py:163
  343.4 2.8 collective-permute-done.69
  346.2 3.2 fusion.1
  350.8 4.3 proj_grad.1
  357.0 6.3 %qkv_grad.2 = (bf16[4,128,768]{2,1,0:T(8,128)(2,1)}, bf16[4,128,768]{2,1,0:T(8,128)(2,1)}, bf16[4,128,768]{2,1,0:T(8,128)(2,1)}, bf16[4,128,768]{2,1,0:T(8,128)(2,1)}) custom-call(s32[4]{0:T(128)} %pad_add_fusion.where, bf16[512,1024]{1,0:T(8,128)(2,1)} %get-tuple-element.723.first.normed, bf16[512,384]{1,0:T(8,128)(2,1)} %get-tuple-element.1257.refs_0_, ...), custom_call_target="tpu_custom_call" | custom-call | flops 11000000512 | bytes 1048576 | tf_op jit(solution)/shard_map/qkv_grad/pallas_call | solution.py:209
  363.4 3.9 collective-permute-done.71.refs_2_.refs_6_
  367.3 7.8 %collective-permute-done.72.refs_3_.refs_7_ = bf16[512,384]{1,0:T(8,128)(2,1)} collective-permute-done((bf16[512,384]{1,0:T(8,128)(2,1)}, bf16[512,384]{1,0:T(8,128)(2,1)}, u32[]{:S(2)}, u32[]{:S(2)}) %collective-permute-start.72) | collective-permute-done | bytes 393248 | tf_op jit(solution)/shard_map/ppermute | solution.py:1165
  376.2 3.0 collective-permute-done.77
  384.6 6.3 %qkv_grad.3 = (bf16[4,128,768]{2,1,0:T(8,128)(2,1)}, bf16[4,128,768]{2,1,0:T(8,128)(2,1)}, bf16[4,128,768]{2,1,0:T(8,128)(2,1)}, bf16[4,128,768]{2,1,0:T(8,128)(2,1)}) custom-call(s32[4]{0:T(128)} %pad_add_fusion.where, bf16[512,1024]{1,0:T(8,128)(2,1)} %get-tuple-element.723.first.normed, bf16[512,384]{1,0:T(8,128)(2,1)} %get-tuple-element.1261.refs_0_.refs_4_, ...), custom_call_target="tpu_custom_call" | custom-call | flops 11000000512 | bytes 1048576 | tf_op jit(solution)/shard_map/qkv_grad/pallas_call | solution.py:209
  390.9 12.3 %collective-permute-done.79 = bf16[4,128,768]{2,1,0:T(8,128)(2,1)} collective-permute-done((bf16[4,128,768]{2,1,0:T(8,128)(2,1)}, bf16[4,128,768]{2,1,0:T(8,128)(2,1)}, u32[]{:S(2)}, u32[]{:S(2)}) %collective-permute-start.79) | collective-permute-done | bytes 786464 | tf_op jit(solution)/shard_map/ppermute | solution.py:950
  411.7 3.4 collective-permute-start.84
  415.7 14.1 %last.1 = (bf16[512,1024]{1,0:T(8,128)(2,1)}, f32[8,16,128]{2,1,0:T(8,128)}) custom-call(s32[4]{0:T(128)} %pad_add_fusion.where, bf16[512,384]{1,0:T(8,128)(2,1)} %get-tuple-element.1257.refs_0_, bf16[512,384]{1,0:T(8,128)(2,1)} %copy-done.75, bf16[512,384]{1,0:T(8,128)(2,1)} %copy-done.76, bf16[512,384]{1,0:T(8,128)(2,1)} %collective-permute-done.67.refs_3_, ...), custom_call_target="tpu_custom_call" | custom-call | flops 13200000000 | bytes 1048576 | tf_op jit(solution)/shard_map/last/pallas_call | solution.py:209
  432.3 3.2 collective-permute-done.83
  440.4 3.5 collective-permute-start.88
  446.0 3.1 collective-permute-done.88
  449.1 10.8 %collective-permute-done.89 = bf16[128,768]{1,0:T(8,128)(2,1)} collective-permute-done((bf16[128,768]{1,0:T(8,128)(2,1)S(1)}, bf16[128,768]{1,0:T(8,128)(2,1)}, u32[]{:S(2)}, u32[]{:S(2)}) %collective-permute-start.89) | collective-permute-done | bytes 196640 | tf_op jit(solution)/shard_map/ppermute | solution.py:987
  478.6 5.6 %collective-permute-done.99 = bf16[128,512]{1,0:T(8,128)(2,1)S(1)} collective-permute-done((bf16[128,512]{1,0:T(8,128)(2,1)S(1)}, bf16[128,512]{1,0:T(8,128)(2,1)S(1)}, u32[]{:S(2)}, u32[]{:S(2)}) %collective-permute-start.99) | collective-permute-done | bytes 131104 | tf_op jit(solution)/shard_map/ppermute | solution.py:987
  487.3 2.7 collective-permute-done.101
  490.2 2.6 collective-permute-start.104
  (441 shorter events, 131.2 us)
Async XLA Ops:
  62.0 18.9 %collective-permute-start.13 = (bf16[128,2560]{1,0:T(8,128)(2,1)S(1)}, bf16[128,2560]{1,0:T(8,128)(2,1)S(1)}, u32[]{:S(2)}, u32[]{:S(2)}) collective-permute-start(bf16[128,2560]{1,0:T(8,128)(2,1)S(1)} %fusion.5), channel_id=1, source_target_pairs={{0,8},{8,16},{16,24},{24,0},{1,9},{9,17},{17,25},{25,1},{2,10},{10... | collective-permute-start | bytes 1966088 | tf_op jit(solution)/shard_map/ppermute | solution.py:273
  62.0 18.9 %collective-permute-start.14 = (bf16[128,2560]{1,0:T(8,128)(2,1)S(1)}, bf16[128,2560]{1,0:T(8,128)(2,1)S(1)}, u32[]{:S(2)}, u32[]{:S(2)}) collective-permute-start(bf16[128,2560]{1,0:T(8,128)(2,1)S(1)} %fusion.5), channel_id=1, source_target_pairs={{0,4},{4,0},{1,5},{5,1},{2,6},{6,2},{3,7},{7,3},{8,12},{12,8},{9,1... | collective-permute-start | bytes 1966088 | tf_op jit(solution)/shard_map/ppermute | solution.py:278
  81.0 20.4 %collective-permute-start.19 = (bf16[128,2560]{1,0:T(8,128)(2,1)S(1)}, bf16[128,2560]{1,0:T(8,128)(2,1)S(1)}, u32[]{:S(2)}, u32[]{:S(2)}) collective-permute-start(bf16[128,2560]{1,0:T(8,128)(2,1)S(1)} %collective-permute-done.13.refs_13_.refs_2_), channel_id=1, source_target_pairs={{0,4},{4,0},{1,5},{5,1},{2,6},{6,2},{3,7},{7,3},{8,12},{12,8},{9,1... | collective-permute-start | bytes 1966088 | tf_op jit(solution)/shard_map/ppermute | solution.py:278
  81.6 19.8 %collective-permute-start.20 = (bf16[128,2560]{1,0:T(8,128)(2,1)S(1)}, bf16[128,2560]{1,0:T(8,128)(2,1)}, u32[]{:S(2)}, u32[]{:S(2)}) collective-permute-start(bf16[128,2560]{1,0:T(8,128)(2,1)S(1)} %collective-permute-done.13.refs_13_.refs_2_), channel_id=1, source_target_pairs={{0,8},{8,16},{16,24},{24,0},{1,9},{9,17},{17,25},{25,1},{2,10},{10... | collective-permute-start | bytes 1966088 | tf_op jit(solution)/shard_map/ppermute | solution.py:273
  83.1 18.3 %collective-permute-start.18 = (bf16[512,384]{1,0:T(8,128)(2,1)}, bf16[512,384]{1,0:T(8,128)(2,1)S(1)}, u32[]{:S(2)}, u32[]{:S(2)}) collective-permute-start(bf16[512,384]{1,0:T(8,128)(2,1)} %get-tuple-element.722), channel_id=1, source_target_pairs={{0,3},{1,2},{2,1},{3,0},{4,7},{5,6},{6,5},{7,4},{8,11},{9,10},{10,... | collective-permute-start | bytes 1179656 | tf_op jit(solution)/shard_map/ppermute | solution.py:1165
  101.4 21.3 %collective-permute-start.24 = (bf16[128,2560]{1,0:T(8,128)(2,1)}, bf16[128,2560]{1,0:T(8,128)(2,1)S(1)}, u32[]{:S(2)}, u32[]{:S(2)}) collective-permute-start(bf16[128,2560]{1,0:T(8,128)(2,1)} %collective-permute-done.20.refs_15_.refs_4_), channel_id=1, source_target_pairs={{0,4},{4,0},{1,5},{5,1},{2,6},{6,2},{3,7},{7,3},{8,12},{12,8},{9,1... | collective-permute-start | bytes 1966088 | tf_op jit(solution)/shard_map/ppermute | solution.py:278
  103.0 19.8 %collective-permute-start.25 = (bf16[128,2560]{1,0:T(8,128)(2,1)}, bf16[128,2560]{1,0:T(8,128)(2,1)S(1)}, u32[]{:S(2)}, u32[]{:S(2)}) collective-permute-start(bf16[128,2560]{1,0:T(8,128)(2,1)} %collective-permute-done.20.refs_15_.refs_4_), channel_id=1, source_target_pairs={{0,8},{8,16},{16,24},{24,0},{1,9},{9,17},{17,25},{25,1},{2,10},{10... | collective-permute-start | bytes 1966088 | tf_op jit(solution)/shard_map/ppermute | solution.py:273
  103.0 17.8 %collective-permute-start.21 = (bf16[512,384]{1,0:T(8,128)(2,1)}, bf16[512,384]{1,0:T(8,128)(2,1)S(1)}, u32[]{:S(2)}, u32[]{:S(2)}) collective-permute-start(bf16[512,384]{1,0:T(8,128)(2,1)} %get-tuple-element.757), channel_id=1, source_target_pairs={{0,1},{1,0},{2,3},{3,2},{4,5},{5,4},{6,7},{7,6},{8,9},{9,8},{10,11... | collective-permute-start | bytes 1179656 | tf_op jit(solution)/shard_map/ppermute | solution.py:1163
  103.0 17.8 %collective-permute-start.22 = (bf16[512,384]{1,0:T(8,128)(2,1)}, bf16[512,384]{1,0:T(8,128)(2,1)S(1)}, u32[]{:S(2)}, u32[]{:S(2)}) collective-permute-start(bf16[512,384]{1,0:T(8,128)(2,1)} %get-tuple-element.758), channel_id=1, source_target_pairs={{0,2},{2,0},{1,3},{3,1},{4,6},{6,4},{5,7},{7,5},{8,10},{10,8},{9,1... | collective-permute-start | bytes 1179656 | tf_op jit(solution)/shard_map/ppermute | solution.py:1164
  104.5 18.3 %collective-permute-start.23 = (bf16[512,384]{1,0:T(8,128)(2,1)}, bf16[512,384]{1,0:T(8,128)(2,1)S(1)}, u32[]{:S(2)}, u32[]{:S(2)}) collective-permute-start(bf16[512,384]{1,0:T(8,128)(2,1)} %get-tuple-element.759), channel_id=1, source_target_pairs={{0,3},{1,2},{2,1},{3,0},{4,7},{5,6},{6,5},{7,4},{8,11},{9,10},{10,... | collective-permute-start | bytes 1179656 | tf_op jit(solution)/shard_map/ppermute | solution.py:1165
  122.8 19.5 %collective-permute-start.29 = (bf16[128,2560]{1,0:T(8,128)(2,1)S(1)}, bf16[128,2560]{1,0:T(8,128)(2,1)S(1)}, u32[]{:S(2)}, u32[]{:S(2)}) collective-permute-start(bf16[128,2560]{1,0:T(8,128)(2,1)S(1)} %collective-permute-done.25.refs_17_.refs_6_), channel_id=1, source_target_pairs={{0,4},{4,0},{1,5},{5,1},{2,6},{6,2},{3,7},{7,3},{8,12},{12,8},{9,1... | collective-permute-start | bytes 1966088 | tf_op jit(solution)/shard_map/ppermute | solution.py:278
  123.4 18.9 %collective-permute-start.30 = (bf16[128,2048]{1,0:T(8,128)(2,1)S(1)}, bf16[128,2048]{1,0:T(8,128)(2,1)S(1)}, u32[]{:S(2)}, u32[]{:S(2)}) collective-permute-start(bf16[128,2048]{1,0:T(8,128)(2,1)S(1)} %copy-done.19), channel_id=1, source_target_pairs={{0,8},{8,16},{16,24},{24,0},{1,9},{9,17},{17,25},{25,1},{2,10},{10... | collective-permute-start | bytes 1572872 | tf_op jit(solution)/shard_map/ppermute | solution.py:273
  126.6 15.6 %collective-permute-start.26 = (bf16[512,128]{1,0:T(8,128)(2,1)S(1)}, bf16[512,128]{1,0:T(8,128)(2,1)S(1)}, u32[]{:S(2)}, u32[]{:S(2)}) collective-permute-start(bf16[512,128]{1,0:T(8,128)(2,1)S(1)} %get-tuple-element.805), channel_id=1, source_target_pairs={{0,1},{1,0},{2,3},{3,2},{4,5},{5,4},{6,7},{7,6},{8,9},{9,8},{10,11... | collective-permute-start | bytes 393224 | tf_op jit(solution)/shard_map/ppermute | solution.py:1163
  126.6 15.6 %collective-permute-start.27 = (bf16[512,128]{1,0:T(8,128)(2,1)S(1)}, bf16[512,128]{1,0:T(8,128)(2,1)S(1)}, u32[]{:S(2)}, u32[]{:S(2)}) collective-permute-start(bf16[512,128]{1,0:T(8,128)(2,1)S(1)} %get-tuple-element.806), channel_id=1, source_target_pairs={{0,2},{2,0},{1,3},{3,1},{4,6},{6,4},{5,7},{7,5},{8,10},{10,8},{9,1... | collective-permute-start | bytes 393224 | tf_op jit(solution)/shard_map/ppermute | solution.py:1164
  142.4 14.3 %collective-permute-start.34 = (bf16[128,2048]{1,0:T(8,128)(2,1)S(1)}, bf16[128,2048]{1,0:T(8,128)(2,1)}, u32[]{:S(2)}, u32[]{:S(2)}) collective-permute-start(bf16[128,2048]{1,0:T(8,128)(2,1)S(1)} %broadcast_select_fusion.2), channel_id=1, source_target_pairs={{0,4},{4,0},{1,5},{5,1},{2,6},{6,2},{3,7},{7,3},{8,12},{12,8},{9,1... | collective-permute-start | bytes 1572872 | tf_op jit(solution)/shard_map/ppermute | solution.py:283
  143.9 15.7 %collective-permute-start.35 = (bf16[128,2048]{1,0:T(8,128)(2,1)S(1)}, bf16[128,2048]{1,0:T(8,128)(2,1)}, u32[]{:S(2)}, u32[]{:S(2)}) collective-permute-start(bf16[128,2048]{1,0:T(8,128)(2,1)S(1)} %collective-permute-done.30.refs_2_), channel_id=1, source_target_pairs={{0,8},{8,16},{16,24},{24,0},{1,9},{9,17},{17,25},{25,1},{2,10},{10... | collective-permute-start | bytes 1572872 | tf_op jit(solution)/shard_map/ppermute | solution.py:273
  166.3 20.4 %collective-permute-start.45 = (bf16[128,2048]{1,0:T(8,128)(2,1)}, bf16[128,2048]{1,0:T(8,128)(2,1)S(1)}, u32[]{:S(2)}, u32[]{:S(2)}) collective-permute-start(bf16[128,2048]{1,0:T(8,128)(2,1)} %collective-permute-done.34.refs_1_), channel_id=1, source_target_pairs={{0,1},{1,0},{2,3},{3,2},{4,5},{5,4},{6,7},{7,6},{8,9},{9,8},{10,11... | collective-permute-start | bytes 1572872 | tf_op jit(solution)/shard_map/ppermute | solution.py:291
  166.8 19.9 %collective-permute-start.46 = (bf16[128,2048]{1,0:T(8,128)(2,1)}, bf16[128,2048]{1,0:T(8,128)(2,1)S(1)}, u32[]{:S(2)}, u32[]{:S(2)}) collective-permute-start(bf16[128,2048]{1,0:T(8,128)(2,1)} %collective-permute-done.34.refs_1_), channel_id=1, source_target_pairs={{0,2},{2,0},{1,3},{3,1},{4,6},{6,4},{5,7},{7,5},{8,10},{10,8},{9,1... | collective-permute-start | bytes 1572872 | tf_op jit(solution)/shard_map/ppermute | solution.py:286
  168.4 18.3 %collective-permute-start.44 = (bf16[128,2048]{1,0:T(8,128)(2,1)}, bf16[128,2048]{1,0:T(8,128)(2,1)S(1)}, u32[]{:S(2)}, u32[]{:S(2)}) collective-permute-start(bf16[128,2048]{1,0:T(8,128)(2,1)} %collective-permute-done.35.refs_4_), channel_id=1, source_target_pairs={{0,1},{1,0},{2,3},{3,2},{4,5},{5,4},{6,7},{7,6},{8,9},{9,8},{10,11... | collective-permute-start | bytes 1572872 | tf_op jit(solution)/shard_map/ppermute | solution.py:291
  168.4 18.3 %collective-permute-start.47 = (bf16[128,2048]{1,0:T(8,128)(2,1)}, bf16[128,2048]{1,0:T(8,128)(2,1)S(1)}, u32[]{:S(2)}, u32[]{:S(2)}) collective-permute-start(bf16[128,2048]{1,0:T(8,128)(2,1)} %collective-permute-done.35.refs_4_), channel_id=1, source_target_pairs={{0,4},{4,0},{1,5},{5,1},{2,6},{6,2},{3,7},{7,3},{8,12},{12,8},{9,1... | collective-permute-start | bytes 1572872 | tf_op jit(solution)/shard_map/ppermute | solution.py:278
  169.0 17.7 %collective-permute-start.48 = (bf16[128,2048]{1,0:T(8,128)(2,1)}, bf16[128,2048]{1,0:T(8,128)(2,1)S(1)}, u32[]{:S(2)}, u32[]{:S(2)}) collective-permute-start(bf16[128,2048]{1,0:T(8,128)(2,1)} %collective-permute-done.35.refs_4_), channel_id=1, source_target_pairs={{0,8},{8,16},{16,24},{24,0},{1,9},{9,17},{17,25},{25,1},{2,10},{10... | collective-permute-start | bytes 1572872 | tf_op jit(solution)/shard_map/ppermute | solution.py:273
  252.6 25.6 %collective-permute-start.56 = (bf16[4,128,4096]{2,1,0:T(8,128)(2,1)}, bf16[4,128,4096]{2,1,0:T(8,128)(2,1)}, u32[]{:S(2)}, u32[]{:S(2)}) collective-permute-start(bf16[4,128,4096]{2,1,0:T(8,128)(2,1)} %get-tuple-element.1100), channel_id=1, source_target_pairs={{0,1},{1,0},{2,3},{3,2},{4,5},{5,4},{6,7},{7,6},{8,9},{9,8},{10,11... | collective-permute-start | bytes 12582920 | tf_op jit(solution)/shard_map/ppermute | solution.py:934
  253.0 25.2 %collective-permute-start.55 = (bf16[1,128,4096]{2,1,0:T(8,128)(2,1)S(1)}, bf16[1,128,4096]{2,1,0:T(8,128)(2,1)S(1)}, u32[]{:S(2)}, u32[]{:S(2)}) collective-permute-start(bf16[1,128,4096]{2,1,0:T(8,128)(2,1)S(1)} %add_convert_fusion.5), channel_id=1, source_target_pairs={{0,4},{4,0},{1,5},{5,1},{2,6},{6,2},{3,7},{7,3},{8,12},{12,8},{9,1... | collective-permute-start | bytes 3145736 | tf_op jit(solution)/shard_map/ppermute | solution.py:950
  287.2 25.6 %collective-permute-start.60 = (bf16[1,128,4096]{2,1,0:T(8,128)(2,1)S(1)}, bf16[1,128,4096]{2,1,0:T(8,128)(2,1)}, u32[]{:S(2)}, u32[]{:S(2)}) collective-permute-start(bf16[1,128,4096]{2,1,0:T(8,128)(2,1)S(1)} %get-tuple-element.1137), channel_id=1, source_target_pairs={{0,4},{4,0},{1,5},{5,1},{2,6},{6,2},{3,7},{7,3},{8,12},{12,8},{9,1... | collective-permute-start | bytes 3145736 | tf_op jit(solution)/shard_map/ppermute | solution.py:950
  288.8 27.6 %collective-permute-start.61 = (bf16[128,4096]{1,0:T(8,128)(2,1)}, bf16[128,4096]{1,0:T(8,128)(2,1)}, u32[]{:S(2)}, u32[]{:S(2)}) collective-permute-start(bf16[128,4096]{1,0:T(8,128)(2,1)} %fusion.3), channel_id=1, source_target_pairs={{0,8},{8,16},{16,24},{24,0},{1,9},{9,17},{17,25},{25,1},{2,10},{10... | collective-permute-start | bytes 3145736 | tf_op jit(solution)/shard_map/ppermute | solution.py:964
  289.5 22.5 %collective-permute-start.62 = (bf16[512,128]{1,0:T(8,128)(2,1)S(1)}, bf16[512,128]{1,0:T(8,128)(2,1)S(1)}, u32[]{:S(2)}, u32[]{:S(2)}) collective-permute-start(bf16[512,128]{1,0:T(8,128)(2,1)S(1)} %copy-done.87), channel_id=1, source_target_pairs={{0,1},{1,0},{2,3},{3,2},{4,5},{5,4},{6,7},{7,6},{8,9},{9,8},{10,11... | collective-permute-start | bytes 393224 | tf_op jit(solution)/shard_map/ppermute | solution.py:1163
  289.5 22.5 %collective-permute-start.63 = (bf16[512,128]{1,0:T(8,128)(2,1)S(1)}, bf16[512,128]{1,0:T(8,128)(2,1)S(1)}, u32[]{:S(2)}, u32[]{:S(2)}) collective-permute-start(bf16[512,128]{1,0:T(8,128)(2,1)S(1)} %copy-done.86), channel_id=1, source_target_pairs={{0,2},{2,0},{1,3},{3,1},{4,6},{6,4},{5,7},{7,5},{8,10},{10,8},{9,1... | collective-permute-start | bytes 393224 | tf_op jit(solution)/shard_map/ppermute | solution.py:1164
  290.1 21.9 %collective-permute-start.64 = (bf16[512,128]{1,0:T(8,128)(2,1)S(1)}, bf16[512,128]{1,0:T(8,128)(2,1)S(1)}, u32[]{:S(2)}, u32[]{:S(2)}) collective-permute-start(bf16[512,128]{1,0:T(8,128)(2,1)S(1)} %copy-done.85), channel_id=1, source_target_pairs={{0,3},{1,2},{2,1},{3,0},{4,7},{5,6},{6,5},{7,4},{8,11},{9,10},{10,... | collective-permute-start | bytes 393224 | tf_op jit(solution)/shard_map/ppermute | solution.py:1165
  319.9 26.3 %collective-permute-start.69 = (bf16[128,4096]{1,0:T(8,128)(2,1)}, bf16[128,4096]{1,0:T(8,128)(2,1)S(1)}, u32[]{:S(2)}, u32[]{:S(2)}) collective-permute-start(bf16[128,4096]{1,0:T(8,128)(2,1)} %fusion.2), channel_id=1, source_target_pairs={{0,8},{8,16},{16,24},{24,0},{1,9},{9,17},{17,25},{25,1},{2,10},{10... | collective-permute-start | bytes 3145736 | tf_op jit(solution)/shard_map/ppermute | solution.py:964
  320.0 26.3 %collective-permute-start.68 = (bf16[1,128,4096]{2,1,0:T(8,128)(2,1)S(1)}, bf16[1,128,4096]{2,1,0:T(8,128)(2,1)}, u32[]{:S(2)}, u32[]{:S(2)}) collective-permute-start(bf16[1,128,4096]{2,1,0:T(8,128)(2,1)S(1)} %get-tuple-element.1150), channel_id=1, source_target_pairs={{0,4},{4,0},{1,5},{5,1},{2,6},{6,2},{3,7},{7,3},{8,12},{12,8},{9,1... | collective-permute-start | bytes 3145736 | tf_op jit(solution)/shard_map/ppermute | solution.py:950
  320.9 22.5 %collective-permute-start.65 = (bf16[512,384]{1,0:T(8,128)(2,1)}, bf16[512,384]{1,0:T(8,128)(2,1)S(1)}, u32[]{:S(2)}, u32[]{:S(2)}) collective-permute-start(bf16[512,384]{1,0:T(8,128)(2,1)} %get-tuple-element.1158), channel_id=1, source_target_pairs={{0,1},{1,0},{2,3},{3,2},{4,5},{5,4},{6,7},{7,6},{8,9},{9,8},{10,11... | collective-permute-start | bytes 1179656 | tf_op jit(solution)/shard_map/ppermute | solution.py:1163
  320.9 22.5 %collective-permute-start.66 = (bf16[512,384]{1,0:T(8,128)(2,1)}, bf16[512,384]{1,0:T(8,128)(2,1)S(1)}, u32[]{:S(2)}, u32[]{:S(2)}) collective-permute-start(bf16[512,384]{1,0:T(8,128)(2,1)} %get-tuple-element.1159), channel_id=1, source_target_pairs={{0,2},{2,0},{1,3},{3,1},{4,6},{6,4},{5,7},{7,5},{8,10},{10,8},{9,1... | collective-permute-start | bytes 1179656 | tf_op jit(solution)/shard_map/ppermute | solution.py:1164
  321.7 21.7 %collective-permute-start.67 = (bf16[512,384]{1,0:T(8,128)(2,1)}, bf16[512,384]{1,0:T(8,128)(2,1)}, u32[]{:S(2)}, u32[]{:S(2)}) collective-permute-start(bf16[512,384]{1,0:T(8,128)(2,1)} %get-tuple-element.1160), channel_id=1, source_target_pairs={{0,3},{1,2},{2,1},{3,0},{4,7},{5,6},{6,5},{7,4},{8,11},{9,10},{10,... | collective-permute-start | bytes 1179656 | tf_op jit(solution)/shard_map/ppermute | solution.py:1165
  349.4 25.7 %collective-permute-start.74 = (bf16[128,4096]{1,0:T(8,128)(2,1)}, bf16[128,4096]{1,0:T(8,128)(2,1)S(1)}, u32[]{:S(2)}, u32[]{:S(2)}) collective-permute-start(bf16[128,4096]{1,0:T(8,128)(2,1)} %fusion.1), channel_id=1, source_target_pairs={{0,8},{8,16},{16,24},{24,0},{1,9},{9,17},{17,25},{25,1},{2,10},{10... | collective-permute-start | bytes 3145736 | tf_op jit(solution)/shard_map/ppermute | solution.py:964
  349.6 25.5 %collective-permute-start.73 = (bf16[1,128,4096]{2,1,0:T(8,128)(2,1)S(1)}, bf16[1,128,4096]{2,1,0:T(8,128)(2,1)S(1)}, u32[]{:S(2)}, u32[]{:S(2)}) collective-permute-start(bf16[1,128,4096]{2,1,0:T(8,128)(2,1)S(1)} %get-tuple-element.1170), channel_id=1, source_target_pairs={{0,4},{4,0},{1,5},{5,1},{2,6},{6,2},{3,7},{7,3},{8,12},{12,8},{9,1... | collective-permute-start | bytes 3145736 | tf_op jit(solution)/shard_map/ppermute | solution.py:950
  356.1 18.9 %collective-permute-start.72 = (bf16[512,384]{1,0:T(8,128)(2,1)}, bf16[512,384]{1,0:T(8,128)(2,1)}, u32[]{:S(2)}, u32[]{:S(2)}) collective-permute-start(bf16[512,384]{1,0:T(8,128)(2,1)} %get-tuple-element.1179), channel_id=1, source_target_pairs={{0,3},{1,2},{2,1},{3,0},{4,7},{5,6},{6,5},{7,4},{8,11},{9,10},{10,... | collective-permute-start | bytes 1179656 | tf_op jit(solution)/shard_map/ppermute | solution.py:1165
  383.3 20.0 %collective-permute-start.79 = (bf16[4,128,768]{2,1,0:T(8,128)(2,1)}, bf16[4,128,768]{2,1,0:T(8,128)(2,1)}, u32[]{:S(2)}, u32[]{:S(2)}) collective-permute-start(bf16[4,128,768]{2,1,0:T(8,128)(2,1)} %add_convert_fusion.7), channel_id=1, source_target_pairs={{0,4},{4,0},{1,5},{5,1},{2,6},{6,2},{3,7},{7,3},{8,12},{12,8},{9,1... | collective-permute-start | bytes 2359304 | tf_op jit(solution)/shard_map/ppermute | solution.py:950
  409.4 22.0 %collective-permute-start.82 = (bf16[4,128,768]{2,1,0:T(8,128)(2,1)S(1)}, bf16[4,128,768]{2,1,0:T(8,128)(2,1)S(1)}, u32[]{:S(2)}, u32[]{:S(2)}) collective-permute-start(bf16[4,128,768]{2,1,0:T(8,128)(2,1)S(1)} %add_convert_fusion.6), channel_id=1, source_target_pairs={{0,4},{4,0},{1,5},{5,1},{2,6},{6,2},{3,7},{7,3},{8,12},{12,8},{9,1... | collective-permute-start | bytes 2359304 | tf_op jit(solution)/shard_map/ppermute | solution.py:950
  410.7 24.8 %collective-permute-start.83 = (bf16[128,4096]{1,0:T(8,128)(2,1)S(1)}, bf16[128,4096]{1,0:T(8,128)(2,1)S(1)}, u32[]{:S(2)}, u32[]{:S(2)}) collective-permute-start(bf16[128,4096]{1,0:T(8,128)(2,1)S(1)} %fusion), channel_id=1, source_target_pairs={{0,2},{2,0},{1,3},{3,1},{4,6},{6,4},{5,7},{7,5},{8,10},{10,8},{9,1... | collective-permute-start | bytes 3145736 | tf_op jit(solution)/shard_map/ppermute | solution.py:1000
  411.7 19.6 %collective-permute-start.84 = (bf16[128,768]{1,0:T(8,128)(2,1)}, bf16[128,768]{1,0:T(8,128)(2,1)}, u32[]{:S(2)}, u32[]{:S(2)}) collective-permute-start(bf16[128,768]{1,0:T(8,128)(2,1)} %get-tuple-element.1277), channel_id=1, source_target_pairs={{0,24},{8,0},{16,8},{24,16},{1,25},{9,1},{17,9},{25,17},{2,26},{10... | collective-permute-start | bytes 589832 | tf_op jit(solution)/shard_map/ppermute | solution.py:987
  415.1 16.2 %collective-permute-start.85 = (bf16[128,768]{1,0:T(8,128)(2,1)}, bf16[128,768]{1,0:T(8,128)(2,1)}, u32[]{:S(2)}, u32[]{:S(2)}) collective-permute-start(bf16[128,768]{1,0:T(8,128)(2,1)} %get-tuple-element.1278), channel_id=1, source_target_pairs={{0,16},{8,24},{16,0},{24,8},{1,17},{9,25},{17,1},{25,9},{2,18},{10... | collective-permute-start | bytes 589832 | tf_op jit(solution)/shard_map/ppermute | solution.py:987
  415.2 16.2 %collective-permute-start.86 = (bf16[128,768]{1,0:T(8,128)(2,1)S(1)}, bf16[128,768]{1,0:T(8,128)(2,1)}, u32[]{:S(2)}, u32[]{:S(2)}) collective-permute-start(bf16[128,768]{1,0:T(8,128)(2,1)S(1)} %get-tuple-element.1279), channel_id=1, source_target_pairs={{0,8},{8,16},{16,24},{24,0},{1,9},{9,17},{17,25},{25,1},{2,10},{10... | collective-permute-start | bytes 589832 | tf_op jit(solution)/shard_map/ppermute | solution.py:987
  435.7 24.2 %collective-permute-start.87 = (bf16[128,4096]{1,0:T(8,128)(2,1)S(1)}, bf16[128,4096]{1,0:T(8,128)(2,1)S(1)}, u32[]{:S(2)}, u32[]{:S(2)}) collective-permute-start(bf16[128,4096]{1,0:T(8,128)(2,1)S(1)} %add_convert_fusion), channel_id=1, source_target_pairs={{0,1},{1,0},{2,3},{3,2},{4,5},{5,4},{6,7},{7,6},{8,9},{9,8},{10,11... | collective-permute-start | bytes 3145736 | tf_op jit(solution)/shard_map/ppermute | solution.py:1006
  436.8 23.2 %collective-permute-start.92 = (bf16[4,128,512]{2,1,0:T(8,128)(2,1)}, bf16[4,128,512]{2,1,0:T(8,128)(2,1)}, u32[]{:S(2)}, u32[]{:S(2)}) collective-permute-start(bf16[4,128,512]{2,1,0:T(8,128)(2,1)} %add_convert_fusion.8), channel_id=1, source_target_pairs={{0,4},{4,0},{1,5},{5,1},{2,6},{6,2},{3,7},{7,3},{8,12},{12,8},{9,1... | collective-permute-start | bytes 1572872 | tf_op jit(solution)/shard_map/ppermute | solution.py:950
  443.9 16.1 %collective-permute-start.89 = (bf16[128,768]{1,0:T(8,128)(2,1)S(1)}, bf16[128,768]{1,0:T(8,128)(2,1)}, u32[]{:S(2)}, u32[]{:S(2)}) collective-permute-start(bf16[128,768]{1,0:T(8,128)(2,1)S(1)} %get-tuple-element.1350), channel_id=1, source_target_pairs={{0,16},{8,24},{16,0},{24,8},{1,17},{9,25},{17,1},{25,9},{2,18},{10... | collective-permute-start | bytes 589832 | tf_op jit(solution)/shard_map/ppermute | solution.py:987
  445.8 14.1 %collective-permute-start.90 = (bf16[128,768]{1,0:T(8,128)(2,1)S(1)}, bf16[128,768]{1,0:T(8,128)(2,1)}, u32[]{:S(2)}, u32[]{:S(2)}) collective-permute-start(bf16[128,768]{1,0:T(8,128)(2,1)S(1)} %get-tuple-element.1349), channel_id=1, source_target_pairs={{0,8},{8,16},{16,24},{24,0},{1,9},{9,17},{17,25},{25,1},{2,10},{10... | collective-permute-start | bytes 589832 | tf_op jit(solution)/shard_map/ppermute | solution.py:987
  462.0 22.2 %collective-permute-start.97 = (bf16[128,768]{1,0:T(8,128)(2,1)S(1)}, bf16[128,768]{1,0:T(8,128)(2,1)S(1)}, u32[]{:S(2)}, u32[]{:S(2)}) collective-permute-start(bf16[128,768]{1,0:T(8,128)(2,1)S(1)} %add_convert_fusion.11), channel_id=1, source_target_pairs={{0,1},{1,0},{2,3},{3,2},{4,5},{5,4},{6,7},{7,6},{8,9},{9,8},{10,11... | collective-permute-start | bytes 589832 | tf_op jit(solution)/shard_map/ppermute | solution.py:1006
  463.5 20.7 %collective-permute-start.96 = (bf16[128,768]{1,0:T(8,128)(2,1)S(1)}, bf16[128,768]{1,0:T(8,128)(2,1)S(1)}, u32[]{:S(2)}, u32[]{:S(2)}) collective-permute-start(bf16[128,768]{1,0:T(8,128)(2,1)S(1)} %add_convert_fusion.10), channel_id=1, source_target_pairs={{0,2},{2,0},{1,3},{3,1},{4,6},{6,4},{5,7},{7,5},{8,10},{10,8},{9,1... | collective-permute-start | bytes 589832 | tf_op jit(solution)/shard_map/ppermute | solution.py:1000
  (154 other events, 1693.9 us)

commit v5 on v4

--- a/solution.py
+++ b/solution.py
@@ -1373,13 +1373,6 @@
         st.sync()
         hops(qkv_a.x)
         qkv_b = qkv_grads(d_mixed_b)
-        st.sync()
-        hops(qkv_b.c)
-        qkv_a.prepare()
-        wide.add()
-        wide.ready = True
-        st.sync()
-        hops(qkv_b.x, wide.y, qkv_a.direct)
     both = st.begin(*d_mixed_a, *d_mixed_b)
     d_mixed_a, d_mixed_b = both[:n_seq], both[n_seq:]
     tokens_grad, small_grads = last(
@@ -1388,9 +1381,16 @@
     if rings:
         vecs = SmallReduce(st, small_grads)
         st.sync()
+        hops(qkv_b.c, vecs.seq)
+        qkv_a.prepare()
+        wide.add()
+        wide.ready = True
+        st.sync()
+        hops(qkv_b.x, wide.y, qkv_a.direct)
+        st.sync()
         hops(wide.last_c, qkv_b.direct, qkv_a.y, proj.x)
         st.sync()
-        hops(vecs.seq, qkv_b.y, qkv_a.last_c, proj.direct)
+        hops(qkv_b.y, qkv_a.last_c, proj.direct)
         low = wide.finish()
         at = ff // 2
         grad_fc1 = jnp.concatenate([half[:, :at] for half in low], axis=1).astype(F32)
@@ -1399,9 +1399,9 @@
         ffs = st.boxes((grad_fc1, grad_fc2))
         st.sync()
         grad_fc1, grad_fc2 = [b.v for b in ffs]
-        hops(vecs.x, qkv_b.last_c, proj.y)
+        hops(qkv_b.last_c, proj.y, vecs.x)
         st.sync()
-        hops(vecs.z, proj.last_c)
+        hops(proj.last_c, vecs.z)
         total_small = vecs.finish()
     else:
         total_small = reduce_small(small_grads, fc1_sum, own)

time: 510 us -> 502 us (0.984)
    ppermute x7, waiting for transfers between devices: 18 us -> 5.81 us  [x(): lax.ppermute(self.out[len(self.from_x)].v, 'x', SWAP)]
    ppermute x9, waiting for transfers between devices: 19.9 us -> 29.7 us  [direct(): lax.ppermute(blocks[i], 'z', [(s, (s - 1 - i) % nz) for s in range(nz)])]
    unnamed x193 -> x191, local copies, waits for them, and re-layouts: 13 us -> 12.4 us
  transfers between devices with their start and end apart: 108 -> 108, of which waited for: 42 -> 42; matrix products, arithmetic and copies ran while one was open for 7% -> 6% of each run, Pallas kernels for 32% -> 33%
where the time goes in v5:
time: 502 us; the launch traced here: 493 us
  Pallas kernels  197 us (39%)
  waiting for transfers between devices  163 us (32%)
  starting transfers between devices  76.6 us (15%)
  other arithmetic  31.8 us (6%)
  local copies, waits for them, and re-layouts  22.2 us (4%)
    pallas_call x12, Pallas kernels, call(): pl.pallas_call(kernel, grid_spec=pltpu.PrefetchScalarGridSpec(num_scalar_...  128 us
    ppermute x10, waiting for transfers between devices, x(): self.others.append(self.box(lax.ppermute(block, 'x', SWAP)))  45.4 us
    pallas_call x2, Pallas kernels, attn_bwd(): pl.pallas_call(functools.partial(bwd_kernel, nh=nh, blk=blk, n=n), grid_s...  41.2 us
    ppermute x9, waiting for transfers between devices, direct(): lax.ppermute(blocks[i], 'z', [(s, (s - 1 - i) % nz) for s in range(nz)])  29.7 us
    pallas_call x2, Pallas kernels, attn_fwd(): pl.pallas_call(functools.partial(fwd_kernel, nh=nh, blk=blk, n=n), grid_s...  27.3 us
    convert_element_type x21, other arithmetic, add_low(): return sum((t.astype(F32) for t in terms)).astype(BF16)  25.6 us
    ppermute x9, waiting for transfers between devices, z(): lax.ppermute(block, 'z', ring(lax.axis_size('z')))  19.6 us
    ppermute x8, waiting for transfers between devices, exchange(): lax.ppermute(blocks[3], SEQ_AXES, both)  19.3 us
  transfers between devices with their start and end apart: 108, of which 42 were waited for; matrix products, arithmetic and copies ran while one was open for 6% of the time, Pallas kernels for 33%

profile of v5, /device:TPU:0, one launch (start us, length us, event | category | flops | bytes accessed | tf_op | source)
XLA Modules:
  0.0 493.1 jit_solution(13517972391451929552)
XLA Ops:
  4.0 2.9 collective-permute-start
  17.1 3.4 collective-permute-done.1.refs_2_.refs_15_
  22.6 10.3 %collective-permute-done.4.refs_3_.refs_16_ = bf16[128,1664]{1,0:T(8,128)(2,1)S(1)} collective-permute-done((bf16[128,1664]{1,0:T(8,128)(2,1)}, bf16[128,1664]{1,0:T(8,128)(2,1)S(1)}, u32[]{:S(2)}, u32[]{:S(2)}) %collective-permute-start.4) | collective-permute-done | bytes 426016 | tf_op jit(solution)/shard_map/ppermute | solution.py:278
  37.4 10.0 %collective-permute-done.8.refs_5_.refs_18_ = bf16[128,1664]{1,0:T(8,128)(2,1)} collective-permute-done((bf16[128,1664]{1,0:T(8,128)(2,1)S(1)}, bf16[128,1664]{1,0:T(8,128)(2,1)}, u32[]{:S(2)}, u32[]{:S(2)}) %collective-permute-start.8) | collective-permute-done | bytes 426016 | tf_op jit(solution)/shard_map/ppermute | solution.py:278
  47.5 3.0 collective-permute-done.9.refs_6_.refs_19_
  51.5 9.9 %collective-permute-done.12.refs_7_.refs_20_ = bf16[128,1664]{1,0:T(8,128)(2,1)} collective-permute-done((bf16[128,1664]{1,0:T(8,128)(2,1)}, bf16[128,1664]{1,0:T(8,128)(2,1)}, u32[]{:S(2)}, u32[]{:S(2)}) %collective-permute-start.12) | collective-permute-done | bytes 426016 | tf_op jit(solution)/shard_map/ppermute | solution.py:278
  64.9 8.0 %qkv.2 = (bf16[512,384]{1,0:T(8,128)(2,1)}, bf16[512,384]{1,0:T(8,128)(2,1)}, bf16[512,384]{1,0:T(8,128)(2,1)}, bf16[512,384]{1,0:T(8,128)(2,1)}, bf16[512,1024]{1,0:T(8,128)(2,1)}) custom-call(s32[4]{0:T(128)} %pad_add_fusion.where, bf16[512,1024]{1,0:T(8,128)(2,1)} %refs_8_.3, f32[16,1024]{1,0:T(8,128)} %get-tuple-element.689.vec.refs_9_.refs_10_, ...), custom_call_target="tpu_custom_call" | custom-call | flops 7699999744 | bytes 1048576 | tf_op jit(solution)/shard_map/qkv/pallas_call | solution.py:209
  72.8 8.1 %collective-permute-done.13.refs_13_.refs_2_ = bf16[128,2560]{1,0:T(8,128)(2,1)S(1)} collective-permute-done((bf16[128,2560]{1,0:T(8,128)(2,1)S(1)}, bf16[128,2560]{1,0:T(8,128)(2,1)S(1)}, u32[]{:S(2)}, u32[]{:S(2)}) %collective-permute-start.13) | collective-permute-done | bytes 655392 | tf_op jit(solution)/shard_map/ppermute | solution.py:273
  83.5 6.9 %qkv.3 = (bf16[512,384]{1,0:T(8,128)(2,1)}, bf16[512,384]{1,0:T(8,128)(2,1)}, bf16[512,384]{1,0:T(8,128)(2,1)}, bf16[512,384]{1,0:T(8,128)(2,1)}) custom-call(s32[4]{0:T(128)} %pad_add_fusion.where, bf16[512,1024]{1,0:T(8,128)(2,1)} %get-tuple-element.718.first.normed, f32[16,1024]{1,0:T(8,128)} %get-tuple-element.689.vec.refs_9_.refs_10_, ...), custom_call_target="tpu_custom_call" | custom-call | flops 7699999744 | bytes 1048576 | tf_op jit(solution)/shard_map/qkv/pallas_call | solution.py:209
  90.4 3.3 collective-permute-done.17.refs_2_
  93.7 7.7 %collective-permute-done.18.refs_3_ = bf16[512,384]{1,0:T(8,128)(2,1)S(1)} collective-permute-done((bf16[512,384]{1,0:T(8,128)(2,1)}, bf16[512,384]{1,0:T(8,128)(2,1)S(1)}, u32[]{:S(2)}, u32[]{:S(2)}) %collective-permute-start.18) | collective-permute-done | bytes 393248 | tf_op jit(solution)/shard_map/ppermute | solution.py:1165
  104.8 13.6 %attn_fwd.2 = (bf16[512,128]{1,0:T(8,128)(2,1)S(1)}, bf16[512,128]{1,0:T(8,128)(2,1)S(1)}, bf16[512,128]{1,0:T(8,128)(2,1)S(1)}, bf16[512,128]{1,0:T(8,128)(2,1)...) custom-call(s32[4]{0:T(128)S(1)} %copy-done, bf16[512,384]{1,0:T(8,128)(2,1)S(1)} %copy-done.8, ...), custom_call_target="tpu_custom_call" | custom-call | flops 9900000256 | bytes 1048576 | tf_op jit(solution)/shard_map/attn_fwd/pallas_call | solution.py:96
  123.4 3.2 collective-permute-start.30
  128.5 13.6 %attn_fwd.3 = (bf16[512,128]{1,0:T(8,128)(2,1)S(1)}, bf16[512,128]{1,0:T(8,128)(2,1)S(1)}, bf16[512,128]{1,0:T(8,128)(2,1)S(1)}, bf16[512,128]{1,0:T(8,128)(2,1)...) custom-call(s32[4]{0:T(128)S(1)} %copy-done, bf16[512,384]{1,0:T(8,128)(2,1)S(1)} %copy-done.7, ...), custom_call_target="tpu_custom_call" | custom-call | flops 9900000256 | bytes 1048576 | tf_op jit(solution)/shard_map/attn_fwd/pallas_call | solution.py:96
  147.9 4.4 collective-permute-done.32.refs_6_
  156.6 3.0 collective-permute-done.35.refs_4_
  160.8 3.6 collective-permute-done.43.refs_9_
  169.7 16.7 %up.1 = (bf16[512,1024]{1,0:T(8,128)(2,1)}, f32[512,1024]{1,0:T(8,128)}, f32[512,1024]{1,0:T(8,128)}, bf16[512,1024]{1,0:T(8,128)(2,1)}, f32[512,4096]{1,0:T(8,128)}, /*index=5*/bf16[512,4096]{1,0:T(8,128)(2,1)}) custom-call(s32[4]{0:T(128)} %pad_add_fusion.where, bf16[512,128]{1,0:T(8,128)(2,1)} %copy-done.11, bf16[512,128]{1,0:T(8,128)(2,1)} %copy-done.78, ...), custom_call_target="tpu_custom_call" | custom-call | flops 22000001024 | bytes 1048576 | tf_op jit(solution)/shard_map/up/pallas_call | solution.py:209
  188.1 12.5 %collective-permute-done.49.refs_7_ = bf16[128,2048]{1,0:T(8,128)(2,1)S(1)} collective-permute-done((bf16[128,2048]{1,0:T(8,128)(2,1)S(1)}, bf16[128,2048]{1,0:T(8,128)(2,1)S(1)}, u32[]{:S(2)}, u32[]{:S(2)}) %collective-permute-start.49) | collective-permute-done | bytes 524320 | tf_op jit(solution)/shard_map/ppermute | solution.py:278
  205.7 25.9 %mid.1 = (bf16[512,1024]{1,0:T(8,128)(2,1)}, bf16[512,1024]{1,0:T(8,128)(2,1)}, bf16[512,4096]{1,0:T(8,128)(2,1)}, f32[16,1024]{1,0:T(8,128)}, f32[1,4096]{1,0:T(1,128)}) custom-call(s32[4]{0:T(128)} %pad_add_fusion.where, bf16[512,4096]{1,0:T(8,128)(2,1)} %get-tuple-element.999.active_in.refs_2_, f32[512,1024]{1,0:T(8,128)} %get-tuple-element.1000.residual_in, ...), custom_call_target="tpu_custom_call" | custom-call | flops 30799998976 | bytes 1048576 | tf_op jit(solution)/shard_map/mid/pallas_call | solution.py:209
  231.6 9.4 %wide_grad.2 = (bf16[4,128,4096]{2,1,0:T(8,128)(2,1)}, bf16[4,128,4096]{2,1,0:T(8,128)(2,1)}) custom-call(s32[4]{0:T(128)} %pad_add_fusion.where, bf16[512,1024]{1,0:T(8,128)(2,1)} %get-tuple-element.1078.refs_0_, bf16[512,4096]{1,0:T(8,128)(2,1)} %get-tuple-element.1092.refs_1_.d_hidden_in, bf16[512,4096]{1,0:T(8,128)(2,1)} %get-tuple-element.999.active_in.refs_2_, ...), custom_call_target="tpu_custom_call" | custom-call | flops 9900000256 | bytes 1048576 | tf_op jit(solution)/shard_map/wide_grad/pallas_call | solution.py:209
  241.3 9.6 %wide_grad.3 = (bf16[4,128,4096]{2,1,0:T(8,128)(2,1)}, bf16[4,128,4096]{2,1,0:T(8,128)(2,1)}) custom-call(s32[4]{0:T(128)} %pad_add_fusion.where, bf16[512,1024]{1,0:T(8,128)(2,1)} %get-tuple-element.1078.refs_0_, bf16[512,4096]{1,0:T(8,128)(2,1)} %get-tuple-element.1092.refs_1_.d_hidden_in, bf16[512,4096]{1,0:T(8,128)(2,1)} %get-tuple-element.999.active_in.refs_2_, ...), custom_call_target="tpu_custom_call" | custom-call | flops 9900000256 | bytes 1048576 | tf_op jit(solution)/shard_map/wide_grad/pallas_call | solution.py:209
  254.6 18.7 %back.1 = (f32[512,1024]{1,0:T(8,128)}, bf16[512,1024]{1,0:T(8,128)(2,1)}, f32[16,1024]{1,0:T(8,128)}, bf16[512,128]{1,0:T(8,128)(2,1)}, bf16[512,128]{1,0:T(8,1...) custom-call(s32[4]{0:T(128)} %pad_add_fusion.where, ...), custom_call_target="tpu_custom_call" | custom-call | flops 22000001024 | bytes 1048576 | tf_op jit(solution)/shard_map/back/pallas_call | solution.py:209
  273.2 5.1 %collective-permute-done.55 = bf16[1,128,4096]{2,1,0:T(8,128)(2,1)S(1)} collective-permute-done((bf16[1,128,4096]{2,1,0:T(8,128)(2,1)S(1)}, bf16[1,128,4096]{2,1,0:T(8,128)(2,1)S(1)}, u32[]{:S(2)}, u32[]{:S(2)}) %collective-permute-start.55) | collective-permute-done | bytes 1048608 | tf_op jit(solution)/shard_map/ppermute | solution.py:950
  280.3 4.2 add_convert_fusion.2
  284.5 2.7 fusion.3
  291.5 20.6 %attn_bwd.2 = (bf16[512,384]{1,0:T(8,128)(2,1)}, bf16[512,384]{1,0:T(8,128)(2,1)}, bf16[512,384]{1,0:T(8,128)(2,1)}, bf16[512,384]{1,0:T(8,128)(2,1)}) custom-call(s32[4]{0:T(128)} %pad_add_fusion.where, bf16[512,384]{1,0:T(8,128)(2,1)} %get-tuple-element.747.refs_0_, bf16[512,384]{1,0:T(8,128)(2,1)} %copy-done.4, bf16[512,384]{1,0:T(8,128)(2,1)} %copy-done.5, ...), custom_call_target="tpu_custom_call" | custom-call | flops 20899999744 | bytes 1048576 | tf_op jit(solution)/shard_map/attn_bwd/pallas_call | solution.py:163
  312.9 3.6 collective-permute-done.61
  316.5 3.5 fusion.2
  322.9 20.6 %attn_bwd.3 = (bf16[512,384]{1,0:T(8,128)(2,1)}, bf16[512,384]{1,0:T(8,128)(2,1)}, bf16[512,384]{1,0:T(8,128)(2,1)}, bf16[512,384]{1,0:T(8,128)(2,1)}) custom-call(s32[4]{0:T(128)} %pad_add_fusion.where, bf16[512,384]{1,0:T(8,128)(2,1)} %get-tuple-element.795.refs_0_, bf16[512,384]{1,0:T(8,128)(2,1)} %copy-done.1, bf16[512,384]{1,0:T(8,128)(2,1)} %copy-done.2, ...), custom_call_target="tpu_custom_call" | custom-call | flops 20899999744 | bytes 1048576 | tf_op jit(solution)/shard_map/attn_bwd/pallas_call | solution.py:163
  343.5 2.8 collective-permute-done.69
  346.3 3.2 fusion.1
  350.9 4.4 proj_grad.1
  357.2 6.3 %qkv_grad.2 = (bf16[4,128,768]{2,1,0:T(8,128)(2,1)}, bf16[4,128,768]{2,1,0:T(8,128)(2,1)}, bf16[4,128,768]{2,1,0:T(8,128)(2,1)}, bf16[4,128,768]{2,1,0:T(8,128)(2,1)}) custom-call(s32[4]{0:T(128)} %pad_add_fusion.where, bf16[512,1024]{1,0:T(8,128)(2,1)} %get-tuple-element.718.first.normed, bf16[512,384]{1,0:T(8,128)(2,1)} %get-tuple-element.1205.refs_0_, ...), custom_call_target="tpu_custom_call" | custom-call | flops 11000000512 | bytes 1048576 | tf_op jit(solution)/shard_map/qkv_grad/pallas_call | solution.py:209
  363.5 4.1 collective-permute-done.71.refs_6_.refs_2_
  367.5 7.6 %collective-permute-done.72.refs_7_.refs_3_ = bf16[512,384]{1,0:T(8,128)(2,1)} collective-permute-done((bf16[512,384]{1,0:T(8,128)(2,1)}, bf16[512,384]{1,0:T(8,128)(2,1)}, u32[]{:S(2)}, u32[]{:S(2)}) %collective-permute-start.72) | collective-permute-done | bytes 393248 | tf_op jit(solution)/shard_map/ppermute | solution.py:1165
  376.2 4.1 collective-permute-done.77
  384.9 14.1 %last.1 = (bf16[512,1024]{1,0:T(8,128)(2,1)}, f32[8,16,128]{2,1,0:T(8,128)}) custom-call(s32[4]{0:T(128)} %pad_add_fusion.where, bf16[512,384]{1,0:T(8,128)(2,1)} %get-tuple-element.1205.refs_0_, bf16[512,384]{1,0:T(8,128)(2,1)} %copy-done.75, bf16[512,384]{1,0:T(8,128)(2,1)} %copy-done.76, bf16[512,384]{1,0:T(8,128)(2,1)} %collective-permute-done.67.refs_3_, ...), custom_call_target="tpu_custom_call" | custom-call | flops 13200000000 | bytes 1048576 | tf_op jit(solution)/shard_map/last/pallas_call | solution.py:209
  399.8 6.3 %qkv_grad.3 = (bf16[4,128,768]{2,1,0:T(8,128)(2,1)}, bf16[4,128,768]{2,1,0:T(8,128)(2,1)}, bf16[4,128,768]{2,1,0:T(8,128)(2,1)}, bf16[4,128,768]{2,1,0:T(8,128)(2,1)}) custom-call(s32[4]{0:T(128)} %pad_add_fusion.where, bf16[512,1024]{1,0:T(8,128)(2,1)} %get-tuple-element.718.first.normed, bf16[512,384]{1,0:T(8,128)(2,1)} %get-tuple-element.1209.refs_4_.refs_0_, ...), custom_call_target="tpu_custom_call" | custom-call | flops 11000000512 | bytes 1048576 | tf_op jit(solution)/shard_map/qkv_grad/pallas_call | solution.py:209
  414.1 3.1 collective-permute-start.87
  417.7 4.8 collective-permute-done.87
  422.5 10.5 %collective-permute-done.88 = bf16[128,768]{1,0:T(8,128)(2,1)S(1)} collective-permute-done((bf16[128,768]{1,0:T(8,128)(2,1)S(1)}, bf16[128,768]{1,0:T(8,128)(2,1)S(1)}, u32[]{:S(2)}, u32[]{:S(2)}) %collective-permute-start.88) | collective-permute-done | bytes 196640 | tf_op jit(solution)/shard_map/ppermute | solution.py:987
  433.1 4.1 collective-permute-done.86
  440.9 3.1 collective-permute-start.91
  446.2 3.4 collective-permute-done.91
  449.6 10.7 %collective-permute-done.92 = bf16[128,768]{1,0:T(8,128)(2,1)} collective-permute-done((bf16[128,768]{1,0:T(8,128)(2,1)S(1)}, bf16[128,768]{1,0:T(8,128)(2,1)}, u32[]{:S(2)}, u32[]{:S(2)}) %collective-permute-start.92) | collective-permute-done | bytes 196640 | tf_op jit(solution)/shard_map/ppermute | solution.py:987
  463.9 2.9 collective-permute-start.98
  480.2 2.9 collective-permute-done.103
  (439 shorter events, 124.2 us)
Async XLA Ops:
  62.0 18.9 %collective-permute-start.13 = (bf16[128,2560]{1,0:T(8,128)(2,1)S(1)}, bf16[128,2560]{1,0:T(8,128)(2,1)S(1)}, u32[]{:S(2)}, u32[]{:S(2)}) collective-permute-start(bf16[128,2560]{1,0:T(8,128)(2,1)S(1)} %fusion.5), channel_id=1, source_target_pairs={{0,8},{8,16},{16,24},{24,0},{1,9},{9,17},{17,25},{25,1},{2,10},{10... | collective-permute-start | bytes 1966088 | tf_op jit(solution)/shard_map/ppermute | solution.py:273
  62.0 18.9 %collective-permute-start.14 = (bf16[128,2560]{1,0:T(8,128)(2,1)S(1)}, bf16[128,2560]{1,0:T(8,128)(2,1)S(1)}, u32[]{:S(2)}, u32[]{:S(2)}) collective-permute-start(bf16[128,2560]{1,0:T(8,128)(2,1)S(1)} %fusion.5), channel_id=1, source_target_pairs={{0,4},{4,0},{1,5},{5,1},{2,6},{6,2},{3,7},{7,3},{8,12},{12,8},{9,1... | collective-permute-start | bytes 1966088 | tf_op jit(solution)/shard_map/ppermute | solution.py:278
  81.0 20.4 %collective-permute-start.19 = (bf16[128,2560]{1,0:T(8,128)(2,1)S(1)}, bf16[128,2560]{1,0:T(8,128)(2,1)}, u32[]{:S(2)}, u32[]{:S(2)}) collective-permute-start(bf16[128,2560]{1,0:T(8,128)(2,1)S(1)} %collective-permute-done.13.refs_13_.refs_2_), channel_id=1, source_target_pairs={{0,4},{4,0},{1,5},{5,1},{2,6},{6,2},{3,7},{7,3},{8,12},{12,8},{9,1... | collective-permute-start | bytes 1966088 | tf_op jit(solution)/shard_map/ppermute | solution.py:278
  81.6 19.8 %collective-permute-start.20 = (bf16[128,2560]{1,0:T(8,128)(2,1)S(1)}, bf16[128,2560]{1,0:T(8,128)(2,1)}, u32[]{:S(2)}, u32[]{:S(2)}) collective-permute-start(bf16[128,2560]{1,0:T(8,128)(2,1)S(1)} %collective-permute-done.13.refs_13_.refs_2_), channel_id=1, source_target_pairs={{0,8},{8,16},{16,24},{24,0},{1,9},{9,17},{17,25},{25,1},{2,10},{10... | collective-permute-start | bytes 1966088 | tf_op jit(solution)/shard_map/ppermute | solution.py:273
  83.1 18.3 %collective-permute-start.18 = (bf16[512,384]{1,0:T(8,128)(2,1)}, bf16[512,384]{1,0:T(8,128)(2,1)S(1)}, u32[]{:S(2)}, u32[]{:S(2)}) collective-permute-start(bf16[512,384]{1,0:T(8,128)(2,1)} %get-tuple-element.717), channel_id=1, source_target_pairs={{0,3},{1,2},{2,1},{3,0},{4,7},{5,6},{6,5},{7,4},{8,11},{9,10},{10,... | collective-permute-start | bytes 1179656 | tf_op jit(solution)/shard_map/ppermute | solution.py:1165
  101.4 21.3 %collective-permute-start.24 = (bf16[128,2560]{1,0:T(8,128)(2,1)}, bf16[128,2560]{1,0:T(8,128)(2,1)S(1)}, u32[]{:S(2)}, u32[]{:S(2)}) collective-permute-start(bf16[128,2560]{1,0:T(8,128)(2,1)} %collective-permute-done.20.refs_15_.refs_4_), channel_id=1, source_target_pairs={{0,4},{4,0},{1,5},{5,1},{2,6},{6,2},{3,7},{7,3},{8,12},{12,8},{9,1... | collective-permute-start | bytes 1966088 | tf_op jit(solution)/shard_map/ppermute | solution.py:278
  103.0 19.8 %collective-permute-start.25 = (bf16[128,2560]{1,0:T(8,128)(2,1)}, bf16[128,2560]{1,0:T(8,128)(2,1)S(1)}, u32[]{:S(2)}, u32[]{:S(2)}) collective-permute-start(bf16[128,2560]{1,0:T(8,128)(2,1)} %collective-permute-done.20.refs_15_.refs_4_), channel_id=1, source_target_pairs={{0,8},{8,16},{16,24},{24,0},{1,9},{9,17},{17,25},{25,1},{2,10},{10... | collective-permute-start | bytes 1966088 | tf_op jit(solution)/shard_map/ppermute | solution.py:273
  103.0 17.8 %collective-permute-start.21 = (bf16[512,384]{1,0:T(8,128)(2,1)}, bf16[512,384]{1,0:T(8,128)(2,1)S(1)}, u32[]{:S(2)}, u32[]{:S(2)}) collective-permute-start(bf16[512,384]{1,0:T(8,128)(2,1)} %get-tuple-element.752), channel_id=1, source_target_pairs={{0,1},{1,0},{2,3},{3,2},{4,5},{5,4},{6,7},{7,6},{8,9},{9,8},{10,11... | collective-permute-start | bytes 1179656 | tf_op jit(solution)/shard_map/ppermute | solution.py:1163
  103.0 17.8 %collective-permute-start.22 = (bf16[512,384]{1,0:T(8,128)(2,1)}, bf16[512,384]{1,0:T(8,128)(2,1)S(1)}, u32[]{:S(2)}, u32[]{:S(2)}) collective-permute-start(bf16[512,384]{1,0:T(8,128)(2,1)} %get-tuple-element.753), channel_id=1, source_target_pairs={{0,2},{2,0},{1,3},{3,1},{4,6},{6,4},{5,7},{7,5},{8,10},{10,8},{9,1... | collective-permute-start | bytes 1179656 | tf_op jit(solution)/shard_map/ppermute | solution.py:1164
  104.5 18.3 %collective-permute-start.23 = (bf16[512,384]{1,0:T(8,128)(2,1)}, bf16[512,384]{1,0:T(8,128)(2,1)S(1)}, u32[]{:S(2)}, u32[]{:S(2)}) collective-permute-start(bf16[512,384]{1,0:T(8,128)(2,1)} %get-tuple-element.754), channel_id=1, source_target_pairs={{0,3},{1,2},{2,1},{3,0},{4,7},{5,6},{6,5},{7,4},{8,11},{9,10},{10,... | collective-permute-start | bytes 1179656 | tf_op jit(solution)/shard_map/ppermute | solution.py:1165
  122.8 19.5 %collective-permute-start.29 = (bf16[128,2560]{1,0:T(8,128)(2,1)S(1)}, bf16[128,2560]{1,0:T(8,128)(2,1)S(1)}, u32[]{:S(2)}, u32[]{:S(2)}) collective-permute-start(bf16[128,2560]{1,0:T(8,128)(2,1)S(1)} %collective-permute-done.25.refs_17_.refs_6_), channel_id=1, source_target_pairs={{0,4},{4,0},{1,5},{5,1},{2,6},{6,2},{3,7},{7,3},{8,12},{12,8},{9,1... | collective-permute-start | bytes 1966088 | tf_op jit(solution)/shard_map/ppermute | solution.py:278
  123.4 18.9 %collective-permute-start.30 = (bf16[128,2048]{1,0:T(8,128)(2,1)S(1)}, bf16[128,2048]{1,0:T(8,128)(2,1)S(1)}, u32[]{:S(2)}, u32[]{:S(2)}) collective-permute-start(bf16[128,2048]{1,0:T(8,128)(2,1)S(1)} %copy-done.19), channel_id=1, source_target_pairs={{0,8},{8,16},{16,24},{24,0},{1,9},{9,17},{17,25},{25,1},{2,10},{10... | collective-permute-start | bytes 1572872 | tf_op jit(solution)/shard_map/ppermute | solution.py:273
  126.6 15.6 %collective-permute-start.26 = (bf16[512,128]{1,0:T(8,128)(2,1)S(1)}, bf16[512,128]{1,0:T(8,128)(2,1)S(1)}, u32[]{:S(2)}, u32[]{:S(2)}) collective-permute-start(bf16[512,128]{1,0:T(8,128)(2,1)S(1)} %get-tuple-element.800), channel_id=1, source_target_pairs={{0,1},{1,0},{2,3},{3,2},{4,5},{5,4},{6,7},{7,6},{8,9},{9,8},{10,11... | collective-permute-start | bytes 393224 | tf_op jit(solution)/shard_map/ppermute | solution.py:1163
  126.6 15.6 %collective-permute-start.27 = (bf16[512,128]{1,0:T(8,128)(2,1)S(1)}, bf16[512,128]{1,0:T(8,128)(2,1)S(1)}, u32[]{:S(2)}, u32[]{:S(2)}) collective-permute-start(bf16[512,128]{1,0:T(8,128)(2,1)S(1)} %get-tuple-element.801), channel_id=1, source_target_pairs={{0,2},{2,0},{1,3},{3,1},{4,6},{6,4},{5,7},{7,5},{8,10},{10,8},{9,1... | collective-permute-start | bytes 393224 | tf_op jit(solution)/shard_map/ppermute | solution.py:1164
  128.1 14.1 %collective-permute-start.28 = (bf16[512,128]{1,0:T(8,128)(2,1)S(1)}, bf16[512,128]{1,0:T(8,128)(2,1)S(1)}, u32[]{:S(2)}, u32[]{:S(2)}) collective-permute-start(bf16[512,128]{1,0:T(8,128)(2,1)S(1)} %get-tuple-element.802), channel_id=1, source_target_pairs={{0,3},{1,2},{2,1},{3,0},{4,7},{5,6},{6,5},{7,4},{8,11},{9,10},{10,... | collective-permute-start | bytes 393224 | tf_op jit(solution)/shard_map/ppermute | solution.py:1165
  142.3 14.3 %collective-permute-start.34 = (bf16[128,2048]{1,0:T(8,128)(2,1)S(1)}, bf16[128,2048]{1,0:T(8,128)(2,1)}, u32[]{:S(2)}, u32[]{:S(2)}) collective-permute-start(bf16[128,2048]{1,0:T(8,128)(2,1)S(1)} %broadcast_select_fusion.2), channel_id=1, source_target_pairs={{0,4},{4,0},{1,5},{5,1},{2,6},{6,2},{3,7},{7,3},{8,12},{12,8},{9,1... | collective-permute-start | bytes 1572872 | tf_op jit(solution)/shard_map/ppermute | solution.py:283
  143.9 15.7 %collective-permute-start.35 = (bf16[128,2048]{1,0:T(8,128)(2,1)S(1)}, bf16[128,2048]{1,0:T(8,128)(2,1)}, u32[]{:S(2)}, u32[]{:S(2)}) collective-permute-start(bf16[128,2048]{1,0:T(8,128)(2,1)S(1)} %collective-permute-done.30.refs_2_), channel_id=1, source_target_pairs={{0,8},{8,16},{16,24},{24,0},{1,9},{9,17},{17,25},{25,1},{2,10},{10... | collective-permute-start | bytes 1572872 | tf_op jit(solution)/shard_map/ppermute | solution.py:273
  166.3 20.2 %collective-permute-start.45 = (bf16[128,2048]{1,0:T(8,128)(2,1)}, bf16[128,2048]{1,0:T(8,128)(2,1)S(1)}, u32[]{:S(2)}, u32[]{:S(2)}) collective-permute-start(bf16[128,2048]{1,0:T(8,128)(2,1)} %collective-permute-done.34.refs_1_), channel_id=1, source_target_pairs={{0,1},{1,0},{2,3},{3,2},{4,5},{5,4},{6,7},{7,6},{8,9},{9,8},{10,11... | collective-permute-start | bytes 1572872 | tf_op jit(solution)/shard_map/ppermute | solution.py:291
  166.7 19.8 %collective-permute-start.46 = (bf16[128,2048]{1,0:T(8,128)(2,1)}, bf16[128,2048]{1,0:T(8,128)(2,1)S(1)}, u32[]{:S(2)}, u32[]{:S(2)}) collective-permute-start(bf16[128,2048]{1,0:T(8,128)(2,1)} %collective-permute-done.34.refs_1_), channel_id=1, source_target_pairs={{0,2},{2,0},{1,3},{3,1},{4,6},{6,4},{5,7},{7,5},{8,10},{10,8},{9,1... | collective-permute-start | bytes 1572872 | tf_op jit(solution)/shard_map/ppermute | solution.py:286
  168.2 18.2 %collective-permute-start.44 = (bf16[128,2048]{1,0:T(8,128)(2,1)}, bf16[128,2048]{1,0:T(8,128)(2,1)S(1)}, u32[]{:S(2)}, u32[]{:S(2)}) collective-permute-start(bf16[128,2048]{1,0:T(8,128)(2,1)} %collective-permute-done.35.refs_4_), channel_id=1, source_target_pairs={{0,1},{1,0},{2,3},{3,2},{4,5},{5,4},{6,7},{7,6},{8,9},{9,8},{10,11... | collective-permute-start | bytes 1572872 | tf_op jit(solution)/shard_map/ppermute | solution.py:291
  168.3 18.2 %collective-permute-start.47 = (bf16[128,2048]{1,0:T(8,128)(2,1)}, bf16[128,2048]{1,0:T(8,128)(2,1)}, u32[]{:S(2)}, u32[]{:S(2)}) collective-permute-start(bf16[128,2048]{1,0:T(8,128)(2,1)} %collective-permute-done.35.refs_4_), channel_id=1, source_target_pairs={{0,4},{4,0},{1,5},{5,1},{2,6},{6,2},{3,7},{7,3},{8,12},{12,8},{9,1... | collective-permute-start | bytes 1572872 | tf_op jit(solution)/shard_map/ppermute | solution.py:278
  168.9 17.7 %collective-permute-start.48 = (bf16[128,2048]{1,0:T(8,128)(2,1)}, bf16[128,2048]{1,0:T(8,128)(2,1)S(1)}, u32[]{:S(2)}, u32[]{:S(2)}) collective-permute-start(bf16[128,2048]{1,0:T(8,128)(2,1)} %collective-permute-done.35.refs_4_), channel_id=1, source_target_pairs={{0,8},{8,16},{16,24},{24,0},{1,9},{9,17},{17,25},{25,1},{2,10},{10... | collective-permute-start | bytes 1572872 | tf_op jit(solution)/shard_map/ppermute | solution.py:273
  186.5 14.0 %collective-permute-start.49 = (bf16[128,2048]{1,0:T(8,128)(2,1)S(1)}, bf16[128,2048]{1,0:T(8,128)(2,1)S(1)}, u32[]{:S(2)}, u32[]{:S(2)}) collective-permute-start(bf16[128,2048]{1,0:T(8,128)(2,1)S(1)} %collective-permute-done.48.refs_6_), channel_id=1, source_target_pairs={{0,4},{4,0},{1,5},{5,1},{2,6},{6,2},{3,7},{7,3},{8,12},{12,8},{9,1... | collective-permute-start | bytes 1572872 | tf_op jit(solution)/shard_map/ppermute | solution.py:278
  252.7 25.6 %collective-permute-start.56 = (bf16[4,128,4096]{2,1,0:T(8,128)(2,1)}, bf16[4,128,4096]{2,1,0:T(8,128)(2,1)}, u32[]{:S(2)}, u32[]{:S(2)}) collective-permute-start(bf16[4,128,4096]{2,1,0:T(8,128)(2,1)} %get-tuple-element.1095), channel_id=1, source_target_pairs={{0,1},{1,0},{2,3},{3,2},{4,5},{5,4},{6,7},{7,6},{8,9},{9,8},{10,11... | collective-permute-start | bytes 12582920 | tf_op jit(solution)/shard_map/ppermute | solution.py:934
  253.1 25.3 %collective-permute-start.55 = (bf16[1,128,4096]{2,1,0:T(8,128)(2,1)S(1)}, bf16[1,128,4096]{2,1,0:T(8,128)(2,1)S(1)}, u32[]{:S(2)}, u32[]{:S(2)}) collective-permute-start(bf16[1,128,4096]{2,1,0:T(8,128)(2,1)S(1)} %add_convert_fusion.5), channel_id=1, source_target_pairs={{0,4},{4,0},{1,5},{5,1},{2,6},{6,2},{3,7},{7,3},{8,12},{12,8},{9,1... | collective-permute-start | bytes 3145736 | tf_op jit(solution)/shard_map/ppermute | solution.py:950
  287.3 25.6 %collective-permute-start.60 = (bf16[1,128,4096]{2,1,0:T(8,128)(2,1)S(1)}, bf16[1,128,4096]{2,1,0:T(8,128)(2,1)}, u32[]{:S(2)}, u32[]{:S(2)}) collective-permute-start(bf16[1,128,4096]{2,1,0:T(8,128)(2,1)S(1)} %get-tuple-element.1132), channel_id=1, source_target_pairs={{0,4},{4,0},{1,5},{5,1},{2,6},{6,2},{3,7},{7,3},{8,12},{12,8},{9,1... | collective-permute-start | bytes 3145736 | tf_op jit(solution)/shard_map/ppermute | solution.py:950
  288.9 27.6 %collective-permute-start.61 = (bf16[128,4096]{1,0:T(8,128)(2,1)}, bf16[128,4096]{1,0:T(8,128)(2,1)}, u32[]{:S(2)}, u32[]{:S(2)}) collective-permute-start(bf16[128,4096]{1,0:T(8,128)(2,1)} %fusion.3), channel_id=1, source_target_pairs={{0,8},{8,16},{16,24},{24,0},{1,9},{9,17},{17,25},{25,1},{2,10},{10... | collective-permute-start | bytes 3145736 | tf_op jit(solution)/shard_map/ppermute | solution.py:964
  289.6 22.5 %collective-permute-start.62 = (bf16[512,128]{1,0:T(8,128)(2,1)S(1)}, bf16[512,128]{1,0:T(8,128)(2,1)S(1)}, u32[]{:S(2)}, u32[]{:S(2)}) collective-permute-start(bf16[512,128]{1,0:T(8,128)(2,1)S(1)} %copy-done.86), channel_id=1, source_target_pairs={{0,1},{1,0},{2,3},{3,2},{4,5},{5,4},{6,7},{7,6},{8,9},{9,8},{10,11... | collective-permute-start | bytes 393224 | tf_op jit(solution)/shard_map/ppermute | solution.py:1163
  289.6 22.5 %collective-permute-start.63 = (bf16[512,128]{1,0:T(8,128)(2,1)S(1)}, bf16[512,128]{1,0:T(8,128)(2,1)S(1)}, u32[]{:S(2)}, u32[]{:S(2)}) collective-permute-start(bf16[512,128]{1,0:T(8,128)(2,1)S(1)} %copy-done.85), channel_id=1, source_target_pairs={{0,2},{2,0},{1,3},{3,1},{4,6},{6,4},{5,7},{7,5},{8,10},{10,8},{9,1... | collective-permute-start | bytes 393224 | tf_op jit(solution)/shard_map/ppermute | solution.py:1164
  290.2 21.9 %collective-permute-start.64 = (bf16[512,128]{1,0:T(8,128)(2,1)S(1)}, bf16[512,128]{1,0:T(8,128)(2,1)S(1)}, u32[]{:S(2)}, u32[]{:S(2)}) collective-permute-start(bf16[512,128]{1,0:T(8,128)(2,1)S(1)} %copy-done.84), channel_id=1, source_target_pairs={{0,3},{1,2},{2,1},{3,0},{4,7},{5,6},{6,5},{7,4},{8,11},{9,10},{10,... | collective-permute-start | bytes 393224 | tf_op jit(solution)/shard_map/ppermute | solution.py:1165
  320.0 26.3 %collective-permute-start.69 = (bf16[128,4096]{1,0:T(8,128)(2,1)}, bf16[128,4096]{1,0:T(8,128)(2,1)S(1)}, u32[]{:S(2)}, u32[]{:S(2)}) collective-permute-start(bf16[128,4096]{1,0:T(8,128)(2,1)} %fusion.2), channel_id=1, source_target_pairs={{0,8},{8,16},{16,24},{24,0},{1,9},{9,17},{17,25},{25,1},{2,10},{10... | collective-permute-start | bytes 3145736 | tf_op jit(solution)/shard_map/ppermute | solution.py:964
  320.1 26.3 %collective-permute-start.68 = (bf16[1,128,4096]{2,1,0:T(8,128)(2,1)S(1)}, bf16[1,128,4096]{2,1,0:T(8,128)(2,1)}, u32[]{:S(2)}, u32[]{:S(2)}) collective-permute-start(bf16[1,128,4096]{2,1,0:T(8,128)(2,1)S(1)} %get-tuple-element.1145), channel_id=1, source_target_pairs={{0,4},{4,0},{1,5},{5,1},{2,6},{6,2},{3,7},{7,3},{8,12},{12,8},{9,1... | collective-permute-start | bytes 3145736 | tf_op jit(solution)/shard_map/ppermute | solution.py:950
  321.0 22.5 %collective-permute-start.65 = (bf16[512,384]{1,0:T(8,128)(2,1)}, bf16[512,384]{1,0:T(8,128)(2,1)S(1)}, u32[]{:S(2)}, u32[]{:S(2)}) collective-permute-start(bf16[512,384]{1,0:T(8,128)(2,1)} %get-tuple-element.1153), channel_id=1, source_target_pairs={{0,1},{1,0},{2,3},{3,2},{4,5},{5,4},{6,7},{7,6},{8,9},{9,8},{10,11... | collective-permute-start | bytes 1179656 | tf_op jit(solution)/shard_map/ppermute | solution.py:1163
  321.0 22.5 %collective-permute-start.66 = (bf16[512,384]{1,0:T(8,128)(2,1)}, bf16[512,384]{1,0:T(8,128)(2,1)S(1)}, u32[]{:S(2)}, u32[]{:S(2)}) collective-permute-start(bf16[512,384]{1,0:T(8,128)(2,1)} %get-tuple-element.1154), channel_id=1, source_target_pairs={{0,2},{2,0},{1,3},{3,1},{4,6},{6,4},{5,7},{7,5},{8,10},{10,8},{9,1... | collective-permute-start | bytes 1179656 | tf_op jit(solution)/shard_map/ppermute | solution.py:1164
  321.8 21.7 %collective-permute-start.67 = (bf16[512,384]{1,0:T(8,128)(2,1)}, bf16[512,384]{1,0:T(8,128)(2,1)}, u32[]{:S(2)}, u32[]{:S(2)}) collective-permute-start(bf16[512,384]{1,0:T(8,128)(2,1)} %get-tuple-element.1155), channel_id=1, source_target_pairs={{0,3},{1,2},{2,1},{3,0},{4,7},{5,6},{6,5},{7,4},{8,11},{9,10},{10,... | collective-permute-start | bytes 1179656 | tf_op jit(solution)/shard_map/ppermute | solution.py:1165
  349.5 25.6 %collective-permute-start.74 = (bf16[128,4096]{1,0:T(8,128)(2,1)}, bf16[128,4096]{1,0:T(8,128)(2,1)S(1)}, u32[]{:S(2)}, u32[]{:S(2)}) collective-permute-start(bf16[128,4096]{1,0:T(8,128)(2,1)} %fusion.1), channel_id=1, source_target_pairs={{0,8},{8,16},{16,24},{24,0},{1,9},{9,17},{17,25},{25,1},{2,10},{10... | collective-permute-start | bytes 3145736 | tf_op jit(solution)/shard_map/ppermute | solution.py:964
  349.7 25.5 %collective-permute-start.73 = (bf16[1,128,4096]{2,1,0:T(8,128)(2,1)S(1)}, bf16[1,128,4096]{2,1,0:T(8,128)(2,1)S(1)}, u32[]{:S(2)}, u32[]{:S(2)}) collective-permute-start(bf16[1,128,4096]{2,1,0:T(8,128)(2,1)S(1)} %get-tuple-element.1165), channel_id=1, source_target_pairs={{0,4},{4,0},{1,5},{5,1},{2,6},{6,2},{3,7},{7,3},{8,12},{12,8},{9,1... | collective-permute-start | bytes 3145736 | tf_op jit(solution)/shard_map/ppermute | solution.py:950
  356.1 19.1 %collective-permute-start.72 = (bf16[512,384]{1,0:T(8,128)(2,1)}, bf16[512,384]{1,0:T(8,128)(2,1)}, u32[]{:S(2)}, u32[]{:S(2)}) collective-permute-start(bf16[512,384]{1,0:T(8,128)(2,1)} %get-tuple-element.1174), channel_id=1, source_target_pairs={{0,3},{1,2},{2,1},{3,0},{4,7},{5,6},{6,5},{7,4},{8,11},{9,10},{10,... | collective-permute-start | bytes 1179656 | tf_op jit(solution)/shard_map/ppermute | solution.py:1165
  383.5 22.6 %collective-permute-start.79 = (bf16[4,128,768]{2,1,0:T(8,128)(2,1)}, bf16[4,128,768]{2,1,0:T(8,128)(2,1)S(1)}, u32[]{:S(2)}, u32[]{:S(2)}) collective-permute-start(bf16[4,128,768]{2,1,0:T(8,128)(2,1)} %add_convert_fusion.7), channel_id=1, source_target_pairs={{0,4},{4,0},{1,5},{5,1},{2,6},{6,2},{3,7},{7,3},{8,12},{12,8},{9,1... | collective-permute-start | bytes 2359304 | tf_op jit(solution)/shard_map/ppermute | solution.py:950
  411.7 25.4 %collective-permute-start.86 = (bf16[128,4096]{1,0:T(8,128)(2,1)S(1)}, bf16[128,4096]{1,0:T(8,128)(2,1)S(1)}, u32[]{:S(2)}, u32[]{:S(2)}) collective-permute-start(bf16[128,4096]{1,0:T(8,128)(2,1)S(1)} %fusion), channel_id=1, source_target_pairs={{0,2},{2,0},{1,3},{3,1},{4,6},{6,4},{5,7},{7,5},{8,10},{10,8},{9,1... | collective-permute-start | bytes 3145736 | tf_op jit(solution)/shard_map/ppermute | solution.py:1000
  412.7 20.4 %collective-permute-start.85 = (bf16[4,128,768]{2,1,0:T(8,128)(2,1)S(1)}, bf16[4,128,768]{2,1,0:T(8,128)(2,1)S(1)}, u32[]{:S(2)}, u32[]{:S(2)}) collective-permute-start(bf16[4,128,768]{2,1,0:T(8,128)(2,1)S(1)} %add_convert_fusion.6), channel_id=1, source_target_pairs={{0,4},{4,0},{1,5},{5,1},{2,6},{6,2},{3,7},{7,3},{8,12},{12,8},{9,1... | collective-permute-start | bytes 2359304 | tf_op jit(solution)/shard_map/ppermute | solution.py:950
  417.2 15.9 %collective-permute-start.88 = (bf16[128,768]{1,0:T(8,128)(2,1)S(1)}, bf16[128,768]{1,0:T(8,128)(2,1)S(1)}, u32[]{:S(2)}, u32[]{:S(2)}) collective-permute-start(bf16[128,768]{1,0:T(8,128)(2,1)S(1)} %get-tuple-element.1263), channel_id=1, source_target_pairs={{0,16},{8,24},{16,0},{24,8},{1,17},{9,25},{17,1},{25,9},{2,18},{10... | collective-permute-start | bytes 589832 | tf_op jit(solution)/shard_map/ppermute | solution.py:987
  417.2 15.9 %collective-permute-start.89 = (bf16[128,768]{1,0:T(8,128)(2,1)S(1)}, bf16[128,768]{1,0:T(8,128)(2,1)S(1)}, u32[]{:S(2)}, u32[]{:S(2)}) collective-permute-start(bf16[128,768]{1,0:T(8,128)(2,1)S(1)} %get-tuple-element.1264), channel_id=1, source_target_pairs={{0,8},{8,16},{16,24},{24,0},{1,9},{9,17},{17,25},{25,1},{2,10},{10... | collective-permute-start | bytes 589832 | tf_op jit(solution)/shard_map/ppermute | solution.py:987
  437.4 23.0 %collective-permute-start.90 = (bf16[128,4096]{1,0:T(8,128)(2,1)S(1)}, bf16[128,4096]{1,0:T(8,128)(2,1)S(1)}, u32[]{:S(2)}, u32[]{:S(2)}) collective-permute-start(bf16[128,4096]{1,0:T(8,128)(2,1)S(1)} %add_convert_fusion), channel_id=1, source_target_pairs={{0,1},{1,0},{2,3},{3,2},{4,5},{5,4},{6,7},{7,6},{8,9},{9,8},{10,11... | collective-permute-start | bytes 3145736 | tf_op jit(solution)/shard_map/ppermute | solution.py:1006
  437.7 22.7 %collective-permute-start.95 = (bf16[4,128,512]{2,1,0:T(8,128)(2,1)S(1)}, bf16[4,128,512]{2,1,0:T(8,128)(2,1)}, u32[]{:S(2)}, u32[]{:S(2)}) collective-permute-start(bf16[4,128,512]{2,1,0:T(8,128)(2,1)S(1)} %add_convert_fusion.8), channel_id=1, source_target_pairs={{0,4},{4,0},{1,5},{5,1},{2,6},{6,2},{3,7},{7,3},{8,12},{12,8},{9,1... | collective-permute-start | bytes 1572872 | tf_op jit(solution)/shard_map/ppermute | solution.py:950
  444.0 16.3 %collective-permute-start.92 = (bf16[128,768]{1,0:T(8,128)(2,1)S(1)}, bf16[128,768]{1,0:T(8,128)(2,1)}, u32[]{:S(2)}, u32[]{:S(2)}) collective-permute-start(bf16[128,768]{1,0:T(8,128)(2,1)S(1)} %get-tuple-element.1340), channel_id=1, source_target_pairs={{0,16},{8,24},{16,0},{24,8},{1,17},{9,25},{17,1},{25,9},{2,18},{10... | collective-permute-start | bytes 589832 | tf_op jit(solution)/shard_map/ppermute | solution.py:987
  446.2 14.1 %collective-permute-start.93 = (bf16[128,768]{1,0:T(8,128)(2,1)S(1)}, bf16[128,768]{1,0:T(8,128)(2,1)}, u32[]{:S(2)}, u32[]{:S(2)}) collective-permute-start(bf16[128,768]{1,0:T(8,128)(2,1)S(1)} %get-tuple-element.1339), channel_id=1, source_target_pairs={{0,8},{8,16},{16,24},{24,0},{1,9},{9,17},{17,25},{25,1},{2,10},{10... | collective-permute-start | bytes 589832 | tf_op jit(solution)/shard_map/ppermute | solution.py:987
  462.7 14.8 %collective-permute-start.100 = (bf16[128,512]{1,0:T(8,128)(2,1)}, bf16[128,512]{1,0:T(8,128)(2,1)S(1)}, u32[]{:S(2)}, u32[]{:S(2)}) collective-permute-start(bf16[128,512]{1,0:T(8,128)(2,1)} %get-tuple-element.1349), channel_id=1, source_target_pairs={{0,8},{8,16},{16,24},{24,0},{1,9},{9,17},{17,25},{25,1},{2,10},{10... | collective-permute-start | bytes 393224 | tf_op jit(solution)/shard_map/ppermute | solution.py:987
  (153 other events, 1678.6 us)
